TPU v7x, 32 devices: a whole 2x2x4 slice. The times are simulated.
32 devices in a mesh: dp: 8 (over y, x, core), tensor: 4 (over z).
Axes of the slice: x: 2, y: 2, z: 4, core: 2. Of those that a mesh axis runs over, the one named last changes fastest.
Arguments:
- tokens: bfloat16 [8192, 2048], P('dp'), may hold values from -6 to 6
- cotangent: bfloat16 [8192, 2048], P('dp'), may hold values from -6 to 6
- segment_ids: int32 [8, 1024], P('dp'), may hold values from 0 to 2, never falling along the last dimension, each value on 1 to 768 neighbouring positions
- step_count: int32 [1], replicated, may hold values from 2 to 4
- norm_gains: float32 [2, 2048], P(None, 'dp'), may hold values from 0.5 to 1.5
- gains_first: float32 [2, 2048], P(None, 'dp'), may hold values from -0.0004272461 to 0.0004272461
- gains_second: float32 [2, 2048], P(None, 'dp'), may hold values from 9.5358565e-09 to 1.5211961e-07
- w_query: float32 [2048, 2048], P('dp', 'tensor'), may hold values from -0.125 to 0.125
- query_first: float32 [2048, 2048], P('dp', 'tensor'), may hold values from -0.00015258789 to 0.00015258789
- query_second: float32 [2048, 2048], P('dp', 'tensor'), may hold values from 1.4757873e-09 to 2.3839641e-08
- w_keyval: float32 [2, 2048, 256], P(None, 'dp', 'tensor'), may hold values from -0.125 to 0.125
- keyval_first: float32 [2, 2048, 256], P(None, 'dp', 'tensor'), may hold values from -0.0004272461 to 0.0004272461
- keyval_second: float32 [2, 2048, 256], P(None, 'dp', 'tensor'), may hold values from 1.0353215e-08 to 1.6710453e-07
- w_out: float32 [2048, 2048], P('tensor', 'dp'), may hold values from -1.5 to 1.5
- out_first: float32 [2048, 2048], P('tensor', 'dp'), may hold values from -1.5258789e-05 to 1.5258789e-05
- out_second: float32 [2048, 2048], P('tensor', 'dp'), may hold values from 1.7709447e-11 to 2.860757e-10
- w_gateup: float32 [2, 2048, 5632], P(None, 'dp', 'tensor'), may hold values from -0.125 to 0.125
- gateup_first: float32 [2, 2048, 5632], P(None, 'dp', 'tensor'), may hold values from -5.340576e-05 to 5.340576e-05
- gateup_second: float32 [2, 2048, 5632], P(None, 'dp', 'tensor'), may hold values from 1.4757873e-10 to 2.3839641e-09
- w_down: float32 [5632, 2048], P('tensor', 'dp'), may hold values from -0.15625 to 0.15625
- down_first: float32 [5632, 2048], P('tensor', 'dp'), may hold values from -4.5776367e-05 to 4.5776367e-05
- down_second: float32 [5632, 2048], P('tensor', 'dp'), may hold values from 1.1806298e-10 to 1.9071713e-09
Outputs:
- layer_out: bfloat16 [8192, 2048], P('dp')
- input_grad: float32 [8192, 2048], P('dp')
- grad_norm: float32 [1], replicated
- gains_moment: float32 [2, 2048], P(None, 'dp')
- gains_square: float32 [2, 2048], P(None, 'dp')
- gains_new: float32 [2, 2048], P(None, 'dp')
- query_moment: float32 [2048, 2048], P('dp', 'tensor')
- query_square: float32 [2048, 2048], P('dp', 'tensor')
- query_new: float32 [2048, 2048], P('dp', 'tensor')
- keyval_moment: float32 [2, 2048, 256], P(None, 'dp', 'tensor')
- keyval_square: float32 [2, 2048, 256], P(None, 'dp', 'tensor')
- keyval_new: float32 [2, 2048, 256], P(None, 'dp', 'tensor')
- out_moment: float32 [2048, 2048], P('tensor', 'dp')
- out_square: float32 [2048, 2048], P('tensor', 'dp')
- out_new: float32 [2048, 2048], P('tensor', 'dp')
- gateup_moment: float32 [2, 2048, 5632], P(None, 'dp', 'tensor')
- gateup_square: float32 [2, 2048, 5632], P(None, 'dp', 'tensor')
- gateup_new: float32 [2, 2048, 5632], P(None, 'dp', 'tensor')
- down_moment: float32 [5632, 2048], P('tensor', 'dp')
- down_square: float32 [5632, 2048], P('tensor', 'dp')
- down_new: float32 [5632, 2048], P('tensor', 'dp')
Inputs may be any that keep to these rules, and one draw needn't show every extreme that they name: `segment_ids`: in each batch row the segment ids never fall, all 3 ids occur, and the longest sequence of a row has 768 tokens; a token attends to the earlier tokens of its own sequence only.
All inputs are finite; a program needn't handle non-finite values.
Results may differ from a plain program's by a relative error of at most 0.017.
Values may be sent and summed in bfloat16 or wider, within the bound.
A program may use at most 320 MiB of HBM per device.

v0:
```python
import jax
import jax.numpy as jnp
from jax import lax
from jax.sharding import PartitionSpec as P

HD = 64


norm_eps = 1e-05
beta_first = 0.9
beta_second = 0.95
adam_eps = 1e-08
weight_decay = 0.1
weight_rate = 0.02
out_rate = 0.1
gain_rate = 0.2
clip_limit = 1.0
masked_value = -1000000000.0


def positions(segment):
    length = segment.shape[0]
    indices = jnp.arange(length, dtype=jnp.int32)
    earlier = jnp.concatenate([segment[:1] - 1, segment[:-1]])
    begins = jnp.where(segment != earlier, indices, jnp.zeros_like(indices))
    return indices - lax.cummax(begins, axis=0)


def rotary_tables(places, width):
    half_width = width // 2
    frequency = jnp.power(10000.0, -jnp.arange(half_width, dtype=jnp.float32) * (2.0 / width))
    angles = places.astype(jnp.float32)[:, None] * frequency[None, :]
    cosine_table = jnp.concatenate([jnp.cos(angles), jnp.cos(angles)], axis=-1)
    sine_table = jnp.concatenate([jnp.sin(angles), jnp.sin(angles)], axis=-1)
    return (cosine_table, sine_table)


def rotate(values, cosine_table, sine_table):
    half_width = values.shape[-1] // 2
    turned = jnp.concatenate([-values[..., half_width:], values[..., :half_width]], axis=-1)
    return values * cosine_table[:, None, :] + turned * sine_table[:, None, :]


def unrotate(gradient, cosine_table, sine_table):
    half_width = gradient.shape[-1] // 2
    along_sine = gradient * sine_table[:, None, :]
    turned = jnp.concatenate([along_sine[..., half_width:], -along_sine[..., :half_width]], axis=-1)
    return gradient * cosine_table[:, None, :] + turned


def over_rows(left, right):
    return lax.dot_general(
        left, right, (((0,), (0,)), ((), ())), preferred_element_type=jnp.float32
    )


def against(left, right):
    return lax.dot_general(
        left, right, (((1,), (1,)), ((), ())), preferred_element_type=jnp.float32
    )


def norm_back(grad_output, unit_rows, inverse, gain):
    scaled = grad_output * gain
    gain_grad = jnp.sum(grad_output * unit_rows, axis=0)
    inner_mean = jnp.mean(scaled * unit_rows, axis=-1, keepdims=True)
    return (inverse * (scaled - unit_rows * inner_mean), gain_grad)


def adam_step(weight, first, second, gradient, clip_factor, step_float, step_rate, decay_rate):
    gradient = gradient * clip_factor
    first = beta_first * first + (1.0 - beta_first) * gradient
    second = beta_second * second + (1.0 - beta_second) * gradient * gradient
    correct_one = 1.0 - jnp.power(beta_first, step_float)
    correct_two = 1.0 - jnp.power(beta_second, step_float)
    update = first / correct_one / (jnp.sqrt(second / correct_two) + adam_eps)
    return (first, second, weight - step_rate * (update + decay_rate * weight))


def on_device(
    tokens,
    cotangent,
    segment_ids,
    step_count,
    norm_gains,
    gains_first,
    gains_second,
    w_query,
    query_first,
    query_second,
    w_keyval,
    keyval_first,
    keyval_second,
    w_out,
    out_first,
    out_second,
    w_gateup,
    gateup_first,
    gateup_second,
    w_down,
    down_first,
    down_second,
):
    gathered = (
        lax.all_gather(norm_gains.astype(jnp.bfloat16), "dp", axis=1, tiled=True),
        lax.all_gather(w_query.astype(jnp.bfloat16), "dp", axis=0, tiled=True),
        lax.all_gather(w_keyval.astype(jnp.bfloat16), "dp", axis=1, tiled=True),
        lax.all_gather(w_out.astype(jnp.bfloat16), "dp", axis=1, tiled=True),
        lax.all_gather(w_gateup.astype(jnp.bfloat16), "dp", axis=1, tiled=True),
        lax.all_gather(w_down.astype(jnp.bfloat16), "dp", axis=1, tiled=True),
    )
    gain_rows, query_weight, keyval_weight, out_weight, gateup_weight, down_weight = gathered
    gain_values = gain_rows.astype(jnp.float32)
    length = tokens.shape[0]
    segment = segment_ids[0]
    local_heads = query_weight.shape[1] // HD
    local_groups = keyval_weight.shape[2] // HD
    group_size = local_heads // local_groups
    cosine_table, sine_table = rotary_tables(positions(segment), HD)
    indices = jnp.arange(length, dtype=jnp.int32)
    block_rows = min(512, length)
    starts = jnp.arange(length // block_rows, dtype=jnp.int32) * block_rows
    inverse_scale = HD ** (-0.5)
    values_in = tokens.astype(jnp.float32)
    inverse_one = lax.rsqrt(jnp.mean(values_in * values_in, axis=-1, keepdims=True) + norm_eps)
    unit_one = values_in * inverse_one
    normed_one = (unit_one * gain_values[0]).astype(jnp.bfloat16)
    query_raw = jnp.dot(normed_one, query_weight, preferred_element_type=jnp.float32)
    queries = rotate(query_raw.reshape(length, local_heads, HD), cosine_table, sine_table).astype(
        jnp.bfloat16
    )
    queries = queries.reshape(length, local_groups, group_size, HD)
    keyval_raw = jnp.einsum(
        "nd,sdk->snk", normed_one, keyval_weight, preferred_element_type=jnp.float32
    )
    key_rows = rotate(
        keyval_raw[0].reshape(length, local_groups, HD), cosine_table, sine_table
    ).astype(jnp.bfloat16)
    value_rows = keyval_raw[1].reshape(length, local_groups, HD).astype(jnp.bfloat16)

    def block_scores(start):
        query_block = lax.dynamic_slice_in_dim(queries, start, block_rows, 0)
        segment_block = lax.dynamic_slice_in_dim(segment, start, block_rows, 0)
        row_index = start + jnp.arange(block_rows, dtype=jnp.int32)
        allowed = (segment_block[:, None] == segment[None, :]) & (
            row_index[:, None] >= indices[None, :]
        )
        raw_scores = jnp.einsum(
            "qkgh,pkh->kgqp", query_block, key_rows, preferred_element_type=jnp.float32
        )
        return (query_block, jnp.where(allowed, raw_scores * inverse_scale, masked_value))

    def forward_block(start):
        query_block, scaled = block_scores(start)
        highest = jnp.max(scaled, axis=-1, keepdims=True)
        lifted = jnp.exp(scaled - highest)
        row_total = jnp.sum(lifted, axis=-1, keepdims=True)
        soft_weights = (lifted / row_total).astype(jnp.bfloat16)
        mixed = jnp.einsum(
            "kgqp,pkh->qkgh", soft_weights, value_rows, preferred_element_type=jnp.float32
        )
        return (
            mixed.astype(jnp.bfloat16).reshape(block_rows, local_heads * HD),
            (highest + jnp.log(row_total))[..., 0],
        )

    mixed_blocks, logsum_blocks = lax.map(forward_block, starts)
    mixture = mixed_blocks.reshape(length, local_heads * HD)
    branch_partial = jnp.dot(mixture, out_weight, preferred_element_type=jnp.float32)
    branch = lax.psum(branch_partial, "tensor")
    middle = values_in + branch
    inverse_two = lax.rsqrt(jnp.mean(middle * middle, axis=-1, keepdims=True) + norm_eps)
    unit_two = middle * inverse_two
    normed_two = (unit_two * gain_values[1]).astype(jnp.bfloat16)
    gateup = jnp.einsum(
        "nd,sdf->snf", normed_two, gateup_weight, preferred_element_type=jnp.float32
    )
    hidden = (jax.nn.silu(gateup[0]) * gateup[1]).astype(jnp.bfloat16)
    feed_out = lax.psum(
        jnp.dot(hidden, down_weight, preferred_element_type=jnp.float32).astype(jnp.bfloat16),
        "tensor",
    ).astype(jnp.float32)
    layer_out = (middle + feed_out).astype(jnp.bfloat16)
    regathered = (
        lax.all_gather(norm_gains.astype(jnp.bfloat16), "dp", axis=1, tiled=True),
        lax.all_gather(w_query.astype(jnp.bfloat16), "dp", axis=0, tiled=True),
        lax.all_gather(w_keyval.astype(jnp.bfloat16), "dp", axis=1, tiled=True),
        lax.all_gather(w_out.astype(jnp.bfloat16), "dp", axis=1, tiled=True),
        lax.all_gather(w_gateup.astype(jnp.bfloat16), "dp", axis=1, tiled=True),
        lax.all_gather(w_down.astype(jnp.bfloat16), "dp", axis=1, tiled=True),
    )
    gain_rows, query_weight, keyval_weight, out_weight, gateup_weight, down_weight = regathered
    gain_values = gain_rows.astype(jnp.float32)
    grad_down_weight = over_rows(hidden, cotangent)
    grad_hidden = against(cotangent, down_weight)
    gate_values = gateup[0]
    up_values = gateup[1]
    sigmoid_gate = jax.nn.sigmoid(gate_values)
    grad_gate = grad_hidden * up_values * sigmoid_gate * (1.0 + gate_values * (1.0 - sigmoid_gate))
    grad_up = grad_hidden * gate_values * sigmoid_gate
    grad_gateup = jnp.stack([grad_gate, grad_up]).astype(jnp.bfloat16)
    grad_gateup_weight = jnp.einsum(
        "nd,snf->sdf", normed_two, grad_gateup, preferred_element_type=jnp.float32
    )
    partial_two = jnp.einsum(
        "snf,sdf->nd", grad_gateup, gateup_weight, preferred_element_type=jnp.float32
    )
    grad_normed_two = lax.psum(partial_two, "tensor")
    grad_from_two, gain_grad_two = norm_back(grad_normed_two, unit_two, inverse_two, gain_values[1])
    grad_middle = cotangent.astype(jnp.float32) + grad_from_two
    grad_branch = grad_middle.astype(jnp.bfloat16)
    grad_out_weight = over_rows(mixture, grad_branch)
    grad_mixture = (
        against(grad_branch, out_weight)
        .astype(jnp.bfloat16)
        .reshape(length, local_groups, group_size, HD)
    )

    def backward_block(carried, pieces):
        start, logsum = pieces
        query_block, scaled = block_scores(start)
        soft_weights = jnp.exp(scaled - logsum[..., None])
        grad_block = lax.dynamic_slice_in_dim(grad_mixture, start, block_rows, 0)
        grad_soft = jnp.einsum(
            "qkgh,pkh->kgqp", grad_block, value_rows, preferred_element_type=jnp.float32
        )
        spread = jnp.sum(soft_weights * grad_soft, axis=-1, keepdims=True)
        grad_scores = (soft_weights * (grad_soft - spread) * inverse_scale).astype(jnp.bfloat16)
        grad_query = jnp.einsum(
            "kgqp,pkh->qkgh", grad_scores, key_rows, preferred_element_type=jnp.float32
        )
        grad_key = carried[0] + jnp.einsum(
            "kgqp,qkgh->pkh", grad_scores, query_block, preferred_element_type=jnp.float32
        )
        grad_value = carried[1] + jnp.einsum(
            "kgqp,qkgh->pkh",
            soft_weights.astype(jnp.bfloat16),
            grad_block,
            preferred_element_type=jnp.float32,
        )
        return ((grad_key, grad_value), grad_query)

    zero_rows = jnp.zeros((length, local_groups, HD), jnp.float32)
    (grad_keys, grad_values), grad_queries = lax.scan(
        backward_block, (zero_rows, zero_rows), (starts, logsum_blocks)
    )
    grad_queries = grad_queries.reshape(length, local_heads, HD)
    grad_query_raw = (
        unrotate(grad_queries, cosine_table, sine_table)
        .astype(jnp.bfloat16)
        .reshape(length, local_heads * HD)
    )
    grad_key_raw = unrotate(grad_keys, cosine_table, sine_table).reshape(length, local_groups * HD)
    grad_keyval = jnp.stack([grad_key_raw, grad_values.reshape(length, local_groups * HD)]).astype(
        jnp.bfloat16
    )
    grad_query_weight = over_rows(normed_one, grad_query_raw)
    grad_keyval_weight = jnp.einsum(
        "nd,snk->sdk", normed_one, grad_keyval, preferred_element_type=jnp.float32
    )
    partial_one = against(grad_query_raw, query_weight) + jnp.einsum(
        "snk,sdk->nd", grad_keyval, keyval_weight, preferred_element_type=jnp.float32
    )
    grad_normed_one = lax.psum(partial_one.astype(jnp.bfloat16), "tensor").astype(jnp.float32)
    grad_from_one, gain_grad_one = norm_back(grad_normed_one, unit_one, inverse_one, gain_values[0])
    input_grad = grad_middle + grad_from_one
    gain_grads = jnp.stack([gain_grad_one, gain_grad_two])
    reduced = (
        lax.psum_scatter(gain_grads, "dp", scatter_dimension=1, tiled=True),
        lax.psum_scatter(grad_query_weight, "dp", scatter_dimension=0, tiled=True),
        lax.psum_scatter(grad_keyval_weight, "dp", scatter_dimension=1, tiled=True),
        lax.psum_scatter(grad_out_weight, "dp", scatter_dimension=1, tiled=True),
        lax.psum_scatter(grad_gateup_weight, "dp", scatter_dimension=1, tiled=True),
        lax.psum_scatter(grad_down_weight, "dp", scatter_dimension=1, tiled=True),
    )
    first_owner = (lax.axis_index("tensor") == 0).astype(jnp.float32)
    local_square = first_owner * jnp.sum(reduced[0] * reduced[0]) + sum(
        (jnp.sum(g * g) for g in reduced[1:])
    )
    square_total = lax.psum(local_square, ("dp", "tensor"))
    grad_norm = jnp.sqrt(square_total)
    clip_factor = jnp.minimum(1.0, clip_limit / (grad_norm + 1e-06))
    step_float = step_count[0].astype(jnp.float32)
    params = (norm_gains, w_query, w_keyval, w_out, w_gateup, w_down)
    states = (
        (gains_first, gains_second),
        (query_first, query_second),
        (keyval_first, keyval_second),
        (out_first, out_second),
        (gateup_first, gateup_second),
        (down_first, down_second),
    )
    step_rates = (gain_rate, weight_rate, weight_rate, out_rate, weight_rate, weight_rate)
    decay_rates = (0.0, weight_decay, weight_decay, weight_decay, weight_decay, weight_decay)
    results = []
    for position_index in range(6):
        first, second = states[position_index]
        results.extend(
            adam_step(
                params[position_index],
                first,
                second,
                reduced[position_index],
                clip_factor,
                step_float,
                step_rates[position_index],
                decay_rates[position_index],
            )
        )
    return (
        layer_out,
        input_grad,
        grad_norm.reshape(1),
        results[0],
        results[1],
        results[2],
        results[3],
        results[4],
        results[5],
        results[6],
        results[7],
        results[8],
        results[9],
        results[10],
        results[11],
        results[12],
        results[13],
        results[14],
        results[15],
        results[16],
        results[17],
    )


def solution(mesh):
    in_specs = (
        P("dp", None),
        P("dp", None),
        P("dp", None),
        P(),
        P(None, "dp"),
        P(None, "dp"),
        P(None, "dp"),
        P("dp", "tensor"),
        P("dp", "tensor"),
        P("dp", "tensor"),
        P(None, "dp", "tensor"),
        P(None, "dp", "tensor"),
        P(None, "dp", "tensor"),
        P("tensor", "dp"),
        P("tensor", "dp"),
        P("tensor", "dp"),
        P(None, "dp", "tensor"),
        P(None, "dp", "tensor"),
        P(None, "dp", "tensor"),
        P("tensor", "dp"),
        P("tensor", "dp"),
        P("tensor", "dp"),
    )
    out_specs = (
        P("dp", None),
        P("dp", None),
        P(),
        P(None, "dp"),
        P(None, "dp"),
        P(None, "dp"),
        P("dp", "tensor"),
        P("dp", "tensor"),
        P("dp", "tensor"),
        P(None, "dp", "tensor"),
        P(None, "dp", "tensor"),
        P(None, "dp", "tensor"),
        P("tensor", "dp"),
        P("tensor", "dp"),
        P("tensor", "dp"),
        P(None, "dp", "tensor"),
        P(None, "dp", "tensor"),
        P(None, "dp", "tensor"),
        P("tensor", "dp"),
        P("tensor", "dp"),
        P("tensor", "dp"),
    )
    return jax.shard_map(
        on_device, mesh=mesh, in_specs=in_specs, out_specs=out_specs, check_vma=False
    )
```

profile of v0, /device:TPU:0, one launch (start us, length us, event | category | flops | bytes accessed | tf_op | source)
XLA Modules:
  0.0 1800.3 jit_solution(3728736641630619204)
XLA Ops:
  11.8 10.5 all_gather.24
  22.9 3.1 fusion.64
  26.0 14.2 all_gather.26
  45.1 5.4 fusion.111
  51.2 37.4 %while.28 = (s32[]{:T(128)}, bf16[2,512,512]{2,1,0:T(8,128)(2,1)}, f32[2,1,8,512]{3,2,1,0:T(8,128)}, s32[2]{0:T(128)S(1)}, s32[1024]{0:T(1024)S(1)}, /*index=5*/...) while((s32[]{:T(128)}, bf16[2,512,512]{2,1,0:T(8,128)(2,1)}, ...), condition=%wide.region_6.7_spmd.clone, body=%wide.region_3.6_spmd.clone.sunk | while | flops 1125904896 | bytes 64371432 | solution.py:167
  55.3 3.1 fusion.168
  58.4 4.4 fusion.169
  63.4 5.3 fusion.170
  73.9 3.2 fusion.168
  77.0 4.4 fusion.169
  82.0 5.3 fusion.170
  88.6 7.7 fusion.122
  96.4 3.2 convert_element_type.148
  100.6 287.2 %all-reduce.5.cloned.1.call-done = f32[1024,2048]{1,0:T(8,128)} async-done(((f32[1024,2048]{1,0:T(8,128)}), f32[1024,2048]{1,0:T(8,128)}) %all-reduce.5.cloned.1.call-update) | async-done | bytes 8388624 | tf_op jit(solution)/shard_map/psum | solution.py:170
  387.8 9.2 multiply_reduce_fusion.2
  397.0 59.8 %all-gather.9.cloned.1.call-done = bf16[2,2048,1408]{2,1,0:T(8,128)(2,1)} async-done(((bf16[2,256,1408]{2,1,0:T(8,128)(2,1)}), bf16[2,2048,1408]{2,1,0:T(8,128)(2,1)}) %all-gather.9.cloned.1.call-update) | async-done | bytes 11534352 | tf_op jit(solution)/shard_map/all_gather | solution.py:109
  456.9 20.5 %convolution_bitcast_fusion.3 = f32[2,1024,1408]{2,1,0:T(8,128)} fusion(bf16[2,2048,1408]{2,1,0:T(8,128)(2,1)} %all-gather.9.cloned.1.call-done, f32[1024,2048]{1,0:T(8,128)} %get-tuple-element.339, f32[2048]{0:T(1024)S(1)} %bitcast.364, f32[1024]{0:T(1024)S(1)} %add_rsqrt_fusion), kind=kOutput, calls=%fused_computation.85 | convolution fusion | flops 11817451520 | bytes 31469568 | tf_op jit(solution)/shard_map/nd,sdf->snf/dot_general | solution.py:175
  477.3 26.2 %all-gather.11.cloned.1.call-done = bf16[1408,2048]{1,0:T(8,128)(2,1)} async-done(((bf16[1408,256]{1,0:T(8,128)(2,1)}), bf16[1408,2048]{1,0:T(8,128)(2,1)}) %all-gather.11.cloned.1.call-update) | async-done | bytes 5767184 | tf_op jit(solution)/shard_map/all_gather | solution.py:110
  503.6 15.6 fusion.71
  521.7 17.0 convolution_bitcast_fusion.4
  538.8 11.0 convolution_convert_fusion
  549.9 279.9 %all-reduce.7.cloned.1.call-done = f32[1024,2048]{1,0:T(8,128)} async-done(((f32[1024,2048]{1,0:T(8,128)}), f32[1024,2048]{1,0:T(8,128)}) %all-reduce.7.cloned.1.call-update) | async-done | bytes 8388624 | tf_op jit(solution)/shard_map/psum | solution.py:208
  829.7 7.6 multiply_reduce_fusion
  839.1 4.7 multiply_add_fusion
  843.9 3.4 copy-done.1
  847.3 3.3 fusion.82
  850.6 129.5 %while.29 = (s32[]{:T(128)}, f32[1024,1,64]{0,2,1:T(8,128)}, f32[1024,1,64]{0,2,1:T(8,128)}, f32[2,512,1,8,64]{1,0,4,3,2:T(2,128)}, s32[2]{0:T(128)S(1)}, /*inde...) while((s32[]{:T(128)}, f32[1024,1,64]{0,2,1:T(8,128)}, ...), condition=%wide.region_14.15_spmd.clone, body=%wide.region_12.14_spmd.clone.sunk | while | flops 2728129024 | bytes 178878960 | solution.py:244
  855.2 3.6 fusion.179
  859.4 10.8 fusion.181
  870.2 7.3 fusion.182
  877.5 3.7 convolution_bitcast_fusion.6
  882.4 19.5 %dynamic_update_slice.22 = f32[2,512,1,8,64]{1,0,4,3,2:T(2,128)} dynamic-update-slice(f32[2,512,1,8,64]{1,0,4,3,2:T(2,128)} %get-tuple-element.553, f32[1,512,1,8,64]{1,0,4,3,2:T(1,128)S(1)} %copy.99, s32[]{:T(128)} %get-tuple-element.550, s32[]{:T(128)} %constant.54.clone.1..sunk.1, s32[]{:T(128)} %constant.54.clone.1..sunk.1, s32[]{:T(128)} %constant.54.clone.1..sunk.1, s32[]{:T(128)} %constant.54.clone.1..sunk.1) | dynamic-update-slice | bytes 2097156 | tf_op jit(solution)/shard_map/while/body/jit(dynamic_update_index_in_dim)/dynamic_update_slice | solution.py:244
  901.9 5.2 fusion.183
  907.1 7.5 fusion.184
  920.0 3.5 fusion.179
  924.1 10.8 fusion.181
  934.9 7.3 fusion.182
  942.2 3.7 convolution_bitcast_fusion.6
  947.1 19.5 %dynamic_update_slice.22 = f32[2,512,1,8,64]{1,0,4,3,2:T(2,128)} dynamic-update-slice(f32[2,512,1,8,64]{1,0,4,3,2:T(2,128)} %get-tuple-element.553, f32[1,512,1,8,64]{1,0,4,3,2:T(1,128)S(1)} %copy.99, s32[]{:T(128)} %get-tuple-element.550, s32[]{:T(128)} %constant.54.clone.1..sunk.1, s32[]{:T(128)} %constant.54.clone.1..sunk.1, s32[]{:T(128)} %constant.54.clone.1..sunk.1, s32[]{:T(128)} %constant.54.clone.1..sunk.1) | dynamic-update-slice | bytes 2097156 | tf_op jit(solution)/shard_map/while/body/jit(dynamic_update_index_in_dim)/dynamic_update_slice | solution.py:244
  966.6 5.2 fusion.183
  971.8 7.6 fusion.184
  982.2 3.5 reshape.481
  991.9 3.3 fusion.65
  995.8 4.6 fusion.72
  1000.5 6.9 fusion.107
  1008.6 7.8 fusion.78
  1016.4 269.4 %all-reduce.9.cloned.1.call-done = (bf16[1024,2048]{1,0:T(8,128)(2,1)}, bf16[1024,2048]{1,0:T(8,128)(2,1)}) async-done(((bf16[1024,2048]{1,0:T(8,128)(2,1)}, bf16[1024,2048]{1,0:T(8,128)(2,1)}), (bf16[1024,2048]{1,0:T(8,128)(2,1)}, bf16[1024,2048]{1,0:T(8,128)(2,1)})) %all-reduce.9.cloned.1.call-update) | async-done | bytes 8388624 | tf_op jit(solution)/shard_map/psum | solution.py:179
  1285.9 5.0 fusion.63
  1292.3 11.3 fusion.124
  1304.4 20.9 %convolution_bitcast_fusion.2 = f32[2,2048,1408]{1,2,0:T(8,128)} fusion(bf16[1,1024,1408]{2,1,0:T(8,128)(2,1)} %copy-done.62, bf16[1,1024,1408]{2,1,0:T(8,128)(2,1)} %copy-done.61, f32[1024,2048]{1,0:T(8,128)} %get-tuple-element.339, f32[2048]{0:T(1024)S(1)} %bitcast.367, f32[1024]{0:T(1024)S(1)} %copy-done.52), kind=kOutput, calls=%fused_computation.61 | convolution fusion | flops 11820335104 | bytes 37236736 | tf_op jit(solution)/shard_map/nd,snf->sdf/dot_general | solution.py:202
  1330.2 3.4 copy.68
  1337.4 42.0 %reduce-scatter.9.cloned.1.call-done = f32[256,512]{1,0:T(8,128)} async-done(((f32[2048,512]{1,0:T(8,128)}), f32[256,512]{1,0:T(8,128)}) %reduce-scatter.9.cloned.1.call-update) | async-done | bytes 524304 | tf_op jit(solution)/shard_map/reduce_scatter | solution.py:270
  1382.5 51.9 %reduce-scatter.13.cloned.1.call-done = f32[512,256]{1,0:T(8,128)} async-done(((f32[512,2048]{1,0:T(8,128)}), f32[512,256]{1,0:T(8,128)}) %reduce-scatter.13.cloned.1.call-update) | async-done | bytes 524304 | tf_op jit(solution)/shard_map/reduce_scatter | solution.py:272
  1436.8 9.5 fusion.60
  1446.2 27.9 %reduce-scatter.19.cloned.1.call-done = f32[256,2]{1,0:T(8,128)} async-done(((f32[2048,2]{1,0:T(8,128)}), f32[256,2]{1,0:T(8,128)}) %reduce-scatter.19.cloned.1.call-update) | async-done | bytes 2064
  1476.4 87.9 %reduce-scatter.17.cloned.1.call-done = f32[1408,256]{1,0:T(8,128)} async-done(((f32[1408,2048]{1,0:T(8,128)}), f32[1408,256]{1,0:T(8,128)}) %reduce-scatter.17.cloned.1.call-update) | async-done | bytes 1441808 | tf_op jit(solution)/shard_map/reduce_scatter | solution.py:274
  1566.6 147.2 %reduce-scatter.15.cloned.1.call-done = f32[2,256,1408]{1,2,0:T(8,128)} async-done(((f32[2,2048,1408]{1,2,0:T(8,128)}), f32[2,256,1408]{1,2,0:T(8,128)}) %reduce-scatter.15.cloned.1.call-update) | async-done | bytes 2883600 | tf_op jit(solution)/shard_map/reduce_scatter | solution.py:273
  1713.8 3.2 multiply_reduce_fusion.3
  1718.3 8.4 add_convert_fusion
  1726.7 39.5 %psum.39 = f32[]{:T(128)} all-reduce(f32[]{:T(128)S(6)} %add.273), channel_id=1, replica_groups=mesh['dp'=8,'tensor'=4] {'dp','tensor'}, use_global_device_ids=true, to_apply=%region_31.32 | all-reduce | flops 1 | bytes 8 | tf_op jit(solution)/shard_map/psum | solution.py:280
  1767.0 6.3 multiply_subtract_fusion
  1773.3 3.4 copy.72
  1776.7 3.5 copy.73
  1783.1 5.5 multiply_subtract_fusion.1
  (260 shorter events, 67.3 us)
Async XLA Ops:
  7.2 18.8 %copy-start.37 = (f32[2,256,64]{1,2,0:T(8,128)S(1)}, f32[2,256,64]{1,2,0:T(8,128)}, u32[]{:S(2)}) copy-start(f32[2,256,64]{1,2,0:T(8,128)} %param.36) | copy-start | bytes 393220
  7.2 37.9 %all-gather.5.cloned.1.call-start = ((), (), s32[]{:S(2)}) async-start(), calls=%async_computation.6 | async-start | bytes 2359296 | tf_op jit(solution)/shard_map/all_gather | solution.py:106
  9.1 79.5 %all-gather.7.cloned.1.call-start = ((), (), s32[]{:S(2)}) async-start(), calls=%async_computation.7 | async-start | bytes 2359296 | tf_op jit(solution)/shard_map/all_gather | solution.py:108
  10.9 376.9 %all-reduce.5.cloned.1.call-start = ((), (), s32[]{:S(2)}) async-start(), calls=%async_computation.8 | async-start | bytes 16777216 | tf_op jit(solution)/shard_map/psum | solution.py:170
  11.0 29.3 %copy-start.2 = (bf16[1024,2048]{1,0:T(8,128)(2,1)S(1)}, bf16[1024,2048]{1,0:T(8,128)(2,1)}, u32[]{:S(2)}) copy-start(bf16[1024,2048]{1,0:T(8,128)(2,1)} %param.26) | copy-start | bytes 12582916
  22.9 22.1 %copy-start.47 = (f32[1,2048]{1,0:T(1,128)}, f32[1,2048]{1,0:T(1,128)S(1)}, u32[]{:S(2)}) copy-start(f32[1,2048]{1,0:T(1,128)S(1)} %get-tuple-element.356) | copy-start | bytes 24580
  26.0 19.1 %copy-start.53 = (f32[1024]{0:T(1024)}, f32[1024]{0:T(1024)S(1)}, u32[]{:S(2)}) copy-start(f32[1024]{0:T(1024)S(1)} %add_rsqrt_fusion.1) | copy-start | bytes 12292
  44.3 6.1 copy-start.32
  44.4 6.2 copy-start.20
  44.4 6.2 copy-start.22
  63.4 5.6 copy-start.34
  82.0 5.6 copy-start.34
  88.6 7.7 copy-start.17
  96.3 3.3 copy-start.16
  96.3 360.6 %all-gather.9.cloned.1.call-start = ((), (), s32[]{:S(2)}) async-start(), calls=%async_computation.9 | async-start | bytes 12976128 | tf_op jit(solution)/shard_map/all_gather | solution.py:109
  99.6 404.0 %all-gather.11.cloned.1.call-start = ((), (), s32[]{:S(2)}) async-start(), calls=%async_computation.10 | async-start | bytes 6488064 | tf_op jit(solution)/shard_map/all_gather | solution.py:110
  100.6 356.3 %copy-start.49 = (f32[1,2048]{1,0:T(1,128)S(1)}, f32[1,2048]{1,0:T(1,128)}, u32[]{:S(2)}) copy-start(f32[1,2048]{1,0:T(1,128)} %get-tuple-element.355) | copy-start | bytes 24580
  100.6 729.1 %all-reduce.7.cloned.1.call-start = ((), (), s32[]{:S(2)}) async-start(), calls=%async_computation.11 | async-start | bytes 16777216 | tf_op jit(solution)/shard_map/psum | solution.py:208
  397.0 440.3 %copy-start.51 = (f32[1024]{0:T(1024)}, f32[1024]{0:T(1024)S(1)}, u32[]{:S(2)}) copy-start(f32[1024]{0:T(1024)S(1)} %add_rsqrt_fusion) | copy-start | bytes 12292
  519.2 2.5 copy-start.62
  538.7 747.1 %all-reduce.9.cloned.1.call-start = ((), (), s32[]{:S(2)}) async-start(), calls=%async_computation.18 | async-start | bytes 16777216 | tf_op jit(solution)/shard_map/psum | solution.py:179
  829.7 8.2 copy-start.5
  829.7 9.4 copy-start.18
  839.1 8.1 copy-start.60
  843.9 3.4 copy-start.1
  850.6 4.6 copy-start.3
  855.2 3.6 copy-start.44
  877.5 3.7 copy-start
  881.3 20.6 %copy-start.7 = (f32[1024,1,64]{0,2,1:T(8,128)S(1)}, f32[1024,1,64]{0,2,1:T(8,128)}, u32[]{:S(2)}) copy-start(f32[1024,1,64]{0,2,1:T(8,128)} %get-tuple-element.551) | copy-start | bytes 786436 | tf_op jit(solution)/shard_map/while
  901.9 5.2 copy-start.6
  901.9 5.2 copy-start.13
  907.1 7.6 copy-start.8
  907.1 8.3 copy-start.4
  915.4 4.6 copy-start.3
  920.0 3.5 copy-start.44
  942.2 3.7 copy-start
  946.0 20.6 %copy-start.7 = (f32[1024,1,64]{0,2,1:T(8,128)S(1)}, f32[1024,1,64]{0,2,1:T(8,128)}, u32[]{:S(2)}) copy-start(f32[1024,1,64]{0,2,1:T(8,128)} %get-tuple-element.551) | copy-start | bytes 786436 | tf_op jit(solution)/shard_map/while
  966.6 5.2 copy-start.6
  966.6 5.2 copy-start.13
  971.8 7.6 copy-start.8
  971.8 8.3 copy-start.4
  980.1 5.6 copy-start.21
  989.4 2.4 copy-start.25
  995.2 340.6 %reduce-scatter.11.cloned.1.call-start = ((), (), s32[]{:S(2)}) async-start(), calls=%async_computation.13 | async-start | bytes 1179648 | tf_op jit(solution)/shard_map/reduce_scatter | solution.py:271
  1000.4 379.0 %reduce-scatter.9.cloned.1.call-start = ((), (), s32[]{:S(2)}) async-start(), calls=%async_computation.12 | async-start | bytes 4718592 | tf_op jit(solution)/shard_map/reduce_scatter | solution.py:270
  1007.4 427.0 %reduce-scatter.13.cloned.1.call-start = ((), (), s32[]{:S(2)}) async-start(), calls=%async_computation.14 | async-start | bytes 4718592 | tf_op jit(solution)/shard_map/reduce_scatter | solution.py:272
  1016.4 457.7 %reduce-scatter.19.cloned.1.call-start = ((), (), s32[]{:S(2)}) async-start(), calls=%async_computation.17 | async-start | bytes 1179648
  1285.9 5.0 copy-start.55
  1292.3 272.0 %reduce-scatter.17.cloned.1.call-start = ((), (), s32[]{:S(2)}) async-start(), calls=%async_computation.16 | async-start | bytes 12976128 | tf_op jit(solution)/shard_map/reduce_scatter | solution.py:274
  1303.7 410.1 %reduce-scatter.15.cloned.1.call-start = ((), (), s32[]{:S(2)}) async-start(), calls=%async_computation.15 | async-start | bytes 25952256 | tf_op jit(solution)/shard_map/reduce_scatter | solution.py:273
  1329.3 4.3 copy-start.19
  1718.3 48.7 %copy-start.10 = (f32[2,256,1408]{1,2,0:T(8,128)S(1)}, f32[2,256,1408]{1,2,0:T(8,128)}, u32[]{:S(2)}) copy-start(f32[2,256,1408]{1,2,0:T(8,128)} %reduce-scatter.15.cloned.1.call-done) | copy-start | bytes 8650756
  1776.7 3.5 copy-start.11
  1783.1 5.6 copy-start.26
  1783.1 5.6 copy-start.29
  1783.1 5.6 copy-start.40
  1783.1 5.6 copy-start.41
  1783.1 7.1 copy-start.38
  1783.1 7.0 copy-start.39
  1783.1 7.0 copy-start.45
  1783.1 7.0 copy-start.46
  1788.7 2.3 copy-start.27
  1788.7 2.2 copy-start.28
  1788.7 2.2 copy-start.42
  (23 other events, 31.5 us)
Sparse Core Ops, SparseCore 0:
  10.5 32.9 all-gather.4
  45.9 28.4 all-gather.6
  96.4 291.3 all-reduce.4
  390.1 66.6 all-gather.8
  459.2 44.3 all-gather.10
  538.9 290.8 all-reduce.6
  995.3 290.5 all-reduce.8
  1289.6 35.0 reduce-scatter.10
  1328.1 51.2 reduce-scatter.8
  1383.0 51.3 reduce-scatter.12
  1438.1 35.9 reduce-scatter.18
  1477.5 86.7 reduce-scatter.16
  1567.9 145.8 reduce-scatter.14
where the time goes:
time: 1810 us; the launch traced here: 1800 us
  waiting for transfers between devices  1280 us (71%)
  matrix products  218 us (12%)
  other arithmetic  120 us (7%)
  local copies, waits for them, and re-layouts  88.1 us (5%)
  blocking collectives  64.2 us (4%)
  between operations  22.1 us (1%)
    psum x1, waiting for transfers between devices, on_device(): branch = lax.psum(branch_partial, 'tensor')  287 us
    psum x1, waiting for transfers between devices, on_device(): grad_normed_two = lax.psum(partial_two, 'tensor')  280 us
    psum x1, waiting for transfers between devices, on_device(): lax.psum(jnp.dot(hidden, down_weight, preferred_element_type=jnp.float32)...  269 us
    reduce_scatter x1, waiting for transfers between devices, on_device(): lax.psum_scatter(grad_gateup_weight, 'dp', scatter_dimension=1, tiled=True)  147 us
    reduce_scatter x1, waiting for transfers between devices, on_device(): lax.psum_scatter(grad_down_weight, 'dp', scatter_dimension=1, tiled=True)  87.9 us
    all_gather x1, waiting for transfers between devices, on_device(): lax.all_gather(w_gateup.astype(jnp.bfloat16), 'dp', axis=1, tiled=True)  59.8 us
    reduce_scatter x1, waiting for transfers between devices, on_device(): lax.psum_scatter(grad_out_weight, 'dp', scatter_dimension=1, tiled=True)  51.9 us
    reduce_scatter x1, waiting for transfers between devices, on_device(): lax.psum_scatter(grad_query_weight, 'dp', scatter_dimension=0, tiled=True)  42 us
  transfers between devices with their start and end apart: 13, of which 10 were waited for; matrix products, arithmetic and copies ran while one was open for 10% of the time, Pallas kernels for 0%

commit v1 on v0

v1 whole, which is shorter than its diff:
```python
import functools

import jax
import jax.numpy as jnp
from jax import lax
from jax.experimental import pallas as pl
from jax.experimental.pallas import tpu as pltpu
from jax.sharding import PartitionSpec as P

HD = 64
MESH = pl.DeviceIdType.MESH


masked_value = -1e9


def dot_t(left, right):
    return lax.dot_general(left, right, (((1,), (1,)), ((), ())), preferred_element_type=jnp.float32)


def dot_n(left, right):
    return lax.dot_general(left, right, (((1,), (0,)), ((), ())), preferred_element_type=jnp.float32)


def swap_halves(values, first_half):
    return jnp.where(first_half, pltpu.roll(values, 96, 1), pltpu.roll(values, 32, 1))


def lane_tests(rows):
    lane = lax.broadcasted_iota(jnp.int32, (rows, 128), 1)
    return lane < 64, (lane % 64) < 32


def block_bias(seg_col_ref, seg_row_ref, i, j, size):
    keys = seg_col_ref[pl.ds(pl.multiple_of(j * size, size), size), :]
    rows = seg_row_ref[:, pl.ds(pl.multiple_of(i * size, size), size)]
    key_at = j * size + lax.broadcasted_iota(jnp.int32, (size, size), 0)
    row_at = i * size + lax.broadcasted_iota(jnp.int32, (size, size), 1)
    return jnp.where((keys == rows) & (key_at <= row_at), 0.0, masked_value)


def stack_pair(pair, low_lanes):
    zero = jnp.zeros_like(pair)
    return jnp.concatenate([jnp.where(low_lanes, pair, zero), jnp.where(low_lanes, zero, pair)], axis=0)


def forward_kernel(size, pairs, first_ref, raw_ref, cos_ref, sin_ref, seg_col_ref, seg_row_ref,
                   mix_ref, q_ref, k_ref, v_ref, lse_ref, bias, scores, v_turned):
    length = raw_ref.shape[0]
    low_lanes, first_half = lane_tests(size)
    low_rows = lax.broadcasted_iota(jnp.int32, (128, size), 0) < 64
    width = pairs * 128

    def prepare(i, carry):
        rows = pl.ds(pl.multiple_of(i * size, size), size)
        cosines, sines = cos_ref[rows, :], sin_ref[rows, :]
        for hp in range(pairs):
            values = raw_ref[rows, hp * 128:(hp + 1) * 128]
            turned = values * cosines + swap_halves(values, first_half) * sines
            q_ref[rows, hp * 128:(hp + 1) * 128] = (turned.astype(jnp.bfloat16).astype(jnp.float32) * 0.125).astype(jnp.bfloat16)
        both = raw_ref[rows, width:width + 128]
        other = pltpu.roll(both, 64, 1)
        keys = jnp.where(low_lanes, both, other)
        k_ref[rows, :] = (keys * cosines + swap_halves(keys, first_half) * sines).astype(jnp.bfloat16)
        values = jnp.where(low_lanes, other, both)
        v_ref[rows, :] = values.astype(jnp.bfloat16)
        v_turned[i] = values.T.astype(jnp.bfloat16)
        return carry

    lax.fori_loop(0, length // size, prepare, 0)

    def row_block(i, carry):
        rows = pl.ds(pl.multiple_of(i * size, size), size)
        begin = first_ref[i]

        def fill(j, c):
            bias[j] = block_bias(seg_col_ref, seg_row_ref, i, j, size)
            return c

        lax.fori_loop(begin, i + 1, fill, 0)

        for hp in range(pairs):
            stacked = stack_pair(q_ref[rows, hp * 128:(hp + 1) * 128], low_lanes)

            def score(j, top):
                keys = k_ref[pl.ds(pl.multiple_of(j * size, size), size), :]
                b = bias[j]
                s = dot_t(keys, stacked) + jnp.concatenate([b, b], axis=1)
                scores[j] = s
                return jnp.maximum(top, jnp.max(s, axis=0, keepdims=True))

            top = lax.fori_loop(begin, i + 1, score, jnp.full((1, 2 * size), -jnp.inf, jnp.float32))

            def mix(j, c):
                total, acc = c
                p = jnp.exp(scores[j] - top)
                total = total + jnp.sum(p, axis=0, keepdims=True)
                return total, acc + dot_n(v_turned[j], p.astype(jnp.bfloat16))

            total, acc = lax.fori_loop(begin, i + 1, mix, (
                jnp.zeros((1, 2 * size), jnp.float32), jnp.zeros((128, 2 * size), jnp.float32)))
            lse_ref[i, hp] = top + jnp.log(total)
            acc = acc / total
            acc = jnp.where(low_rows, acc[:, :size], acc[:, size:])
            mix_ref[rows, hp * 128:(hp + 1) * 128] = acc.T.astype(jnp.bfloat16)
        return carry

    lax.fori_loop(0, length // size, row_block, 0)


def attention_forward(raw, cosines, sines, seg_col, seg_row, first, size):
    length, wide = raw.shape
    width = wide - 128
    pairs = width // 128
    blocks = length // size
    vmem = pl.BlockSpec(memory_space=pltpu.VMEM)
    return pl.pallas_call(
        functools.partial(forward_kernel, size, pairs),
        out_shape=(
            jax.ShapeDtypeStruct((length, width), jnp.bfloat16),
            jax.ShapeDtypeStruct((length, width), jnp.bfloat16),
            jax.ShapeDtypeStruct((length, 128), jnp.bfloat16),
            jax.ShapeDtypeStruct((length, 128), jnp.bfloat16),
            jax.ShapeDtypeStruct((blocks, pairs, 1, 2 * size), jnp.float32),
        ),
        in_specs=[pl.BlockSpec(memory_space=pltpu.SMEM)] + [vmem] * 5,
        out_specs=(vmem,) * 5,
        scratch_shapes=[
            pltpu.VMEM((blocks, size, size), jnp.float32),
            pltpu.VMEM((blocks, size, 2 * size), jnp.float32),
            pltpu.VMEM((blocks, 128, size), jnp.bfloat16),
        ],
        compiler_params=pltpu.CompilerParams(vmem_limit_bytes=40 << 20),
        cost_estimate=pl.CostEstimate(flops=10 * length * length * width, bytes_accessed=8 * length * width,
                                      transcendentals=length * length * pairs),
    )(first, raw, cosines, sines, seg_col, seg_row)


def backward_kernel(size, pairs, first_ref, q_ref, k_ref, v_ref, mix_ref, grad_ref, lse_ref, cos_ref, sin_ref,
                    seg_col_ref, seg_row_ref, out_ref, bias, k_turned, grad_k, grad_v):
    length = q_ref.shape[0]
    width = pairs * 128
    low_lanes, first_half = lane_tests(size)
    low_rows = lax.broadcasted_iota(jnp.int32, (128, size), 0) < 64

    def prepare(i, carry):
        rows = pl.ds(pl.multiple_of(i * size, size), size)
        k_turned[i] = k_ref[rows, :].astype(jnp.float32).T.astype(jnp.bfloat16)
        grad_k[i] = jnp.zeros((size, 128), jnp.float32)
        grad_v[i] = jnp.zeros((size, 128), jnp.float32)
        return carry

    lax.fori_loop(0, length // size, prepare, 0)

    def row_block(i, carry):
        rows = pl.ds(pl.multiple_of(i * size, size), size)
        begin = first_ref[i]
        cosines, sines = cos_ref[rows, :], sin_ref[rows, :]

        def fill(j, c):
            bias[j] = block_bias(seg_col_ref, seg_row_ref, i, j, size)
            return c

        lax.fori_loop(begin, i + 1, fill, 0)

        for hp in range(pairs):
            columns = slice(hp * 128, (hp + 1) * 128)
            stacked = stack_pair(q_ref[rows, columns], low_lanes)
            grad_pair = grad_ref[rows, columns]
            grad_stacked = stack_pair(grad_pair, low_lanes)
            product = (grad_pair.astype(jnp.float32) * mix_ref[rows, columns].astype(jnp.float32)).T
            spread = jnp.concatenate([
                jnp.sum(product[:64], axis=0, keepdims=True), jnp.sum(product[64:], axis=0, keepdims=True)], axis=1)
            logsum = lse_ref[i, hp]

            def piece(j, acc):
                at = pl.ds(pl.multiple_of(j * size, size), size)
                b = bias[j]
                s = dot_t(k_ref[at, :], stacked) + jnp.concatenate([b, b], axis=1)
                p = jnp.exp(s - logsum)
                grad_p = dot_t(v_ref[at, :], grad_stacked)
                grad_s = (p * (grad_p - spread)).astype(jnp.bfloat16)
                grad_v[j] += dot_n(p.astype(jnp.bfloat16), grad_stacked)
                grad_k[j] += dot_n(grad_s, stacked)
                return acc + dot_n(k_turned[j], grad_s)

            acc = lax.fori_loop(begin, i + 1, piece, jnp.zeros((128, 2 * size), jnp.float32))
            acc = jnp.where(low_rows, acc[:, :size], acc[:, size:]).T * 0.125
            out_ref[rows, columns] = (acc * cosines - swap_halves(acc, first_half) * sines).astype(jnp.bfloat16)
        return carry

    lax.fori_loop(0, length // size, row_block, 0)

    def finish(i, carry):
        rows = pl.ds(pl.multiple_of(i * size, size), size)
        cosines, sines = cos_ref[rows, :], sin_ref[rows, :]
        dk = grad_k[i] + pltpu.roll(grad_k[i], 64, 1)
        dk = dk * cosines - swap_halves(dk, first_half) * sines
        dv = grad_v[i] + pltpu.roll(grad_v[i], 64, 1)
        out_ref[rows, width:width + 128] = jnp.where(low_lanes, dk, dv).astype(jnp.bfloat16)
        return carry

    lax.fori_loop(0, length // size, finish, 0)


def attention_backward(q, k, v, mix, grad, lse, cosines, sines, seg_col, seg_row, first, size):
    length, width = q.shape
    pairs = width // 128
    blocks = length // size
    vmem = pl.BlockSpec(memory_space=pltpu.VMEM)
    return pl.pallas_call(
        functools.partial(backward_kernel, size, pairs),
        out_shape=jax.ShapeDtypeStruct((length, width + 128), jnp.bfloat16),
        in_specs=[pl.BlockSpec(memory_space=pltpu.SMEM)] + [vmem] * 10,
        out_specs=vmem,
        scratch_shapes=[
            pltpu.VMEM((blocks, size, size), jnp.float32),
            pltpu.VMEM((blocks, 128, size), jnp.bfloat16),
            pltpu.VMEM((blocks, size, 128), jnp.float32),
            pltpu.VMEM((blocks, size, 128), jnp.float32),
        ],
        compiler_params=pltpu.CompilerParams(vmem_limit_bytes=40 << 20),
        cost_estimate=pl.CostEstimate(flops=20 * length * length * width, bytes_accessed=8 * length * width,
                                      transcendentals=length * length * pairs),
    )(first, q, k, v, mix, grad, lse, cosines, sines, seg_col, seg_row)


def line_reduce(partial, n, chunks, cid, lagk=1):
    rows, width = partial.shape
    half = rows // 2
    rc = half // chunks

    def kernel(in_ref, out_ref, got, send_a, recv_a, send_g, recv_g):
        me = lax.axis_index("tensor")
        barrier = pltpu.get_barrier_semaphore()

        @pl.when(me > 0)
        def _():
            pl.semaphore_signal(barrier, inc=1, device_id={"tensor": me - 1}, device_id_type=MESH)

        @pl.when(me < n - 1)
        def _():
            pl.semaphore_signal(barrier, inc=1, device_id={"tensor": me + 1}, device_id_type=MESH)

        @pl.when((me > 0) & (me < n - 1))
        def _():
            pl.semaphore_wait(barrier, 2)

        @pl.when((me == 0) | (me == n - 1))
        def _():
            pl.semaphore_wait(barrier, 1)

        def rs(stream, c, nxt, src):
            return pltpu.make_async_remote_copy(
                src_ref=src, dst_ref=got.at[stream, c],
                send_sem=send_a.at[stream, c], recv_sem=recv_a.at[stream, c],
                device_id={"tensor": nxt}, device_id_type=MESH)

        def ag(stream, c, nxt):
            r0 = pl.multiple_of(stream * half + c * rc, rc)
            return pltpu.make_async_remote_copy(
                src_ref=out_ref.at[pl.ds(r0, rc)], dst_ref=out_ref.at[pl.ds(r0, rc)],
                send_sem=send_g.at[stream, c], recv_sem=recv_g.at[stream, c],
                device_id={"tensor": nxt}, device_id_type=MESH)

        K = lagk
        steps = chunks + 2 * K * (n - 1)

        def body(s, carry):
            for stream in (0, 1):
                pos = me if stream == 0 else n - 1 - me
                fwd = me + 1 if stream == 0 else me - 1
                bwd = me - 1 if stream == 0 else me + 1
                c = s - K * pos

                @pl.when((c >= 0) & (c < chunks))
                def _():
                    r0 = pl.multiple_of(stream * half + c * rc, rc)

                    def summed():
                        rs(stream, c, fwd, got.at[stream, c]).wait_recv()
                        return (
                            in_ref[pl.ds(r0, rc)].astype(jnp.float32) + got[stream, c].astype(jnp.float32)
                        ).astype(out_ref.dtype)

                    @pl.when(pos == 0)
                    def _():
                        rs(stream, c, fwd, in_ref.at[pl.ds(r0, rc)]).start()

                    @pl.when((pos > 0) & (pos < n - 1))
                    def _():
                        got[stream, c] = summed()
                        rs(stream, c, fwd, got.at[stream, c]).start()

                    @pl.when(pos == n - 1)
                    def _():
                        out_ref[pl.ds(r0, rc)] = summed()
                        ag(stream, c, bwd).start()
                d = s - K * (n - 1) - K * (n - 1 - pos)

                @pl.when((d >= 0) & (d < chunks) & (pos < n - 1))
                def _():
                    ag(stream, d, bwd).wait_recv()

                    @pl.when(pos > 0)
                    def _():
                        ag(stream, d, bwd).start()
            return carry

        lax.fori_loop(0, steps, body, 0)

        def drain(c, carry):
            for stream in (0, 1):
                pos = me if stream == 0 else n - 1 - me
                fwd = me + 1 if stream == 0 else me - 1
                bwd = me - 1 if stream == 0 else me + 1

                @pl.when(pos < n - 1)
                def _():
                    rs(stream, c, fwd, got.at[stream, c]).wait_send()

                @pl.when(pos > 0)
                def _():
                    ag(stream, c, bwd).wait_send()
            return carry

        lax.fori_loop(0, chunks, drain, 0)

    return pl.pallas_call(
        kernel,
        out_shape=jax.ShapeDtypeStruct((rows, width), partial.dtype),
        in_specs=[pl.BlockSpec(memory_space=pltpu.VMEM)],
        out_specs=pl.BlockSpec(memory_space=pltpu.VMEM),
        scratch_shapes=[
            pltpu.VMEM((2, chunks, rc, width), partial.dtype),
            pltpu.SemaphoreType.DMA((2, chunks)),
            pltpu.SemaphoreType.DMA((2, chunks)),
            pltpu.SemaphoreType.DMA((2, chunks)),
            pltpu.SemaphoreType.DMA((2, chunks)),
        ],
        compiler_params=pltpu.CompilerParams(collective_id=cid, has_side_effects=True, vmem_limit_bytes=40 << 20),
        cost_estimate=pl.CostEstimate(flops=rows * width * 2, bytes_accessed=rows * width * 4 * 30, transcendentals=0),
    )(partial)


def total_kernel(n, m, in_ref, out_ref, line, got_line, got_plane, send_line, recv_line, send_plane, recv_plane):
    z = lax.axis_index("tensor")
    d = lax.axis_index("dp")
    barrier = pltpu.get_barrier_semaphore()
    for k in range(1, n):
        pl.semaphore_signal(barrier, inc=1, device_id={"tensor": lax.rem(z + k, n)}, device_id_type=MESH)
    for k in range(1, m):
        pl.semaphore_signal(barrier, inc=1, device_id={"dp": lax.rem(d + k, m)}, device_id_type=MESH)
    pl.semaphore_wait(barrier, n - 1 + m - 1)

    def along_line(k, sender):
        return pltpu.make_async_remote_copy(
            src_ref=in_ref, dst_ref=got_line.at[sender], send_sem=send_line.at[k], recv_sem=recv_line.at[sender],
            device_id={"tensor": lax.rem(z + k, n)}, device_id_type=MESH)

    def over_plane(k, sender):
        return pltpu.make_async_remote_copy(
            src_ref=line, dst_ref=got_plane.at[sender], send_sem=send_plane.at[k], recv_sem=recv_plane.at[sender],
            device_id={"dp": lax.rem(d + k, m)}, device_id_type=MESH)

    for k in range(1, n):
        along_line(k, z).start()
    got_line[z] = in_ref[...]
    for k in range(1, n):
        along_line(k, z).wait_send()
        along_line(k, lax.rem(z + n - k, n)).wait_recv()
    whole = got_line[0]
    for k in range(1, n):
        whole = whole + got_line[k]
    line[...] = whole
    for k in range(1, m):
        over_plane(k, d).start()
    got_plane[d] = line[...]
    for k in range(1, m):
        over_plane(k, d).wait_send()
        over_plane(k, lax.rem(d + m - k, m)).wait_recv()
    whole = got_plane[0]
    for k in range(1, m):
        whole = whole + got_plane[k]
    out_ref[...] = whole


def total_sum(value, n, m, cid):
    tile = jnp.broadcast_to(value.reshape(1, 1), (8, 128))
    vmem = pl.BlockSpec(memory_space=pltpu.VMEM)
    total = pl.pallas_call(
        functools.partial(total_kernel, n, m),
        out_shape=jax.ShapeDtypeStruct((8, 128), jnp.float32),
        in_specs=[vmem],
        out_specs=vmem,
        scratch_shapes=[
            pltpu.VMEM((8, 128), jnp.float32),
            pltpu.VMEM((n, 8, 128), jnp.float32),
            pltpu.VMEM((m, 8, 128), jnp.float32),
            pltpu.SemaphoreType.DMA((n,)),
            pltpu.SemaphoreType.DMA((n,)),
            pltpu.SemaphoreType.DMA((m,)),
            pltpu.SemaphoreType.DMA((m,)),
        ],
        compiler_params=pltpu.CompilerParams(collective_id=cid, has_side_effects=True),
    )(tile)
    return total[0, 0]


norm_eps = 1e-05
beta_first = 0.9
beta_second = 0.95
adam_eps = 1e-08
weight_decay = 0.1
weight_rate = 0.02
out_rate = 0.1
gain_rate = 0.2
clip_limit = 1.0


def positions(segment):
    length = segment.shape[0]
    indices = jnp.arange(length, dtype=jnp.int32)
    earlier = jnp.concatenate([segment[:1] - 1, segment[:-1]])
    begins = jnp.where(segment != earlier, indices, jnp.zeros_like(indices))
    return indices - lax.cummax(begins, axis=0)


def paired_tables(places):
    frequency = jnp.power(10000.0, -jnp.arange(HD // 2, dtype=jnp.float32) * (2.0 / HD))
    angles = places.astype(jnp.float32)[:, None] * frequency[None, :]
    cosines, sines = jnp.cos(angles), jnp.sin(angles)
    return (
        jnp.concatenate([cosines] * 4, axis=-1),
        jnp.concatenate([-sines, sines, -sines, sines], axis=-1),
    )


def over_rows(left, right):
    return lax.dot_general(
        left, right, (((0,), (0,)), ((), ())), preferred_element_type=jnp.float32
    )


def against(left, right):
    return lax.dot_general(
        left, right, (((1,), (1,)), ((), ())), preferred_element_type=jnp.float32
    )


def norm_back(grad_output, unit_rows, inverse, gain):
    scaled = grad_output * gain
    gain_grad = jnp.sum(grad_output * unit_rows, axis=0)
    inner_mean = jnp.mean(scaled * unit_rows, axis=-1, keepdims=True)
    return (inverse * (scaled - unit_rows * inner_mean), gain_grad)


def adam_step(weight, first, second, gradient, clip_factor, step_float, step_rate, decay_rate):
    gradient = gradient * clip_factor
    first = beta_first * first + (1.0 - beta_first) * gradient
    second = beta_second * second + (1.0 - beta_second) * gradient * gradient
    correct_one = 1.0 - jnp.power(beta_first, step_float)
    correct_two = 1.0 - jnp.power(beta_second, step_float)
    update = first / correct_one / (jnp.sqrt(second / correct_two) + adam_eps)
    return (first, second, weight - step_rate * (update + decay_rate * weight))


def on_device(
    n,
    m,
    tokens,
    cotangent,
    segment_ids,
    step_count,
    norm_gains,
    gains_first,
    gains_second,
    w_query,
    query_first,
    query_second,
    w_keyval,
    keyval_first,
    keyval_second,
    w_out,
    out_first,
    out_second,
    w_gateup,
    gateup_first,
    gateup_second,
    w_down,
    down_first,
    down_second,
):
    low = jnp.bfloat16
    width = w_query.shape[1]
    kv_width = w_keyval.shape[2]
    gain_rows = lax.all_gather(norm_gains.astype(low), "dp", axis=1, tiled=True)
    qkv_shard = jnp.concatenate([w_query, w_keyval[0], w_keyval[1]], axis=1).astype(low)
    qkv_weight = lax.all_gather(qkv_shard, "dp", axis=0, tiled=True)
    out_weight = lax.all_gather(w_out.astype(low), "dp", axis=1, tiled=True)
    gateup_weight = lax.all_gather(w_gateup.astype(low), "dp", axis=1, tiled=True)
    down_weight = lax.all_gather(w_down.astype(low), "dp", axis=1, tiled=True)
    gain_values = gain_rows.astype(jnp.float32)
    length = tokens.shape[0]
    size = min(256, length)
    segment = segment_ids[0]
    places = positions(segment)
    cosines, sines = paired_tables(places)
    first = (jnp.arange(length, dtype=jnp.int32) - places)[::size] // size
    seg_col, seg_row = segment[:, None], segment[None, :]

    values_in = tokens.astype(jnp.float32)
    inverse_one = lax.rsqrt(jnp.mean(values_in * values_in, axis=-1, keepdims=True) + norm_eps)
    unit_one = values_in * inverse_one
    normed_one = (unit_one * gain_values[0]).astype(low)
    raw = jnp.dot(normed_one, qkv_weight, preferred_element_type=jnp.float32)
    mixture, q, k, v, lse = attention_forward(raw, cosines, sines, seg_col, seg_row, first, size)
    branch_part = jnp.dot(mixture, out_weight, preferred_element_type=jnp.float32).astype(low)
    branch = line_reduce(branch_part, n, 16, 1, 2)
    middle = values_in + branch.astype(jnp.float32)
    inverse_two = lax.rsqrt(jnp.mean(middle * middle, axis=-1, keepdims=True) + norm_eps)
    unit_two = middle * inverse_two
    normed_two = (unit_two * gain_values[1]).astype(low)
    gateup = jnp.einsum(
        "nd,sdf->snf", normed_two, gateup_weight, preferred_element_type=jnp.float32
    )
    gate_values = gateup[0]
    up_values = gateup[1]
    sigmoid_gate = jax.nn.sigmoid(gate_values)
    silu_gate = gate_values * sigmoid_gate
    hidden = (silu_gate * up_values).astype(low)
    grad_hidden = against(cotangent, down_weight)
    grad_gate = grad_hidden * up_values * sigmoid_gate * (1.0 + gate_values * (1.0 - sigmoid_gate))
    grad_up = grad_hidden * silu_gate
    grad_gateup = jnp.stack([grad_gate, grad_up]).astype(low)
    partial_two = jnp.einsum(
        "snf,sdf->nd", grad_gateup, gateup_weight, preferred_element_type=jnp.float32
    ).astype(low)
    grad_down_weight = over_rows(hidden, cotangent).astype(low)
    grad_gateup_weight = jnp.einsum(
        "nd,snf->sdf", normed_two, grad_gateup, preferred_element_type=jnp.float32
    ).astype(low)
    partial_two, grad_gateup_weight, grad_down_weight = lax.optimization_barrier(
        (partial_two, grad_gateup_weight, grad_down_weight)
    )
    gateup_reduced = lax.psum_scatter(grad_gateup_weight, "dp", scatter_dimension=1, tiled=True)
    down_reduced = lax.psum_scatter(grad_down_weight, "dp", scatter_dimension=1, tiled=True)
    grad_normed_two = line_reduce(partial_two, n, 16, 2, 2)
    feed_part = jnp.dot(hidden, down_weight, preferred_element_type=jnp.float32).astype(low)
    feed_out = lax.psum(feed_part, "tensor").astype(jnp.float32)
    layer_out = (middle + feed_out).astype(low)
    grad_from_two, gain_grad_two = norm_back(
        grad_normed_two.astype(jnp.float32), unit_two, inverse_two, gain_values[1]
    )
    grad_middle = cotangent.astype(jnp.float32) + grad_from_two
    grad_branch = grad_middle.astype(low)
    grad_mixture = against(grad_branch, out_weight).astype(low)
    grad_qkv = attention_backward(
        q, k, v, mixture, grad_mixture, lse, cosines, sines, seg_col, seg_row, first, size
    )
    partial_one = against(grad_qkv, qkv_weight).astype(low)
    grad_out_weight = over_rows(mixture, grad_branch).astype(low)
    grad_qkv_weight = over_rows(normed_one, grad_qkv).astype(low)
    partial_one, grad_out_weight, grad_qkv_weight = lax.optimization_barrier(
        (partial_one, grad_out_weight, grad_qkv_weight)
    )
    out_reduced = lax.psum_scatter(grad_out_weight, "dp", scatter_dimension=1, tiled=True)
    qkv_reduced = lax.psum_scatter(grad_qkv_weight, "dp", scatter_dimension=0, tiled=True)
    grad_normed_one = line_reduce(partial_one, n, 16, 3, 2).astype(jnp.float32)
    grad_from_one, gain_grad_one = norm_back(grad_normed_one, unit_one, inverse_one, gain_values[0])
    input_grad = grad_middle + grad_from_one
    gain_grads = jnp.stack([gain_grad_one, gain_grad_two])
    gains_reduced = lax.psum_scatter(gain_grads, "dp", scatter_dimension=1, tiled=True)
    qkv_reduced = qkv_reduced.astype(jnp.float32)
    reduced = (
        gains_reduced,
        qkv_reduced[:, :width],
        jnp.stack([qkv_reduced[:, width : width + kv_width], qkv_reduced[:, width + kv_width :]]),
        out_reduced.astype(jnp.float32),
        gateup_reduced.astype(jnp.float32),
        down_reduced.astype(jnp.float32),
    )
    first_owner = (lax.axis_index("tensor") == 0).astype(jnp.float32)
    local_square = first_owner * jnp.sum(reduced[0] * reduced[0]) + sum(
        (jnp.sum(g * g) for g in reduced[1:])
    )
    square_total = total_sum(local_square, n, m, 4)
    grad_norm = jnp.sqrt(square_total)
    clip_factor = jnp.minimum(1.0, clip_limit / (grad_norm + 1e-06))
    step_float = step_count[0].astype(jnp.float32)
    params = (norm_gains, w_query, w_keyval, w_out, w_gateup, w_down)
    states = (
        (gains_first, gains_second),
        (query_first, query_second),
        (keyval_first, keyval_second),
        (out_first, out_second),
        (gateup_first, gateup_second),
        (down_first, down_second),
    )
    step_rates = (gain_rate, weight_rate, weight_rate, out_rate, weight_rate, weight_rate)
    decay_rates = (0.0, weight_decay, weight_decay, weight_decay, weight_decay, weight_decay)
    results = []
    for position_index in range(6):
        one, two = states[position_index]
        results.extend(
            adam_step(
                params[position_index],
                one,
                two,
                reduced[position_index],
                clip_factor,
                step_float,
                step_rates[position_index],
                decay_rates[position_index],
            )
        )
    return (layer_out, input_grad, grad_norm.reshape(1), *results)


def solution(mesh):
    rows = P("dp", None)
    gains = P(None, "dp")
    query = P("dp", "tensor")
    stacked = P(None, "dp", "tensor")
    turned = P("tensor", "dp")
    states = (gains,) * 3 + (query,) * 3 + (stacked,) * 3 + (turned,) * 3 + (stacked,) * 3 + (turned,) * 3
    return jax.shard_map(
        functools.partial(on_device, mesh.shape["tensor"], mesh.shape["dp"]),
        mesh=mesh,
        in_specs=(rows, rows, rows, P()) + states,
        out_specs=(rows, rows, P()) + states,
        check_vma=False,
    )
```

time: 1810 us -> 1020 us (0.56)
  waiting for transfers between devices: 1280 us -> 265 us
  Pallas kernels: 0 us -> 480 us
  matrix products: 218 us -> 122 us
  blocking collectives: 64.2 us -> 10.6 us
  other arithmetic: 120 us -> 69.4 us
  local copies, waits for them, and re-layouts: 88.1 us -> 41.3 us
    psum x3 -> x1, waiting for transfers between devices: 836 us -> 0.02 us  [on_device(): feed_out = lax.psum(feed_part, 'tensor').astype(jnp.float32)]
    pallas_call x0 -> x6, Pallas kernels: none -> 480 us  [the longest x3 429 us: line_reduce(): pl.pallas_call(kernel, out_shape=jax.ShapeDtypeStruct((rows, width), part...]
    dot_general x19 -> x3, matrix products: 110 us -> 21.1 us  [the longest x1 10.9 us: on_device(): jnp.dot(hidden, down_weight, preferred_element_type=jnp.float32).astype(low)]
    all_gather x4, waiting for transfers between devices: 86.1 us -> 15.5 us  [the longest x1 10.8 us: on_device(): qkv_weight = lax.all_gather(qkv_shard, 'dp', axis=0, tiled=True)]
    reduce_scatter x1, waiting for transfers between devices: 147 us -> 88.4 us  [on_device(): lax.psum_scatter(grad_gateup_weight, 'dp', scatter_dimension=1, tiled=True)]
    dynamic_update_slice x8 -> x0, local copies, waits for them, and re-layouts: 41.7 us -> none  [the longest x4 41.2 us: on_device(): lax.scan(backward_block, (zero_rows, zero_rows), (starts, logsum_blocks))]
    psum x1 -> x0, blocking collectives: 39.5 us -> none  [on_device(): square_total = lax.psum(local_square, ('dp', 'tensor'))]
    reduce_scatter x1, waiting for transfers between devices: 87.9 us -> 57.6 us  [on_device(): lax.psum_scatter(grad_down_weight, 'dp', scatter_dimension=1, tiled=True)]
  transfers between devices with their start and end apart: 13 -> 10, of which waited for: 10 -> 7; matrix products, arithmetic and copies ran while one was open for 10% -> 11% of each run, Pallas kernels for 0% -> 34%
where the time goes in v1:
time: 1020 us; the launch traced here: 1010 us
  Pallas kernels  480 us (47%)
  waiting for transfers between devices  265 us (26%)
  matrix products  122 us (12%)
  other arithmetic  69.4 us (7%)
  local copies, waits for them, and re-layouts  41.3 us (4%)
  between operations  22.4 us (2%)
  blocking collectives  10.6 us (1%)
    pallas_call x3, Pallas kernels, line_reduce(): pl.pallas_call(kernel, out_shape=jax.ShapeDtypeStruct((rows, width), part...  429 us
    reduce_scatter x1, waiting for transfers between devices, on_device(): lax.psum_scatter(grad_gateup_weight, 'dp', scatter_dimension=1, tiled=True)  88.4 us
    reduce_scatter x1, waiting for transfers between devices, on_device(): lax.psum_scatter(grad_down_weight, 'dp', scatter_dimension=1, tiled=True)  57.6 us
    reduce_scatter x1, waiting for transfers between devices, on_device(): lax.psum_scatter(grad_qkv_weight, 'dp', scatter_dimension=0, tiled=True)  45.3 us
    reduce_scatter x1, waiting for transfers between devices, on_device(): lax.psum_scatter(grad_out_weight, 'dp', scatter_dimension=1, tiled=True)  42.6 us
    unnamed x94, local copies, waits for them, and re-layouts  38.2 us
    dot_general x3, matrix products, against(): lax.dot_general(left, right, (((1,), (1,)), ((), ())), preferred_element_...  27.6 us
    pallas_call x1, Pallas kernels, attention_backward(): pl.pallas_call(functools.partial(backward_kernel, size, pairs), out_shape...  21.2 us
  transfers between devices with their start and end apart: 10, of which 7 were waited for; matrix products, arithmetic and copies ran while one was open for 11% of the time, Pallas kernels for 34%

profile of v1, /device:TPU:0, one launch (start us, length us, event | category | flops | bytes accessed | tf_op | source)
XLA Modules:
  0.0 1011.9 jit_solution(5052571583608238582)
XLA Ops:
  7.2 1.1 convert.20
  8.6 1.1 convert.19
  10.5 1.8 convert_element_type.109
  12.4 1.2 convert_element_type.113
  13.7 2.3 convert_element_type.115
  18.3 10.6 %all_gather.15 = bf16[2,2048]{1,0:T(2,128)(2,1)S(1)} all-gather(bf16[2,256]{1,0:T(2,128)(2,1)S(1)} %convert_element_type.105), channel_id=1, replica_groups=mesh['dp'=8,'tensor'=4] {'dp'}, dimensions={1}, use_global_device_ids=true | all-gather | bytes 9216 | tf_op jit(solution)/shard_map/all_gather | solution.py:497
  28.9 1.9 fusion.44
  32.7 10.8 %all-gather.5.cloned.1.call-done = bf16[2048,640]{1,0:T(8,128)(2,1)} async-done(((bf16[256,640]{1,0:T(8,128)(2,1)}), bf16[2048,640]{1,0:T(8,128)(2,1)}) %all-gather.5.cloned.1.call-update) | async-done | bytes 2621456 | tf_op jit(solution)/shard_map/all_gather | solution.py:499
  43.5 6.2 fusion.37.raw_ref
  49.8 18.9 %shard_map.373 = (bf16[1024,512]{1,0:T(8,128)(2,1)S(1)}, bf16[1024,512]{1,0:T(8,128)(2,1)S(1)}, bf16[1024,128]{1,0:T(8,128)(2,1)S(1)}, bf16[1024,128]{1,0:T(8,128)(2,1)S(1)}, f32[4,4,1,512]{3,2,1,0:T(1,128)S(1)}) custom-call(s32[4]{0:T(128)S(1)} %and_select_fusion.first_ref, f32[1024,640]{1,0:T(8,128)S(1)} %fusion.37.raw_ref, ...), custom_call_target="tpu_custom_call" | custom-call | flops 5368709120 | bytes 4194304 | tf_op jit(solution)/shard_map/pallas_call | solution.py:117
  69.6 4.6 all-gather.7.cloned.1.call-done
  74.2 3.9 convolution_convert_fusion.3.in_ref
  78.2 110.2 %shard_map.374 = bf16[1024,2048]{1,0:T(8,128)(2,1)S(1)} custom-call(bf16[1024,2048]{1,0:T(8,128)(2,1)S(1)} %convolution_convert_fusion.3.in_ref), custom_call_target="tpu_custom_call" | custom-call | flops 4194304 | bytes 251658240 | tf_op jit(solution)/shard_map/pallas_call | solution.py:329
  188.4 1.4 multiply_reduce_fusion
  190.5 20.2 %convolution_bitcast_fusion = f32[2,1024,1408]{2,1,0:T(8,128)} fusion(bf16[2,2048,1408]{2,1,0:T(8,128)(2,1)} %all-gather.9.cloned.1.call-done, bf16[1024,2048]{1,0:T(8,128)(2,1)} %copy-done, bf16[1024,2048]{1,0:T(8,128)(2,1)} %param.22, f32[2048]{0:T(1024)S(1)} %bitcast.94, f32[1024]{0:T(1024)S(1)} %add_rsqrt_fusion), kind=kOutput, calls=%fused_computation.30 | convolution fusion | flops 11823742976 | bytes 31469568 | tf_op jit(solution)/shard_map/nd,sdf->snf/dot_general | solution.py:524
  210.6 16.2 %fusion.25 = (bf16[1,1024,1408]{2,1,0:T(8,128)(2,1)}, bf16[1,1024,1408]{2,1,0:T(8,128)(2,1)}, bf16[1024,1408]{1,0:T(8,128)(2,1)S(1)}) fusion(f32[2,1024,1408]{2,1,0:T(8,128)} %convolution_bitcast_fusion, bf16[1024,2048]{1,0:T(8,128)(2,1)} %param.23, bf16[1408,2048]{1,0:T(8,128)(2,1)} %all-gather.11.cloned.1.call-done), kind=kOutput, calls=%fused_computation.54 | convolution fusion | flops 5927206912 | bytes 30146560 | tf_op jit(solution)/shard_map/dot_general | solution.py:446
  226.8 1.6 copy-done.39
  228.4 8.1 convolution_convert_fusion
  236.5 10.9 %convolution_convert_fusion.2 = bf16[1024,2048]{1,0:T(8,128)(2,1)} fusion(bf16[1024,1408]{1,0:T(8,128)(2,1)} %copy-done.39, bf16[1408,2048]{1,0:T(8,128)(2,1)} %all-gather.11.cloned.1.call-done), kind=kOutput, calls=%fused_computation.42 | convolution fusion | flops 5907677184 | bytes 12845056 | tf_op jit(solution)/shard_map/dot_general | solution.py:549
  247.5 19.9 %convert_bitcast_fusion = bf16[2,2048,1408]{1,2,0:T(8,128)(2,1)} fusion(bf16[1,1024,1408]{2,1,0:T(8,128)(2,1)} %get-tuple-element.150, bf16[1,1024,1408]{2,1,0:T(8,128)(2,1)} %get-tuple-element.149, bf16[1024,2048]{1,0:T(8,128)(2,1)} %copy-done, bf16[1024,2048]{1,0:T(8,128)(2,1)} %param.22, f32[2048]{0:T(1024)S(1)} %bitcast.95, f32[1024]{0:T(1024)S(1)} %add_rsqrt_fusion), kind=kOutput, calls=%fused_computation.7 | convolution fusion | flops 11832393728 | bytes 25702400 | tf_op jit(solution)/shard_map/nd,snf->sdf/dot_general | solution.py:540
  267.4 16.7 %bitcast_convert_fusion.in_ref = bf16[1024,2048]{1,0:T(8,128)(2,1)S(1)} fusion(bf16[2,2048,1408]{2,1,0:T(8,128)(2,1)} %all-gather.9.cloned.1.call-done, bf16[1,1024,1408]{2,1,0:T(8,128)(2,1)} %get-tuple-element.150, bf16[1,1024,1408]{2,1,0:T(8,128)(2,1)} %get-tuple-element.149), kind=kOutput, calls=%fused_computation.24 | convolution fusion | flops 11816140800 | bytes 21495808 | tf_op jit(solution)/shard_map/snf,sdf->nd/dot_general | solution.py:536
  284.2 211.6 %shard_map.375 = bf16[1024,2048]{1,0:T(8,128)(2,1)S(1)} custom-call(bf16[1024,2048]{1,0:T(8,128)(2,1)S(1)} %bitcast_convert_fusion.in_ref), custom_call_target="tpu_custom_call" | custom-call | flops 4194304 | bytes 251658240 | tf_op jit(solution)/shard_map/pallas_call | solution.py:329
  495.8 3.5 fusion.12
  499.3 11.7 %fusion.11 = (f32[1024,2048]{1,0:T(8,128)S(1)}, bf16[1024,2048]{1,0:T(8,128)(2,1)}) fusion(bf16[1024,2048]{1,0:T(8,128)(2,1)} %copy-done.3, bf16[1024,2048]{1,0:T(8,128)(2,1)} %param.23, bf16[1024,2048]{1,0:T(8,128)(2,1)} %copy-done, bf16[1024,2048]{1,0:T(8,128)(2,1)} %param.22, f32[1024]{0:T(1024)S(1)} %broadcast_multiply_fusion.1, f32[2048]{0:T(1024)S(1)} %bitcast.97, ...), kind=kLoop, calls=%fused_computation.18 | loop fusion | flops 29360128 | bytes 33570816 | tf_op jit(solution)/shard_map/add | solution.py:555
  511.0 3.4 copy-done.13
  514.4 3.8 convolution_convert_fusion.5
  518.2 6.4 fusion.30.grad_ref
  524.7 21.2 %shard_map.376 = bf16[1024,640]{1,0:T(8,128)(2,1)S(1)} custom-call(s32[4]{0:T(128)S(1)} %and_select_fusion.first_ref, bf16[1024,512]{1,0:T(8,128)(2,1)S(1)} %copy-done.7, bf16[1024,128]{1,0:T(8,128)(2,1)S(1)} %get-tuple-element.35.k_ref, bf16[1024,128]{1,0:T(8,128)(2,1)S(1)} %get-tuple-element.36.v_ref, bf16[1024,512]{1,0:T(8,128)(2,1)S(1)} %get-tuple-element.32.mix_ref, ...), custom_call_target="tpu_custom_call" | custom-call | flops 10737418240 | bytes 4194304 | tf_op jit(solution)/shard_map/pallas_call | solution.py:211
  545.9 1.0 copy-done.5
  546.9 4.6 convolution_convert_fusion.4
  551.6 5.0 convolution_convert_fusion.1.in_ref
  556.6 107.6 %shard_map.377 = bf16[1024,2048]{1,0:T(8,128)(2,1)S(1)} custom-call(bf16[1024,2048]{1,0:T(8,128)(2,1)S(1)} %convolution_convert_fusion.1.in_ref), custom_call_target="tpu_custom_call" | custom-call | flops 4194304 | bytes 251658240 | tf_op jit(solution)/shard_map/pallas_call | solution.py:329
  664.2 2.9 fusion.15
  667.2 1.3 copy.121
  671.9 1.0 copy.108
  672.9 2.2 copy.112
  676.0 1.0 copy.106
  677.0 2.0 copy.105
  679.0 3.4 copy.110
  682.5 2.2 copy.109
  684.7 9.5 fusion.8
  694.1 13.2 %reduce-scatter.16.cloned.1.call-done = f32[256,2]{1,0:T(8,128)} async-done(((f32[2048,2]{1,0:T(8,128)}), f32[256,2]{1,0:T(8,128)}) %reduce-scatter.16.cloned.1.call-update) | async-done | bytes 2064
  707.3 1.0 copy.122
  709.6 42.6 %reduce-scatter.10.cloned.1.call-done = bf16[512,256]{1,0:T(8,128)(2,1)} async-done(((bf16[512,2048]{1,0:T(8,128)(2,1)}), bf16[512,256]{1,0:T(8,128)(2,1)}) %reduce-scatter.10.cloned.1.call-update) | async-done | bytes 262160 | tf_op jit(solution)/shard_map/reduce_scatter | solution.py:567
  752.2 1.7 fusion.41
  753.9 45.3 %reduce-scatter.8.cloned.1.call-done = bf16[256,640]{0,1:T(8,128)(2,1)} async-done(((bf16[2048,640]{0,1:T(8,128)(2,1)}), bf16[256,640]{0,1:T(8,128)(2,1)}) %reduce-scatter.8.cloned.1.call-update) | async-done | bytes 327696 | tf_op jit(solution)/shard_map/reduce_scatter | solution.py:568
  799.2 1.0 convert_element_type.131
  804.2 57.6 %reduce-scatter.14.cloned.1.call-done = bf16[1408,256]{1,0:T(8,128)(2,1)} async-done(((bf16[1408,2048]{1,0:T(8,128)(2,1)}), bf16[1408,256]{1,0:T(8,128)(2,1)}) %reduce-scatter.14.cloned.1.call-update) | async-done | bytes 720912 | tf_op jit(solution)/shard_map/reduce_scatter | solution.py:547
  861.8 2.1 fusion.34
  863.9 88.4 %reduce-scatter.12.cloned.1.call-done = bf16[2,256,1408]{1,2,0:T(8,128)(2,1)} async-done(((bf16[2,2048,1408]{1,2,0:T(8,128)(2,1)}), bf16[2,256,1408]{1,2,0:T(8,128)(2,1)}) %reduce-scatter.12.cloned.1.call-update) | async-done | bytes 1441808 | tf_op jit(solution)/shard_map/reduce_scatter | solution.py:546
  952.3 2.7 fusion.22
  956.9 10.9 %shard_map.378 = f32[8,128]{1,0:T(8,128)} custom-call(f32[8,128]{1,0:T(8,128)} %broadcast_in_dim.5.in_ref), custom_call_target="tpu_custom_call" | custom-call | tf_op jit(solution)/shard_map/pallas_call | solution.py:391
  967.9 1.2 slice.69
  969.8 2.7 multiply_subtract_fusion.3
  972.5 2.0 copy.113
  974.6 2.0 copy.114
  976.6 2.0 copy.115
  978.6 6.1 multiply_subtract_fusion
  984.8 3.4 copy.116
  988.1 3.5 copy.117
  991.7 2.2 copy.118
  994.6 2.1 multiply_subtract_fusion.4
  996.8 2.7 multiply_subtract_fusion.2
  999.4 4.1 multiply_subtract_fusion.1
  (130 shorter events, 13.5 us)
Async XLA Ops:
  7.2 5.2 copy-start.14
  7.2 36.3 %all-gather.5.cloned.1.call-start = ((), (), s32[]{:S(2)}) async-start(), calls=%async_computation.5 | async-start | bytes 2949120 | tf_op jit(solution)/shard_map/all_gather | solution.py:499
  10.5 63.8 %all-gather.7.cloned.1.call-start = ((), (), s32[]{:S(2)}) async-start(), calls=%async_computation.6 | async-start | bytes 2359296 | tf_op jit(solution)/shard_map/all_gather | solution.py:500
  12.3 3.8 copy-start.4
  12.4 5.7 copy-start.34
  12.4 178.1 %all-gather.9.cloned.1.call-start = ((), (), s32[]{:S(2)}) async-start(), calls=%async_computation.7 | async-start | bytes 12976128 | tf_op jit(solution)/shard_map/all_gather | solution.py:501
  13.7 196.9 %all-gather.11.cloned.1.call-start = ((), (), s32[]{:S(2)}) async-start(), calls=%async_computation.8 | async-start | bytes 6488064 | tf_op jit(solution)/shard_map/all_gather | solution.py:502
  16.1 483.2 %all-reduce.2.cloned.1.call-start = ((), (), s32[]{:S(2)}) async-start(), calls=%async_computation.9 | async-start | bytes 8388608 | tf_op jit(solution)/shard_map/psum | solution.py:550
  18.3 13.5 %copy-start.8 = (bf16[1024,2048]{1,0:T(8,128)(2,1)S(1)}, bf16[1024,2048]{1,0:T(8,128)(2,1)}, u32[]{:S(2)}) copy-start(bf16[1024,2048]{1,0:T(8,128)(2,1)} %param.22) | copy-start | bytes 12582916
  32.6 17.1 %copy-start.32 = (f32[1024]{0:T(1024)}, f32[1024]{0:T(1024)S(1)}, u32[]{:S(2)}) copy-start(f32[1024]{0:T(1024)S(1)} %add_rsqrt_fusion.1) | copy-start | bytes 12292
  32.7 17.1 %copy-start.30 = (f32[1,2048]{1,0:T(1,128)}, f32[1,2048]{1,0:T(1,128)S(1)}, u32[]{:S(2)}) copy-start(f32[1,2048]{1,0:T(1,128)S(1)} %get-tuple-element.159) | copy-start | bytes 24580
  68.6 1.0 copy-start.6
  78.2 110.2 %copy-start.9 = (bf16[1024,2048]{1,0:T(8,128)(2,1)S(1)}, bf16[1024,2048]{1,0:T(8,128)(2,1)}, u32[]{:S(2)}) copy-start(bf16[1024,2048]{1,0:T(8,128)(2,1)} %param.22) | copy-start | bytes 12582916
  188.4 2.0 copy-start
  210.6 17.8 %copy-start.19 = (bf16[1024,2048]{1,0:T(8,128)(2,1)S(1)}, bf16[1024,2048]{1,0:T(8,128)(2,1)}, u32[]{:S(2)}) copy-start(bf16[1024,2048]{1,0:T(8,128)(2,1)} %param.23) | copy-start | bytes 12582916
  226.8 1.6 copy-start.39
  247.4 459.9 %reduce-scatter.16.cloned.1.call-start = ((), (), s32[]{:S(2)}) async-start(), calls=%async_computation.14 | async-start | bytes 1179648
  284.1 211.6 %copy-start.1 = (bf16[1024,2048]{1,0:T(8,128)(2,1)S(1)}, bf16[1024,2048]{1,0:T(8,128)(2,1)}, u32[]{:S(2)}) copy-start(bf16[1024,2048]{1,0:T(8,128)(2,1)} %copy-done) | copy-start | bytes 12582916
  284.2 211.6 %copy-start.10 = (bf16[1024,2048]{1,0:T(8,128)(2,1)S(1)}, bf16[1024,2048]{1,0:T(8,128)(2,1)}, u32[]{:S(2)}) copy-start(bf16[1024,2048]{1,0:T(8,128)(2,1)} %param.22) | copy-start | bytes 12582916
  495.8 3.5 copy-start.3
  511.0 3.4 copy-start.13
  518.2 6.4 copy-start.7
  524.7 22.3 %copy-start.11 = (bf16[1024,2048]{1,0:T(8,128)(2,1)S(1)}, bf16[1024,2048]{1,0:T(8,128)(2,1)}, u32[]{:S(2)}) copy-start(bf16[1024,2048]{1,0:T(8,128)(2,1)} %param.22) | copy-start | bytes 12582916
  524.7 22.3 %copy-start.31 = (f32[1,2048]{1,0:T(1,128)S(1)}, f32[1,2048]{1,0:T(1,128)}, u32[]{:S(2)}) copy-start(f32[1,2048]{1,0:T(1,128)} %copy-done.30) | copy-start | bytes 24580
  524.7 22.3 %copy-start.33 = (f32[1024]{0:T(1024)S(1)}, f32[1024]{0:T(1024)}, u32[]{:S(2)}) copy-start(f32[1024]{0:T(1024)} %copy-done.32) | copy-start | bytes 12292
  545.9 1.1 copy-start.5
  546.9 4.6 copy-start.38
  556.6 107.7 %copy-start.12 = (bf16[1024,2048]{1,0:T(8,128)(2,1)S(1)}, bf16[1024,2048]{1,0:T(8,128)(2,1)}, u32[]{:S(2)}) copy-start(bf16[1024,2048]{1,0:T(8,128)(2,1)} %param.22) | copy-start | bytes 12582916
  664.2 3.0 copy-start.2
  668.6 83.6 %reduce-scatter.10.cloned.1.call-start = ((), (), s32[]{:S(2)}) async-start(), calls=%async_computation.11 | async-start | bytes 2359296 | tf_op jit(solution)/shard_map/reduce_scatter | solution.py:567
  669.3 129.9 %reduce-scatter.8.cloned.1.call-start = ((), (), s32[]{:S(2)}) async-start(), calls=%async_computation.10 | async-start | bytes 2949120 | tf_op jit(solution)/shard_map/reduce_scatter | solution.py:568
  670.1 191.7 %reduce-scatter.14.cloned.1.call-start = ((), (), s32[]{:S(2)}) async-start(), calls=%async_computation.13 | async-start | bytes 6488064 | tf_op jit(solution)/shard_map/reduce_scatter | solution.py:547
  670.8 1.0 copy-start.22
  670.8 2.0 copy-start.15
  670.9 281.4 %reduce-scatter.12.cloned.1.call-start = ((), (), s32[]{:S(2)}) async-start(), calls=%async_computation.12 | async-start | bytes 12976128 | tf_op jit(solution)/shard_map/reduce_scatter | solution.py:546
  672.9 3.1 copy-start.29
  675.1 7.4 copy-start.20
  800.3 0.6 copy-start.25
  800.3 1.3 copy-start.27
  863.9 114.8 %copy-start.16 = (f32[2,256,1408]{1,2,0:T(8,128)S(1)}, f32[2,256,1408]{1,2,0:T(8,128)}, u32[]{:S(2)}) copy-start(f32[2,256,1408]{1,2,0:T(8,128)} %copy.112) | copy-start | bytes 8650756
  988.1 3.6 copy-start.17
  991.7 2.3 copy-start.35
  991.7 2.3 copy-start.36
  991.7 2.3 copy-start.37
  991.7 2.9 copy-start.26
  991.7 2.9 copy-start.28
  991.7 5.1 copy-start.23
  994.0 5.5 copy-start.18
  994.0 5.5 copy-start.21
  994.0 5.5 copy-start.24
Sparse Core Ops, SparseCore 0:
  10.6 32.8 all-gather.4
  45.9 28.2 all-gather.6
  76.7 67.6 all-gather.8
  146.7 44.3 all-gather.10
  247.5 225.2 all-reduce.1
  668.7 38.5 reduce-scatter.15
  711.0 41.1 reduce-scatter.9
  755.5 43.6 reduce-scatter.7
  802.7 59.0 reduce-scatter.13
  865.5 86.7 reduce-scatter.11

commit v2 on v1

--- a/solution.py
+++ b/solution.py
@@ -343,7 +343,8 @@
     )(partial)
 
 
-def total_kernel(n, m, in_ref, out_ref, line, got_line, got_plane, send_line, recv_line, send_plane, recv_plane):
+def total_kernel(n, m, gains_ref, square_ref, total_ref, gain_ref, line, got_gains, got_line, got_plane,
+                 send_gains, recv_gains, send_line, recv_line, send_plane, recv_plane):
     z = lax.axis_index("tensor")
     d = lax.axis_index("dp")
     barrier = pltpu.get_barrier_semaphore()
@@ -353,58 +354,76 @@
         pl.semaphore_signal(barrier, inc=1, device_id={"dp": lax.rem(d + k, m)}, device_id_type=MESH)
     pl.semaphore_wait(barrier, n - 1 + m - 1)
 
+    def gains_to(k, sender):
+        peer = lax.rem(d + k, m)
+        return pltpu.make_async_remote_copy(
+            src_ref=gains_ref.at[peer], dst_ref=got_gains.at[sender], send_sem=send_gains.at[k],
+            recv_sem=recv_gains.at[sender], device_id={"dp": peer}, device_id_type=MESH)
+
     def along_line(k, sender):
         return pltpu.make_async_remote_copy(
-            src_ref=in_ref, dst_ref=got_line.at[sender], send_sem=send_line.at[k], recv_sem=recv_line.at[sender],
+            src_ref=line.at[0], dst_ref=got_line.at[sender], send_sem=send_line.at[k], recv_sem=recv_line.at[sender],
             device_id={"tensor": lax.rem(z + k, n)}, device_id_type=MESH)
 
     def over_plane(k, sender):
         return pltpu.make_async_remote_copy(
-            src_ref=line, dst_ref=got_plane.at[sender], send_sem=send_plane.at[k], recv_sem=recv_plane.at[sender],
+            src_ref=line.at[1], dst_ref=got_plane.at[sender], send_sem=send_plane.at[k], recv_sem=recv_plane.at[sender],
             device_id={"dp": lax.rem(d + k, m)}, device_id_type=MESH)
 
+    def summed(ref, count):
+        whole = ref[0]
+        for k in range(1, count):
+            whole = whole + ref[k]
+        return whole
+
+    for k in range(1, m):
+        gains_to(k, d).start()
+    got_gains[d] = gains_ref[d]
+    for k in range(1, m):
+        gains_to(k, d).wait_send()
+        gains_to(k, lax.rem(d + m - k, m)).wait_recv()
+    gains = summed(got_gains, m)
+    gain_ref[...] = gains
+    own = jnp.sum(jnp.sum(gains * gains, axis=1, keepdims=True), axis=0, keepdims=True)
+    own = jnp.where(z == 0, own, jnp.zeros_like(own))
+    line[0] = square_ref[...] + jnp.broadcast_to(own, square_ref.shape)
     for k in range(1, n):
         along_line(k, z).start()
-    got_line[z] = in_ref[...]
+    got_line[z] = line[0]
     for k in range(1, n):
         along_line(k, z).wait_send()
         along_line(k, lax.rem(z + n - k, n)).wait_recv()
-    whole = got_line[0]
-    for k in range(1, n):
-        whole = whole + got_line[k]
-    line[...] = whole
+    line[1] = summed(got_line, n)
     for k in range(1, m):
         over_plane(k, d).start()
-    got_plane[d] = line[...]
+    got_plane[d] = line[1]
     for k in range(1, m):
         over_plane(k, d).wait_send()
         over_plane(k, lax.rem(d + m - k, m)).wait_recv()
-    whole = got_plane[0]
-    for k in range(1, m):
-        whole = whole + got_plane[k]
-    out_ref[...] = whole
-
-
-def total_sum(value, n, m, cid):
-    tile = jnp.broadcast_to(value.reshape(1, 1), (8, 128))
+    total_ref[...] = summed(got_plane, m)
+
+
+def reduce_tail(gains, square, n, m, cid):
+    share = gains.shape[1] // m
+    parts = gains.reshape(2, m, share).transpose(1, 0, 2)
+    tile = jnp.broadcast_to(square.reshape(1, 1), (8, 128))
     vmem = pl.BlockSpec(memory_space=pltpu.VMEM)
-    total = pl.pallas_call(
+    dma = pltpu.SemaphoreType.DMA
+    total, gain = pl.pallas_call(
         functools.partial(total_kernel, n, m),
-        out_shape=jax.ShapeDtypeStruct((8, 128), jnp.float32),
-        in_specs=[vmem],
-        out_specs=vmem,
+        out_shape=(jax.ShapeDtypeStruct((8, 128), jnp.float32), jax.ShapeDtypeStruct((2, share), jnp.float32)),
+        in_specs=[vmem, vmem],
+        out_specs=(vmem, vmem),
         scratch_shapes=[
-            pltpu.VMEM((8, 128), jnp.float32),
+            pltpu.VMEM((2, 8, 128), jnp.float32),
+            pltpu.VMEM((m, 2, share), jnp.float32),
             pltpu.VMEM((n, 8, 128), jnp.float32),
             pltpu.VMEM((m, 8, 128), jnp.float32),
-            pltpu.SemaphoreType.DMA((n,)),
-            pltpu.SemaphoreType.DMA((n,)),
-            pltpu.SemaphoreType.DMA((m,)),
-            pltpu.SemaphoreType.DMA((m,)),
+            dma((m,)), dma((m,)), dma((n,)), dma((n,)), dma((m,)), dma((m,)),
         ],
         compiler_params=pltpu.CompilerParams(collective_id=cid, has_side_effects=True),
-    )(tile)
-    return total[0, 0]
+    )(parts, tile)
+    return total[0, 0], gain
 
 
 norm_eps = 1e-05
@@ -546,9 +565,8 @@
     gateup_reduced = lax.psum_scatter(grad_gateup_weight, "dp", scatter_dimension=1, tiled=True)
     down_reduced = lax.psum_scatter(grad_down_weight, "dp", scatter_dimension=1, tiled=True)
     grad_normed_two = line_reduce(partial_two, n, 16, 2, 2)
+    grad_normed_two, gateup_reduced = lax.optimization_barrier((grad_normed_two, gateup_reduced))
     feed_part = jnp.dot(hidden, down_weight, preferred_element_type=jnp.float32).astype(low)
-    feed_out = lax.psum(feed_part, "tensor").astype(jnp.float32)
-    layer_out = (middle + feed_out).astype(low)
     grad_from_two, gain_grad_two = norm_back(
         grad_normed_two.astype(jnp.float32), unit_two, inverse_two, gain_values[1]
     )
@@ -561,30 +579,28 @@
     partial_one = against(grad_qkv, qkv_weight).astype(low)
     grad_out_weight = over_rows(mixture, grad_branch).astype(low)
     grad_qkv_weight = over_rows(normed_one, grad_qkv).astype(low)
-    partial_one, grad_out_weight, grad_qkv_weight = lax.optimization_barrier(
-        (partial_one, grad_out_weight, grad_qkv_weight)
+    partial_one, grad_out_weight, grad_qkv_weight, down_reduced = lax.optimization_barrier(
+        (partial_one, grad_out_weight, grad_qkv_weight, down_reduced)
     )
     out_reduced = lax.psum_scatter(grad_out_weight, "dp", scatter_dimension=1, tiled=True)
     qkv_reduced = lax.psum_scatter(grad_qkv_weight, "dp", scatter_dimension=0, tiled=True)
-    grad_normed_one = line_reduce(partial_one, n, 16, 3, 2).astype(jnp.float32)
+    summed = line_reduce(jnp.concatenate([partial_one, feed_part]), n, 32, 3, 2).astype(jnp.float32)
+    grad_normed_one = summed[:length]
+    layer_out = (middle + summed[length:]).astype(low)
     grad_from_one, gain_grad_one = norm_back(grad_normed_one, unit_one, inverse_one, gain_values[0])
     input_grad = grad_middle + grad_from_one
     gain_grads = jnp.stack([gain_grad_one, gain_grad_two])
-    gains_reduced = lax.psum_scatter(gain_grads, "dp", scatter_dimension=1, tiled=True)
     qkv_reduced = qkv_reduced.astype(jnp.float32)
     reduced = (
-        gains_reduced,
         qkv_reduced[:, :width],
         jnp.stack([qkv_reduced[:, width : width + kv_width], qkv_reduced[:, width + kv_width :]]),
         out_reduced.astype(jnp.float32),
         gateup_reduced.astype(jnp.float32),
         down_reduced.astype(jnp.float32),
     )
-    first_owner = (lax.axis_index("tensor") == 0).astype(jnp.float32)
-    local_square = first_owner * jnp.sum(reduced[0] * reduced[0]) + sum(
-        (jnp.sum(g * g) for g in reduced[1:])
-    )
-    square_total = total_sum(local_square, n, m, 4)
+    local_square = sum((jnp.sum(g * g) for g in reduced))
+    square_total, gains_reduced = reduce_tail(gain_grads, local_square, n, m, 4)
+    reduced = (gains_reduced, *reduced)
     grad_norm = jnp.sqrt(square_total)
     clip_factor = jnp.minimum(1.0, clip_limit / (grad_norm + 1e-06))
     step_float = step_count[0].astype(jnp.float32)

time: 1020 us -> 794 us (0.78)
  waiting for transfers between devices: 265 us -> 11.5 us
  other arithmetic: 69.4 us -> 90.9 us
    reduce_scatter x1, waiting for transfers between devices: 88.4 us -> 0.01 us  [on_device(): lax.psum_scatter(grad_gateup_weight, 'dp', scatter_dimension=1, tiled=True)]
    reduce_scatter x1, waiting for transfers between devices: 57.6 us -> 0.01 us  [on_device(): lax.psum_scatter(grad_down_weight, 'dp', scatter_dimension=1, tiled=True)]
    reduce_scatter x1, waiting for transfers between devices: 45.3 us -> 0.01 us  [on_device(): lax.psum_scatter(grad_qkv_weight, 'dp', scatter_dimension=0, tiled=True)]
    reduce_scatter x1, waiting for transfers between devices: 42.6 us -> 0.01 us  [on_device(): lax.psum_scatter(grad_out_weight, 'dp', scatter_dimension=1, tiled=True)]
    pallas_call x3, Pallas kernels: 429 us -> 413 us  [line_reduce(): pl.pallas_call(kernel, out_shape=jax.ShapeDtypeStruct((rows, width), part...]
    unnamed x11 -> x8, waiting for transfers between devices: 15.9 us -> 0.64 us
    convert_element_type x0 -> x1, other arithmetic: none -> 11.4 us  [on_device(): line_reduce(jnp.concatenate([partial_one, feed_part]), n, 32, 3, 2)]
    unnamed x94 -> x108, local copies, waits for them, and re-layouts: 38.2 us -> 42.3 us
  transfers between devices with their start and end apart: 10 -> 8, of which waited for: 7 -> 1; matrix products, arithmetic and copies ran while one was open for 11% -> 18% of each run, Pallas kernels for 34% -> 59%
where the time goes in v2:
time: 794 us; the launch traced here: 787 us
  Pallas kernels  484 us (61%)
  matrix products  123 us (15%)
  other arithmetic  90.9 us (11%)
  local copies, waits for them, and re-layouts  45.4 us (6%)
  between operations  21.8 us (3%)
  waiting for transfers between devices  11.5 us (1%)
  blocking collectives  10.6 us (1%)
    pallas_call x3, Pallas kernels, line_reduce(): pl.pallas_call(kernel, out_shape=jax.ShapeDtypeStruct((rows, width), part...  413 us
    unnamed x108, local copies, waits for them, and re-layouts  42.3 us
    pallas_call x1, Pallas kernels, attention_backward(): pl.pallas_call(functools.partial(backward_kernel, size, pairs), out_shape...  27.1 us
    pallas_call x1, Pallas kernels, attention_forward(): pl.pallas_call(functools.partial(forward_kernel, size, pairs), out_shape=...  25 us
    dot_general x3, matrix products, against(): lax.dot_general(left, right, (((1,), (1,)), ((), ())), preferred_element_...  23.6 us
    dot_general x3, matrix products, over_rows(): lax.dot_general(left, right, (((0,), (0,)), ((), ())), preferred_element_...  20.4 us
    dot_general x1, matrix products, on_device(): jnp.einsum('nd,sdf->snf', normed_two, gateup_weight, preferred_element_ty...  20.2 us
    dot_general x1, matrix products, on_device(): jnp.einsum('nd,snf->sdf', normed_two, grad_gateup, preferred_element_type...  19.4 us
  transfers between devices with their start and end apart: 8, of which 1 were waited for; matrix products, arithmetic and copies ran while one was open for 18% of the time, Pallas kernels for 59%

profile of v2, /device:TPU:0, one launch (start us, length us, event | category | flops | bytes accessed | tf_op | source)
XLA Modules:
  0.0 787.2 jit_solution(10348904532466943575)
XLA Ops:
  7.2 1.1 convert.20
  8.6 1.1 convert.19
  10.5 1.8 convert_element_type.105
  12.4 1.2 convert_element_type.111
  13.7 2.3 convert_element_type.109
  18.3 10.6 %all_gather.15 = bf16[2,2048]{1,0:T(2,128)(2,1)S(1)} all-gather(bf16[2,256]{1,0:T(2,128)(2,1)S(1)} %convert_element_type.101), channel_id=1, replica_groups=mesh['dp'=8,'tensor'=4] {'dp'}, dimensions={1}, use_global_device_ids=true | all-gather | bytes 9216 | tf_op jit(solution)/shard_map/all_gather | solution.py:516
  28.9 1.9 fusion.45
  30.8 0.9 pad_maximum_fusion.4
  31.7 0.9 fusion.16
  32.7 10.8 %all-gather.5.cloned.1.call-done = bf16[2048,640]{1,0:T(8,128)(2,1)} async-done(((bf16[256,640]{1,0:T(8,128)(2,1)}), bf16[2048,640]{1,0:T(8,128)(2,1)}) %all-gather.5.cloned.1.call-update) | async-done | bytes 2621456 | tf_op jit(solution)/shard_map/all_gather | solution.py:518
  43.5 6.3 fusion.38.raw_ref
  49.8 25.0 %shard_map.373 = (bf16[1024,512]{1,0:T(8,128)(2,1)S(1)}, bf16[1024,512]{1,0:T(8,128)(2,1)S(1)}, bf16[1024,128]{1,0:T(8,128)(2,1)S(1)}, bf16[1024,128]{1,0:T(8,128)(2,1)S(1)}, f32[4,4,1,512]{3,2,1,0:T(1,128)S(1)}) custom-call(s32[4]{0:T(128)S(1)} %and_select_fusion.first_ref, f32[1024,640]{1,0:T(8,128)S(1)} %fusion.38.raw_ref, ...), custom_call_target="tpu_custom_call" | custom-call | flops 5368709120 | bytes 4194304 | tf_op jit(solution)/shard_map/pallas_call | solution.py:117
  74.8 1.0 copy-done.8
  75.7 3.9 convolution_convert_fusion.3.in_ref
  79.7 109.3 %shard_map.374 = bf16[1024,2048]{1,0:T(8,128)(2,1)S(1)} custom-call(bf16[1024,2048]{1,0:T(8,128)(2,1)S(1)} %convolution_convert_fusion.3.in_ref), custom_call_target="tpu_custom_call" | custom-call | flops 4194304 | bytes 251658240 | tf_op jit(solution)/shard_map/pallas_call | solution.py:329
  189.0 1.4 multiply_reduce_fusion
  191.0 20.2 %convolution_bitcast_fusion = f32[2,1024,1408]{2,1,0:T(8,128)} fusion(bf16[2,2048,1408]{2,1,0:T(8,128)(2,1)} %all-gather.11.cloned.1.call-done, bf16[1024,2048]{1,0:T(8,128)(2,1)} %copy-done, bf16[1024,2048]{1,0:T(8,128)(2,1)} %param.22, f32[2048]{0:T(1024)S(1)} %bitcast.88, f32[1024]{0:T(1024)S(1)} %add_rsqrt_fusion), kind=kOutput, calls=%fused_computation.32 | convolution fusion | flops 11823742976 | bytes 31469568 | tf_op jit(solution)/shard_map/nd,sdf->snf/dot_general | solution.py:543
  211.2 16.2 %fusion.26 = (bf16[1,1024,1408]{2,1,0:T(8,128)(2,1)}, bf16[1,1024,1408]{2,1,0:T(8,128)(2,1)}, bf16[1024,1408]{1,0:T(8,128)(2,1)S(1)}) fusion(f32[2,1024,1408]{2,1,0:T(8,128)} %convolution_bitcast_fusion, bf16[1024,2048]{1,0:T(8,128)(2,1)} %param.23, bf16[1408,2048]{1,0:T(8,128)(2,1)} %all-gather.9.cloned.1.call-done), kind=kOutput, calls=%fused_computation.56 | convolution fusion | flops 5927206912 | bytes 30146560 | tf_op jit(solution)/shard_map/dot_general | solution.py:465
  227.4 1.6 copy-done.47
  229.0 8.5 %convolution_convert_fusion = bf16[1408,2048]{1,0:T(8,128)(2,1)} fusion(bf16[1024,1408]{1,0:T(8,128)(2,1)S(1)} %get-tuple-element.142, bf16[1024,2048]{1,0:T(8,128)(2,1)S(1)} %copy-done.20), kind=kOutput, calls=%fused_computation.30 | convolution fusion | flops 5908463616 | bytes 12845056 | tf_op jit(solution)/shard_map/dot_general | solution.py:459
  237.5 19.4 %convert_bitcast_fusion = bf16[2,2048,1408]{1,2,0:T(8,128)(2,1)} fusion(bf16[1,1024,1408]{2,1,0:T(8,128)(2,1)} %get-tuple-element.141, bf16[1,1024,1408]{2,1,0:T(8,128)(2,1)} %get-tuple-element.140, bf16[1024,2048]{1,0:T(8,128)(2,1)} %copy-done, bf16[1024,2048]{1,0:T(8,128)(2,1)} %param.22, f32[2048]{0:T(1024)S(1)} %bitcast.89, f32[1024]{0:T(1024)S(1)} %add_rsqrt_fusion), kind=kOutput, calls=%fused_computation.7 | convolution fusion | flops 11832393728 | bytes 25702400 | tf_op jit(solution)/shard_map/nd,snf->sdf/dot_general | solution.py:559
  256.9 18.0 %bitcast_convert_fusion.in_ref = bf16[1024,2048]{1,0:T(8,128)(2,1)} fusion(bf16[2,2048,1408]{2,1,0:T(8,128)(2,1)} %all-gather.11.cloned.1.call-done, bf16[1,1024,1408]{2,1,0:T(8,128)(2,1)} %get-tuple-element.141, bf16[1,1024,1408]{2,1,0:T(8,128)(2,1)} %get-tuple-element.140), kind=kOutput, calls=%fused_computation.26 | convolution fusion | flops 11816140800 | bytes 21495808 | tf_op jit(solution)/shard_map/snf,sdf->nd/dot_general | solution.py:555
  275.6 2.2 copy-done.6
  277.7 106.8 %shard_map.375 = bf16[1024,2048]{1,0:T(8,128)(2,1)S(1)} custom-call(bf16[1024,2048]{1,0:T(8,128)(2,1)S(1)} %copy-done.6), custom_call_target="tpu_custom_call" | custom-call | flops 4194304 | bytes 251658240 | tf_op jit(solution)/shard_map/pallas_call | solution.py:329
  384.5 2.0 copy-done.3
  386.5 7.5 fusion.9
  394.6 1.2 copy-done.12
  395.8 6.7 fusion.8
  402.5 2.4 fusion.31.grad_ref
  404.9 1.0 copy-done.14
  405.9 27.1 %shard_map.376 = bf16[1024,640]{1,0:T(8,128)(2,1)S(1)} custom-call(s32[4]{0:T(128)S(1)} %and_select_fusion.first_ref, bf16[1024,512]{1,0:T(8,128)(2,1)S(1)} %copy-done.9, bf16[1024,128]{1,0:T(8,128)(2,1)S(1)} %get-tuple-element.39.k_ref, bf16[1024,128]{1,0:T(8,128)(2,1)S(1)} %get-tuple-element.40.v_ref, bf16[1024,512]{1,0:T(8,128)(2,1)S(1)} %get-tuple-element.37.mix_ref, ...), custom_call_target="tpu_custom_call" | custom-call | flops 10737418240 | bytes 4194304 | tf_op jit(solution)/shard_map/pallas_call | solution.py:211
  433.0 5.1 convolution_convert_fusion.2
  438.1 4.8 convolution_convert_fusion.4
  442.9 7.1 convolution_convert_fusion.5
  450.1 1.0 copy.89
  451.1 0.9 copy-done.16
  452.0 2.2 copy.93
  455.2 1.0 copy.87
  456.2 2.1 copy.86
  458.2 3.5 copy.91
  461.7 2.2 copy.90
  464.0 11.0 %convolution_convert_fusion.1 = bf16[1024,2048]{1,0:T(8,128)(2,1)} fusion(bf16[1024,1408]{1,0:T(8,128)(2,1)} %copy-done.47, bf16[1408,2048]{1,0:T(8,128)(2,1)} %all-gather.9.cloned.1.call-done), kind=kOutput, calls=%fused_computation.43 | convolution fusion | flops 5907677184 | bytes 12845056 | tf_op jit(solution)/shard_map/dot_general | solution.py:569
  474.9 8.5 %pad_maximum_fusion.in_ref = bf16[2048,2048]{1,0:T(8,128)(2,1)} fusion(bf16[1024,2048]{1,0:T(8,128)(2,1)} %convolution_convert_fusion.1, bf16[1024,2048]{1,0:T(8,128)(2,1)} %convolution_convert_fusion.2), kind=kLoop, calls=%fused_computation.25 | loop fusion | flops 16777216 | bytes 16777216 | tf_op jit(solution)/shard_map/concatenate | solution.py:587
  483.4 196.8 %shard_map.377 = bf16[2048,2048]{1,0:T(8,128)(2,1)S(1)} custom-call(bf16[2048,2048]{1,0:T(8,128)(2,1)} %pad_maximum_fusion.in_ref), custom_call_target="tpu_custom_call" | custom-call | flops 8388608 | bytes 503316480 | tf_op jit(solution)/shard_map/pallas_call | solution.py:329
  680.2 3.3 copy-done.5
  683.5 11.4 %convert_element_type.124 = f32[2048,2048]{1,0:T(8,128)} convert(bf16[2048,2048]{1,0:T(8,128)(2,1)} %copy-done.5) | non-fusion elementwise | flops 4194304 | bytes 25165824 | tf_op jit(solution)/shard_map/convert_element_type | solution.py:587
  694.9 4.9 fusion.15
  700.5 1.0 fusion.35
  701.4 1.3 fusion.23
  702.8 13.8 %fusion.14 = (f32[1024,2048]{1,0:T(8,128)}, bf16[1024,2048]{1,0:T(8,128)(2,1)}) fusion(f32[1024,2048]{1,0:T(8,128)} %copy-done.14, bf16[1024,2048]{1,0:T(8,128)(2,1)S(1)} %copy-done.13, f32[2048,2048]{1,0:T(8,128)} %convert_element_type.124, f32[1024]{0:T(1024)S(1)} %broadcast_multiply_fusion, f32[2048]{0:T(1024)S(1)} %bitcast.95, f32[1024]{0:T(1024)S(1)} %copy-done.39, ...), kind=kLoop, calls=%fused_computation.20 | loop fusion | flops 23068672 | bytes 46153728 | tf_op jit(solution)/shard_map/add | solution.py:591
  716.6 1.7 fusion.42
  718.3 1.2 convert_element_type.126
  725.3 19.1 %shard_map.378 = (f32[8,128]{1,0:T(8,128)}, f32[2,256]{1,0:T(2,128)}) custom-call(f32[8,2,256]{2,1,0:T(2,128)} %maximum_bitcast_fusion.gains_ref, f32[8,128]{1,0:T(8,128)} %broadcast_in_dim.5.square_ref), custom_call_target="tpu_custom_call" | custom-call | tf_op jit(solution)/shard_map/pallas_call | solution.py:412
  744.5 1.2 slice.77
  746.4 2.7 multiply_subtract_fusion.3
  749.1 2.0 copy.94
  751.2 2.0 copy.95
  753.2 2.0 copy.96
  755.2 6.1 multiply_subtract_fusion
  761.4 3.4 copy.97
  764.8 3.5 copy.98
  768.3 2.2 copy.99
  771.4 5.4 multiply_subtract_fusion.1
  777.4 1.4 multiply_subtract_fusion.2
  (139 shorter events, 9.5 us)
Async XLA Ops:
  7.2 5.2 copy-start.15
  7.2 36.3 %all-gather.5.cloned.1.call-start = ((), (), s32[]{:S(2)}) async-start(), calls=%async_computation.4 | async-start | bytes 2949120 | tf_op jit(solution)/shard_map/all_gather | solution.py:518
  10.5 65.2 %all-gather.7.cloned.1.call-start = ((), (), s32[]{:S(2)}) async-start(), calls=%async_computation.5 | async-start | bytes 2359296 | tf_op jit(solution)/shard_map/all_gather | solution.py:519
  12.3 3.8 copy-start.7
  12.4 5.7 copy-start.40
  12.4 178.7 %all-gather.11.cloned.1.call-start = ((), (), s32[]{:S(2)}) async-start(), calls=%async_computation.7 | async-start | bytes 12976128 | tf_op jit(solution)/shard_map/all_gather | solution.py:520
  13.7 197.5 %all-gather.9.cloned.1.call-start = ((), (), s32[]{:S(2)}) async-start(), calls=%async_computation.6 | async-start | bytes 6488064 | tf_op jit(solution)/shard_map/all_gather | solution.py:521
  16.1 370.4 %reduce-scatter.5.cloned.1.call-start = ((), (), s32[]{:S(2)}) async-start(), calls=%async_computation.8 | async-start | bytes 12976128 | tf_op jit(solution)/shard_map/reduce_scatter | solution.py:565
  18.3 13.5 %copy-start.10 = (bf16[1024,2048]{1,0:T(8,128)(2,1)S(1)}, bf16[1024,2048]{1,0:T(8,128)(2,1)}, u32[]{:S(2)}) copy-start(bf16[1024,2048]{1,0:T(8,128)(2,1)} %param.22) | copy-start | bytes 12582916
  32.6 17.1 %copy-start.38 = (f32[1024]{0:T(1024)}, f32[1024]{0:T(1024)S(1)}, u32[]{:S(2)}) copy-start(f32[1024]{0:T(1024)S(1)} %add_rsqrt_fusion.1) | copy-start | bytes 12292
  32.7 17.1 %copy-start.36 = (f32[1,2048]{1,0:T(1,128)}, f32[1,2048]{1,0:T(1,128)S(1)}, u32[]{:S(2)}) copy-start(f32[1,2048]{1,0:T(1,128)S(1)} %get-tuple-element.148) | copy-start | bytes 24580
  74.7 1.0 copy-start.8
  79.7 109.3 %copy-start.11 = (bf16[1024,2048]{1,0:T(8,128)(2,1)S(1)}, bf16[1024,2048]{1,0:T(8,128)(2,1)}, u32[]{:S(2)}) copy-start(bf16[1024,2048]{1,0:T(8,128)(2,1)} %param.22) | copy-start | bytes 12582916
  189.0 2.0 copy-start
  211.2 17.8 %copy-start.20 = (bf16[1024,2048]{1,0:T(8,128)(2,1)S(1)}, bf16[1024,2048]{1,0:T(8,128)(2,1)}, u32[]{:S(2)}) copy-start(bf16[1024,2048]{1,0:T(8,128)(2,1)} %param.23) | copy-start | bytes 12582916
  227.4 1.6 copy-start.47
  274.9 175.1 %reduce-scatter.7.cloned.1.call-start = ((), (), s32[]{:S(2)}) async-start(), calls=%async_computation.9 | async-start | bytes 6488064 | tf_op jit(solution)/shard_map/reduce_scatter | solution.py:566
  275.5 441.1 %reduce-scatter.11.cloned.1.call-start = ((), (), s32[]{:S(2)}) async-start(), calls=%async_computation.11 | async-start | bytes 2359296 | tf_op jit(solution)/shard_map/reduce_scatter | solution.py:585
  275.5 2.2 copy-start.6
  384.5 2.0 copy-start.3
  386.5 7.5 copy-start.1
  386.5 8.1 %copy-start.4 = (bf16[1024,2048]{1,0:T(8,128)(2,1)S(1)}, bf16[1024,2048]{1,0:T(8,128)(2,1)}, u32[]{:S(2)}) copy-start(bf16[1024,2048]{1,0:T(8,128)(2,1)} %copy-done.3) | copy-start | bytes 12582916
  386.5 9.3 %copy-start.12 = (bf16[1024,2048]{1,0:T(8,128)(2,1)S(1)}, bf16[1024,2048]{1,0:T(8,128)(2,1)}, u32[]{:S(2)}) copy-start(bf16[1024,2048]{1,0:T(8,128)(2,1)} %param.22) | copy-start | bytes 12582916
  395.8 6.7 copy-start.46
  402.5 3.4 copy-start.14
  402.5 3.4 copy-start.9
  405.9 27.1 %copy-start.45 = (bf16[2048,640]{1,0:T(8,128)(2,1)S(1)}, bf16[2048,640]{1,0:T(8,128)(2,1)}, u32[]{:S(2)}) copy-start(bf16[2048,640]{1,0:T(8,128)(2,1)} %all-gather.5.cloned.1.call-done) | copy-start | bytes 7864324
  433.0 5.1 copy-start.37
  433.0 5.1 copy-start.39
  442.9 7.2 copy-start.23
  450.0 2.0 copy-start.16
  450.1 268.2 %reduce-scatter.9.cloned.1.call-start = ((), (), s32[]{:S(2)}) async-start(), calls=%async_computation.10 | async-start | bytes 2949120 | tf_op jit(solution)/shard_map/reduce_scatter | solution.py:586
  452.0 3.1 copy-start.30
  454.3 7.5 copy-start.21
  680.2 3.3 copy-start.5
  683.5 11.4 %copy-start.13 = (bf16[1024,2048]{1,0:T(8,128)(2,1)S(1)}, bf16[1024,2048]{1,0:T(8,128)(2,1)}, u32[]{:S(2)}) copy-start(bf16[1024,2048]{1,0:T(8,128)(2,1)} %param.22) | copy-start | bytes 12582916
  694.9 5.6 copy-start.22
  694.9 6.5 copy-start.19
  694.9 7.9 copy-start.2
  718.3 36.9 %copy-start.17 = (f32[2,256,1408]{1,2,0:T(8,128)S(1)}, f32[2,256,1408]{1,2,0:T(8,128)}, u32[]{:S(2)}) copy-start(f32[2,256,1408]{1,2,0:T(8,128)} %copy.93) | copy-start | bytes 8650756
  720.2 0.6 copy-start.26
  720.2 0.6 copy-start.28
  764.7 3.6 copy-start.18
  768.3 2.3 copy-start.27
  768.3 2.3 copy-start.29
  768.3 2.3 copy-start.31
  768.3 2.3 copy-start.34
  768.3 2.3 copy-start.35
  771.4 5.4 copy-start.41
  771.4 5.4 copy-start.42
  771.4 5.4 copy-start.43
  771.4 5.4 copy-start.44
  771.4 6.0 copy-start.24
  771.4 6.0 copy-start.25
  771.4 6.0 copy-start.32
  771.4 6.0 copy-start.33
Sparse Core Ops, SparseCore 0:
  10.6 32.8 all-gather.4
  45.9 28.2 all-gather.6
  76.7 67.6 all-gather.10
  146.7 44.3 all-gather.8
  275.0 86.5 reduce-scatter.4
  365.0 59.0 reduce-scatter.6
  450.2 42.1 reduce-scatter.10
  495.7 43.6 reduce-scatter.8

commit v3 on v2

--- a/solution.py
+++ b/solution.py
@@ -225,122 +225,350 @@
     )(first, q, k, v, mix, grad, lse, cosines, sines, seg_col, seg_row)
 
 
-def line_reduce(partial, n, chunks, cid, lagk=1):
-    rows, width = partial.shape
-    half = rows // 2
-    rc = half // chunks
-
-    def kernel(in_ref, out_ref, got, send_a, recv_a, send_g, recv_g):
-        me = lax.axis_index("tensor")
-        barrier = pltpu.get_barrier_semaphore()
-
-        @pl.when(me > 0)
-        def _():
-            pl.semaphore_signal(barrier, inc=1, device_id={"tensor": me - 1}, device_id_type=MESH)
-
-        @pl.when(me < n - 1)
-        def _():
-            pl.semaphore_signal(barrier, inc=1, device_id={"tensor": me + 1}, device_id_type=MESH)
-
-        @pl.when((me > 0) & (me < n - 1))
-        def _():
-            pl.semaphore_wait(barrier, 2)
-
-        @pl.when((me == 0) | (me == n - 1))
-        def _():
-            pl.semaphore_wait(barrier, 1)
-
-        def rs(stream, c, nxt, src):
-            return pltpu.make_async_remote_copy(
-                src_ref=src, dst_ref=got.at[stream, c],
-                send_sem=send_a.at[stream, c], recv_sem=recv_a.at[stream, c],
-                device_id={"tensor": nxt}, device_id_type=MESH)
-
-        def ag(stream, c, nxt):
-            r0 = pl.multiple_of(stream * half + c * rc, rc)
-            return pltpu.make_async_remote_copy(
-                src_ref=out_ref.at[pl.ds(r0, rc)], dst_ref=out_ref.at[pl.ds(r0, rc)],
-                send_sem=send_g.at[stream, c], recv_sem=recv_g.at[stream, c],
-                device_id={"tensor": nxt}, device_id_type=MESH)
-
-        K = lagk
-        steps = chunks + 2 * K * (n - 1)
-
-        def body(s, carry):
-            for stream in (0, 1):
-                pos = me if stream == 0 else n - 1 - me
-                fwd = me + 1 if stream == 0 else me - 1
-                bwd = me - 1 if stream == 0 else me + 1
-                c = s - K * pos
-
-                @pl.when((c >= 0) & (c < chunks))
+class Line:
+    def __init__(self, n, chunks, rc, lag, part, got, out, sems):
+        self.n, self.chunks, self.rc, self.lag = n, chunks, rc, lag
+        self.part, self.got, self.out = part, got, out
+        self.send_a, self.recv_a, self.send_g, self.recv_g = sems
+        self.me = lax.axis_index("tensor")
+        self.steps = chunks + 2 * lag * (n - 1)
+
+    def rows(self, stream, c):
+        return pl.ds(pl.multiple_of((stream * self.chunks + c) * self.rc, self.rc), self.rc)
+
+    def side(self, stream):
+        pos = self.me if stream == 0 else self.n - 1 - self.me
+        fwd = self.me + 1 if stream == 0 else self.me - 1
+        bwd = self.me - 1 if stream == 0 else self.me + 1
+        return pos, fwd, bwd
+
+    def toward(self, stream, c, nxt, src):
+        return pltpu.make_async_remote_copy(
+            src_ref=src, dst_ref=self.got.at[stream, c],
+            send_sem=self.send_a.at[stream, c], recv_sem=self.recv_a.at[stream, c],
+            device_id={"tensor": nxt}, device_id_type=MESH)
+
+    def back(self, stream, c, nxt):
+        where = self.rows(stream, c)
+        return pltpu.make_async_remote_copy(
+            src_ref=self.out.at[where], dst_ref=self.out.at[where],
+            send_sem=self.send_g.at[stream, c], recv_sem=self.recv_g.at[stream, c],
+            device_id={"tensor": nxt}, device_id_type=MESH)
+
+    def step(self, s):
+        n, lag = self.n, self.lag
+        for stream in (0, 1):
+            pos, fwd, bwd = self.side(stream)
+            c = s - lag * pos
+
+            @pl.when((c >= 0) & (c < self.chunks))
+            def _():
+                where = self.rows(stream, c)
+                slot = self.got.at[stream, c]
+
+                def summed():
+                    self.toward(stream, c, fwd, slot).wait_recv()
+                    return (
+                        self.part[where, :].astype(jnp.float32) + self.got[stream, c].astype(jnp.float32)
+                    ).astype(self.out.dtype)
+
+                @pl.when(pos == 0)
                 def _():
-                    r0 = pl.multiple_of(stream * half + c * rc, rc)
-
-                    def summed():
-                        rs(stream, c, fwd, got.at[stream, c]).wait_recv()
-                        return (
-                            in_ref[pl.ds(r0, rc)].astype(jnp.float32) + got[stream, c].astype(jnp.float32)
-                        ).astype(out_ref.dtype)
-
-                    @pl.when(pos == 0)
-                    def _():
-                        rs(stream, c, fwd, in_ref.at[pl.ds(r0, rc)]).start()
-
-                    @pl.when((pos > 0) & (pos < n - 1))
-                    def _():
-                        got[stream, c] = summed()
-                        rs(stream, c, fwd, got.at[stream, c]).start()
-
-                    @pl.when(pos == n - 1)
-                    def _():
-                        out_ref[pl.ds(r0, rc)] = summed()
-                        ag(stream, c, bwd).start()
-                d = s - K * (n - 1) - K * (n - 1 - pos)
-
-                @pl.when((d >= 0) & (d < chunks) & (pos < n - 1))
+                    self.toward(stream, c, fwd, self.part.at[where]).start()
+
+                @pl.when((pos > 0) & (pos < n - 1))
                 def _():
-                    ag(stream, d, bwd).wait_recv()
-
-                    @pl.when(pos > 0)
-                    def _():
-                        ag(stream, d, bwd).start()
-            return carry
-
-        lax.fori_loop(0, steps, body, 0)
-
-        def drain(c, carry):
-            for stream in (0, 1):
-                pos = me if stream == 0 else n - 1 - me
-                fwd = me + 1 if stream == 0 else me - 1
-                bwd = me - 1 if stream == 0 else me + 1
-
-                @pl.when(pos < n - 1)
+                    self.got[stream, c] = summed()
+                    self.toward(stream, c, fwd, slot).start()
+
+                @pl.when(pos == n - 1)
                 def _():
-                    rs(stream, c, fwd, got.at[stream, c]).wait_send()
+                    self.out[where, :] = summed()
+                    self.back(stream, c, bwd).start()
+            d = s - lag * (n - 1) - lag * (n - 1 - pos)
+
+            @pl.when((d >= 0) & (d < self.chunks) & (pos < n - 1))
+            def _():
+                self.back(stream, d, bwd).wait_recv()
 
                 @pl.when(pos > 0)
                 def _():
-                    ag(stream, c, bwd).wait_send()
+                    self.back(stream, d, bwd).start()
+
+    def drain(self):
+        def one(c, carry):
+            for stream in (0, 1):
+                pos, fwd, bwd = self.side(stream)
+
+                @pl.when(pos < self.n - 1)
+                def _():
+                    self.toward(stream, c, fwd, self.got.at[stream, c]).wait_send()
+
+                @pl.when(pos > 0)
+                def _():
+                    self.back(stream, c, bwd).wait_send()
             return carry
 
-        lax.fori_loop(0, chunks, drain, 0)
-
+        lax.fori_loop(0, self.chunks, one, 0)
+
+
+def greet(n):
+    me = lax.axis_index("tensor")
+    barrier = pltpu.get_barrier_semaphore()
+
+    @pl.when(me > 0)
+    def _():
+        pl.semaphore_signal(barrier, inc=1, device_id={"tensor": me - 1}, device_id_type=MESH)
+
+    @pl.when(me < n - 1)
+    def _():
+        pl.semaphore_signal(barrier, inc=1, device_id={"tensor": me + 1}, device_id_type=MESH)
+
+    @pl.when((me > 0) & (me < n - 1))
+    def _():
+        pl.semaphore_wait(barrier, 2)
+
+    @pl.when((me == 0) | (me == n - 1))
+    def _():
+        pl.semaphore_wait(barrier, 1)
+
+
+def line_scratch(chunks, rc, width):
+    return [pltpu.VMEM((2, chunks, rc, width), jnp.bfloat16)] + [pltpu.SemaphoreType.DMA((2, chunks))] * 4
+
+
+def line_kernel(n, chunks, lag, count, *refs):
+    parts, outs, scratch = refs[:count], refs[count:2 * count], refs[2 * count:]
+    rc = parts[0].shape[0] // (2 * chunks)
+    lines = [
+        Line(n, chunks, rc, lag, parts[k], scratch[5 * k], outs[k], scratch[5 * k + 1:5 * k + 5])
+        for k in range(count)
+    ]
+    greet(n)
+
+    def step(s, carry):
+        for k, line in enumerate(lines):
+            line.step(s - k * chunks)
+        return carry
+
+    lax.fori_loop(0, lines[0].steps + (count - 1) * chunks, step, 0)
+    for line in lines:
+        line.drain()
+
+
+def line_reduce(parts, n, chunks, cid, lag=2):
+    rows, width = parts[0].shape
+    count = len(parts)
+    rc = rows // (2 * chunks)
+    scratch = []
+    for _ in parts:
+        scratch += line_scratch(chunks, rc, width)
+    vmem = pl.BlockSpec(memory_space=pltpu.VMEM)
     return pl.pallas_call(
-        kernel,
-        out_shape=jax.ShapeDtypeStruct((rows, width), partial.dtype),
-        in_specs=[pl.BlockSpec(memory_space=pltpu.VMEM)],
-        out_specs=pl.BlockSpec(memory_space=pltpu.VMEM),
-        scratch_shapes=[
-            pltpu.VMEM((2, chunks, rc, width), partial.dtype),
-            pltpu.SemaphoreType.DMA((2, chunks)),
-            pltpu.SemaphoreType.DMA((2, chunks)),
-            pltpu.SemaphoreType.DMA((2, chunks)),
-            pltpu.SemaphoreType.DMA((2, chunks)),
+        functools.partial(line_kernel, n, chunks, lag, count),
+        out_shape=tuple(jax.ShapeDtypeStruct((rows, width), jnp.bfloat16) for _ in parts),
+        in_specs=[vmem] * count,
+        out_specs=(vmem,) * count,
+        scratch_shapes=scratch,
+        compiler_params=pltpu.CompilerParams(collective_id=cid, has_side_effects=True, vmem_limit_bytes=40 << 20),
+        cost_estimate=pl.CostEstimate(flops=rows * width * 2 * count, bytes_accessed=rows * width * 120 * count,
+                                      transcendentals=0),
+    )(*parts)
+
+
+def ff_kernel(n, chunks, lag, eps, part, gain, x_hbm, cot_hbm, gu_hbm, down_hbm,
+              branch, two_sum, hidden_hbm, gg_hbm, feed_hbm, normed_hbm,
+              got_one, sa1, ra1, sg1, rg1, got_two, sa2, ra2, sg2, rg2,
+              two_part, gu_w, down_w, x_buf, cot_buf, normed, hidden, gg, feed,
+              w_sem, x_sem, cot_sem, out_sem):
+    rows, width = part.shape
+    ff = down_w.shape[0]
+    rc = rows // (2 * chunks)
+    per = 4
+    half = rows // 2
+    hb = per * rc
+    blocks = chunks // per
+    one = Line(n, chunks, rc, lag, part, got_one, branch, (sa1, ra1, sg1, rg1))
+    two = Line(n, chunks, rc, lag, two_part, got_two, two_sum, (sa2, ra2, sg2, rg2))
+    ready = 2 * lag * (n - 1) + per
+    tile = 256
+    full, rest = ff // tile, ff % tile
+
+    weights = (
+        pltpu.make_async_copy(gu_hbm, gu_w, w_sem.at[0]),
+        pltpu.make_async_copy(down_hbm, down_w, w_sem.at[1]),
+    )
+    for copy in weights:
+        copy.start()
+
+    def sides(b):
+        for k in (0, 1):
+            yield k, pl.ds(pl.multiple_of(k * half + b * hb, hb), hb), pl.ds(k * hb, hb)
+
+    def load(src, buf, sem, b):
+        return [pltpu.make_async_copy(src.at[where], buf.at[local], sem.at[k]) for k, where, local in sides(b)]
+
+    def saves(b, which):
+        copies = []
+        for k, where, local in sides(b):
+            if which == "normed":
+                copies.append(pltpu.make_async_copy(normed.at[local], normed_hbm.at[where], out_sem.at[0, k]))
+            if which == "tiles":
+                copies.append(pltpu.make_async_copy(hidden.at[local], hidden_hbm.at[where], out_sem.at[1, k]))
+                for t in (0, 1):
+                    copies.append(pltpu.make_async_copy(gg.at[t, local], gg_hbm.at[t, where], out_sem.at[2 + t, k]))
+            if which == "feed":
+                copies.append(pltpu.make_async_copy(feed.at[local], feed_hbm.at[where], out_sem.at[4, k]))
+        return copies
+
+    def start(copies):
+        for copy in copies:
+            copy.start()
+
+    def wait(copies):
+        for copy in copies:
+            copy.wait()
+
+    start(load(x_hbm, x_buf, x_sem, 0))
+    start(load(cot_hbm, cot_buf, cot_sem, 0))
+    greet(n)
+
+    def normalize(b):
+        sub = 32
+
+        def some(r, carry):
+            for k, _, _ in sides(b):
+                at = pl.ds(pl.multiple_of(k * hb + r * sub, sub), sub)
+                where = pl.ds(pl.multiple_of(k * half + b * hb + r * sub, sub), sub)
+                middle = x_buf[at, :].astype(jnp.float32) + branch[where, :].astype(jnp.float32)
+                inverse = lax.rsqrt(jnp.mean(middle * middle, axis=-1, keepdims=True) + eps)
+                normed[at, :] = (middle * inverse * gain[...]).astype(jnp.bfloat16)
+            return carry
+
+        lax.fori_loop(0, hb // sub, some, 0)
+
+    def units(at, count):
+        columns = pl.ds(at, count)
+        gate = dot_n(normed[...], gu_w[0, :, columns])
+        up = dot_n(normed[...], gu_w[1, :, columns])
+        grad_hidden = dot_t(cot_buf[...], down_w[columns, :])
+        sg = 1.0 / (1.0 + jnp.exp(-gate))
+        silu = gate * sg
+        hidden[:, columns] = (silu * up).astype(jnp.bfloat16)
+        gg[0, :, columns] = (grad_hidden * up * sg * (1.0 + gate * (1.0 - sg))).astype(jnp.bfloat16)
+        gg[1, :, columns] = (grad_hidden * silu).astype(jnp.bfloat16)
+
+    def unit_tile(t, carry):
+        units(pl.multiple_of(t * tile, tile), tile)
+        return carry
+
+    def step(s, carry):
+        one.step(s)
+        two.step(s - ready - per)
+        u = s - ready
+        b = u // per
+        phase = u - b * per
+        live = (u >= 0) & (u < chunks)
+
+        @pl.when(live & (phase == 0))
+        def _():
+            wait(load(x_hbm, x_buf, x_sem, b))
+
+            @pl.when(b == 0)
+            def _():
+                wait(weights)
+
+            @pl.when(b > 0)
+            def _():
+                wait(saves(b - 1, "normed"))
+            normalize(b)
+            start(saves(b, "normed"))
+            wait(load(cot_hbm, cot_buf, cot_sem, b))
+
+            @pl.when(b > 0)
+            def _():
+                wait(saves(b - 1, "tiles"))
+
+        @pl.when(live & (phase < 2))
+        def _():
+            lax.fori_loop(phase * 2, jnp.where(phase == 0, 2, full), unit_tile, 0)
+
+        @pl.when(live & (phase == 1) & (b + 1 < blocks))
+        def _():
+            start(load(x_hbm, x_buf, x_sem, b + 1))
+
+        @pl.when(live & (phase == 2))
+        def _():
+            if rest:
+                units(full * tile, rest)
+            start(saves(b, "tiles"))
+
+            @pl.when(b + 1 < blocks)
+            def _():
+                start(load(cot_hbm, cot_buf, cot_sem, b + 1))
+
+            @pl.when(b > 0)
+            def _():
+                wait(saves(b - 1, "feed"))
+
+            def feed_tile(t, c):
+                columns = pl.ds(pl.multiple_of(t * tile, tile), tile)
+                feed[:, columns] = dot_n(hidden[...], down_w[:, columns]).astype(jnp.bfloat16)
+                return c
+
+            lax.fori_loop(0, width // tile, feed_tile, 0)
+            start(saves(b, "feed"))
+
+        @pl.when(live & (phase == 3))
+        def _():
+            def two_tile(t, c):
+                at = pl.ds(pl.multiple_of(t * tile, tile), tile)
+                value = (dot_t(gg[0], gu_w[0, at, :]) + dot_t(gg[1], gu_w[1, at, :])).astype(jnp.bfloat16)
+                for k, where, _ in sides(b):
+                    two_part[where, at] = value[k * hb:(k + 1) * hb]
+                return c
+
+            lax.fori_loop(0, width // tile, two_tile, 0)
+        return carry
+
+    lax.fori_loop(0, ready + per + two.steps, step, 0)
+    one.drain()
+    two.drain()
+    for which in ("normed", "tiles", "feed"):
+        wait(saves(blocks - 1, which))
+
+
+def feed_forward(part, gain, x, cot, gateup_w, down_w, n, cid, chunks=16, lag=2):
+    rows, width = part.shape
+    ff = down_w.shape[0]
+    rc = rows // (2 * chunks)
+    block = 8 * rc
+    low = jnp.bfloat16
+    vmem = pl.BlockSpec(memory_space=pltpu.VMEM)
+    hbm = pl.BlockSpec(memory_space=pl.ANY)
+    dma = pltpu.SemaphoreType.DMA
+    full = jax.ShapeDtypeStruct((rows, width), low)
+    return pl.pallas_call(
+        functools.partial(ff_kernel, n, chunks, lag, norm_eps),
+        out_shape=(full, full, jax.ShapeDtypeStruct((rows, ff), low), jax.ShapeDtypeStruct((2, rows, ff), low), full, full),
+        in_specs=[vmem, vmem, hbm, hbm, hbm, hbm],
+        out_specs=(vmem, vmem, hbm, hbm, hbm, hbm),
+        scratch_shapes=line_scratch(chunks, rc, width) + line_scratch(chunks, rc, width) + [
+            pltpu.VMEM((rows, width), low),
+            pltpu.VMEM((2, width, ff), low),
+            pltpu.VMEM((ff, width), low),
+            pltpu.VMEM((block, width), low),
+            pltpu.VMEM((block, width), low),
+            pltpu.VMEM((block, width), low),
+            pltpu.VMEM((block, ff), low),
+            pltpu.VMEM((2, block, ff), low),
+            pltpu.VMEM((block, width), low),
+            dma((2,)), dma((2,)), dma((2,)), dma((5, 2)),
         ],
-        compiler_params=pltpu.CompilerParams(collective_id=cid, has_side_effects=True, vmem_limit_bytes=40 << 20),
-        cost_estimate=pl.CostEstimate(flops=rows * width * 2, bytes_accessed=rows * width * 4 * 30, transcendentals=0),
-    )(partial)
+        compiler_params=pltpu.CompilerParams(collective_id=cid, has_side_effects=True, vmem_limit_bytes=62 << 20),
+        cost_estimate=pl.CostEstimate(flops=12 * rows * width * ff, bytes_accessed=rows * width * 250,
+                                      transcendentals=rows * ff),
+    )(part, gain, x, cot, gateup_w, down_w)
 
 
 def total_kernel(n, m, gains_ref, square_ref, total_ref, gain_ref, line, got_gains, got_line, got_plane,
@@ -535,38 +763,21 @@
     raw = jnp.dot(normed_one, qkv_weight, preferred_element_type=jnp.float32)
     mixture, q, k, v, lse = attention_forward(raw, cosines, sines, seg_col, seg_row, first, size)
     branch_part = jnp.dot(mixture, out_weight, preferred_element_type=jnp.float32).astype(low)
-    branch = line_reduce(branch_part, n, 16, 1, 2)
+    branch, grad_normed_two, hidden, grad_gateup, feed_part, normed_two = feed_forward(
+        branch_part, gain_values[1:], tokens, cotangent, gateup_weight, down_weight, n, 1
+    )
     middle = values_in + branch.astype(jnp.float32)
     inverse_two = lax.rsqrt(jnp.mean(middle * middle, axis=-1, keepdims=True) + norm_eps)
     unit_two = middle * inverse_two
-    normed_two = (unit_two * gain_values[1]).astype(low)
-    gateup = jnp.einsum(
-        "nd,sdf->snf", normed_two, gateup_weight, preferred_element_type=jnp.float32
-    )
-    gate_values = gateup[0]
-    up_values = gateup[1]
-    sigmoid_gate = jax.nn.sigmoid(gate_values)
-    silu_gate = gate_values * sigmoid_gate
-    hidden = (silu_gate * up_values).astype(low)
-    grad_hidden = against(cotangent, down_weight)
-    grad_gate = grad_hidden * up_values * sigmoid_gate * (1.0 + gate_values * (1.0 - sigmoid_gate))
-    grad_up = grad_hidden * silu_gate
-    grad_gateup = jnp.stack([grad_gate, grad_up]).astype(low)
-    partial_two = jnp.einsum(
-        "snf,sdf->nd", grad_gateup, gateup_weight, preferred_element_type=jnp.float32
-    ).astype(low)
+    grad_gate_weight = over_rows(normed_two, grad_gateup[0]).astype(low)
+    grad_up_weight = over_rows(normed_two, grad_gateup[1]).astype(low)
     grad_down_weight = over_rows(hidden, cotangent).astype(low)
-    grad_gateup_weight = jnp.einsum(
-        "nd,snf->sdf", normed_two, grad_gateup, preferred_element_type=jnp.float32
-    ).astype(low)
-    partial_two, grad_gateup_weight, grad_down_weight = lax.optimization_barrier(
-        (partial_two, grad_gateup_weight, grad_down_weight)
-    )
-    gateup_reduced = lax.psum_scatter(grad_gateup_weight, "dp", scatter_dimension=1, tiled=True)
+    grad_normed_two, grad_gate_weight, grad_up_weight, grad_down_weight = lax.optimization_barrier(
+        (grad_normed_two, grad_gate_weight, grad_up_weight, grad_down_weight)
+    )
+    gate_reduced = lax.psum_scatter(grad_gate_weight, "dp", scatter_dimension=0, tiled=True)
+    up_reduced = lax.psum_scatter(grad_up_weight, "dp", scatter_dimension=0, tiled=True)
     down_reduced = lax.psum_scatter(grad_down_weight, "dp", scatter_dimension=1, tiled=True)
-    grad_normed_two = line_reduce(partial_two, n, 16, 2, 2)
-    grad_normed_two, gateup_reduced = lax.optimization_barrier((grad_normed_two, gateup_reduced))
-    feed_part = jnp.dot(hidden, down_weight, preferred_element_type=jnp.float32).astype(low)
     grad_from_two, gain_grad_two = norm_back(
         grad_normed_two.astype(jnp.float32), unit_two, inverse_two, gain_values[1]
     )
@@ -579,14 +790,14 @@
     partial_one = against(grad_qkv, qkv_weight).astype(low)
     grad_out_weight = over_rows(mixture, grad_branch).astype(low)
     grad_qkv_weight = over_rows(normed_one, grad_qkv).astype(low)
-    partial_one, grad_out_weight, grad_qkv_weight, down_reduced = lax.optimization_barrier(
-        (partial_one, grad_out_weight, grad_qkv_weight, down_reduced)
+    partial_one, grad_out_weight, grad_qkv_weight, gate_reduced = lax.optimization_barrier(
+        (partial_one, grad_out_weight, grad_qkv_weight, gate_reduced)
     )
     out_reduced = lax.psum_scatter(grad_out_weight, "dp", scatter_dimension=1, tiled=True)
     qkv_reduced = lax.psum_scatter(grad_qkv_weight, "dp", scatter_dimension=0, tiled=True)
-    summed = line_reduce(jnp.concatenate([partial_one, feed_part]), n, 32, 3, 2).astype(jnp.float32)
-    grad_normed_one = summed[:length]
-    layer_out = (middle + summed[length:]).astype(low)
+    feed_out, grad_normed_one = line_reduce((feed_part, partial_one), n, 16, 3)
+    grad_normed_one = grad_normed_one.astype(jnp.float32)
+    layer_out = (middle + feed_out.astype(jnp.float32)).astype(low)
     grad_from_one, gain_grad_one = norm_back(grad_normed_one, unit_one, inverse_one, gain_values[0])
     input_grad = grad_middle + grad_from_one
     gain_grads = jnp.stack([gain_grad_one, gain_grad_two])
@@ -595,7 +806,7 @@
         qkv_reduced[:, :width],
         jnp.stack([qkv_reduced[:, width : width + kv_width], qkv_reduced[:, width + kv_width :]]),
         out_reduced.astype(jnp.float32),
-        gateup_reduced.astype(jnp.float32),
+        jnp.stack([gate_reduced, up_reduced]).astype(jnp.float32),
         down_reduced.astype(jnp.float32),
     )
     local_square = sum((jnp.sum(g * g) for g in reduced))

time: 794 us -> 807 us (1.016)
  waiting for transfers between devices: 11.5 us -> 121 us
  matrix products: 123 us -> 65.1 us
  local copies, waits for them, and re-layouts: 45.4 us -> 23.3 us
  other arithmetic: 90.9 us -> 81.6 us
    all_gather x1, waiting for transfers between devices: 0.01 us -> 70.1 us  [on_device(): lax.all_gather(w_gateup.astype(low), 'dp', axis=1, tiled=True)]
    dot_general x4 -> x0, matrix products: 68.5 us -> none  [the longest x1 20.2 us: on_device(): jnp.einsum('nd,sdf->snf', normed_two, gateup_weight, preferred_element_ty...]
    all_gather x1, waiting for transfers between devices: 0.01 us -> 39.5 us  [on_device(): down_weight = lax.all_gather(w_down.astype(low), 'dp', axis=1, tiled=True)]
    dot_general x3 -> x5, matrix products: 20.4 us -> 45.5 us  [over_rows(): lax.dot_general(left, right, (((0,), (0,)), ((), ())), preferred_element_...]
    unnamed x108 -> x98, local copies, waits for them, and re-layouts: 42.3 us -> 19.6 us
    dot_general x3 -> x2, matrix products: 23.6 us -> 7.36 us  [against(): lax.dot_general(left, right, (((1,), (1,)), ((), ())), preferred_element_...]
    convert_element_type x1 -> x0, other arithmetic: 11.4 us -> none  [on_device(): line_reduce(jnp.concatenate([partial_one, feed_part]), n, 32, 3, 2)]
    concatenate x1 -> x0, other arithmetic: 8.46 us -> none  [on_device(): jnp.concatenate([partial_one, feed_part])]
  transfers between devices with their start and end apart: 8 -> 9, of which waited for: 1 -> 3; matrix products, arithmetic and copies ran while one was open for 18% -> 12% of each run, Pallas kernels for 59% -> 31%
where the time goes in v3:
time: 807 us; the launch traced here: 800 us
  Pallas kernels  476 us (59%)
  waiting for transfers between devices  121 us (15%)
  other arithmetic  81.6 us (10%)
  matrix products  65.1 us (8%)
  local copies, waits for them, and re-layouts  23.3 us (3%)
  between operations  21.3 us (3%)
  blocking collectives  10.6 us (1%)
    pallas_call x1, Pallas kernels, feed_forward(): pl.pallas_call(functools.partial(ff_kernel, n, chunks, lag, norm_eps), ou...  212 us
    pallas_call x1, Pallas kernels, line_reduce(): pl.pallas_call(functools.partial(line_kernel, n, chunks, lag, count), out...  198 us
    all_gather x1, waiting for transfers between devices, on_device(): lax.all_gather(w_gateup.astype(low), 'dp', axis=1, tiled=True)  70.1 us
    dot_general x5, matrix products, over_rows(): lax.dot_general(left, right, (((0,), (0,)), ((), ())), preferred_element_...  45.5 us
    all_gather x1, waiting for transfers between devices, on_device(): down_weight = lax.all_gather(w_down.astype(low), 'dp', axis=1, tiled=True)  39.5 us
    pallas_call x1, Pallas kernels, attention_backward(): pl.pallas_call(functools.partial(backward_kernel, size, pairs), out_shape...  27.1 us
    pallas_call x1, Pallas kernels, attention_forward(): pl.pallas_call(functools.partial(forward_kernel, size, pairs), out_shape=...  25 us
    unnamed x98, local copies, waits for them, and re-layouts  19.6 us
  transfers between devices with their start and end apart: 9, of which 3 were waited for; matrix products, arithmetic and copies ran while one was open for 12% of the time, Pallas kernels for 31%

profile of v3, /device:TPU:0, one launch (start us, length us, event | category | flops | bytes accessed | tf_op | source)
XLA Modules:
  0.0 799.5 jit_solution(4926348920198083282)
XLA Ops:
  7.2 1.0 convert.12
  8.5 1.1 convert.11
  9.6 0.8 pad_maximum_fusion.3
  10.5 1.8 convert_element_type.95
  12.4 0.9 convert_element_type.98
  13.4 3.1 convert_element_type.97
  16.5 0.5 slice.54
  18.7 10.6 %all_gather.15 = bf16[2,2048]{1,0:T(2,128)(2,1)S(1)} all-gather(bf16[2,256]{1,0:T(2,128)(2,1)S(1)} %convert_element_type.91), channel_id=1, replica_groups=mesh['dp'=8,'tensor'=4] {'dp'}, dimensions={1}, use_global_device_ids=true | all-gather | bytes 9216 | tf_op jit(solution)/shard_map/all_gather | solution.py:744
  29.3 1.9 fusion.44
  31.2 0.9 pad_maximum_fusion.1
  32.2 0.9 fusion.16
  33.1 0.6 fusion.58
  33.7 9.8 %all-gather.5.cloned.1.call-done = bf16[2048,640]{1,0:T(8,128)(2,1)} async-done(((bf16[256,640]{1,0:T(8,128)(2,1)}), bf16[2048,640]{1,0:T(8,128)(2,1)}) %all-gather.5.cloned.1.call-update) | async-done | bytes 2621456 | tf_op jit(solution)/shard_map/all_gather | solution.py:746
  43.4 6.2 fusion.37.raw_ref
  49.7 25.0 %shard_map.373 = (bf16[1024,512]{1,0:T(8,128)(2,1)S(1)}, bf16[1024,512]{1,0:T(8,128)(2,1)S(1)}, bf16[1024,128]{1,0:T(8,128)(2,1)S(1)}, bf16[1024,128]{1,0:T(8,128)(2,1)S(1)}, f32[4,4,1,512]{3,2,1,0:T(1,128)S(1)}) custom-call(s32[4]{0:T(128)S(1)} %and_select_fusion.first_ref, f32[1024,640]{1,0:T(8,128)S(1)} %fusion.37.raw_ref, ...), custom_call_target="tpu_custom_call" | custom-call | flops 5368709120 | bytes 4194304 | tf_op jit(solution)/shard_map/pallas_call | solution.py:117
  74.7 1.0 copy-done.8
  75.7 6.0 convolution_convert_fusion.4.part
  81.7 39.5 %all-gather.11.cloned.1.call-done.down_hbm = bf16[1408,2048]{1,0:T(8,128)(2,1)} async-done(((bf16[1408,256]{1,0:T(8,128)(2,1)}), bf16[1408,2048]{1,0:T(8,128)(2,1)}) %all-gather.11.cloned.1.call-update) | async-done | bytes 5767184 | tf_op jit(solution)/shard_map/all_gather | solution.py:749
  121.2 70.1 %all-gather.9.cloned.1.call-done.gu_hbm = bf16[2,2048,1408]{2,1,0:T(8,128)(2,1)} async-done(((bf16[2,256,1408]{2,1,0:T(8,128)(2,1)}), bf16[2,2048,1408]{2,1,0:T(8,128)(2,1)}) %all-gather.9.cloned.1.call-update) | async-done | bytes 11534352 | tf_op jit(solution)/shard_map/all_gather | solution.py:748
  191.3 211.9 %shard_map.374 = (bf16[1024,2048]{1,0:T(8,128)(2,1)}, bf16[1024,2048]{1,0:T(8,128)(2,1)}, bf16[1024,1408]{1,0:T(8,128)(2,1)}, bf16[2,1024,1408]{2,1,0:T(8,128)(2...) custom-call(bf16[1024,2048]{1,0:T(8,128)(2,1)} %convolution_convert_fusion.4.part, ...), custom_call_target="tpu_custom_call" | custom-call | flops 35433480192 | bytes 524288000 | tf_op jit(solution)/shard_map/pallas_call | solution.py:551
  403.2 11.0 %convolution_convert_fusion.1 = bf16[2048,1408]{1,0:T(8,128)(2,1)} fusion(bf16[1024,2048]{1,0:T(8,128)(2,1)} %get-tuple-element.51, bf16[2,1024,1408]{2,1,0:T(8,128)(2,1)} %get-tuple-element.52), kind=kOutput, calls=%fused_computation.26 | convolution fusion | flops 5908463616 | bytes 12845056 | tf_op jit(solution)/shard_map/dot_general | solution.py:687
  414.2 11.0 %convolution_convert_fusion.2 = bf16[2048,1408]{1,0:T(8,128)(2,1)} fusion(bf16[1024,2048]{1,0:T(8,128)(2,1)} %get-tuple-element.51, bf16[2,1024,1408]{2,1,0:T(8,128)(2,1)} %get-tuple-element.52), kind=kOutput, calls=%fused_computation.27 | convolution fusion | flops 5908463616 | bytes 12845056 | tf_op jit(solution)/shard_map/dot_general | solution.py:687
  425.1 10.5 %convolution_convert_fusion = bf16[1408,2048]{1,0:T(8,128)(2,1)} fusion(bf16[1024,1408]{1,0:T(8,128)(2,1)} %get-tuple-element.53, bf16[1024,2048]{1,0:T(8,128)(2,1)} %cot_hbm.1), kind=kOutput, calls=%fused_computation.25 | convolution fusion | flops 5908463616 | bytes 12845056 | tf_op jit(solution)/shard_map/dot_general | solution.py:687
  435.6 0.5 reduce-scatter.12.cloned.1.call-update
  436.2 0.7 reduce-scatter.14.cloned.1.call-update
  437.0 5.0 multiply_reduce_fusion
  442.1 1.6 copy-done.15
  443.7 13.5 %fusion.12 = (f32[2048]{0:T(1024)S(1)}, f32[1024]{0:T(1024)S(1)}) fusion(bf16[1024,2048]{1,0:T(8,128)(2,1)} %get-tuple-element.54, bf16[1024,2048]{1,0:T(8,128)(2,1)S(1)} %copy-done.15, bf16[1024,2048]{1,0:T(8,128)(2,1)S(1)} %copy-done.13, f32[1024]{0:T(1024)S(1)} %add_rsqrt_fusion, f32[2048]{0:T(1024)S(1)} %bitcast.62), kind=kLoop, calls=%fused_computation.18 | loop fusion | flops 20968448 | bytes 12607488 | tf_op jit(solution)/shard_map/reduce_sum | solution.py:700
  457.3 7.0 fusion.11
  464.3 2.4 fusion.30.grad_ref
  466.7 1.2 copy-done.14
  468.0 27.1 %shard_map.375 = bf16[1024,640]{1,0:T(8,128)(2,1)S(1)} custom-call(s32[4]{0:T(128)S(1)} %and_select_fusion.first_ref, bf16[1024,512]{1,0:T(8,128)(2,1)S(1)} %copy-done.9, bf16[1024,128]{1,0:T(8,128)(2,1)S(1)} %get-tuple-element.48.k_ref, bf16[1024,128]{1,0:T(8,128)(2,1)S(1)} %copy-done.11, bf16[1024,512]{1,0:T(8,128)(2,1)S(1)} %get-tuple-element.44.mix_ref, ...), custom_call_target="tpu_custom_call" | custom-call | flops 10737418240 | bytes 4194304 | tf_op jit(solution)/shard_map/pallas_call | solution.py:211
  495.0 5.0 convolution_convert_fusion.3.refs_1_
  500.0 4.7 convolution_convert_fusion.5
  504.8 8.3 %convolution_convert_fusion.6 = bf16[512,2048]{1,0:T(8,128)(2,1)} fusion(bf16[1024,512]{1,0:T(8,128)(2,1)S(1)} %get-tuple-element.44.mix_ref, f32[1024,2048]{1,0:T(8,128)} %copy-done.14), kind=kOutput, calls=%fused_computation.36 | convolution fusion | flops 2150629376 | bytes 11534336 | tf_op jit(solution)/shard_map/dot_general | solution.py:687
  513.2 0.7 reduce-scatter.8.cloned.1.call-update
  514.2 1.0 copy.72
  515.9 1.0 copy.69
  516.9 1.0 copy.70
  517.9 2.2 copy-done.2
  520.1 197.6 %shard_map.376 = (bf16[1024,2048]{1,0:T(8,128)(2,1)S(1)}, bf16[1024,2048]{1,0:T(8,128)(2,1)S(1)}) custom-call(bf16[1024,2048]{1,0:T(8,128)(2,1)S(1)} %copy-done.2, bf16[1024,2048]{1,0:T(8,128)(2,1)} %convolution_convert_fusion.3.refs_1_), custom_call_target="tpu_custom_call" | custom-call | flops 8388608 | bytes 503316480 | tf_op jit(solution)/shard_map/pallas_call | solution.py:367
  717.7 2.0 copy-done
  719.7 1.9 copy-done.1
  721.7 2.5 fusion.20
  724.1 5.0 fusion.15
  729.1 0.6 maximum_bitcast_fusion.gains_ref
  729.7 2.1 fusion.34
  731.8 13.8 %fusion.8 = (f32[1024,2048]{1,0:T(8,128)}, bf16[1024,2048]{1,0:T(8,128)(2,1)}) fusion(f32[1024,2048]{1,0:T(8,128)} %copy-done.14, bf16[1024,2048]{1,0:T(8,128)(2,1)} %copy-done, bf16[1024,2048]{1,0:T(8,128)(2,1)} %x_hbm.1, f32[1024]{0:T(1024)S(1)} %broadcast_multiply_fusion, f32[2048]{0:T(1024)S(1)} %bitcast.67, f32[1024]{0:T(1024)S(1)} %add_rsqrt_fusion.1, ...), kind=kLoop, calls=%fused_computation.14 | loop fusion | flops 27262976 | bytes 37765120 | tf_op jit(solution)/shard_map/add | solution.py:802
  745.6 1.7 fusion.41
  747.3 1.2 convert_element_type.113
  748.5 0.7 multiply_reduce_fusion.1
  749.2 0.6 multiply_reduce_fusion.2
  753.1 0.6 broadcast_in_dim.5.square_ref
  753.7 14.3 %shard_map.377 = (f32[8,128]{1,0:T(8,128)}, f32[2,256]{1,0:T(2,128)}) custom-call(f32[8,2,256]{2,1,0:T(2,128)} %maximum_bitcast_fusion.gains_ref, f32[8,128]{1,0:T(8,128)} %broadcast_in_dim.5.square_ref), custom_call_target="tpu_custom_call" | custom-call | tf_op jit(solution)/shard_map/pallas_call | solution.py:640
  768.1 1.2 slice.69
  770.0 2.7 multiply_subtract_fusion.3
  772.7 2.0 copy.73
  774.8 2.0 copy.74
  776.8 2.0 copy.75
  779.0 6.8 multiply_subtract_fusion
  785.8 0.8 multiply_subtract_fusion.4
  786.6 0.6 multiply_subtract_fusion.5
  787.3 2.8 multiply_subtract_fusion.1
  790.1 1.4 multiply_subtract_fusion.2
  (126 shorter events, 2.3 us)
Async XLA Ops:
  7.2 5.2 copy-start.18
  7.2 36.2 %all-gather.5.cloned.1.call-start = ((), (), s32[]{:S(2)}) async-start(), calls=%async_computation.5 | async-start | bytes 2949120 | tf_op jit(solution)/shard_map/all_gather | solution.py:746
  10.4 65.2 %all-gather.7.cloned.1.call-start = ((), (), s32[]{:S(2)}) async-start(), calls=%async_computation.6 | async-start | bytes 2359296 | tf_op jit(solution)/shard_map/all_gather | solution.py:747
  12.3 4.2 copy-start.7
  12.3 5.9 copy-start.39
  12.3 108.9 %all-gather.11.cloned.1.call-start = ((), (), s32[]{:S(2)}) async-start(), calls=%async_computation.8 | async-start | bytes 6488064 | tf_op jit(solution)/shard_map/all_gather | solution.py:749
  13.3 177.9 %all-gather.9.cloned.1.call-start = ((), (), s32[]{:S(2)}) async-start(), calls=%async_computation.7 | async-start | bytes 12976128 | tf_op jit(solution)/shard_map/all_gather | solution.py:748
  16.5 496.7 %reduce-scatter.6.cloned.1.call-start = ((), (), s32[]{:S(2)}) async-start(), calls=%async_computation.9 | async-start | bytes 6488064 | tf_op jit(solution)/shard_map/reduce_scatter | solution.py:778
  18.7 31.0 %copy-start.5 = (s32[1024,1]{1,0:T(8,128)}, s32[1024,1]{1,0:T(8,128)S(1)}, u32[]{:S(2)}) copy-start(s32[1024,1]{1,0:T(8,128)S(1)} %copy.66.seg_col_ref) | copy-start | bytes 12292
  18.7 13.5 %copy-start.12 = (bf16[1024,2048]{1,0:T(8,128)(2,1)S(1)}, bf16[1024,2048]{1,0:T(8,128)(2,1)}, u32[]{:S(2)}) copy-start(bf16[1024,2048]{1,0:T(8,128)(2,1)} %x_hbm.1) | copy-start | bytes 12582916
  32.1 17.6 %copy-start.3 = (f32[1024,128]{1,0:T(8,128)}, f32[1024,128]{1,0:T(8,128)S(1)}, u32[]{:S(2)}) copy-start(f32[1024,128]{1,0:T(8,128)S(1)} %get-tuple-element.166.sin_ref) | copy-start | bytes 1572868
  74.7 1.0 copy-start.8
  75.6 6.0 copy-start.10
  435.6 286.1 %reduce-scatter.12.cloned.1.call-start = ((), (), s32[]{:S(2)}) async-start(), calls=%async_computation.12 | async-start | bytes 6488064 | tf_op jit(solution)/shard_map/reduce_scatter | solution.py:779
  436.2 293.6 %reduce-scatter.14.cloned.1.call-start = ((), (), s32[]{:S(2)}) async-start(), calls=%async_computation.13 | async-start | bytes 6488064 | tf_op jit(solution)/shard_map/reduce_scatter | solution.py:780
  436.9 308.7 %reduce-scatter.10.cloned.1.call-start = ((), (), s32[]{:S(2)}) async-start(), calls=%async_computation.11 | async-start | bytes 2359296 | tf_op jit(solution)/shard_map/reduce_scatter | solution.py:796
  437.0 5.1 copy-start.13
  437.0 6.7 copy-start.15
  437.0 6.7 copy-start.38
  443.7 13.5 %copy-start.16 = (bf16[1024,2048]{1,0:T(8,128)(2,1)S(1)}, bf16[1024,2048]{1,0:T(8,128)(2,1)}, u32[]{:S(2)}) copy-start(bf16[1024,2048]{1,0:T(8,128)(2,1)} %get-tuple-element.54) | copy-start | bytes 12582916
  457.2 7.0 copy-start.45
  464.3 3.7 copy-start.14
  464.3 3.7 copy-start.4
  464.3 3.6 copy-start.6
  464.3 3.6 copy-start.9
  464.3 3.6 copy-start.11
  467.9 27.1 %copy-start.44 = (bf16[2048,640]{1,0:T(8,128)(2,1)S(1)}, bf16[2048,640]{1,0:T(8,128)(2,1)}, u32[]{:S(2)}) copy-start(bf16[2048,640]{1,0:T(8,128)(2,1)} %all-gather.5.cloned.1.call-done) | copy-start | bytes 7864324
  513.1 1.1 copy-start.22
  513.1 2.8 copy-start.31
  513.1 3.8 copy-start.32
  513.1 234.1 %reduce-scatter.8.cloned.1.call-start = ((), (), s32[]{:S(2)}) async-start(), calls=%async_computation.10 | async-start | bytes 2949120 | tf_op jit(solution)/shard_map/reduce_scatter | solution.py:797
  517.9 2.2 copy-start.2
  520.1 201.6 %copy-start.20 = (bf16[256,1408]{1,0:T(8,128)(2,1)S(1)}, bf16[256,1408]{1,0:T(8,128)(2,1)}, u32[]{:S(2)}) copy-start(bf16[256,1408]{1,0:T(8,128)(2,1)} %reduce-scatter.6.cloned.1.call-done) | copy-start | bytes 2162692
  717.7 2.0 copy-start
  719.7 2.0 copy-start.1
  747.3 31.6 %copy-start.17 = (f32[2,256,1408]{2,1,0:T(8,128)S(1)}, f32[2,256,1408]{2,1,0:T(8,128)}, u32[]{:S(2)}) copy-start(f32[2,256,1408]{2,1,0:T(8,128)} %param.38) | copy-start | bytes 8650756
  748.5 0.8 copy-start.27
  748.5 0.8 copy-start.29
  778.8 6.9 copy-start.28
  778.8 6.9 copy-start.30
  778.8 6.9 copy-start.33
  778.9 6.9 copy-start.36
  778.9 6.9 copy-start.37
  778.9 7.7 copy-start.40
  778.9 7.7 copy-start.41
  778.9 7.7 copy-start.42
  778.9 7.7 copy-start.43
  778.9 8.3 %copy-start.19 = (f32[1408,256]{1,0:T(8,128)S(1)}, f32[1408,256]{1,0:T(8,128)}, u32[]{:S(2)}) copy-start(f32[1408,256]{1,0:T(8,128)} %param.41) | copy-start | bytes 4325380
  778.9 8.3 %copy-start.21 = (bf16[1408,256]{1,0:T(8,128)(2,1)S(1)}, bf16[1408,256]{1,0:T(8,128)(2,1)}, u32[]{:S(2)}) copy-start(bf16[1408,256]{1,0:T(8,128)(2,1)} %reduce-scatter.14.cloned.1.call-done) | copy-start | bytes 2162692
  778.9 8.3 %copy-start.24 = (f32[1408,256]{1,0:T(8,128)S(1)}, f32[1408,256]{1,0:T(8,128)}, u32[]{:S(2)}) copy-start(f32[1408,256]{1,0:T(8,128)} %param.43) | copy-start | bytes 4325380
  779.0 8.3 %copy-start.25 = (f32[1408,256]{1,0:T(8,128)S(1)}, f32[1408,256]{1,0:T(8,128)}, u32[]{:S(2)}) copy-start(f32[1408,256]{1,0:T(8,128)} %param.42) | copy-start | bytes 4325380
  787.3 2.8 copy-start.23
  787.3 2.8 copy-start.26
  787.3 2.8 copy-start.34
  787.3 2.8 copy-start.35
Sparse Core Ops, SparseCore 0:
  10.6 32.8 all-gather.4
  45.9 28.2 all-gather.6
  76.6 44.5 all-gather.10
  123.5 67.6 all-gather.8
  435.7 58.5 reduce-scatter.5
  498.0 59.0 reduce-scatter.11
  560.5 59.0 reduce-scatter.13
  623.8 41.2 reduce-scatter.9
  669.0 43.6 reduce-scatter.7

commit v4 on v3

--- a/solution.py
+++ b/solution.py
@@ -376,23 +376,27 @@
     )(*parts)
 
 
-def ff_kernel(n, chunks, lag, eps, part, gain, x_hbm, cot_hbm, gu_hbm, down_hbm,
-              branch, two_sum, hidden_hbm, gg_hbm, feed_hbm, normed_hbm,
-              got_one, sa1, ra1, sg1, rg1, got_two, sa2, ra2, sg2, rg2,
-              two_part, gu_w, down_w, x_buf, cot_buf, normed, hidden, gg, feed,
-              w_sem, x_sem, cot_sem, out_sem):
-    rows, width = part.shape
+def dot_rows(left, right):
+    return lax.dot_general(left, right, (((0,), (0,)), ((), ())), preferred_element_type=jnp.float32)
+
+
+def ff_kernel(n, chunks, lag, eps, branch, gain, x, cot_hbm, gu_hbm, down_hbm,
+              feed_hbm, middle_hbm, low_hbm, gain_out, gate_grad_hbm, up_grad_hbm, down_grad_hbm,
+              got, sa, ra, sg, rg, two_sum, two_part, gu_w, down_w, cot, normed, hidden, gg, feed,
+              middle_stage, low_stage, unit_stage, down_stage, w_sem, cot_sem, feed_sem, stage_sem, grad_sem):
+    rows, width = branch.shape
     ff = down_w.shape[0]
     rc = rows // (2 * chunks)
     per = 4
     half = rows // 2
     hb = per * rc
+    block = 2 * hb
     blocks = chunks // per
-    one = Line(n, chunks, rc, lag, part, got_one, branch, (sa1, ra1, sg1, rg1))
-    two = Line(n, chunks, rc, lag, two_part, got_two, two_sum, (sa2, ra2, sg2, rg2))
-    ready = 2 * lag * (n - 1) + per
+    line = Line(n, chunks, rc, lag, two_part, got, two_sum, (sa, ra, sg, rg))
+    landed = 2 * lag * (n - 1) + per
     tile = 256
     full, rest = ff // tile, ff % tile
+    wide = width // tile
 
     weights = (
         pltpu.make_async_copy(gu_hbm, gu_w, w_sem.at[0]),
@@ -401,25 +405,37 @@
     for copy in weights:
         copy.start()
 
-    def sides(b):
+    def natural(k, b):
+        return pl.ds(pl.multiple_of(k * half + b * hb, hb), hb)
+
+    def blocked(k, b):
+        return pl.ds(pl.multiple_of(b * block + k * hb, hb), hb)
+
+    def load_cot(b):
+        return [pltpu.make_async_copy(cot_hbm.at[natural(k, b)], cot.at[blocked(k, b)], cot_sem.at[b, k])
+                for k in (0, 1)]
+
+    def save_feed(b):
+        return [pltpu.make_async_copy(feed.at[pl.ds(k * hb, hb)], feed_hbm.at[natural(k, b)], feed_sem.at[k])
+                for k in (0, 1)]
+
+    def save_rows(d):
+        copies = []
         for k in (0, 1):
-            yield k, pl.ds(pl.multiple_of(k * half + b * hb, hb), hb), pl.ds(k * hb, hb)
-
-    def load(src, buf, sem, b):
-        return [pltpu.make_async_copy(src.at[where], buf.at[local], sem.at[k]) for k, where, local in sides(b)]
-
-    def saves(b, which):
-        copies = []
-        for k, where, local in sides(b):
-            if which == "normed":
-                copies.append(pltpu.make_async_copy(normed.at[local], normed_hbm.at[where], out_sem.at[0, k]))
-            if which == "tiles":
-                copies.append(pltpu.make_async_copy(hidden.at[local], hidden_hbm.at[where], out_sem.at[1, k]))
-                for t in (0, 1):
-                    copies.append(pltpu.make_async_copy(gg.at[t, local], gg_hbm.at[t, where], out_sem.at[2 + t, k]))
-            if which == "feed":
-                copies.append(pltpu.make_async_copy(feed.at[local], feed_hbm.at[where], out_sem.at[4, k]))
+            where = line.rows(k, d)
+            copies.append(pltpu.make_async_copy(middle_stage.at[k], middle_hbm.at[where], stage_sem.at[0, k]))
+            copies.append(pltpu.make_async_copy(low_stage.at[k], low_hbm.at[where], stage_sem.at[1, k]))
         return copies
+
+    def save_units(w):
+        at = pl.ds(pl.multiple_of(w * tile, tile), tile)
+        return [
+            pltpu.make_async_copy(unit_stage.at[0], gate_grad_hbm.at[at], grad_sem.at[0]),
+            pltpu.make_async_copy(unit_stage.at[1], up_grad_hbm.at[at], grad_sem.at[1]),
+        ]
+
+    def save_down(at, count):
+        return [pltpu.make_async_copy(down_stage.at[pl.ds(0, count)], down_grad_hbm.at[pl.ds(at, count)], grad_sem.at[2])]
 
     def start(copies):
         for copy in copies:
@@ -429,146 +445,188 @@
         for copy in copies:
             copy.wait()
 
-    start(load(x_hbm, x_buf, x_sem, 0))
-    start(load(cot_hbm, cot_buf, cot_sem, 0))
+    for b in range(blocks):
+        start(load_cot(b))
+    gain_out[...] = jnp.zeros_like(gain_out)
     greet(n)
 
+    def unit_rows(where):
+        middle = x[where, :].astype(jnp.float32) + branch[where, :].astype(jnp.float32)
+        inverse = lax.rsqrt(jnp.mean(middle * middle, axis=-1, keepdims=True) + eps)
+        return middle * inverse, inverse
+
     def normalize(b):
-        sub = 32
-
         def some(r, carry):
-            for k, _, _ in sides(b):
-                at = pl.ds(pl.multiple_of(k * hb + r * sub, sub), sub)
-                where = pl.ds(pl.multiple_of(k * half + b * hb + r * sub, sub), sub)
-                middle = x_buf[at, :].astype(jnp.float32) + branch[where, :].astype(jnp.float32)
-                inverse = lax.rsqrt(jnp.mean(middle * middle, axis=-1, keepdims=True) + eps)
-                normed[at, :] = (middle * inverse * gain[...]).astype(jnp.bfloat16)
+            for k in (0, 1):
+                where = pl.ds(pl.multiple_of(k * half + b * hb + r * rc, rc), rc)
+                at = pl.ds(pl.multiple_of(b * block + k * hb + r * rc, rc), rc)
+                normed[at, :] = (unit_rows(where)[0] * gain[...]).astype(jnp.bfloat16)
             return carry
 
-        lax.fori_loop(0, hb // sub, some, 0)
-
-    def units(at, count):
-        columns = pl.ds(at, count)
-        gate = dot_n(normed[...], gu_w[0, :, columns])
-        up = dot_n(normed[...], gu_w[1, :, columns])
-        grad_hidden = dot_t(cot_buf[...], down_w[columns, :])
-        sg = 1.0 / (1.0 + jnp.exp(-gate))
-        silu = gate * sg
-        hidden[:, columns] = (silu * up).astype(jnp.bfloat16)
-        gg[0, :, columns] = (grad_hidden * up * sg * (1.0 + gate * (1.0 - sg))).astype(jnp.bfloat16)
-        gg[1, :, columns] = (grad_hidden * silu).astype(jnp.bfloat16)
-
-    def unit_tile(t, carry):
-        units(pl.multiple_of(t * tile, tile), tile)
-        return carry
+        lax.fori_loop(0, per, some, 0)
 
     def step(s, carry):
-        one.step(s)
-        two.step(s - ready - per)
-        u = s - ready
-        b = u // per
-        phase = u - b * per
-        live = (u >= 0) & (u < chunks)
+        line.step(s - per)
+        b = s // per
+        phase = s - b * per
+        live = s < chunks
+        mine = pl.ds(pl.multiple_of(b * block, block), block)
+
+        def units(at, count):
+            columns = pl.ds(at, count)
+            gate = dot_n(normed[mine, :], gu_w[0, :, columns])
+            up = dot_n(normed[mine, :], gu_w[1, :, columns])
+            grad_hidden = dot_t(cot[mine, :], down_w[columns, :])
+            sg_gate = 1.0 / (1.0 + jnp.exp(-gate))
+            silu = gate * sg_gate
+            hidden[mine, columns] = (silu * up).astype(jnp.bfloat16)
+            gg[0, mine, columns] = (grad_hidden * up * sg_gate * (1.0 + gate * (1.0 - sg_gate))).astype(jnp.bfloat16)
+            gg[1, mine, columns] = (grad_hidden * silu).astype(jnp.bfloat16)
+
+        def unit_tile(t, c):
+            units(pl.multiple_of(t * tile, tile), tile)
+            return c
 
         @pl.when(live & (phase == 0))
         def _():
-            wait(load(x_hbm, x_buf, x_sem, b))
+            normalize(b)
 
             @pl.when(b == 0)
             def _():
                 wait(weights)
-
-            @pl.when(b > 0)
-            def _():
-                wait(saves(b - 1, "normed"))
-            normalize(b)
-            start(saves(b, "normed"))
-            wait(load(cot_hbm, cot_buf, cot_sem, b))
-
-            @pl.when(b > 0)
-            def _():
-                wait(saves(b - 1, "tiles"))
+            wait(load_cot(b))
 
         @pl.when(live & (phase < 2))
         def _():
             lax.fori_loop(phase * 2, jnp.where(phase == 0, 2, full), unit_tile, 0)
-
-        @pl.when(live & (phase == 1) & (b + 1 < blocks))
-        def _():
-            start(load(x_hbm, x_buf, x_sem, b + 1))
 
         @pl.when(live & (phase == 2))
         def _():
             if rest:
                 units(full * tile, rest)
-            start(saves(b, "tiles"))
-
-            @pl.when(b + 1 < blocks)
-            def _():
-                start(load(cot_hbm, cot_buf, cot_sem, b + 1))
 
             @pl.when(b > 0)
             def _():
-                wait(saves(b - 1, "feed"))
+                wait(save_feed(b - 1))
 
             def feed_tile(t, c):
                 columns = pl.ds(pl.multiple_of(t * tile, tile), tile)
-                feed[:, columns] = dot_n(hidden[...], down_w[:, columns]).astype(jnp.bfloat16)
+                feed[:, columns] = dot_n(hidden[mine, :], down_w[:, columns]).astype(jnp.bfloat16)
                 return c
 
-            lax.fori_loop(0, width // tile, feed_tile, 0)
-            start(saves(b, "feed"))
+            lax.fori_loop(0, wide, feed_tile, 0)
+            start(save_feed(b))
 
         @pl.when(live & (phase == 3))
         def _():
             def two_tile(t, c):
                 at = pl.ds(pl.multiple_of(t * tile, tile), tile)
-                value = (dot_t(gg[0], gu_w[0, at, :]) + dot_t(gg[1], gu_w[1, at, :])).astype(jnp.bfloat16)
-                for k, where, _ in sides(b):
-                    two_part[where, at] = value[k * hb:(k + 1) * hb]
+                value = (dot_t(gg[0, mine, :], gu_w[0, at, :]) + dot_t(gg[1, mine, :], gu_w[1, at, :])).astype(jnp.bfloat16)
+                for k in (0, 1):
+                    two_part[natural(k, b), at] = value[k * hb:(k + 1) * hb]
                 return c
 
-            lax.fori_loop(0, width // tile, two_tile, 0)
+            lax.fori_loop(0, wide, two_tile, 0)
+
+        d = s - landed
+
+        @pl.when(d >= 0)
+        def _():
+            @pl.when(d > 0)
+            def _():
+                wait(save_rows(d - 1))
+            for k in (0, 1):
+                where = line.rows(k, d)
+                at = pl.ds(pl.multiple_of((d // per) * block + k * hb + (d - (d // per) * per) * rc, rc), rc)
+                unit, inverse = unit_rows(where)
+                grad = two_sum[where, :].astype(jnp.float32)
+                scaled = grad * gain[...]
+                inner = jnp.mean(scaled * unit, axis=-1, keepdims=True)
+                value = cot[at, :].astype(jnp.float32) + inverse * (scaled - unit * inner)
+                middle_stage[k] = value
+                low_stage[k] = value.astype(jnp.bfloat16)
+                gain_out[...] += jnp.sum(grad * unit, axis=0, keepdims=True)
+            start(save_rows(d))
+
+        w = s - chunks
+
+        @pl.when((w >= 0) & (w < wide))
+        def _():
+            @pl.when(w > 0)
+            def _():
+                wait(save_units(w - 1))
+            columns = pl.ds(pl.multiple_of(w * tile, tile), tile)
+            left = normed[:, columns]
+            for t in (0, 1):
+                unit_stage[t] = dot_rows(left, gg[t]).astype(jnp.bfloat16)
+            start(save_units(w))
+
+        v = w - wide
+
+        @pl.when((v >= 0) & (v < full))
+        def _():
+            @pl.when(v > 0)
+            def _():
+                wait(save_down((v - 1) * tile, tile))
+            at = pl.multiple_of(v * tile, tile)
+            down_stage[...] = dot_rows(hidden[:, pl.ds(at, tile)], cot[...]).astype(jnp.bfloat16)
+            start(save_down(at, tile))
+
+        if rest:
+            @pl.when(v == full)
+            def _():
+                wait(save_down((full - 1) * tile, tile))
+                down_stage[pl.ds(0, rest), :] = dot_rows(hidden[:, full * tile:], cot[...]).astype(jnp.bfloat16)
+                start(save_down(full * tile, rest))
         return carry
 
-    lax.fori_loop(0, ready + per + two.steps, step, 0)
-    one.drain()
-    two.drain()
-    for which in ("normed", "tiles", "feed"):
-        wait(saves(blocks - 1, which))
-
-
-def feed_forward(part, gain, x, cot, gateup_w, down_w, n, cid, chunks=16, lag=2):
-    rows, width = part.shape
+    lax.fori_loop(0, per + line.steps, step, 0)
+    line.drain()
+    wait(save_feed(blocks - 1))
+    wait(save_rows(chunks - 1))
+    wait(save_units(wide - 1))
+    wait(save_down(full * tile, rest) if rest else save_down((full - 1) * tile, tile))
+
+
+def feed_forward(branch, gain, x, cot, gateup_w, down_w, n, cid, chunks=16, lag=2):
+    rows, width = branch.shape
     ff = down_w.shape[0]
     rc = rows // (2 * chunks)
     block = 8 * rc
+    blocks = chunks // 4
     low = jnp.bfloat16
     vmem = pl.BlockSpec(memory_space=pltpu.VMEM)
     hbm = pl.BlockSpec(memory_space=pl.ANY)
     dma = pltpu.SemaphoreType.DMA
-    full = jax.ShapeDtypeStruct((rows, width), low)
+    shape = jax.ShapeDtypeStruct
     return pl.pallas_call(
         functools.partial(ff_kernel, n, chunks, lag, norm_eps),
-        out_shape=(full, full, jax.ShapeDtypeStruct((rows, ff), low), jax.ShapeDtypeStruct((2, rows, ff), low), full, full),
-        in_specs=[vmem, vmem, hbm, hbm, hbm, hbm],
-        out_specs=(vmem, vmem, hbm, hbm, hbm, hbm),
-        scratch_shapes=line_scratch(chunks, rc, width) + line_scratch(chunks, rc, width) + [
+        out_shape=(
+            shape((rows, width), low), shape((rows, width), jnp.float32), shape((rows, width), low),
+            shape((1, width), jnp.float32), shape((width, ff), low), shape((width, ff), low), shape((ff, width), low),
+        ),
+        in_specs=[vmem, vmem, vmem, hbm, hbm, hbm],
+        out_specs=(hbm, hbm, hbm, vmem, hbm, hbm, hbm),
+        scratch_shapes=line_scratch(chunks, rc, width) + [
+            pltpu.VMEM((rows, width), low),
             pltpu.VMEM((rows, width), low),
             pltpu.VMEM((2, width, ff), low),
             pltpu.VMEM((ff, width), low),
+            pltpu.VMEM((rows, width), low),
+            pltpu.VMEM((rows, width), low),
+            pltpu.VMEM((rows, ff), low),
+            pltpu.VMEM((2, rows, ff), low),
             pltpu.VMEM((block, width), low),
-            pltpu.VMEM((block, width), low),
-            pltpu.VMEM((block, width), low),
-            pltpu.VMEM((block, ff), low),
-            pltpu.VMEM((2, block, ff), low),
-            pltpu.VMEM((block, width), low),
-            dma((2,)), dma((2,)), dma((2,)), dma((5, 2)),
+            pltpu.VMEM((2, rc, width), jnp.float32),
+            pltpu.VMEM((2, rc, width), low),
+            pltpu.VMEM((2, 256, ff), low),
+            pltpu.VMEM((256, width), low),
+            dma((2,)), dma((blocks, 2)), dma((2,)), dma((2, 2)), dma((3,)),
         ],
-        compiler_params=pltpu.CompilerParams(collective_id=cid, has_side_effects=True, vmem_limit_bytes=62 << 20),
-        cost_estimate=pl.CostEstimate(flops=12 * rows * width * ff, bytes_accessed=rows * width * 250,
+        compiler_params=pltpu.CompilerParams(collective_id=cid, has_side_effects=True, vmem_limit_bytes=63 << 20),
+        cost_estimate=pl.CostEstimate(flops=18 * rows * width * ff, bytes_accessed=rows * width * 150,
                                       transcendentals=rows * ff),
-    )(part, gain, x, cot, gateup_w, down_w)
+    )(branch, gain, x, cot, gateup_w, down_w)
 
 
 def total_kernel(n, m, gains_ref, square_ref, total_ref, gain_ref, line, got_gains, got_line, got_plane,
@@ -763,26 +821,13 @@
     raw = jnp.dot(normed_one, qkv_weight, preferred_element_type=jnp.float32)
     mixture, q, k, v, lse = attention_forward(raw, cosines, sines, seg_col, seg_row, first, size)
     branch_part = jnp.dot(mixture, out_weight, preferred_element_type=jnp.float32).astype(low)
-    branch, grad_normed_two, hidden, grad_gateup, feed_part, normed_two = feed_forward(
-        branch_part, gain_values[1:], tokens, cotangent, gateup_weight, down_weight, n, 1
-    )
-    middle = values_in + branch.astype(jnp.float32)
-    inverse_two = lax.rsqrt(jnp.mean(middle * middle, axis=-1, keepdims=True) + norm_eps)
-    unit_two = middle * inverse_two
-    grad_gate_weight = over_rows(normed_two, grad_gateup[0]).astype(low)
-    grad_up_weight = over_rows(normed_two, grad_gateup[1]).astype(low)
-    grad_down_weight = over_rows(hidden, cotangent).astype(low)
-    grad_normed_two, grad_gate_weight, grad_up_weight, grad_down_weight = lax.optimization_barrier(
-        (grad_normed_two, grad_gate_weight, grad_up_weight, grad_down_weight)
+    (branch,) = line_reduce((branch_part,), n, 16, 1)
+    feed_part, grad_middle, grad_branch, gain_grad_two, grad_gate_weight, grad_up_weight, grad_down_weight = feed_forward(
+        branch, gain_values[1:], tokens, cotangent, gateup_weight, down_weight, n, 2
     )
     gate_reduced = lax.psum_scatter(grad_gate_weight, "dp", scatter_dimension=0, tiled=True)
     up_reduced = lax.psum_scatter(grad_up_weight, "dp", scatter_dimension=0, tiled=True)
     down_reduced = lax.psum_scatter(grad_down_weight, "dp", scatter_dimension=1, tiled=True)
-    grad_from_two, gain_grad_two = norm_back(
-        grad_normed_two.astype(jnp.float32), unit_two, inverse_two, gain_values[1]
-    )
-    grad_middle = cotangent.astype(jnp.float32) + grad_from_two
-    grad_branch = grad_middle.astype(low)
     grad_mixture = against(grad_branch, out_weight).astype(low)
     grad_qkv = attention_backward(
         q, k, v, mixture, grad_mixture, lse, cosines, sines, seg_col, seg_row, first, size
@@ -797,10 +842,11 @@
     qkv_reduced = lax.psum_scatter(grad_qkv_weight, "dp", scatter_dimension=0, tiled=True)
     feed_out, grad_normed_one = line_reduce((feed_part, partial_one), n, 16, 3)
     grad_normed_one = grad_normed_one.astype(jnp.float32)
+    middle = values_in + branch.astype(jnp.float32)
     layer_out = (middle + feed_out.astype(jnp.float32)).astype(low)
     grad_from_one, gain_grad_one = norm_back(grad_normed_one, unit_one, inverse_one, gain_values[0])
     input_grad = grad_middle + grad_from_one
-    gain_grads = jnp.stack([gain_grad_one, gain_grad_two])
+    gain_grads = jnp.concatenate([gain_grad_one[None], gain_grad_two])
     qkv_reduced = qkv_reduced.astype(jnp.float32)
     reduced = (
         qkv_reduced[:, :width],

time: 807 us -> 691 us (0.86)
  waiting for transfers between devices: 121 us -> 31.8 us
  matrix products: 65.1 us -> 32 us
  Pallas kernels: 476 us -> 508 us
  other arithmetic: 81.6 us -> 56.1 us
    pallas_call x1 -> x2, Pallas kernels: 198 us -> 313 us  [line_reduce(): pl.pallas_call(functools.partial(line_kernel, n, chunks, lag, count), out...]
    pallas_call x1, Pallas kernels: 212 us -> 142 us  [feed_forward(): pl.pallas_call(functools.partial(ff_kernel, n, chunks, lag, norm_eps), ou...]
    all_gather x1, waiting for transfers between devices: 70.1 us -> 0.9 us  [on_device(): lax.all_gather(w_gateup.astype(low), 'dp', axis=1, tiled=True)]
    all_gather x1, waiting for transfers between devices: 39.5 us -> 0.01 us  [on_device(): down_weight = lax.all_gather(w_down.astype(low), 'dp', axis=1, tiled=True)]
    dot_general x5 -> x2, matrix products: 45.5 us -> 10.5 us  [over_rows(): lax.dot_general(left, right, (((0,), (0,)), ((), ())), preferred_element_...]
    reduce_scatter x1, waiting for transfers between devices: 0.01 us -> 14.6 us  [on_device(): lax.psum_scatter(grad_gate_weight, 'dp', scatter_dimension=0, tiled=True)]
    reduce_sum x2 -> x1, other arithmetic: 18.5 us -> 5.06 us  [norm_back(): gain_grad = jnp.sum(grad_output * unit_rows, axis=0)]
    unnamed x98 -> x94, local copies, waits for them, and re-layouts: 19.6 us -> 18.7 us
  transfers between devices with their start and end apart: 9 -> 9, of which waited for: 3 -> 4; matrix products, arithmetic and copies ran while one was open for 12% -> 11% of each run, Pallas kernels for 31% -> 52%
where the time goes in v4:
time: 691 us; the launch traced here: 683 us
  Pallas kernels  508 us (74%)
  other arithmetic  56.1 us (8%)
  matrix products  32 us (5%)
  waiting for transfers between devices  31.8 us (5%)
  local copies, waits for them, and re-layouts  22.4 us (3%)
  between operations  21.4 us (3%)
  blocking collectives  10.6 us (2%)
    pallas_call x2, Pallas kernels, line_reduce(): pl.pallas_call(functools.partial(line_kernel, n, chunks, lag, count), out...  313 us
    pallas_call x1, Pallas kernels, feed_forward(): pl.pallas_call(functools.partial(ff_kernel, n, chunks, lag, norm_eps), ou...  142 us
    pallas_call x1, Pallas kernels, attention_backward(): pl.pallas_call(functools.partial(backward_kernel, size, pairs), out_shape...  21 us
    pallas_call x1, Pallas kernels, attention_forward(): pl.pallas_call(functools.partial(forward_kernel, size, pairs), out_shape=...  18.9 us
    unnamed x94, local copies, waits for them, and re-layouts  18.7 us
    sub x6, other arithmetic, adam_step(): return (first, second, weight - step_rate * (update + decay_rate * weight))  15.2 us
    reduce_scatter x1, waiting for transfers between devices, on_device(): lax.psum_scatter(grad_gate_weight, 'dp', scatter_dimension=0, tiled=True)  14.6 us
  transfers between devices with their start and end apart: 9, of which 4 were waited for; matrix products, arithmetic and copies ran while one was open for 11% of the time, Pallas kernels for 52%

profile of v4, /device:TPU:0, one launch (start us, length us, event | category | flops | bytes accessed | tf_op | source)
XLA Modules:
  0.0 682.9 jit_solution(17069139983752149528)
XLA Ops:
  7.2 1.0 convert.12
  8.4 0.1 copy.64
  8.5 1.1 convert.11
  9.6 0.8 pad_maximum_fusion.3
  10.5 1.8 convert_element_type.77
  12.3 0.9 convert_element_type.81
  13.4 3.1 convert_element_type.80
  16.5 0.5 slice.47
  17.8 0.3 reduce-window.9
  18.5 0.2 copy.66.seg_col_ref
  18.7 10.6 %all_gather.15 = bf16[2,2048]{1,0:T(2,128)(2,1)S(1)} all-gather(bf16[2,256]{1,0:T(2,128)(2,1)S(1)} %convert_element_type.73), channel_id=1, replica_groups=mesh['dp'=8,'tensor'=4] {'dp'}, dimensions={1}, use_global_device_ids=true | all-gather | bytes 9216 | tf_op jit(solution)/shard_map/all_gather | solution.py:802
  29.3 1.9 fusion.29
  31.2 0.9 pad_maximum_fusion.1
  32.2 0.9 fusion.10
  33.1 0.6 fusion.43
  33.7 9.8 %all-gather.5.cloned.1.call-done = bf16[2048,640]{1,0:T(8,128)(2,1)} async-done(((bf16[256,640]{1,0:T(8,128)(2,1)}), bf16[2048,640]{1,0:T(8,128)(2,1)}) %all-gather.5.cloned.1.call-update) | async-done | bytes 2621456 | tf_op jit(solution)/shard_map/all_gather | solution.py:804
  43.4 6.3 fusion.22.raw_ref
  49.7 18.9 %shard_map.373 = (bf16[1024,512]{1,0:T(8,128)(2,1)S(1)}, bf16[1024,512]{1,0:T(8,128)(2,1)S(1)}, bf16[1024,128]{1,0:T(8,128)(2,1)S(1)}, bf16[1024,128]{1,0:T(8,128)(2,1)S(1)}, f32[4,4,1,512]{3,2,1,0:T(1,128)S(1)}) custom-call(s32[4]{0:T(128)S(1)} %and_select_fusion.first_ref, f32[1024,640]{1,0:T(8,128)S(1)} %fusion.22.raw_ref, ...), custom_call_target="tpu_custom_call" | custom-call | flops 5368709120 | bytes 4194304 | tf_op jit(solution)/shard_map/pallas_call | solution.py:117
  68.6 1.0 copy-done.11
  69.6 4.6 all-gather.7.cloned.1.call-done
  74.2 3.9 convolution_convert_fusion.1.refs_0_
  78.1 110.0 %shard_map.374.branch = bf16[1024,2048]{1,0:T(8,128)(2,1)S(1)} custom-call(bf16[1024,2048]{1,0:T(8,128)(2,1)S(1)} %convolution_convert_fusion.1.refs_0_), custom_call_target="tpu_custom_call" | custom-call | flops 4194304 | bytes 251658240 | tf_op jit(solution)/shard_map/pallas_call | solution.py:367
  188.2 2.0 copy-done.1
  190.2 0.9 all-gather.9.cloned.1.call-done.gu_hbm
  191.1 142.0 %shard_map.375 = (bf16[1024,2048]{1,0:T(8,128)(2,1)}, f32[1024,2048]{1,0:T(8,128)}, bf16[1024,2048]{1,0:T(8,128)(2,1)}, f32[1,2048]{1,0:T(1,128)}, bf16[2048,140...) custom-call(bf16[1024,2048]{1,0:T(8,128)(2,1)} %copy-done.1, ...), custom_call_target="tpu_custom_call" | custom-call | flops 53150220288 | bytes 314572800 | tf_op jit(solution)/shard_map/pallas_call | solution.py:602
  333.2 0.5 reduce-scatter.12.cloned.1.call-update
  333.8 0.7 reduce-scatter.14.cloned.1.call-update
  334.5 0.3 reduce-scatter.10.cloned.1.call-start
  334.7 0.3 copy-done.10
  335.0 5.9 convolution_convert_fusion.3
  340.9 6.3 convolution_convert_fusion.4.grad_ref
  347.2 21.0 %shard_map.376 = bf16[1024,640]{1,0:T(8,128)(2,1)S(1)} custom-call(s32[4]{0:T(128)S(1)} %and_select_fusion.first_ref, bf16[1024,512]{1,0:T(8,128)(2,1)S(1)} %copy-done.12, bf16[1024,128]{1,0:T(8,128)(2,1)S(1)} %get-tuple-element.44.k_ref, bf16[1024,128]{1,0:T(8,128)(2,1)S(1)} %copy-done.14, bf16[1024,512]{1,0:T(8,128)(2,1)S(1)} %copy-done.10, ...), custom_call_target="tpu_custom_call" | custom-call | flops 10737418240 | bytes 4194304 | tf_op jit(solution)/shard_map/pallas_call | solution.py:211
  368.2 5.0 convolution_convert_fusion.refs_1_
  373.2 4.6 convolution_convert_fusion.2
  377.8 14.6 %reduce-scatter.6.cloned.1.call-done = bf16[256,1408]{1,0:T(8,128)(2,1)} async-done(((bf16[2048,1408]{1,0:T(8,128)(2,1)}), bf16[256,1408]{1,0:T(8,128)(2,1)}) %reduce-scatter.6.cloned.1.call-update) | async-done | bytes 720912 | tf_op jit(solution)/shard_map/reduce_scatter | solution.py:828
  392.5 0.7 reduce-scatter.8.cloned.1.call-update
  393.2 1.0 copy.72
  395.0 1.0 copy.69
  396.0 1.0 copy.70
  397.0 2.2 copy-done.3
  399.1 202.8 %shard_map.377 = (bf16[1024,2048]{1,0:T(8,128)(2,1)S(1)}, bf16[1024,2048]{1,0:T(8,128)(2,1)S(1)}) custom-call(bf16[1024,2048]{1,0:T(8,128)(2,1)S(1)} %copy-done.3, bf16[1024,2048]{1,0:T(8,128)(2,1)} %convolution_convert_fusion.refs_1_), custom_call_target="tpu_custom_call" | custom-call | flops 8388608 | bytes 503316480 | tf_op jit(solution)/shard_map/pallas_call | solution.py:367
  602.0 2.0 copy-done
  604.0 2.0 copy-done.2
  606.0 2.5 fusion.15
  608.5 5.1 fusion.9
  613.5 0.6 maximum_bitcast_fusion.gains_ref
  614.2 2.1 fusion.19
  616.3 13.8 %fusion.6 = (f32[1024,2048]{1,0:T(8,128)}, bf16[1024,2048]{1,0:T(8,128)(2,1)}) fusion(f32[1024,2048]{1,0:T(8,128)} %get-tuple-element.51, bf16[1024,2048]{1,0:T(8,128)(2,1)} %copy-done, bf16[1024,2048]{1,0:T(8,128)(2,1)} %x.1, f32[1024]{0:T(1024)S(1)} %broadcast_multiply_fusion, f32[2048]{0:T(1024)S(1)} %bitcast.56, f32[1024]{0:T(1024)S(1)} %add_rsqrt_fusion, ...), kind=kLoop, calls=%fused_computation.10 | loop fusion | flops 27262976 | bytes 37765120 | tf_op jit(solution)/shard_map/add | solution.py:848
  630.0 1.7 fusion.26
  631.7 1.0 convert_element_type.89
  632.8 0.7 multiply_reduce_fusion
  633.5 0.6 multiply_reduce_fusion.1
  637.4 0.6 broadcast_in_dim.5.square_ref
  638.0 13.3 %shard_map.378 = (f32[8,128]{1,0:T(8,128)}, f32[2,256]{1,0:T(2,128)}) custom-call(f32[8,2,256]{2,1,0:T(2,128)} %maximum_bitcast_fusion.gains_ref, f32[8,128]{1,0:T(8,128)} %broadcast_in_dim.5.square_ref), custom_call_target="tpu_custom_call" | custom-call | tf_op jit(solution)/shard_map/pallas_call | solution.py:698
  651.3 1.2 slice.60
  653.3 2.9 multiply_subtract_fusion.3
  656.1 2.0 copy.73
  658.2 2.0 copy.74
  660.2 2.0 copy.75
  662.4 6.8 multiply_subtract_fusion
  669.2 0.8 multiply_subtract_fusion.4
  670.0 0.6 multiply_subtract_fusion.5
  670.7 2.8 multiply_subtract_fusion.1
  673.4 1.4 multiply_subtract_fusion.2
  (115 shorter events, 1.3 us)
Async XLA Ops:
  7.2 5.2 copy-start.18
  7.2 36.2 %all-gather.5.cloned.1.call-start = ((), (), s32[]{:S(2)}) async-start(), calls=%async_computation.5 | async-start | bytes 2949120 | tf_op jit(solution)/shard_map/all_gather | solution.py:804
  10.4 63.8 %all-gather.7.cloned.1.call-start = ((), (), s32[]{:S(2)}) async-start(), calls=%async_computation.6 | async-start | bytes 2359296 | tf_op jit(solution)/shard_map/all_gather | solution.py:805
  12.3 177.9 %all-gather.11.cloned.1.call-start = ((), (), s32[]{:S(2)}) async-start(), calls=%async_computation.8 | async-start | bytes 6488064 | tf_op jit(solution)/shard_map/all_gather | solution.py:807
  13.3 3.2 copy-start.8
  13.3 4.8 copy-start.39
  13.3 177.8 %all-gather.9.cloned.1.call-start = ((), (), s32[]{:S(2)}) async-start(), calls=%async_computation.7 | async-start | bytes 12976128 | tf_op jit(solution)/shard_map/all_gather | solution.py:806
  16.5 376.0 %reduce-scatter.6.cloned.1.call-start = ((), (), s32[]{:S(2)}) async-start(), calls=%async_computation.9 | async-start | bytes 6488064 | tf_op jit(solution)/shard_map/reduce_scatter | solution.py:828
  18.7 31.0 %copy-start.6 = (s32[1024,1]{1,0:T(8,128)}, s32[1024,1]{1,0:T(8,128)S(1)}, u32[]{:S(2)}) copy-start(s32[1024,1]{1,0:T(8,128)S(1)} %copy.66.seg_col_ref) | copy-start | bytes 12292
  18.7 13.5 %copy-start.15 = (bf16[1024,2048]{1,0:T(8,128)(2,1)S(1)}, bf16[1024,2048]{1,0:T(8,128)(2,1)}, u32[]{:S(2)}) copy-start(bf16[1024,2048]{1,0:T(8,128)(2,1)} %x.1) | copy-start | bytes 12582916
  32.1 17.6 %copy-start.4 = (f32[1024,128]{1,0:T(8,128)}, f32[1024,128]{1,0:T(8,128)S(1)}, u32[]{:S(2)}) copy-start(f32[1024,128]{1,0:T(8,128)S(1)} %get-tuple-element.158.sin_ref) | copy-start | bytes 1572868
  68.6 1.0 copy-start.11
  69.6 8.5 %copy-start.9 = (bf16[1024,512]{1,0:T(8,128)(2,1)}, bf16[1024,512]{1,0:T(8,128)(2,1)S(1)}, u32[]{:S(2)}) copy-start(bf16[1024,512]{1,0:T(8,128)(2,1)S(1)} %get-tuple-element.41.mix_ref) | copy-start | bytes 3145732
  69.6 8.5 %copy-start.13 = (bf16[1024,128]{1,0:T(8,128)(2,1)}, bf16[1024,128]{1,0:T(8,128)(2,1)S(1)}, u32[]{:S(2)}) copy-start(bf16[1024,128]{1,0:T(8,128)(2,1)S(1)} %get-tuple-element.45.v_ref) | copy-start | bytes 786436
  188.2 2.0 copy-start.1
  333.1 272.9 %reduce-scatter.12.cloned.1.call-start = ((), (), s32[]{:S(2)}) async-start(), calls=%async_computation.12 | async-start | bytes 6488064 | tf_op jit(solution)/shard_map/reduce_scatter | solution.py:829
  333.7 280.4 %reduce-scatter.14.cloned.1.call-start = ((), (), s32[]{:S(2)}) async-start(), calls=%async_computation.13 | async-start | bytes 6488064 | tf_op jit(solution)/shard_map/reduce_scatter | solution.py:830
  333.8 1.2 copy-start.10
  334.5 295.6 %reduce-scatter.10.cloned.1.call-start = ((), (), s32[]{:S(2)}) async-start(), calls=%async_computation.11 | async-start | bytes 2359296 | tf_op jit(solution)/shard_map/reduce_scatter | solution.py:841
  340.9 6.3 copy-start.5
  340.9 6.3 copy-start.7
  340.9 6.3 copy-start.12
  340.9 6.3 copy-start.14
  347.2 21.0 %copy-start.43 = (bf16[2048,640]{1,0:T(8,128)(2,1)S(1)}, bf16[2048,640]{1,0:T(8,128)(2,1)}, u32[]{:S(2)}) copy-start(bf16[2048,640]{1,0:T(8,128)(2,1)} %all-gather.5.cloned.1.call-done) | copy-start | bytes 7864324
  368.2 5.0 copy-start.16
  377.8 15.4 %copy-start.22 = (f32[256,512]{1,0:T(8,128)S(1)}, f32[256,512]{1,0:T(8,128)}, u32[]{:S(2)}) copy-start(f32[256,512]{1,0:T(8,128)} %param.29) | copy-start | bytes 1572868
  377.8 17.1 %copy-start.31 = (f32[256,512]{1,0:T(8,128)S(1)}, f32[256,512]{1,0:T(8,128)}, u32[]{:S(2)}) copy-start(f32[256,512]{1,0:T(8,128)} %param.30) | copy-start | bytes 1572868
  392.5 3.5 copy-start.32
  392.5 239.2 %reduce-scatter.8.cloned.1.call-start = ((), (), s32[]{:S(2)}) async-start(), calls=%async_computation.10 | async-start | bytes 2949120 | tf_op jit(solution)/shard_map/reduce_scatter | solution.py:842
  397.0 2.2 copy-start.3
  399.1 206.9 %copy-start.20 = (bf16[256,1408]{1,0:T(8,128)(2,1)S(1)}, bf16[256,1408]{1,0:T(8,128)(2,1)}, u32[]{:S(2)}) copy-start(bf16[256,1408]{1,0:T(8,128)(2,1)} %reduce-scatter.6.cloned.1.call-done) | copy-start | bytes 2162692
  602.0 2.0 copy-start
  604.0 2.0 copy-start.2
  608.5 5.1 copy-start.38
  632.8 0.8 copy-start.27
  632.8 0.8 copy-start.29
  653.2 9.0 %copy-start.17 = (f32[2,256,1408]{2,1,0:T(8,128)S(1)}, f32[2,256,1408]{2,1,0:T(8,128)}, u32[]{:S(2)}) copy-start(f32[2,256,1408]{2,1,0:T(8,128)} %param.38) | copy-start | bytes 8650756
  662.3 6.9 %copy-start.28 = (f32[1,256,64]{1,2,0:T(8,128)S(1)}, f32[1,256,64]{1,2,0:T(8,128)}, u32[]{:S(2)}) copy-start(f32[1,256,64]{1,2,0:T(8,128)} %copy-done.27) | copy-start | bytes 196612
  662.3 6.9 %copy-start.30 = (f32[1,256,64]{1,2,0:T(8,128)S(1)}, f32[1,256,64]{1,2,0:T(8,128)}, u32[]{:S(2)}) copy-start(f32[1,256,64]{1,2,0:T(8,128)} %copy-done.29) | copy-start | bytes 196612
  662.3 6.9 %copy-start.33 = (f32[2,256,64]{1,2,0:T(8,128)S(1)}, f32[2,256,64]{1,2,0:T(8,128)}, u32[]{:S(2)}) copy-start(f32[2,256,64]{1,2,0:T(8,128)} %param.32) | copy-start | bytes 393220
  662.3 6.9 %copy-start.36 = (f32[2,256,64]{1,2,0:T(8,128)S(1)}, f32[2,256,64]{1,2,0:T(8,128)}, u32[]{:S(2)}) copy-start(f32[2,256,64]{1,2,0:T(8,128)} %param.34) | copy-start | bytes 393220
  662.3 6.9 %copy-start.37 = (f32[2,256,64]{1,2,0:T(8,128)S(1)}, f32[2,256,64]{1,2,0:T(8,128)}, u32[]{:S(2)}) copy-start(f32[2,256,64]{1,2,0:T(8,128)} %param.33) | copy-start | bytes 393220
  662.3 7.7 %copy-start.40 = (f32[2,256]{1,0:T(2,128)S(1)}, f32[2,256]{1,0:T(2,128)}, u32[]{:S(2)}) copy-start(f32[2,256]{1,0:T(2,128)} %param.28) | copy-start | bytes 6148
  662.3 7.7 %copy-start.41 = (f32[2,256]{1,0:T(2,128)S(1)}, f32[2,256]{1,0:T(2,128)}, u32[]{:S(2)}) copy-start(f32[2,256]{1,0:T(2,128)} %param.27) | copy-start | bytes 6148
  662.3 7.7 %copy-start.42 = (f32[2,256]{1,0:T(2,128)S(1)}, f32[2,256]{1,0:T(2,128)}, u32[]{:S(2)}) copy-start(f32[2,256]{1,0:T(2,128)} %get-tuple-element.60) | copy-start | bytes 6148
  662.3 8.3 %copy-start.19 = (f32[1408,256]{1,0:T(8,128)S(1)}, f32[1408,256]{1,0:T(8,128)}, u32[]{:S(2)}) copy-start(f32[1408,256]{1,0:T(8,128)} %param.41) | copy-start | bytes 4325380
  662.3 8.3 %copy-start.21 = (bf16[1408,256]{1,0:T(8,128)(2,1)S(1)}, bf16[1408,256]{1,0:T(8,128)(2,1)}, u32[]{:S(2)}) copy-start(bf16[1408,256]{1,0:T(8,128)(2,1)} %reduce-scatter.14.cloned.1.call-done) | copy-start | bytes 2162692
  662.3 8.3 %copy-start.24 = (f32[1408,256]{1,0:T(8,128)S(1)}, f32[1408,256]{1,0:T(8,128)}, u32[]{:S(2)}) copy-start(f32[1408,256]{1,0:T(8,128)} %param.43) | copy-start | bytes 4325380
  662.4 8.3 %copy-start.25 = (f32[1408,256]{1,0:T(8,128)S(1)}, f32[1408,256]{1,0:T(8,128)}, u32[]{:S(2)}) copy-start(f32[1408,256]{1,0:T(8,128)} %param.42) | copy-start | bytes 4325380
  670.6 2.8 copy-start.23
  670.6 2.8 copy-start.26
  670.7 2.8 copy-start.34
  670.7 2.8 copy-start.35
Sparse Core Ops, SparseCore 0:
  10.6 32.8 all-gather.4
  45.9 28.2 all-gather.6
  76.6 44.3 all-gather.10
  123.3 67.6 all-gather.8
  333.3 59.1 reduce-scatter.5
  396.1 59.0 reduce-scatter.11
  458.7 58.9 reduce-scatter.13
  521.9 41.2 reduce-scatter.9
  567.1 43.6 reduce-scatter.7

commit v5 on v4

--- a/solution.py
+++ b/solution.py
@@ -136,97 +136,9 @@
     )(first, raw, cosines, sines, seg_col, seg_row)
 
 
-def backward_kernel(size, pairs, first_ref, q_ref, k_ref, v_ref, mix_ref, grad_ref, lse_ref, cos_ref, sin_ref,
-                    seg_col_ref, seg_row_ref, out_ref, bias, k_turned, grad_k, grad_v):
-    length = q_ref.shape[0]
-    width = pairs * 128
-    low_lanes, first_half = lane_tests(size)
-    low_rows = lax.broadcasted_iota(jnp.int32, (128, size), 0) < 64
-
-    def prepare(i, carry):
-        rows = pl.ds(pl.multiple_of(i * size, size), size)
-        k_turned[i] = k_ref[rows, :].astype(jnp.float32).T.astype(jnp.bfloat16)
-        grad_k[i] = jnp.zeros((size, 128), jnp.float32)
-        grad_v[i] = jnp.zeros((size, 128), jnp.float32)
-        return carry
-
-    lax.fori_loop(0, length // size, prepare, 0)
-
-    def row_block(i, carry):
-        rows = pl.ds(pl.multiple_of(i * size, size), size)
-        begin = first_ref[i]
-        cosines, sines = cos_ref[rows, :], sin_ref[rows, :]
-
-        def fill(j, c):
-            bias[j] = block_bias(seg_col_ref, seg_row_ref, i, j, size)
-            return c
-
-        lax.fori_loop(begin, i + 1, fill, 0)
-
-        for hp in range(pairs):
-            columns = slice(hp * 128, (hp + 1) * 128)
-            stacked = stack_pair(q_ref[rows, columns], low_lanes)
-            grad_pair = grad_ref[rows, columns]
-            grad_stacked = stack_pair(grad_pair, low_lanes)
-            product = (grad_pair.astype(jnp.float32) * mix_ref[rows, columns].astype(jnp.float32)).T
-            spread = jnp.concatenate([
-                jnp.sum(product[:64], axis=0, keepdims=True), jnp.sum(product[64:], axis=0, keepdims=True)], axis=1)
-            logsum = lse_ref[i, hp]
-
-            def piece(j, acc):
-                at = pl.ds(pl.multiple_of(j * size, size), size)
-                b = bias[j]
-                s = dot_t(k_ref[at, :], stacked) + jnp.concatenate([b, b], axis=1)
-                p = jnp.exp(s - logsum)
-                grad_p = dot_t(v_ref[at, :], grad_stacked)
-                grad_s = (p * (grad_p - spread)).astype(jnp.bfloat16)
-                grad_v[j] += dot_n(p.astype(jnp.bfloat16), grad_stacked)
-                grad_k[j] += dot_n(grad_s, stacked)
-                return acc + dot_n(k_turned[j], grad_s)
-
-            acc = lax.fori_loop(begin, i + 1, piece, jnp.zeros((128, 2 * size), jnp.float32))
-            acc = jnp.where(low_rows, acc[:, :size], acc[:, size:]).T * 0.125
-            out_ref[rows, columns] = (acc * cosines - swap_halves(acc, first_half) * sines).astype(jnp.bfloat16)
-        return carry
-
-    lax.fori_loop(0, length // size, row_block, 0)
-
-    def finish(i, carry):
-        rows = pl.ds(pl.multiple_of(i * size, size), size)
-        cosines, sines = cos_ref[rows, :], sin_ref[rows, :]
-        dk = grad_k[i] + pltpu.roll(grad_k[i], 64, 1)
-        dk = dk * cosines - swap_halves(dk, first_half) * sines
-        dv = grad_v[i] + pltpu.roll(grad_v[i], 64, 1)
-        out_ref[rows, width:width + 128] = jnp.where(low_lanes, dk, dv).astype(jnp.bfloat16)
-        return carry
-
-    lax.fori_loop(0, length // size, finish, 0)
-
-
-def attention_backward(q, k, v, mix, grad, lse, cosines, sines, seg_col, seg_row, first, size):
-    length, width = q.shape
-    pairs = width // 128
-    blocks = length // size
-    vmem = pl.BlockSpec(memory_space=pltpu.VMEM)
-    return pl.pallas_call(
-        functools.partial(backward_kernel, size, pairs),
-        out_shape=jax.ShapeDtypeStruct((length, width + 128), jnp.bfloat16),
-        in_specs=[pl.BlockSpec(memory_space=pltpu.SMEM)] + [vmem] * 10,
-        out_specs=vmem,
-        scratch_shapes=[
-            pltpu.VMEM((blocks, size, size), jnp.float32),
-            pltpu.VMEM((blocks, 128, size), jnp.bfloat16),
-            pltpu.VMEM((blocks, size, 128), jnp.float32),
-            pltpu.VMEM((blocks, size, 128), jnp.float32),
-        ],
-        compiler_params=pltpu.CompilerParams(vmem_limit_bytes=40 << 20),
-        cost_estimate=pl.CostEstimate(flops=20 * length * length * width, bytes_accessed=8 * length * width,
-                                      transcendentals=length * length * pairs),
-    )(first, q, k, v, mix, grad, lse, cosines, sines, seg_col, seg_row)
-
-
 class Line:
-    def __init__(self, n, chunks, rc, lag, part, got, out, sems):
+    def __init__(self, n, chunks, rc, lag, part, got, out, sems, order=None):
+        self.order = order
         self.n, self.chunks, self.rc, self.lag = n, chunks, rc, lag
         self.part, self.got, self.out = part, got, out
         self.send_a, self.recv_a, self.send_g, self.recv_g = sems
@@ -234,7 +146,8 @@
         self.steps = chunks + 2 * lag * (n - 1)
 
     def rows(self, stream, c):
-        return pl.ds(pl.multiple_of((stream * self.chunks + c) * self.rc, self.rc), self.rc)
+        begin = (stream * self.chunks + c) * self.rc if self.order is None else self.order(stream, c)
+        return pl.ds(pl.multiple_of(begin, self.rc), self.rc)
 
     def side(self, stream):
         pos = self.me if stream == 0 else self.n - 1 - self.me
@@ -381,9 +294,9 @@
 
 
 def ff_kernel(n, chunks, lag, eps, branch, gain, x, cot_hbm, gu_hbm, down_hbm,
-              feed_hbm, middle_hbm, low_hbm, gain_out, gate_grad_hbm, up_grad_hbm, down_grad_hbm,
+              feed_hbm, middle_hbm, low_hbm, gain_out, grads_hbm,
               got, sa, ra, sg, rg, two_sum, two_part, gu_w, down_w, cot, normed, hidden, gg, feed,
-              middle_stage, low_stage, unit_stage, down_stage, w_sem, cot_sem, feed_sem, stage_sem, grad_sem):
+              middle_stage, low_stage, unit_stage, w_sem, cot_sem, feed_sem, stage_sem, grad_sem):
     rows, width = branch.shape
     ff = down_w.shape[0]
     rc = rows // (2 * chunks)
@@ -428,14 +341,7 @@
         return copies
 
     def save_units(w):
-        at = pl.ds(pl.multiple_of(w * tile, tile), tile)
-        return [
-            pltpu.make_async_copy(unit_stage.at[0], gate_grad_hbm.at[at], grad_sem.at[0]),
-            pltpu.make_async_copy(unit_stage.at[1], up_grad_hbm.at[at], grad_sem.at[1]),
-        ]
-
-    def save_down(at, count):
-        return [pltpu.make_async_copy(down_stage.at[pl.ds(0, count)], down_grad_hbm.at[pl.ds(at, count)], grad_sem.at[2])]
+        return [pltpu.make_async_copy(unit_stage, grads_hbm.at[pl.ds(pl.multiple_of(w * tile, tile), tile)], grad_sem.at[0])]
 
     def start(copies):
         for copy in copies:
@@ -558,26 +464,9 @@
             columns = pl.ds(pl.multiple_of(w * tile, tile), tile)
             left = normed[:, columns]
             for t in (0, 1):
-                unit_stage[t] = dot_rows(left, gg[t]).astype(jnp.bfloat16)
+                unit_stage[:, t * ff:(t + 1) * ff] = dot_rows(left, gg[t]).astype(jnp.bfloat16)
+            unit_stage[:, 2 * ff:] = dot_rows(cot[:, columns], hidden[...]).astype(jnp.bfloat16)
             start(save_units(w))
-
-        v = w - wide
-
-        @pl.when((v >= 0) & (v < full))
-        def _():
-            @pl.when(v > 0)
-            def _():
-                wait(save_down((v - 1) * tile, tile))
-            at = pl.multiple_of(v * tile, tile)
-            down_stage[...] = dot_rows(hidden[:, pl.ds(at, tile)], cot[...]).astype(jnp.bfloat16)
-            start(save_down(at, tile))
-
-        if rest:
-            @pl.when(v == full)
-            def _():
-                wait(save_down((full - 1) * tile, tile))
-                down_stage[pl.ds(0, rest), :] = dot_rows(hidden[:, full * tile:], cot[...]).astype(jnp.bfloat16)
-                start(save_down(full * tile, rest))
         return carry
 
     lax.fori_loop(0, per + line.steps, step, 0)
@@ -585,7 +474,6 @@
     wait(save_feed(blocks - 1))
     wait(save_rows(chunks - 1))
     wait(save_units(wide - 1))
-    wait(save_down(full * tile, rest) if rest else save_down((full - 1) * tile, tile))
 
 
 def feed_forward(branch, gain, x, cot, gateup_w, down_w, n, cid, chunks=16, lag=2):
@@ -603,10 +491,10 @@
         functools.partial(ff_kernel, n, chunks, lag, norm_eps),
         out_shape=(
             shape((rows, width), low), shape((rows, width), jnp.float32), shape((rows, width), low),
-            shape((1, width), jnp.float32), shape((width, ff), low), shape((width, ff), low), shape((ff, width), low),
+            shape((1, width), jnp.float32), shape((width, 3 * ff), low),
         ),
         in_specs=[vmem, vmem, vmem, hbm, hbm, hbm],
-        out_specs=(hbm, hbm, hbm, vmem, hbm, hbm, hbm),
+        out_specs=(hbm, hbm, hbm, vmem, hbm),
         scratch_shapes=line_scratch(chunks, rc, width) + [
             pltpu.VMEM((rows, width), low),
             pltpu.VMEM((rows, width), low),
@@ -619,14 +507,341 @@
             pltpu.VMEM((block, width), low),
             pltpu.VMEM((2, rc, width), jnp.float32),
             pltpu.VMEM((2, rc, width), low),
-            pltpu.VMEM((2, 256, ff), low),
-            pltpu.VMEM((256, width), low),
-            dma((2,)), dma((blocks, 2)), dma((2,)), dma((2, 2)), dma((3,)),
+            pltpu.VMEM((256, 3 * ff), low),
+            dma((2,)), dma((blocks, 2)), dma((2,)), dma((2, 2)), dma((1,)),
         ],
         compiler_params=pltpu.CompilerParams(collective_id=cid, has_side_effects=True, vmem_limit_bytes=63 << 20),
         cost_estimate=pl.CostEstimate(flops=18 * rows * width * ff, bytes_accessed=rows * width * 150,
                                       transcendentals=rows * ff),
     )(branch, gain, x, cot, gateup_w, down_w)
+
+
+def back_kernel(n, m, chunks, lag, eps, size, pairs,
+                feed_part, grad_low, gain, q_ref, k_ref, v_ref, mix_ref, lse_ref, cos_ref, sin_ref,
+                seg_col_ref, seg_row_ref, out_w, x_hbm, qkv_hbm, branch_hbm, middle_hbm,
+                layer_hbm, input_hbm, gain_out, reduced,
+                got2, sa2, ra2, sg2, rg2, got4, sa4, ra4, sg4, rg4, feed_sum, part, grad_sum,
+                x, qkv_w, normed, grad_mix, bias, k_turned, grad_k, grad_v, grad_qkv, send, recv,
+                branch_stage, layer_stage, middle_stage, input_stage,
+                w_sem, branch_sem, middle_sem, layer_sem, input_sem, send_sem, recv_sem):
+    rows, width = feed_part.shape
+    q_width = pairs * 128
+    z = lax.axis_index("tensor")
+    dp = lax.axis_index("dp")
+    rc = rows // (2 * chunks)
+    per = size // (2 * rc)
+    hb = size // 2
+    blocks = rows // size
+    tile = 256
+    wide = width // tile
+    share = width // m
+    owners = tile // share
+    lead = 2 * lag * (n - 1)
+    low_lanes, first_half = lane_tests(size)
+    low_rows = lax.broadcasted_iota(jnp.int32, (128, size), 0) < 64
+
+    def descending(stream, c):
+        b = c // per
+        return (blocks - 1 - b) * size + stream * hb + (c - b * per) * rc
+
+    two = Line(n, chunks, rc, lag, feed_part, got2, feed_sum, (sa2, ra2, sg2, rg2))
+    four = Line(n, chunks, rc, lag, part, got4, grad_sum, (sa4, ra4, sg4, rg4), descending)
+    loads = (
+        pltpu.make_async_copy(x_hbm, x, w_sem.at[0]),
+        pltpu.make_async_copy(qkv_hbm, qkv_w, w_sem.at[1]),
+    )
+    for copy in loads:
+        copy.start()
+
+    def start(copies):
+        for copy in copies:
+            copy.start()
+
+    def wait(copies):
+        for copy in copies:
+            copy.wait()
+
+    def load_branch(d, slot):
+        return [pltpu.make_async_copy(branch_hbm.at[two.rows(k, d)], branch_stage.at[slot, k], branch_sem.at[slot, k])
+                for k in (0, 1)]
+
+    def load_middle(d, slot):
+        return [pltpu.make_async_copy(middle_hbm.at[four.rows(k, d)], middle_stage.at[slot, k], middle_sem.at[slot, k])
+                for k in (0, 1)]
+
+    def save_layer(d):
+        return [pltpu.make_async_copy(layer_stage.at[k], layer_hbm.at[two.rows(k, d)], layer_sem.at[k]) for k in (0, 1)]
+
+    def save_input(d):
+        return [pltpu.make_async_copy(input_stage.at[k], input_hbm.at[four.rows(k, d)], input_sem.at[k]) for k in (0, 1)]
+
+    def to_owner(w, o):
+        owner = w * owners + o
+        return pltpu.make_async_remote_copy(
+            src_ref=send.at[w, pl.ds(o * share, share)], dst_ref=recv.at[dp], send_sem=send_sem.at[owner],
+            recv_sem=recv_sem.at[dp], device_id={"dp": owner}, device_id_type=MESH)
+
+    gain_out[...] = jnp.zeros_like(gain_out)
+
+    def prepare(i, carry):
+        at = pl.ds(pl.multiple_of(i * size, size), size)
+        k_turned[i] = k_ref[at, :].astype(jnp.float32).T.astype(jnp.bfloat16)
+        grad_k[i] = jnp.zeros((size, 128), jnp.float32)
+        grad_v[i] = jnp.zeros((size, 128), jnp.float32)
+        return carry
+
+    lax.fori_loop(0, blocks, prepare, 0)
+
+    barrier = pltpu.get_barrier_semaphore()
+
+    @pl.when(z > 0)
+    def _():
+        pl.semaphore_signal(barrier, inc=1, device_id={"tensor": z - 1}, device_id_type=MESH)
+
+    @pl.when(z < n - 1)
+    def _():
+        pl.semaphore_signal(barrier, inc=1, device_id={"tensor": z + 1}, device_id_type=MESH)
+
+    for k in range(1, m):
+        pl.semaphore_signal(barrier, inc=1, device_id={"dp": lax.rem(dp + k, m)}, device_id_type=MESH)
+
+    @pl.when((z > 0) & (z < n - 1))
+    def _():
+        pl.semaphore_wait(barrier, m + 1)
+
+    @pl.when((z == 0) | (z == n - 1))
+    def _():
+        pl.semaphore_wait(barrier, m)
+
+    def unit_rows(where):
+        values = x[where, :].astype(jnp.float32)
+        inverse = lax.rsqrt(jnp.mean(values * values, axis=-1, keepdims=True) + eps)
+        return values * inverse, inverse
+
+    def attend(i, hp):
+        at_rows = pl.ds(pl.multiple_of(i * size, size), size)
+        columns = pl.ds(pl.multiple_of(hp * 128, 128), 128)
+        stacked = stack_pair(q_ref[at_rows, columns], low_lanes)
+        grad_pair = grad_mix[:, columns]
+        grad_stacked = stack_pair(grad_pair, low_lanes)
+        product = (grad_pair.astype(jnp.float32) * mix_ref[at_rows, columns].astype(jnp.float32)).T
+        spread = jnp.concatenate([
+            jnp.sum(product[:64], axis=0, keepdims=True), jnp.sum(product[64:], axis=0, keepdims=True)], axis=1)
+        logsum = lse_ref[i, hp]
+
+        def piece(j, acc):
+            at = pl.ds(pl.multiple_of(j * size, size), size)
+            b = bias[j]
+            s = dot_t(k_ref[at, :], stacked) + jnp.concatenate([b, b], axis=1)
+            p = jnp.exp(s - logsum)
+            grad_p = dot_t(v_ref[at, :], grad_stacked)
+            grad_s = (p * (grad_p - spread)).astype(jnp.bfloat16)
+            grad_v[j] += dot_n(p.astype(jnp.bfloat16), grad_stacked)
+            grad_k[j] += dot_n(grad_s, stacked)
+            return acc + dot_n(k_turned[j], grad_s)
+
+        acc = lax.fori_loop(0, i + 1, piece, jnp.zeros((128, 2 * size), jnp.float32))
+        acc = jnp.where(low_rows, acc[:, :size], acc[:, size:]).T * 0.125
+        turned = acc * cos_ref[at_rows, :] - swap_halves(acc, first_half) * sin_ref[at_rows, :]
+        grad_qkv[at_rows, columns] = turned.astype(jnp.bfloat16)
+
+    def step(s, carry):
+        two.step(s)
+        four.step(s - per)
+        b = s // per
+        hp = s - b * per
+        i = blocks - 1 - b
+        live = s < blocks * per
+        at_rows = pl.ds(pl.multiple_of(i * size, size), size)
+
+        @pl.when(s == 0)
+        def _():
+            wait(loads)
+
+        @pl.when(live & (hp == 0))
+        def _():
+            grad_mix[...] = dot_t(grad_low[at_rows, :], out_w[...]).astype(jnp.bfloat16)
+
+            def fill(j, c):
+                bias[j] = block_bias(seg_col_ref, seg_row_ref, i, j, size)
+                return c
+
+            lax.fori_loop(0, i + 1, fill, 0)
+
+        @pl.when(live)
+        def _():
+            def each(h, c):
+                attend(i, h)
+                return c
+
+            lax.fori_loop(hp * pairs // per, (hp + 1) * pairs // per, each, 0)
+
+            def some(r, c):
+                at = pl.ds(pl.multiple_of(s * 2 * rc + r * rc, rc), rc)
+                normed[at, :] = (unit_rows(at)[0] * gain[...]).astype(jnp.bfloat16)
+                return c
+
+            lax.fori_loop(0, 2, some, 0)
+
+        @pl.when(live & (hp == per - 1))
+        def _():
+            cosines, sines = cos_ref[at_rows, :], sin_ref[at_rows, :]
+            dk = grad_k[i] + pltpu.roll(grad_k[i], 64, 1)
+            dk = dk * cosines - swap_halves(dk, first_half) * sines
+            dv = grad_v[i] + pltpu.roll(grad_v[i], 64, 1)
+            grad_qkv[at_rows, q_width:] = jnp.where(low_lanes, dk, dv).astype(jnp.bfloat16)
+
+            def part_tile(t, c):
+                at = pl.ds(pl.multiple_of(t * tile, tile), tile)
+                part[at_rows, at] = dot_t(grad_qkv[at_rows, :], qkv_w[at, :]).astype(jnp.bfloat16)
+                return c
+
+            lax.fori_loop(0, wide, part_tile, 0)
+
+        w = s - blocks * per
+
+        @pl.when((w >= 0) & (w < wide))
+        def _():
+            columns = pl.ds(pl.multiple_of(w * tile, tile), tile)
+            send[w, :, :q_width + 128] = dot_rows(normed[:, columns], grad_qkv[...]).astype(jnp.bfloat16)
+            send[w, :, q_width + 128:] = dot_rows(grad_low[:, columns], mix_ref[...]).astype(jnp.bfloat16)
+            for o in range(owners):
+                owner = w * owners + o
+
+                @pl.when(owner != dp)
+                def _():
+                    to_owner(w, o).start()
+
+                @pl.when(owner == dp)
+                def _():
+                    recv[dp] = send[w, o * share:(o + 1) * share, :]
+
+        e = s - lead + 1
+
+        @pl.when((e >= 0) & (e < chunks))
+        def _():
+            start(load_branch(e, e % 2))
+
+        d = s - lead
+
+        @pl.when((d >= 0) & (d < chunks))
+        def _():
+            wait(load_branch(d, d % 2))
+
+            @pl.when(d > 0)
+            def _():
+                wait(save_layer(d - 1))
+            for k in (0, 1):
+                where = two.rows(k, d)
+                layer_stage[k] = (
+                    x[where, :].astype(jnp.float32) + branch_stage[d % 2, k].astype(jnp.float32)
+                    + feed_sum[where, :].astype(jnp.float32)
+                ).astype(jnp.bfloat16)
+            start(save_layer(d))
+
+        e4 = s - lead - per + 1
+
+        @pl.when((e4 >= 0) & (e4 < chunks))
+        def _():
+            start(load_middle(e4, e4 % 2))
+
+        d4 = s - lead - per
+
+        @pl.when(d4 >= 0)
+        def _():
+            wait(load_middle(d4, d4 % 2))
+
+            @pl.when(d4 > 0)
+            def _():
+                wait(save_input(d4 - 1))
+            for k in (0, 1):
+                where = four.rows(k, d4)
+                unit, inverse = unit_rows(where)
+                grad = grad_sum[where, :].astype(jnp.float32)
+                scaled = grad * gain[...]
+                inner = jnp.mean(scaled * unit, axis=-1, keepdims=True)
+                input_stage[k] = middle_stage[d4 % 2, k] + inverse * (scaled - unit * inner)
+                gain_out[...] += jnp.sum(grad * unit, axis=0, keepdims=True)
+            start(save_input(d4))
+        return carry
+
+    lax.fori_loop(0, per + four.steps, step, 0)
+    two.drain()
+    four.drain()
+    wait(save_layer(chunks - 1))
+    wait(save_input(chunks - 1))
+
+    def finish(k, carry):
+        owner = lax.rem(dp + k, m)
+        w = owner // owners
+
+        def copy(peer):
+            return pltpu.make_async_remote_copy(
+                src_ref=send.at[0, pl.ds(0, share)], dst_ref=recv.at[peer], send_sem=send_sem.at[peer],
+                recv_sem=recv_sem.at[peer], device_id={"dp": peer}, device_id_type=MESH)
+
+        copy(owner).wait_send()
+        copy(owner).wait_recv()
+        return carry
+
+    lax.fori_loop(1, m, finish, 0)
+    reduced[...] = recv[0].astype(jnp.float32)
+
+    def add(k, carry):
+        reduced[...] += recv[k].astype(jnp.float32)
+        return carry
+
+    lax.fori_loop(1, m, add, 0)
+
+
+def attention_back(feed_part, grad_low, gain, q, k, v, mix, lse, cosines, sines, seg_col, seg_row, out_w,
+                   x, qkv_w, branch, grad_middle, n, m, cid, size, chunks=16, lag=2):
+    rows, width = feed_part.shape
+    q_width = q.shape[1]
+    pairs = q_width // 128
+    rc = rows // (2 * chunks)
+    blocks = rows // size
+    share = width // m
+    cat = 2 * q_width + 128
+    low = jnp.bfloat16
+    vmem = pl.BlockSpec(memory_space=pltpu.VMEM)
+    hbm = pl.BlockSpec(memory_space=pl.ANY)
+    dma = pltpu.SemaphoreType.DMA
+    shape = jax.ShapeDtypeStruct
+    return pl.pallas_call(
+        functools.partial(back_kernel, n, m, chunks, lag, norm_eps, size, pairs),
+        out_shape=(
+            shape((rows, width), low), shape((rows, width), jnp.float32), shape((1, width), jnp.float32),
+            shape((share, cat), jnp.float32),
+        ),
+        in_specs=[vmem] * 13 + [hbm] * 4,
+        out_specs=(hbm, hbm, vmem, vmem),
+        scratch_shapes=line_scratch(chunks, rc, width) + line_scratch(chunks, rc, width) + [
+            pltpu.VMEM((rows, width), low),
+            pltpu.VMEM((rows, width), low),
+            pltpu.VMEM((rows, width), low),
+            pltpu.VMEM((rows, width), low),
+            pltpu.VMEM((width, q_width + 128), low),
+            pltpu.VMEM((rows, width), low),
+            pltpu.VMEM((size, q_width), low),
+            pltpu.VMEM((blocks, size, size), jnp.float32),
+            pltpu.VMEM((blocks, 128, size), low),
+            pltpu.VMEM((blocks, size, 128), jnp.float32),
+            pltpu.VMEM((blocks, size, 128), jnp.float32),
+            pltpu.VMEM((rows, q_width + 128), low),
+            pltpu.VMEM((width // 256, 256, cat), low),
+            pltpu.VMEM((m, share, cat), low),
+            pltpu.VMEM((2, 2, rc, width), low),
+            pltpu.VMEM((2, rc, width), low),
+            pltpu.VMEM((2, 2, rc, width), jnp.float32),
+            pltpu.VMEM((2, rc, width), jnp.float32),
+            dma((2,)), dma((2, 2)), dma((2, 2)), dma((2,)), dma((2,)), dma((m,)), dma((m,)),
+        ],
+        compiler_params=pltpu.CompilerParams(collective_id=cid, has_side_effects=True, vmem_limit_bytes=63 << 20),
+        cost_estimate=pl.CostEstimate(flops=40 * rows * width * q_width, bytes_accessed=rows * width * 260,
+                                      transcendentals=rows * rows * pairs),
+    )(feed_part, grad_low, gain, q, k, v, mix, lse, cosines, sines, seg_col, seg_row, out_w,
+      x, qkv_w, branch, grad_middle)
 
 
 def total_kernel(n, m, gains_ref, square_ref, total_ref, gain_ref, line, got_gains, got_line, got_plane,
@@ -739,25 +954,6 @@
         jnp.concatenate([cosines] * 4, axis=-1),
         jnp.concatenate([-sines, sines, -sines, sines], axis=-1),
     )
-
-
-def over_rows(left, right):
-    return lax.dot_general(
-        left, right, (((0,), (0,)), ((), ())), preferred_element_type=jnp.float32
-    )
-
-
-def against(left, right):
-    return lax.dot_general(
-        left, right, (((1,), (1,)), ((), ())), preferred_element_type=jnp.float32
-    )
-
-
-def norm_back(grad_output, unit_rows, inverse, gain):
-    scaled = grad_output * gain
-    gain_grad = jnp.sum(grad_output * unit_rows, axis=0)
-    inner_mean = jnp.mean(scaled * unit_rows, axis=-1, keepdims=True)
-    return (inverse * (scaled - unit_rows * inner_mean), gain_grad)
 
 
 def adam_step(weight, first, second, gradient, clip_factor, step_float, step_rate, decay_rate):
@@ -822,42 +1018,28 @@
     mixture, q, k, v, lse = attention_forward(raw, cosines, sines, seg_col, seg_row, first, size)
     branch_part = jnp.dot(mixture, out_weight, preferred_element_type=jnp.float32).astype(low)
     (branch,) = line_reduce((branch_part,), n, 16, 1)
-    feed_part, grad_middle, grad_branch, gain_grad_two, grad_gate_weight, grad_up_weight, grad_down_weight = feed_forward(
+    feed_part, grad_middle, grad_branch, gain_grad_two, grad_ff_weight = feed_forward(
         branch, gain_values[1:], tokens, cotangent, gateup_weight, down_weight, n, 2
     )
-    gate_reduced = lax.psum_scatter(grad_gate_weight, "dp", scatter_dimension=0, tiled=True)
-    up_reduced = lax.psum_scatter(grad_up_weight, "dp", scatter_dimension=0, tiled=True)
-    down_reduced = lax.psum_scatter(grad_down_weight, "dp", scatter_dimension=1, tiled=True)
-    grad_mixture = against(grad_branch, out_weight).astype(low)
-    grad_qkv = attention_backward(
-        q, k, v, mixture, grad_mixture, lse, cosines, sines, seg_col, seg_row, first, size
+    ff_reduced = lax.psum_scatter(grad_ff_weight, "dp", scatter_dimension=0, tiled=True)
+    layer_out, input_grad, gain_grad_one, head_reduced = attention_back(
+        feed_part, grad_branch, gain_values[:1], q, k, v, mixture, lse, cosines, sines, seg_col, seg_row,
+        out_weight, tokens, qkv_weight, branch, grad_middle, n, m, 3, size
     )
-    partial_one = against(grad_qkv, qkv_weight).astype(low)
-    grad_out_weight = over_rows(mixture, grad_branch).astype(low)
-    grad_qkv_weight = over_rows(normed_one, grad_qkv).astype(low)
-    partial_one, grad_out_weight, grad_qkv_weight, gate_reduced = lax.optimization_barrier(
-        (partial_one, grad_out_weight, grad_qkv_weight, gate_reduced)
+    gain_grads = jnp.concatenate([gain_grad_one, gain_grad_two])
+    ff_reduced = ff_reduced.astype(jnp.float32)
+    ff = w_down.shape[0]
+    wide = width + 2 * kv_width
+    local_square = jnp.sum(head_reduced * head_reduced) + jnp.sum(ff_reduced * ff_reduced)
+    square_total, gains_reduced = reduce_tail(gain_grads, local_square, n, m, 4)
+    reduced = (
+        gains_reduced,
+        head_reduced[:, :width],
+        jnp.stack([head_reduced[:, width : width + kv_width], head_reduced[:, width + kv_width : wide]]),
+        head_reduced[:, wide:].T,
+        jnp.stack([ff_reduced[:, :ff], ff_reduced[:, ff : 2 * ff]]),
+        ff_reduced[:, 2 * ff :].T,
     )
-    out_reduced = lax.psum_scatter(grad_out_weight, "dp", scatter_dimension=1, tiled=True)
-    qkv_reduced = lax.psum_scatter(grad_qkv_weight, "dp", scatter_dimension=0, tiled=True)
-    feed_out, grad_normed_one = line_reduce((feed_part, partial_one), n, 16, 3)
-    grad_normed_one = grad_normed_one.astype(jnp.float32)
-    middle = values_in + branch.astype(jnp.float32)
-    layer_out = (middle + feed_out.astype(jnp.float32)).astype(low)
-    grad_from_one, gain_grad_one = norm_back(grad_normed_one, unit_one, inverse_one, gain_values[0])
-    input_grad = grad_middle + grad_from_one
-    gain_grads = jnp.concatenate([gain_grad_one[None], gain_grad_two])
-    qkv_reduced = qkv_reduced.astype(jnp.float32)
-    reduced = (
-        qkv_reduced[:, :width],
-        jnp.stack([qkv_reduced[:, width : width + kv_width], qkv_reduced[:, width + kv_width :]]),
-        out_reduced.astype(jnp.float32),
-        jnp.stack([gate_reduced, up_reduced]).astype(jnp.float32),
-        down_reduced.astype(jnp.float32),
-    )
-    local_square = sum((jnp.sum(g * g) for g in reduced))
-    square_total, gains_reduced = reduce_tail(gain_grads, local_square, n, m, 4)
-    reduced = (gains_reduced, *reduced)
     grad_norm = jnp.sqrt(square_total)
     clip_factor = jnp.minimum(1.0, clip_limit / (grad_norm + 1e-06))
     step_float = step_count[0].astype(jnp.float32)

time: 691 us -> 656 us (0.949); the launches traced: 683 us -> 655 us
  local copies, waits for them, and re-layouts: 22.4 us -> 45.8 us
  matrix products: 32 us -> 10.2 us
  other arithmetic: 56.1 us -> 35.9 us
  waiting for transfers between devices: 31.8 us -> 15.1 us
  Pallas kernels: 508 us -> 519 us
    pallas_call x1, Pallas kernels: 21 us -> 229 us  [attention_back(): pl.pallas_call(functools.partial(back_kernel, n, m, chunks, lag, norm_eps...]
    pallas_call x2 -> x1, Pallas kernels: 313 us -> 110 us  [line_reduce(): pl.pallas_call(functools.partial(line_kernel, n, chunks, lag, count), out...]
    dot_general x4 -> x0, matrix products: 21.8 us -> none  [the longest x2 11.3 us: against(): lax.dot_general(left, right, (((1,), (1,)), ((), ())), preferred_element_...]
    unnamed x94 -> x96, local copies, waits for them, and re-layouts: 18.7 us -> 38.8 us
    reduce_scatter x5 -> x1, waiting for transfers between devices: 14.6 us -> 0.01 us  [on_device(): lax.psum_scatter(grad_ff_weight, 'dp', scatter_dimension=0, tiled=True)]
    add x1 -> x0, other arithmetic: 13.8 us -> none  [on_device(): input_grad = grad_middle + grad_from_one]
    reduce_sum x6 -> x2, other arithmetic: 12.7 us -> 5.65 us  [the longest x1 3.48 us: on_device(): jnp.sum(ff_reduced * ff_reduced)]
  transfers between devices with their start and end apart: 9 -> 5, of which waited for: 4 -> 3; matrix products, arithmetic and copies ran while one was open for 11% -> 6% of each run, Pallas kernels for 52% -> 55%
where the time goes in v5:
time: 656 us; the launch traced here: 655 us
  Pallas kernels  519 us (79%)
  local copies, waits for them, and re-layouts  45.8 us (7%)
  other arithmetic  35.9 us (5%)
  between operations  18.8 us (3%)
  waiting for transfers between devices  15.1 us (2%)
  blocking collectives  10.6 us (2%)
  matrix products  10.2 us (2%)
    pallas_call x1, Pallas kernels, attention_back(): pl.pallas_call(functools.partial(back_kernel, n, m, chunks, lag, norm_eps...  229 us
    pallas_call x1, Pallas kernels, feed_forward(): pl.pallas_call(functools.partial(ff_kernel, n, chunks, lag, norm_eps), ou...  142 us
    pallas_call x1, Pallas kernels, line_reduce(): pl.pallas_call(functools.partial(line_kernel, n, chunks, lag, count), out...  110 us
    unnamed x96, local copies, waits for them, and re-layouts  38.8 us
    pallas_call x1, Pallas kernels, reduce_tail(): pl.pallas_call(functools.partial(total_kernel, n, m), out_shape=(jax.Shap...  19.1 us
    pallas_call x1, Pallas kernels, attention_forward(): pl.pallas_call(functools.partial(forward_kernel, size, pairs), out_shape=...  18.9 us
    sub x6, other arithmetic, adam_step(): return (first, second, weight - step_rate * (update + decay_rate * weight))  17.1 us
  transfers between devices with their start and end apart: 5, of which 3 were waited for; matrix products, arithmetic and copies ran while one was open for 6% of the time, Pallas kernels for 55%

profile of v5, /device:TPU:0, one launch (start us, length us, event | category | flops | bytes accessed | tf_op | source)
XLA Modules:
  0.0 655.4 jit_solution(18083010042956176844)
XLA Ops:
  7.2 1.0 copy.89
  8.3 1.2 convert.11
  9.6 0.8 pad_maximum_fusion.2
  10.5 1.8 convert_element_type.44
  12.3 2.3 convert_element_type.47
  14.7 1.2 convert_element_type.46
  16.0 0.5 slice.59
  17.3 0.3 reduce-window.9
  17.7 0.1 slice_reduce_fusion
  18.0 0.2 copy.91.seg_col_ref
  18.2 10.6 %all_gather.15 = bf16[2,2048]{1,0:T(2,128)(2,1)S(1)} all-gather(bf16[2,256]{1,0:T(2,128)(2,1)S(1)} %convert_element_type.40), channel_id=1, replica_groups=mesh['dp'=8,'tensor'=4] {'dp'}, dimensions={1}, use_global_device_ids=true | all-gather | bytes 9216 | tf_op jit(solution)/shard_map/all_gather | solution.py:998
  28.8 1.9 fusion.14
  30.8 0.9 pad_maximum_fusion
  31.7 0.9 fusion
  32.6 0.6 fusion.25
  33.2 10.2 %all-gather.5.cloned.1.call-done.qkv_hbm = bf16[2048,640]{1,0:T(8,128)(2,1)} async-done(((bf16[256,640]{1,0:T(8,128)(2,1)}), bf16[2048,640]{1,0:T(8,128)(2,1)}) %all-gather.5.cloned.1.call-update) | async-done | bytes 2621456 | tf_op jit(solution)/shard_map/all_gather | solution.py:1000
  43.4 6.3 fusion.3.raw_ref
  49.7 18.9 %shard_map.373 = (bf16[1024,512]{1,0:T(8,128)(2,1)S(1)}, bf16[1024,512]{1,0:T(8,128)(2,1)S(1)}, bf16[1024,128]{1,0:T(8,128)(2,1)S(1)}, bf16[1024,128]{1,0:T(8,128)(2,1)S(1)}, f32[4,4,1,512]{3,2,1,0:T(1,128)S(1)}) custom-call(s32[4]{0:T(128)S(1)} %and_select_fusion.first_ref, f32[1024,640]{1,0:T(8,128)S(1)} %fusion.3.raw_ref, ...), custom_call_target="tpu_custom_call" | custom-call | flops 5368709120 | bytes 4194304 | tf_op jit(solution)/shard_map/pallas_call | solution.py:117
  68.6 1.0 copy-done.6
  69.6 0.7 copy-done.8
  70.3 3.9 all-gather.7.cloned.1.call-done.out_w
  74.2 3.9 convolution_convert_fusion.refs_0_
  78.2 110.0 %shard_map.374.branch.branch_hbm = bf16[1024,2048]{1,0:T(8,128)(2,1)S(1)} custom-call(bf16[1024,2048]{1,0:T(8,128)(2,1)S(1)} %convolution_convert_fusion.refs_0_), custom_call_target="tpu_custom_call" | custom-call | flops 4194304 | bytes 251658240 | tf_op jit(solution)/shard_map/pallas_call | solution.py:280
  188.2 2.0 copy-done
  190.2 0.9 all-gather.9.cloned.1.call-done.gu_hbm
  191.1 141.9 %shard_map.375 = (bf16[1024,2048]{1,0:T(8,128)(2,1)}, f32[1024,2048]{1,0:T(8,128)}, bf16[1024,2048]{1,0:T(8,128)(2,1)}, f32[1,2048]{1,0:T(1,128)}, bf16[2048,4224]{1,0:T(8,128)(2,1)}) custom-call(bf16[1024,2048]{1,0:T(8,128)(2,1)} %copy-done, f32[1,2048]{1,0:T(1,128)} %get-tuple-element.140.gain, bf16[1024,2048]{1,0:T(8,128)(2,1)} %x_hbm.1, ...), custom_call_target="tpu_custom_call" | custom-call | flops 53150220288 | bytes 314572800 | tf_op jit(solution)/shard_map/pallas_call | solution.py:490
  333.0 1.3 copy-done.13
  334.3 1.5 copy.105
  335.9 1.0 copy.101
  337.6 3.4 copy.102
  341.0 1.5 copy.103
  342.6 1.0 copy.98
  343.6 1.0 copy.99
  344.6 0.1 copy.93
  344.7 0.9 copy.95
  345.6 229.1 %shard_map.376 = (bf16[1024,2048]{1,0:T(8,128)(2,1)}, f32[1024,2048]{1,0:T(8,128)}, f32[1,2048]{1,0:T(1,128)}, f32[256,1152]{1,0:T(8,128)}) custom-call(bf16[1024,2048]{1,0:T(8,128)(2,1)} %get-tuple-element.38.feed_part, bf16[1024,2048]{1,0:T(8,128)(2,1)} %get-tuple-element.39.grad_low, f32[1,2048]{1,0:T(1,128)} %copy-done.30, bf16[1024,512]{1,0:T(8,128)(2,1)} %copy-done.6, ...), custom_call_target="tpu_custom_call" | custom-call | flops 42949672960 | bytes 545259520 | tf_op jit(solution)/shard_map/pallas_call | solution.py:811
  574.7 2.2 multiply_reduce_fusion.1
  576.8 1.3 pad_maximum_fusion.3
  578.2 1.7 slice_bitcast_fusion.3
  579.9 3.5 multiply_reduce_fusion
  584.7 0.6 broadcast_in_dim.5.square_ref
  585.3 19.1 %shard_map.377 = (f32[8,128]{1,0:T(8,128)}, f32[2,256]{1,0:T(2,128)}) custom-call(f32[8,2,256]{2,1,0:T(2,128)} %bitcast.60, f32[8,128]{1,0:T(8,128)} %broadcast_in_dim.5.square_ref), custom_call_target="tpu_custom_call" | custom-call | tf_op jit(solution)/shard_map/pallas_call | solution.py:913
  604.3 1.2 slice.69
  606.3 0.3 convert_element_type.48
  606.6 1.8 slice_bitcast_fusion.1
  608.4 1.0 copy-done.15
  609.4 0.4 copy-done.16
  609.8 2.2 multiply_subtract_fusion.1
  612.1 2.9 copy.112
  615.0 1.5 copy.113
  616.5 1.5 copy.114
  618.1 2.5 multiply_subtract_fusion.2
  620.5 2.0 copy.109
  622.5 1.0 copy.110
  623.5 1.0 copy.111
  624.5 1.0 multiply_subtract_fusion.4
  625.6 1.9 copy.106
  627.4 1.7 copy.107
  629.2 1.7 copy.108
  630.9 3.1 multiply_subtract_fusion.3
  634.0 0.6 multiply_subtract_fusion.5
  634.6 7.8 %multiply_subtract_fusion = (f32[2,256,1408]{2,1,0:T(8,128)}, f32[2,256,1408]{2,1,0:T(8,128)}, f32[2,256,1408]{2,1,0:T(8,128)}) fusion(f32[2,256,1408]{2,1,0:T(8,128)S(1)} %copy-done.11, f32[]{:T(128)} %bitcast.14, f32[]{:T(128)} %bitcast.13, f32[]{:T(128)} %bitcast.12, f32[1,256,1408]{2,1,0:T(8,128)} %get-tuple-element.135, ...), kind=kLoop, calls=%fused_computation.13 | loop fusion | flops 12255232 | bytes 20185100 | tf_op jit(solution)/shard_map/sub | solution.py:966
  642.4 2.0 copy.118
  644.4 3.4 copy.119
  (94 shorter events, 0.9 us)
Async XLA Ops:
  7.2 36.2 %all-gather.5.cloned.1.call-start = ((), (), s32[]{:S(2)}) async-start(), calls=%async_computation.1 | async-start | bytes 2949120 | tf_op jit(solution)/shard_map/all_gather | solution.py:1000
  8.3 6.4 copy-start.10
  10.4 63.8 %all-gather.7.cloned.1.call-start = ((), (), s32[]{:S(2)}) async-start(), calls=%async_computation.2 | async-start | bytes 2359296 | tf_op jit(solution)/shard_map/all_gather | solution.py:1001
  12.2 177.9 %all-gather.11.cloned.1.call-start = ((), (), s32[]{:S(2)}) async-start(), calls=%async_computation.4 | async-start | bytes 6488064 | tf_op jit(solution)/shard_map/all_gather | solution.py:1003
  14.6 1.4 copy-start.4
  14.6 3.0 copy-start.32
  14.6 176.4 %all-gather.9.cloned.1.call-start = ((), (), s32[]{:S(2)}) async-start(), calls=%async_computation.3 | async-start | bytes 12976128 | tf_op jit(solution)/shard_map/all_gather | solution.py:1002
  16.0 563.9 %reduce-scatter.2.cloned.1.call-start = ((), (), s32[]{:S(2)}) async-start(), calls=%async_computation.5 | async-start | bytes 19464192 | tf_op jit(solution)/shard_map/reduce_scatter | solution.py:1024
  18.2 31.5 %copy-start.3 = (s32[1024,1]{1,0:T(8,128)}, s32[1024,1]{1,0:T(8,128)S(1)}, u32[]{:S(2)}) copy-start(s32[1024,1]{1,0:T(8,128)S(1)} %copy.91.seg_col_ref) | copy-start | bytes 12292
  18.2 13.5 %copy-start.17 = (bf16[1024,2048]{1,0:T(8,128)(2,1)S(1)}, bf16[1024,2048]{1,0:T(8,128)(2,1)}, u32[]{:S(2)}) copy-start(bf16[1024,2048]{1,0:T(8,128)(2,1)} %x_hbm.1) | copy-start | bytes 12582916
  31.6 18.1 %copy-start.1 = (f32[1024,128]{1,0:T(8,128)}, f32[1024,128]{1,0:T(8,128)S(1)}, u32[]{:S(2)}) copy-start(f32[1024,128]{1,0:T(8,128)S(1)} %get-tuple-element.147.cos_ref) | copy-start | bytes 1572868
  31.7 18.1 %copy-start.2 = (f32[1024,128]{1,0:T(8,128)}, f32[1024,128]{1,0:T(8,128)S(1)}, u32[]{:S(2)}) copy-start(f32[1024,128]{1,0:T(8,128)S(1)} %get-tuple-element.148.sin_ref) | copy-start | bytes 1572868
  33.2 16.5 %copy-start.30 = (f32[1,2048]{1,0:T(1,128)}, f32[1,2048]{1,0:T(1,128)S(1)}, u32[]{:S(2)}) copy-start(f32[1,2048]{1,0:T(1,128)S(1)} %get-tuple-element.141.gain) | copy-start | bytes 24580
  68.6 1.0 copy-start.6
  69.6 0.7 copy-start.8
  70.3 7.9 %copy-start.5 = (bf16[1024,512]{1,0:T(8,128)(2,1)}, bf16[1024,512]{1,0:T(8,128)(2,1)S(1)}, u32[]{:S(2)}) copy-start(bf16[1024,512]{1,0:T(8,128)(2,1)S(1)} %get-tuple-element.37.mix_ref) | copy-start | bytes 3145732
  70.3 7.9 %copy-start.7 = (bf16[1024,128]{1,0:T(8,128)(2,1)}, bf16[1024,128]{1,0:T(8,128)(2,1)S(1)}, u32[]{:S(2)}) copy-start(bf16[1024,128]{1,0:T(8,128)(2,1)S(1)} %get-tuple-element.41.k_ref) | copy-start | bytes 786436
  70.3 7.9 %copy-start.9 = (f32[4,4,1,512]{3,2,1,0:T(1,128)}, f32[4,4,1,512]{3,2,1,0:T(1,128)S(1)}, u32[]{:S(2)}) copy-start(f32[4,4,1,512]{3,2,1,0:T(1,128)S(1)} %get-tuple-element.43.lse_ref) | copy-start | bytes 98308
  188.2 2.0 copy-start
  333.0 1.4 copy-start.13
  334.3 1.5 copy-start.19
  335.9 5.2 copy-start.22
  337.6 5.0 copy-start.24
  337.6 6.0 copy-start.25
  341.0 3.5 copy-start.28
  341.0 3.7 copy-start.29
  345.6 231.3 %copy-start.31 = (f32[1,2048]{1,0:T(1,128)S(1)}, f32[1,2048]{1,0:T(1,128)}, u32[]{:S(2)}) copy-start(f32[1,2048]{1,0:T(1,128)} %get-tuple-element.48) | copy-start | bytes 24580
  579.9 26.4 %copy-start.12 = (bf16[256,4224]{1,0:T(8,128)(2,1)S(1)}, bf16[256,4224]{1,0:T(8,128)(2,1)}, u32[]{:S(2)}) copy-start(bf16[256,4224]{1,0:T(8,128)(2,1)} %reduce-scatter.2.cloned.1.call-done) | copy-start | bytes 6488068
  606.6 1.9 copy-start.14
  606.6 2.8 copy-start.15
  606.6 3.3 copy-start.16
  616.5 1.5 copy-start.20
  616.5 1.5 copy-start.21
  618.0 6.5 copy-start.23
  618.0 6.5 copy-start.26
  618.0 6.5 copy-start.27
  625.5 8.4 %copy-start.33 = (f32[2,256]{1,0:T(2,128)S(1)}, f32[2,256]{1,0:T(2,128)}, u32[]{:S(2)}) copy-start(f32[2,256]{1,0:T(2,128)} %param.28) | copy-start | bytes 6148
  625.5 8.4 %copy-start.34 = (f32[2,256]{1,0:T(2,128)S(1)}, f32[2,256]{1,0:T(2,128)}, u32[]{:S(2)}) copy-start(f32[2,256]{1,0:T(2,128)} %param.27) | copy-start | bytes 6148
  625.5 8.4 %copy-start.35 = (f32[2,256]{1,0:T(2,128)S(1)}, f32[2,256]{1,0:T(2,128)}, u32[]{:S(2)}) copy-start(f32[2,256]{1,0:T(2,128)} %get-tuple-element.52) | copy-start | bytes 6148
  625.6 9.0 %copy-start.11 = (f32[2,256,1408]{2,1,0:T(8,128)S(1)}, f32[2,256,1408]{2,1,0:T(8,128)}, u32[]{:S(2)}) copy-start(f32[2,256,1408]{2,1,0:T(8,128)} %param.38) | copy-start | bytes 8650756
  630.9 13.5 %slice-start = ((s8[8388608]{0:T(1024)(128)(4,1)}), s8[4194304]{0:T(1024)(128)(4,1)S(1)}, s32[]{:S(2)}) async-start(s8[8388608]{0:T(1024)(128)(4,1)} %bitcast.58), calls=%async_computation.6 | async-start | bytes 8388608
  634.6 7.8 %copy-start.18 = (bf16[1024,2048]{1,0:T(8,128)(2,1)S(1)}, bf16[1024,2048]{1,0:T(8,128)(2,1)}, u32[]{:S(2)}) copy-start(bf16[1024,2048]{1,0:T(8,128)(2,1)} %get-tuple-element.170) | copy-start | bytes 12582916
  634.6 9.8 %slice-start.1 = ((s8[8388608]{0:T(1024)(128)(4,1)}), s8[4194304]{0:T(1024)(128)(4,1)S(1)}, s32[]{:S(2)}) async-start(s8[8388608]{0:T(1024)(128)(4,1)} %bitcast.58), calls=%async_computation.7 | async-start | bytes 8388608
Sparse Core Ops, SparseCore 0:
  10.5 32.8 all-gather.4
  45.8 28.2 all-gather.6
  76.6 44.3 all-gather.10
  123.3 67.6 all-gather.8
  333.1 118.6 reduce-scatter.1

commit v6 on v5

--- a/solution.py
+++ b/solution.py
@@ -844,10 +844,26 @@
       x, qkv_w, branch, grad_middle)
 
 
-def total_kernel(n, m, gains_ref, square_ref, total_ref, gain_ref, line, got_gains, got_line, got_plane,
-                 send_gains, recv_gains, send_line, recv_line, send_plane, recv_plane):
+def tail_kernel(n, m, rates, kv_width, gains_ref, correct_ref, ff_hbm, head_ref, *refs):
+    count = len(rates)
+    params = refs[:3 * count]
+    norm_ref, outs = refs[3 * count], refs[3 * count + 1:6 * count + 1]
+    (line, got_gains, got_line, got_plane, ff_grad, turned), rest = refs[6 * count + 1:6 * count + 7], refs[6 * count + 7:]
+    held, rest = rest[:3 * count], rest[3 * count:]
+    (send_gains, recv_gains, send_line, recv_line, send_plane, recv_plane, ff_sem, load_sem, save_sem) = rest
     z = lax.axis_index("tensor")
     d = lax.axis_index("dp")
+    share = head_ref.shape[0]
+    q_width = outs[3].shape[1]
+    ff = outs[12].shape[2]
+
+    ff_load = pltpu.make_async_copy(ff_hbm, ff_grad, ff_sem)
+    ff_load.start()
+    loads = [pltpu.make_async_copy(params[k], held[k], load_sem.at[k]) for k in range(3 * count)]
+    saves = [pltpu.make_async_copy(held[k], outs[k], save_sem.at[k]) for k in range(3 * count)]
+    for copy in loads:
+        copy.start()
+
     barrier = pltpu.get_barrier_semaphore()
     for k in range(1, n):
         pl.semaphore_signal(barrier, inc=1, device_id={"tensor": lax.rem(z + k, n)}, device_id_type=MESH)
@@ -871,23 +887,39 @@
             src_ref=line.at[1], dst_ref=got_plane.at[sender], send_sem=send_plane.at[k], recv_sem=recv_plane.at[sender],
             device_id={"dp": lax.rem(d + k, m)}, device_id_type=MESH)
 
-    def summed(ref, count):
+    def summed(ref, number):
         whole = ref[0]
-        for k in range(1, count):
+        for k in range(1, number):
             whole = whole + ref[k]
         return whole
+
+    def squares(value):
+        return jnp.sum(jnp.sum(value * value, axis=0, keepdims=True), axis=1, keepdims=True)
 
     for k in range(1, m):
         gains_to(k, d).start()
     got_gains[d] = gains_ref[d]
+    sub = 32
+
+    def head_rows(r, acc):
+        value = head_ref[pl.ds(pl.multiple_of(r * sub, sub), sub), :]
+        return acc + squares(value)
+
+    local = lax.fori_loop(0, share // sub, head_rows, jnp.zeros((1, 1), jnp.float32))
+    ff_load.wait()
+
+    def ff_rows(r, acc):
+        value = ff_grad[pl.ds(pl.multiple_of(r * sub, sub), sub), :].astype(jnp.float32)
+        return acc + squares(value)
+
+    local = lax.fori_loop(0, share // sub, ff_rows, local)
     for k in range(1, m):
         gains_to(k, d).wait_send()
         gains_to(k, lax.rem(d + m - k, m)).wait_recv()
     gains = summed(got_gains, m)
-    gain_ref[...] = gains
-    own = jnp.sum(jnp.sum(gains * gains, axis=1, keepdims=True), axis=0, keepdims=True)
-    own = jnp.where(z == 0, own, jnp.zeros_like(own))
-    line[0] = square_ref[...] + jnp.broadcast_to(own, square_ref.shape)
+    own = squares(gains)
+    local = local + jnp.where(z == 0, own, jnp.zeros_like(own))
+    line[0] = jnp.broadcast_to(local, (8, 128))
     for k in range(1, n):
         along_line(k, z).start()
     got_line[z] = line[0]
@@ -901,30 +933,104 @@
     for k in range(1, m):
         over_plane(k, d).wait_send()
         over_plane(k, lax.rem(d + m - k, m)).wait_recv()
-    total_ref[...] = summed(got_plane, m)
-
-
-def reduce_tail(gains, square, n, m, cid):
+    norm = jnp.sqrt(summed(got_plane, m))
+    norm_ref[...] = norm
+    factor = jnp.minimum(1.0, clip_limit / (norm[:1, :1] + 1e-06))
+    one, two = correct_ref[0], correct_ref[1]
+
+    def update(which, where, gradient):
+        rate, decay = rates[which]
+        p, a, b = (held[3 * which + k] for k in range(3))
+        gradient = gradient * factor
+        first = beta_first * a[where] + (1.0 - beta_first) * gradient
+        second = beta_second * b[where] + (1.0 - beta_second) * gradient * gradient
+        a[where] = first
+        b[where] = second
+        change = first / one / (jnp.sqrt(second / two) + adam_eps)
+        old = p[where]
+        p[where] = old - rate * (change + decay * old)
+
+    def load(which):
+        for k in range(3):
+            loads[3 * which + k].wait()
+
+    def save(which):
+        for k in range(3):
+            saves[3 * which + k].start()
+
+    def by_rows(which, body):
+        load(which)
+        lax.fori_loop(0, share // sub, lambda r, c: (body(pl.ds(pl.multiple_of(r * sub, sub), sub)), c)[1], 0)
+        save(which)
+
+    def gateup_rows(where):
+        for t in (0, 1):
+            update(4, (t, where, slice(None)), ff_grad[where, t * ff:(t + 1) * ff].astype(jnp.float32))
+
+    by_rows(4, gateup_rows)
+    load(5)
+
+    def down_tile(t, carry):
+        at = pl.ds(pl.multiple_of(t * 128, 128), 128)
+        source = pl.ds(pl.multiple_of(2 * ff + t * 128, 128), 128)
+        update(5, (at, slice(None)), ff_grad[:, source].astype(jnp.float32).T)
+        return carry
+
+    lax.fori_loop(0, ff // 128, down_tile, 0)
+    save(5)
+    by_rows(1, lambda where: update(1, (where, slice(None)), head_ref[where, :q_width]))
+    load(3)
+
+    def out_tile(t, carry):
+        at = pl.ds(pl.multiple_of(t * 128, 128), 128)
+        source = pl.ds(pl.multiple_of(q_width + 2 * kv_width + t * 128, 128), 128)
+        update(3, (at, slice(None)), head_ref[:, source].T)
+        return carry
+
+    lax.fori_loop(0, outs[9].shape[0] // 128, out_tile, 0)
+    save(3)
+
+    def keyval_rows(where):
+        both = head_ref[where, q_width:q_width + 2 * kv_width]
+        for t in (0, 1):
+            update(2, (t, where, slice(None)), both[:, t * kv_width:(t + 1) * kv_width])
+
+    by_rows(2, keyval_rows)
+    load(0)
+    update(0, (slice(None), slice(None)), gains)
+    save(0)
+    for copy in saves:
+        copy.wait()
+
+
+def finish_step(gains, correct, ff_grad, head_grad, params, rates, kv_width, n, m, cid):
     share = gains.shape[1] // m
     parts = gains.reshape(2, m, share).transpose(1, 0, 2)
-    tile = jnp.broadcast_to(square.reshape(1, 1), (8, 128))
     vmem = pl.BlockSpec(memory_space=pltpu.VMEM)
+    hbm = pl.BlockSpec(memory_space=pl.ANY)
     dma = pltpu.SemaphoreType.DMA
-    total, gain = pl.pallas_call(
-        functools.partial(total_kernel, n, m),
-        out_shape=(jax.ShapeDtypeStruct((8, 128), jnp.float32), jax.ShapeDtypeStruct((2, share), jnp.float32)),
-        in_specs=[vmem, vmem],
-        out_specs=(vmem, vmem),
+    shapes = [jax.ShapeDtypeStruct(p.shape, jnp.float32) for p in params]
+    size = sum(p.size for p in params)
+    norm, *outs = pl.pallas_call(
+        functools.partial(tail_kernel, n, m, rates, kv_width),
+        out_shape=(jax.ShapeDtypeStruct((8, 128), jnp.float32), *shapes),
+        in_specs=[vmem, pl.BlockSpec(memory_space=pltpu.SMEM), hbm, vmem] + [hbm] * len(params),
+        out_specs=(vmem,) + (hbm,) * len(params),
         scratch_shapes=[
             pltpu.VMEM((2, 8, 128), jnp.float32),
             pltpu.VMEM((m, 2, share), jnp.float32),
             pltpu.VMEM((n, 8, 128), jnp.float32),
             pltpu.VMEM((m, 8, 128), jnp.float32),
-            dma((m,)), dma((m,)), dma((n,)), dma((n,)), dma((m,)), dma((m,)),
+            pltpu.VMEM(ff_grad.shape, ff_grad.dtype),
+            pltpu.VMEM((8, 128), jnp.float32),
+        ] + [pltpu.VMEM(p.shape, jnp.float32) for p in params] + [
+            dma((m,)), dma((m,)), dma((n,)), dma((n,)), dma((m,)), dma((m,)), dma,
+            dma((len(params),)), dma((len(params),)),
         ],
-        compiler_params=pltpu.CompilerParams(collective_id=cid, has_side_effects=True),
-    )(parts, tile)
-    return total[0, 0], gain
+        compiler_params=pltpu.CompilerParams(collective_id=cid, has_side_effects=True, vmem_limit_bytes=60 << 20),
+        cost_estimate=pl.CostEstimate(flops=20 * size, bytes_accessed=8 * size, transcendentals=size),
+    )(parts, correct, ff_grad, head_grad, *params)
+    return norm, outs
 
 
 norm_eps = 1e-05
@@ -954,16 +1060,6 @@
         jnp.concatenate([cosines] * 4, axis=-1),
         jnp.concatenate([-sines, sines, -sines, sines], axis=-1),
     )
-
-
-def adam_step(weight, first, second, gradient, clip_factor, step_float, step_rate, decay_rate):
-    gradient = gradient * clip_factor
-    first = beta_first * first + (1.0 - beta_first) * gradient
-    second = beta_second * second + (1.0 - beta_second) * gradient * gradient
-    correct_one = 1.0 - jnp.power(beta_first, step_float)
-    correct_two = 1.0 - jnp.power(beta_second, step_float)
-    update = first / correct_one / (jnp.sqrt(second / correct_two) + adam_eps)
-    return (first, second, weight - step_rate * (update + decay_rate * weight))
 
 
 def on_device(
@@ -1027,49 +1123,32 @@
         out_weight, tokens, qkv_weight, branch, grad_middle, n, m, 3, size
     )
     gain_grads = jnp.concatenate([gain_grad_one, gain_grad_two])
-    ff_reduced = ff_reduced.astype(jnp.float32)
-    ff = w_down.shape[0]
-    wide = width + 2 * kv_width
-    local_square = jnp.sum(head_reduced * head_reduced) + jnp.sum(ff_reduced * ff_reduced)
-    square_total, gains_reduced = reduce_tail(gain_grads, local_square, n, m, 4)
-    reduced = (
-        gains_reduced,
-        head_reduced[:, :width],
-        jnp.stack([head_reduced[:, width : width + kv_width], head_reduced[:, width + kv_width : wide]]),
-        head_reduced[:, wide:].T,
-        jnp.stack([ff_reduced[:, :ff], ff_reduced[:, ff : 2 * ff]]),
-        ff_reduced[:, 2 * ff :].T,
+    step_float = step_count[0].astype(jnp.float32)
+    correct = jnp.stack([1.0 - jnp.power(beta_first, step_float), 1.0 - jnp.power(beta_second, step_float)])
+    params = (
+        (norm_gains, gains_first, gains_second),
+        (w_query, query_first, query_second),
+        (w_keyval, keyval_first, keyval_second),
+        (w_out, out_first, out_second),
+        (w_gateup, gateup_first, gateup_second),
+        (w_down, down_first, down_second),
     )
-    grad_norm = jnp.sqrt(square_total)
-    clip_factor = jnp.minimum(1.0, clip_limit / (grad_norm + 1e-06))
-    step_float = step_count[0].astype(jnp.float32)
-    params = (norm_gains, w_query, w_keyval, w_out, w_gateup, w_down)
-    states = (
-        (gains_first, gains_second),
-        (query_first, query_second),
-        (keyval_first, keyval_second),
-        (out_first, out_second),
-        (gateup_first, gateup_second),
-        (down_first, down_second),
+    rates = (
+        (gain_rate, 0.0),
+        (weight_rate, weight_decay),
+        (weight_rate, weight_decay),
+        (out_rate, weight_decay),
+        (weight_rate, weight_decay),
+        (weight_rate, weight_decay),
     )
-    step_rates = (gain_rate, weight_rate, weight_rate, out_rate, weight_rate, weight_rate)
-    decay_rates = (0.0, weight_decay, weight_decay, weight_decay, weight_decay, weight_decay)
+    norm, updated = finish_step(
+        gain_grads, correct, ff_reduced, head_reduced, [a for group in params for a in group], rates, kv_width, n, m, 4
+    )
     results = []
-    for position_index in range(6):
-        one, two = states[position_index]
-        results.extend(
-            adam_step(
-                params[position_index],
-                one,
-                two,
-                reduced[position_index],
-                clip_factor,
-                step_float,
-                step_rates[position_index],
-                decay_rates[position_index],
-            )
-        )
-    return (layer_out, input_grad, grad_norm.reshape(1), *results)
+    for k in range(len(params)):
+        weight, first_state, second_state = updated[3 * k : 3 * k + 3]
+        results += [first_state, second_state, weight]
+    return (layer_out, input_grad, norm[0, :1], *results)
 
 
 def solution(mesh):

time: 656 us -> 638 us (0.973)
  other arithmetic: 35.9 us -> 13.4 us
  Pallas kernels: 519 us -> 532 us
    sub x6 -> x0, other arithmetic: 17.1 us -> none  [adam_step(): return (first, second, weight - step_rate * (update + decay_rate * weight))]
    pallas_call x1, Pallas kernels: 19.1 us -> 30.8 us  [finish_step(): pl.pallas_call(functools.partial(tail_kernel, n, m, rates, kv_width), out...]
    unnamed x96 -> x91, local copies, waits for them, and re-layouts: 38.8 us -> 40 us
  transfers between devices with their start and end apart: 5 -> 5, of which waited for: 3 -> 2; matrix products, arithmetic and copies ran while one was open for 6% -> 4% of each run, Pallas kernels for 55% -> 56%
where the time goes in v6:
time: 638 us; the launch traced here: 637 us
  Pallas kernels  532 us (83%)
  local copies, waits for them, and re-layouts  42.8 us (7%)
  between operations  15.6 us (2%)
  other arithmetic  13.4 us (2%)
  waiting for transfers between devices  11.1 us (2%)
  matrix products  10.7 us (2%)
  blocking collectives  10.6 us (2%)
    pallas_call x1, Pallas kernels, attention_back(): pl.pallas_call(functools.partial(back_kernel, n, m, chunks, lag, norm_eps...  227 us
    pallas_call x1, Pallas kernels, feed_forward(): pl.pallas_call(functools.partial(ff_kernel, n, chunks, lag, norm_eps), ou...  142 us
    pallas_call x1, Pallas kernels, line_reduce(): pl.pallas_call(functools.partial(line_kernel, n, chunks, lag, count), out...  107 us
    unnamed x91, local copies, waits for them, and re-layouts  40 us
    pallas_call x1, Pallas kernels, finish_step(): pl.pallas_call(functools.partial(tail_kernel, n, m, rates, kv_width), out...  30.8 us
    pallas_call x1, Pallas kernels, attention_forward(): pl.pallas_call(functools.partial(forward_kernel, size, pairs), out_shape=...  25 us
  transfers between devices with their start and end apart: 5, of which 2 were waited for; matrix products, arithmetic and copies ran while one was open for 4% of the time, Pallas kernels for 56%

profile of v6, /device:TPU:0, one launch (start us, length us, event | category | flops | bytes accessed | tf_op | source)
XLA Modules:
  0.0 636.9 jit_solution(14265624057274104245)
XLA Ops:
  7.2 1.0 copy.59.refs_6_
  8.3 1.2 convert.11
  9.6 0.8 pad_maximum_fusion.2
  10.5 1.8 convert_element_type.41
  12.3 0.0 all-gather.11.cloned.1.call-start
  12.3 2.3 convert_element_type.44
  14.7 0.0 all-gather.9.cloned.1.call-start
  14.7 1.2 convert_element_type.43
  16.1 0.5 slice.38
  17.2 0.1 add_select_fusion
  17.3 0.3 reduce-window.9
  17.6 0.1 slice.41
  17.7 0.1 slice_reduce_fusion
  17.8 0.1 fusion.9
  17.9 0.1 slice.43
  18.0 0.2 copy.61.seg_col_ref
  18.2 10.6 %all_gather.15 = bf16[2,2048]{1,0:T(2,128)(2,1)S(1)} all-gather(bf16[2,256]{1,0:T(2,128)(2,1)S(1)} %convert_element_type.37), channel_id=1, replica_groups=mesh['dp'=8,'tensor'=4] {'dp'}, dimensions={1}, use_global_device_ids=true | all-gather | bytes 9216 | tf_op jit(solution)/shard_map/all_gather | solution.py:1094
  28.9 1.9 fusion.7
  30.8 0.9 pad_maximum_fusion
  31.7 0.9 fusion
  32.6 0.6 fusion.10
  33.2 10.2 %all-gather.5.cloned.1.call-done.qkv_hbm = bf16[2048,640]{1,0:T(8,128)(2,1)} async-done(((bf16[256,640]{1,0:T(8,128)(2,1)}), bf16[2048,640]{1,0:T(8,128)(2,1)}) %all-gather.5.cloned.1.call-update) | async-done | bytes 2621456 | tf_op jit(solution)/shard_map/all_gather | solution.py:1096
  43.4 6.3 fusion.3.raw_ref
  49.7 25.0 %shard_map.373 = (bf16[1024,512]{1,0:T(8,128)(2,1)S(1)}, bf16[1024,512]{1,0:T(8,128)(2,1)S(1)}, bf16[1024,128]{1,0:T(8,128)(2,1)S(1)}, bf16[1024,128]{1,0:T(8,128)(2,1)S(1)}, f32[4,4,1,512]{3,2,1,0:T(1,128)S(1)}) custom-call(s32[4]{0:T(128)S(1)} %and_select_fusion.first_ref, f32[1024,640]{1,0:T(8,128)S(1)} %fusion.3.raw_ref, ...), custom_call_target="tpu_custom_call" | custom-call | flops 5368709120 | bytes 4194304 | tf_op jit(solution)/shard_map/pallas_call | solution.py:117
  74.7 1.0 copy-done.6
  75.7 0.7 copy-done.8
  76.4 4.4 convolution_convert_fusion.refs_0_
  80.8 107.4 %shard_map.374.branch.branch_hbm = bf16[1024,2048]{1,0:T(8,128)(2,1)S(1)} custom-call(bf16[1024,2048]{1,0:T(8,128)(2,1)S(1)} %convolution_convert_fusion.refs_0_), custom_call_target="tpu_custom_call" | custom-call | flops 4194304 | bytes 251658240 | tf_op jit(solution)/shard_map/pallas_call | solution.py:280
  188.2 2.0 copy-done
  190.2 0.9 all-gather.9.cloned.1.call-done.gu_hbm
  191.1 141.9 %shard_map.375 = (bf16[1024,2048]{1,0:T(8,128)(2,1)}, f32[1024,2048]{1,0:T(8,128)}, bf16[1024,2048]{1,0:T(8,128)(2,1)}, f32[1,2048]{1,0:T(1,128)}, bf16[2048,4224]{1,0:T(8,128)(2,1)}) custom-call(bf16[1024,2048]{1,0:T(8,128)(2,1)} %copy-done, f32[1,2048]{1,0:T(1,128)} %get-tuple-element.152.gain, bf16[1024,2048]{1,0:T(8,128)(2,1)} %x_hbm.1, ...), custom_call_target="tpu_custom_call" | custom-call | flops 53150220288 | bytes 314572800 | tf_op jit(solution)/shard_map/pallas_call | solution.py:490
  333.8 0.1 copy-done.26
  333.9 0.8 copy.64.refs_7_
  334.7 0.8 copy.65.refs_8_
  335.6 0.6 pad_maximum_fusion.4.correct_ref
  336.2 227.3 %shard_map.376 = (bf16[1024,2048]{1,0:T(8,128)(2,1)}, f32[1024,2048]{1,0:T(8,128)}, f32[1,2048]{1,0:T(1,128)}, f32[256,1152]{1,0:T(8,128)}) custom-call(bf16[1024,2048]{1,0:T(8,128)(2,1)} %get-tuple-element.55.feed_part, bf16[1024,2048]{1,0:T(8,128)(2,1)} %get-tuple-element.56.grad_low, f32[1,2048]{1,0:T(1,128)} %copy-done.29, bf16[1024,512]{1,0:T(8,128)(2,1)} %copy-done.6, ...), custom_call_target="tpu_custom_call" | custom-call | flops 42949672960 | bytes 545259520 | tf_op jit(solution)/shard_map/pallas_call | solution.py:811
  563.5 1.3 pad_maximum_fusion.3
  564.9 30.8 %shard_map.377 = (f32[8,128]{1,0:T(8,128)}, f32[2,256]{1,0:T(2,128)}, f32[2,256]{1,0:T(2,128)}, f32[2,256]{1,0:T(2,128)}, f32[256,512]{1,0:T(8,128)}, /*index=5*...) custom-call(f32[8,2,256]{2,1,0:T(2,128)} %bitcast.32, ...), custom_call_target="tpu_custom_call" | custom-call | flops 82606080 | bytes 33042432 | tf_op jit(solution)/shard_map/pallas_call | solution.py:1014
  595.7 1.7 copy.66
  597.4 1.7 copy.67
  599.1 1.7 copy.68
  600.8 1.2 slice.48
  602.0 5.1 copy.87
  607.1 1.1 copy-done.11
  608.2 3.4 copy.88
  611.6 0.6 copy.89
  612.2 0.6 copy.90
  612.8 0.6 copy.91
  613.4 0.8 copy.92
  614.2 0.8 copy.93
  615.0 0.8 copy.94
  615.7 0.8 copy.95
  616.5 0.8 copy.96
  617.3 0.8 copy.97
  618.1 1.6 copy.98
  619.7 1.3 copy-done.14
  621.0 1.6 copy.99
  622.6 1.3 copy-done.13
  623.9 1.6 copy.100
  625.4 0.8 copy-done.19
  626.3 1.1 copy.101
  627.4 0.8 copy-done.18
  628.1 1.1 copy.102
  629.2 1.1 copy.103
  (77 shorter events, 0.4 us)
Async XLA Ops:
  7.2 36.2 %all-gather.5.cloned.1.call-start = ((), (), s32[]{:S(2)}) async-start(), calls=%async_computation.1 | async-start | bytes 2949120 | tf_op jit(solution)/shard_map/all_gather | solution.py:1096
  8.3 6.4 copy-start.16
  8.3 6.4 %copy-start.10 = (f32[2,256,1408]{2,1,0:T(8,128)S(1)}, f32[2,256,1408]{2,1,0:T(8,128)}, u32[]{:S(2)}) copy-start(f32[2,256,1408]{2,1,0:T(8,128)} %refs_12_.1) | copy-start | bytes 8650756
  10.4 66.0 %all-gather.7.cloned.1.call-start = ((), (), s32[]{:S(2)}) async-start(), calls=%async_computation.2 | async-start | bytes 2359296 | tf_op jit(solution)/shard_map/all_gather | solution.py:1097
  12.3 178.0 %all-gather.11.cloned.1.call-start = ((), (), s32[]{:S(2)}) async-start(), calls=%async_computation.4 | async-start | bytes 6488064 | tf_op jit(solution)/shard_map/all_gather | solution.py:1099
  14.6 1.4 copy-start.4
  14.6 3.0 copy-start.28
  14.7 176.5 %all-gather.9.cloned.1.call-start = ((), (), s32[]{:S(2)}) async-start(), calls=%async_computation.3 | async-start | bytes 12976128 | tf_op jit(solution)/shard_map/all_gather | solution.py:1098
  16.0 548.9 %reduce-scatter.2.cloned.1.call-start = ((), (), s32[]{:S(2)}) async-start(), calls=%async_computation.5 | async-start | bytes 19464192 | tf_op jit(solution)/shard_map/reduce_scatter | solution.py:1120
  18.2 31.5 %copy-start.3 = (s32[1024,1]{1,0:T(8,128)}, s32[1024,1]{1,0:T(8,128)S(1)}, u32[]{:S(2)}) copy-start(s32[1024,1]{1,0:T(8,128)S(1)} %copy.61.seg_col_ref) | copy-start | bytes 12292
  18.2 13.5 %copy-start.12 = (bf16[1024,2048]{1,0:T(8,128)(2,1)S(1)}, bf16[1024,2048]{1,0:T(8,128)(2,1)}, u32[]{:S(2)}) copy-start(bf16[1024,2048]{1,0:T(8,128)(2,1)} %x_hbm.1) | copy-start | bytes 12582916
  31.7 18.1 %copy-start.1 = (f32[1024,128]{1,0:T(8,128)}, f32[1024,128]{1,0:T(8,128)S(1)}, u32[]{:S(2)}) copy-start(f32[1024,128]{1,0:T(8,128)S(1)} %get-tuple-element.159.cos_ref) | copy-start | bytes 1572868
  31.7 18.1 %copy-start.2 = (f32[1024,128]{1,0:T(8,128)}, f32[1024,128]{1,0:T(8,128)S(1)}, u32[]{:S(2)}) copy-start(f32[1024,128]{1,0:T(8,128)S(1)} %get-tuple-element.160.sin_ref) | copy-start | bytes 1572868
  33.2 16.5 %copy-start.29 = (f32[1,2048]{1,0:T(1,128)}, f32[1,2048]{1,0:T(1,128)S(1)}, u32[]{:S(2)}) copy-start(f32[1,2048]{1,0:T(1,128)S(1)} %get-tuple-element.153.gain) | copy-start | bytes 24580
  74.7 1.0 copy-start.6
  75.7 0.7 copy-start.8
  76.4 4.4 copy-start.5
  76.4 4.4 copy-start.7
  76.4 4.5 copy-start.9
  188.2 2.0 copy-start
  333.0 0.9 copy-start.26
  333.0 1.7 copy-start.27
  336.2 227.4 %copy-start.30 = (f32[1,2048]{1,0:T(1,128)S(1)}, f32[1,2048]{1,0:T(1,128)}, u32[]{:S(2)}) copy-start(f32[1,2048]{1,0:T(1,128)} %get-tuple-element.65) | copy-start | bytes 24580
  602.0 6.2 copy-start.11
  608.2 3.4 copy-start.33
  608.2 4.0 copy-start.32
  608.2 4.6 copy-start.31
  608.2 5.2 copy-start.25
  608.2 6.0 copy-start.24
  608.2 6.8 %copy-start.23 = (f32[256,512]{1,0:T(8,128)S(1)}, f32[256,512]{1,0:T(8,128)}, u32[]{:S(2)}) copy-start(f32[256,512]{1,0:T(8,128)} %get-tuple-element.190) | copy-start | bytes 1572868
  611.6 4.1 copy-start.22
  611.6 4.9 copy-start.21
  611.6 5.7 copy-start.20
  614.2 4.0 copy-start.15
  618.1 2.9 copy-start.14
  621.0 2.9 copy-start.13
  623.9 2.4 copy-start.19
  626.3 1.9 copy-start.18
  626.3 3.0 copy-start.17
Sparse Core Ops, SparseCore 0:
  10.5 32.8 all-gather.4
  45.9 28.3 all-gather.6
  76.7 44.3 all-gather.10
  123.4 67.6 all-gather.8
  333.2 147.2 reduce-scatter.1

commit v7 on v6

--- a/solution.py
+++ b/solution.py
@@ -42,98 +42,6 @@
 def stack_pair(pair, low_lanes):
     zero = jnp.zeros_like(pair)
     return jnp.concatenate([jnp.where(low_lanes, pair, zero), jnp.where(low_lanes, zero, pair)], axis=0)
-
-
-def forward_kernel(size, pairs, first_ref, raw_ref, cos_ref, sin_ref, seg_col_ref, seg_row_ref,
-                   mix_ref, q_ref, k_ref, v_ref, lse_ref, bias, scores, v_turned):
-    length = raw_ref.shape[0]
-    low_lanes, first_half = lane_tests(size)
-    low_rows = lax.broadcasted_iota(jnp.int32, (128, size), 0) < 64
-    width = pairs * 128
-
-    def prepare(i, carry):
-        rows = pl.ds(pl.multiple_of(i * size, size), size)
-        cosines, sines = cos_ref[rows, :], sin_ref[rows, :]
-        for hp in range(pairs):
-            values = raw_ref[rows, hp * 128:(hp + 1) * 128]
-            turned = values * cosines + swap_halves(values, first_half) * sines
-            q_ref[rows, hp * 128:(hp + 1) * 128] = (turned.astype(jnp.bfloat16).astype(jnp.float32) * 0.125).astype(jnp.bfloat16)
-        both = raw_ref[rows, width:width + 128]
-        other = pltpu.roll(both, 64, 1)
-        keys = jnp.where(low_lanes, both, other)
-        k_ref[rows, :] = (keys * cosines + swap_halves(keys, first_half) * sines).astype(jnp.bfloat16)
-        values = jnp.where(low_lanes, other, both)
-        v_ref[rows, :] = values.astype(jnp.bfloat16)
-        v_turned[i] = values.T.astype(jnp.bfloat16)
-        return carry
-
-    lax.fori_loop(0, length // size, prepare, 0)
-
-    def row_block(i, carry):
-        rows = pl.ds(pl.multiple_of(i * size, size), size)
-        begin = first_ref[i]
-
-        def fill(j, c):
-            bias[j] = block_bias(seg_col_ref, seg_row_ref, i, j, size)
-            return c
-
-        lax.fori_loop(begin, i + 1, fill, 0)
-
-        for hp in range(pairs):
-            stacked = stack_pair(q_ref[rows, hp * 128:(hp + 1) * 128], low_lanes)
-
-            def score(j, top):
-                keys = k_ref[pl.ds(pl.multiple_of(j * size, size), size), :]
-                b = bias[j]
-                s = dot_t(keys, stacked) + jnp.concatenate([b, b], axis=1)
-                scores[j] = s
-                return jnp.maximum(top, jnp.max(s, axis=0, keepdims=True))
-
-            top = lax.fori_loop(begin, i + 1, score, jnp.full((1, 2 * size), -jnp.inf, jnp.float32))
-
-            def mix(j, c):
-                total, acc = c
-                p = jnp.exp(scores[j] - top)
-                total = total + jnp.sum(p, axis=0, keepdims=True)
-                return total, acc + dot_n(v_turned[j], p.astype(jnp.bfloat16))
-
-            total, acc = lax.fori_loop(begin, i + 1, mix, (
-                jnp.zeros((1, 2 * size), jnp.float32), jnp.zeros((128, 2 * size), jnp.float32)))
-            lse_ref[i, hp] = top + jnp.log(total)
-            acc = acc / total
-            acc = jnp.where(low_rows, acc[:, :size], acc[:, size:])
-            mix_ref[rows, hp * 128:(hp + 1) * 128] = acc.T.astype(jnp.bfloat16)
-        return carry
-
-    lax.fori_loop(0, length // size, row_block, 0)
-
-
-def attention_forward(raw, cosines, sines, seg_col, seg_row, first, size):
-    length, wide = raw.shape
-    width = wide - 128
-    pairs = width // 128
-    blocks = length // size
-    vmem = pl.BlockSpec(memory_space=pltpu.VMEM)
-    return pl.pallas_call(
-        functools.partial(forward_kernel, size, pairs),
-        out_shape=(
-            jax.ShapeDtypeStruct((length, width), jnp.bfloat16),
-            jax.ShapeDtypeStruct((length, width), jnp.bfloat16),
-            jax.ShapeDtypeStruct((length, 128), jnp.bfloat16),
-            jax.ShapeDtypeStruct((length, 128), jnp.bfloat16),
-            jax.ShapeDtypeStruct((blocks, pairs, 1, 2 * size), jnp.float32),
-        ),
-        in_specs=[pl.BlockSpec(memory_space=pltpu.SMEM)] + [vmem] * 5,
-        out_specs=(vmem,) * 5,
-        scratch_shapes=[
-            pltpu.VMEM((blocks, size, size), jnp.float32),
-            pltpu.VMEM((blocks, size, 2 * size), jnp.float32),
-            pltpu.VMEM((blocks, 128, size), jnp.bfloat16),
-        ],
-        compiler_params=pltpu.CompilerParams(vmem_limit_bytes=40 << 20),
-        cost_estimate=pl.CostEstimate(flops=10 * length * length * width, bytes_accessed=8 * length * width,
-                                      transcendentals=length * length * pairs),
-    )(first, raw, cosines, sines, seg_col, seg_row)
 
 
 class Line:
@@ -516,6 +424,242 @@
     )(branch, gain, x, cot, gateup_w, down_w)
 
 
+def head_kernel(n, m, chunks, lag, eps, size, pairs,
+                x, gain_part, qkv_shard, out_shard, cos_ref, sin_ref, seg_col_ref, seg_row_ref,
+                branch, mix_ref, q_ref, k_ref, v_ref, lse_ref, qkv_w, out_w, gain,
+                got, sa, ra, sg, rg, part, normed, raw, bias, scores, v_turned, got_gain,
+                send_gain, recv_gain, send_direct, send_forward, recv_w):
+    rows, width = x.shape
+    q_width = pairs * 128
+    z = lax.axis_index("tensor")
+    dp = lax.axis_index("dp")
+    share = width // m
+    chips = m // 2
+    chip, core = dp // 2, dp % 2
+    rc = rows // (2 * chunks)
+    per = size // (2 * rc)
+    hb = size // 2
+    blocks = rows // size
+    tile = 256
+    wide = width // tile
+    low_lanes, first_half = lane_tests(size)
+    low_rows = lax.broadcasted_iota(jnp.int32, (128, size), 0) < 64
+    shards, wholes = (qkv_shard, out_shard), (qkv_w, out_w)
+
+    def ascending(stream, c):
+        b = c // per
+        return b * size + stream * hb + (c - b * per) * rc
+
+    line = Line(n, chunks, rc, lag, part, got, branch, (sa, ra, sg, rg), ascending)
+
+    def shard_rows(s):
+        return pl.ds(pl.multiple_of(s * share, share), share)
+
+    def direct(kind, k):
+        peer = 2 * lax.rem(chip + k, chips) + core
+        return pltpu.make_async_remote_copy(
+            src_ref=shards[kind], dst_ref=wholes[kind].at[shard_rows(dp)], send_sem=send_direct.at[kind, k],
+            recv_sem=recv_w.at[kind, dp], device_id={"dp": peer}, device_id_type=MESH)
+
+    def forward(kind, c, side):
+        shard = 2 * c + side
+        where = shard_rows(shard)
+        return pltpu.make_async_remote_copy(
+            src_ref=wholes[kind].at[where], dst_ref=wholes[kind].at[where], send_sem=send_forward.at[kind, c],
+            recv_sem=recv_w.at[kind, shard], device_id={"dp": 2 * chip + 1 - core}, device_id_type=MESH)
+
+    def send_gains(k, sender):
+        return pltpu.make_async_remote_copy(
+            src_ref=gain_part, dst_ref=got_gain.at[sender], send_sem=send_gain.at[k], recv_sem=recv_gain.at[sender],
+            device_id={"dp": lax.rem(dp + k, m)}, device_id_type=MESH)
+
+    barrier = pltpu.get_barrier_semaphore()
+
+    @pl.when(z > 0)
+    def _():
+        pl.semaphore_signal(barrier, inc=1, device_id={"tensor": z - 1}, device_id_type=MESH)
+
+    @pl.when(z < n - 1)
+    def _():
+        pl.semaphore_signal(barrier, inc=1, device_id={"tensor": z + 1}, device_id_type=MESH)
+
+    for k in range(1, m):
+        pl.semaphore_signal(barrier, inc=1, device_id={"dp": lax.rem(dp + k, m)}, device_id_type=MESH)
+
+    for kind in (0, 1):
+        wholes[kind][shard_rows(dp), :] = shards[kind][...]
+    got_gain[dp] = gain_part[...]
+
+    @pl.when((z > 0) & (z < n - 1))
+    def _():
+        pl.semaphore_wait(barrier, m + 1)
+
+    @pl.when((z == 0) | (z == n - 1))
+    def _():
+        pl.semaphore_wait(barrier, m)
+
+    for k in range(1, m):
+        send_gains(k, dp).start()
+    for kind in (0, 1):
+        for k in range(1, chips):
+            direct(kind, k).start()
+        forward(kind, chip, core).start()
+    for k in range(1, m):
+        send_gains(k, lax.rem(dp + m - k, m)).wait_recv()
+    whole = got_gain[0]
+    for k in range(1, m):
+        whole = whole + got_gain[k]
+    gain[...] = whole.astype(jnp.bfloat16).astype(jnp.float32)
+
+    def norm_rows(r, carry):
+        where = pl.ds(pl.multiple_of(r * rc, rc), rc)
+        values = x[where, :].astype(jnp.float32)
+        inverse = lax.rsqrt(jnp.mean(values * values, axis=-1, keepdims=True) + eps)
+        normed[where, :] = (values * inverse * gain[0:1, :]).astype(jnp.bfloat16)
+        return carry
+
+    lax.fori_loop(0, rows // rc, norm_rows, 0)
+
+    def gather(kind):
+        for k in range(1, chips):
+            c = lax.rem(chip + chips - k, chips)
+            forward(kind, c, core).wait_recv()
+            forward(kind, c, core).start()
+        for c in range(chips):
+            forward(kind, c, 1 - core).wait_recv()
+
+    gather(0)
+
+    def prepare(i, carry):
+        where = pl.ds(pl.multiple_of(i * size, size), size)
+        raw[...] = dot_n(normed[where, :], qkv_w[...])
+        cosines, sines = cos_ref[where, :], sin_ref[where, :]
+        for hp in range(pairs):
+            values = raw[:, hp * 128:(hp + 1) * 128]
+            turned = values * cosines + swap_halves(values, first_half) * sines
+            q_ref[where, hp * 128:(hp + 1) * 128] = (
+                turned.astype(jnp.bfloat16).astype(jnp.float32) * 0.125).astype(jnp.bfloat16)
+        both = raw[:, q_width:q_width + 128]
+        other = pltpu.roll(both, 64, 1)
+        keys = jnp.where(low_lanes, both, other)
+        k_ref[where, :] = (keys * cosines + swap_halves(keys, first_half) * sines).astype(jnp.bfloat16)
+        values = jnp.where(low_lanes, other, both)
+        v_ref[where, :] = values.astype(jnp.bfloat16)
+        v_turned[i] = values.T.astype(jnp.bfloat16)
+        return carry
+
+    lax.fori_loop(0, blocks, prepare, 0)
+    gather(1)
+
+    def attend(i, hp):
+        where = pl.ds(pl.multiple_of(i * size, size), size)
+        columns = pl.ds(pl.multiple_of(hp * 128, 128), 128)
+        stacked = stack_pair(q_ref[where, columns], low_lanes)
+
+        def score(j, top):
+            keys = k_ref[pl.ds(pl.multiple_of(j * size, size), size), :]
+            b = bias[j]
+            s = dot_t(keys, stacked) + jnp.concatenate([b, b], axis=1)
+            scores[j] = s
+            return jnp.maximum(top, jnp.max(s, axis=0, keepdims=True))
+
+        top = lax.fori_loop(0, i + 1, score, jnp.full((1, 2 * size), -jnp.inf, jnp.float32))
+
+        def mix(j, c):
+            total, acc = c
+            p = jnp.exp(scores[j] - top)
+            total = total + jnp.sum(p, axis=0, keepdims=True)
+            return total, acc + dot_n(v_turned[j], p.astype(jnp.bfloat16))
+
+        total, acc = lax.fori_loop(0, i + 1, mix, (
+            jnp.zeros((1, 2 * size), jnp.float32), jnp.zeros((128, 2 * size), jnp.float32)))
+        lse_ref[i, hp] = top + jnp.log(total)
+        acc = acc / total
+        acc = jnp.where(low_rows, acc[:, :size], acc[:, size:])
+        mix_ref[where, columns] = acc.T.astype(jnp.bfloat16)
+
+    def step(s, carry):
+        line.step(s - per)
+        i = s // per
+        hp = s - i * per
+        live = s < blocks * per
+
+        @pl.when(live & (hp == 0))
+        def _():
+            def fill(j, c):
+                bias[j] = block_bias(seg_col_ref, seg_row_ref, i, j, size)
+                return c
+
+            lax.fori_loop(0, i + 1, fill, 0)
+
+        @pl.when(live)
+        def _():
+            def each(h, c):
+                attend(i, h)
+                return c
+
+            lax.fori_loop(hp * pairs // per, (hp + 1) * pairs // per, each, 0)
+
+        @pl.when(live & (hp == per - 1))
+        def _():
+            where = pl.ds(pl.multiple_of(i * size, size), size)
+
+            def part_tile(t, c):
+                at = pl.ds(pl.multiple_of(t * tile, tile), tile)
+                part[where, at] = dot_t(mix_ref[where, :], out_w[at, :]).astype(jnp.bfloat16)
+                return c
+
+            lax.fori_loop(0, wide, part_tile, 0)
+        return carry
+
+    lax.fori_loop(0, per + line.steps, step, 0)
+    line.drain()
+    for k in range(1, m):
+        send_gains(k, dp).wait_send()
+    for kind in (0, 1):
+        for k in range(1, chips):
+            direct(kind, k).wait_send()
+        for c in range(chips):
+            forward(kind, c, core).wait_send()
+
+
+def attention_head(x, gain_part, qkv_shard, out_shard, cosines, sines, seg_col, seg_row, n, m, cid, size,
+                   chunks=16, lag=2):
+    rows, width = x.shape
+    q_width = out_shard.shape[1]
+    pairs = q_width // 128
+    rc = rows // (2 * chunks)
+    blocks = rows // size
+    chips = m // 2
+    low = jnp.bfloat16
+    vmem = pl.BlockSpec(memory_space=pltpu.VMEM)
+    dma = pltpu.SemaphoreType.DMA
+    shape = jax.ShapeDtypeStruct
+    return pl.pallas_call(
+        functools.partial(head_kernel, n, m, chunks, lag, norm_eps, size, pairs),
+        out_shape=(
+            shape((rows, width), low), shape((rows, q_width), low), shape((rows, q_width), low),
+            shape((rows, 128), low), shape((rows, 128), low), shape((blocks, pairs, 1, 2 * size), jnp.float32),
+            shape((width, q_width + 128), low), shape((width, q_width), low), shape((2, width), jnp.float32),
+        ),
+        in_specs=[vmem] * 8,
+        out_specs=(vmem,) * 9,
+        scratch_shapes=line_scratch(chunks, rc, width) + [
+            pltpu.VMEM((rows, width), low),
+            pltpu.VMEM((rows, width), low),
+            pltpu.VMEM((size, q_width + 128), jnp.float32),
+            pltpu.VMEM((blocks, size, size), jnp.float32),
+            pltpu.VMEM((blocks, size, 2 * size), jnp.float32),
+            pltpu.VMEM((blocks, 128, size), low),
+            pltpu.VMEM((m, 2, width), jnp.float32),
+            dma((m,)), dma((m,)), dma((2, chips)), dma((2, chips)), dma((2, m)),
+        ],
+        compiler_params=pltpu.CompilerParams(collective_id=cid, has_side_effects=True, vmem_limit_bytes=56 << 20),
+        cost_estimate=pl.CostEstimate(flops=20 * rows * width * q_width, bytes_accessed=rows * width * 170,
+                                      transcendentals=rows * rows * pairs),
+    )(x, gain_part, qkv_shard, out_shard, cosines, sines, seg_col, seg_row)
+
+
 def back_kernel(n, m, chunks, lag, eps, size, pairs,
                 feed_part, grad_low, gain, q_ref, k_ref, v_ref, mix_ref, lse_ref, cos_ref, sin_ref,
                 seg_col_ref, seg_row_ref, out_w, x_hbm, qkv_hbm, branch_hbm, middle_hbm,
@@ -660,7 +804,7 @@
 
         @pl.when(live & (hp == 0))
         def _():
-            grad_mix[...] = dot_t(grad_low[at_rows, :], out_w[...]).astype(jnp.bfloat16)
+            grad_mix[...] = dot_n(grad_low[at_rows, :], out_w[...]).astype(jnp.bfloat16)
 
             def fill(j, c):
                 bias[j] = block_bias(seg_col_ref, seg_row_ref, i, j, size)
@@ -844,25 +988,11 @@
       x, qkv_w, branch, grad_middle)
 
 
-def tail_kernel(n, m, rates, kv_width, gains_ref, correct_ref, ff_hbm, head_ref, *refs):
-    count = len(rates)
-    params = refs[:3 * count]
-    norm_ref, outs = refs[3 * count], refs[3 * count + 1:6 * count + 1]
-    (line, got_gains, got_line, got_plane, ff_grad, turned), rest = refs[6 * count + 1:6 * count + 7], refs[6 * count + 7:]
-    held, rest = rest[:3 * count], rest[3 * count:]
-    (send_gains, recv_gains, send_line, recv_line, send_plane, recv_plane, ff_sem, load_sem, save_sem) = rest
+def norm_kernel(n, m, gains_ref, ff_ref, head_ref, norm_ref, gain_ref, line, got_gains, got_line, got_plane,
+                send_gains, recv_gains, send_line, recv_line, send_plane, recv_plane):
     z = lax.axis_index("tensor")
     d = lax.axis_index("dp")
     share = head_ref.shape[0]
-    q_width = outs[3].shape[1]
-    ff = outs[12].shape[2]
-
-    ff_load = pltpu.make_async_copy(ff_hbm, ff_grad, ff_sem)
-    ff_load.start()
-    loads = [pltpu.make_async_copy(params[k], held[k], load_sem.at[k]) for k in range(3 * count)]
-    saves = [pltpu.make_async_copy(held[k], outs[k], save_sem.at[k]) for k in range(3 * count)]
-    for copy in loads:
-        copy.start()
 
     barrier = pltpu.get_barrier_semaphore()
     for k in range(1, n):
@@ -906,10 +1036,9 @@
         return acc + squares(value)
 
     local = lax.fori_loop(0, share // sub, head_rows, jnp.zeros((1, 1), jnp.float32))
-    ff_load.wait()
 
     def ff_rows(r, acc):
-        value = ff_grad[pl.ds(pl.multiple_of(r * sub, sub), sub), :].astype(jnp.float32)
+        value = ff_ref[pl.ds(pl.multiple_of(r * sub, sub), sub), :].astype(jnp.float32)
         return acc + squares(value)
 
     local = lax.fori_loop(0, share // sub, ff_rows, local)
@@ -917,6 +1046,7 @@
         gains_to(k, d).wait_send()
         gains_to(k, lax.rem(d + m - k, m)).wait_recv()
     gains = summed(got_gains, m)
+    gain_ref[...] = gains
     own = squares(gains)
     local = local + jnp.where(z == 0, own, jnp.zeros_like(own))
     line[0] = jnp.broadcast_to(local, (8, 128))
@@ -935,7 +1065,39 @@
         over_plane(k, lax.rem(d + m - k, m)).wait_recv()
     norm = jnp.sqrt(summed(got_plane, m))
     norm_ref[...] = norm
-    factor = jnp.minimum(1.0, clip_limit / (norm[:1, :1] + 1e-06))
+
+
+def adam_kernel(rates, kv_width, correct_ref, norm_ref, gain_ref, ff_hbm, head_hbm, layer_hbm, input_hbm, *refs):
+    count = len(rates)
+    params, refs = refs[:3 * count], refs[3 * count:]
+    norm_out, layer_out, input_out, outs, refs = refs[0], refs[1], refs[2], refs[3:3 * count + 3], refs[3 * count + 3:]
+    (ff_grad, head_ref), held, (grad_sem, load_sem, save_sem, whole_sem) = refs[:2], refs[2:3 * count + 2], refs[3 * count + 2:]
+    share = gain_ref.shape[1]
+    q_width = outs[3].shape[1]
+    ff = outs[12].shape[2]
+    sub = 32
+
+    grads = (
+        pltpu.make_async_copy(ff_hbm, ff_grad, grad_sem.at[0]),
+        pltpu.make_async_copy(head_hbm, head_ref, grad_sem.at[1]),
+    )
+    loads = [pltpu.make_async_copy(params[k], held[k], load_sem.at[k]) for k in range(3 * count)]
+    saves = [pltpu.make_async_copy(held[k], outs[k], save_sem.at[k]) for k in range(3 * count)]
+    quarter = layer_hbm.shape[0] // 4
+    moves = []
+    for k in range(4):
+        at = pl.ds(k * quarter, quarter)
+        moves.append(pltpu.make_async_copy(layer_hbm.at[at], layer_out.at[at], whole_sem.at[0, k]))
+        moves.append(pltpu.make_async_copy(input_hbm.at[at], input_out.at[at], whole_sem.at[1, k]))
+    for copy in grads:
+        copy.start()
+    for which in (1, 2, 3, 5, 4, 0):
+        for k in range(3):
+            loads[3 * which + k].start()
+    for copy in moves:
+        copy.start()
+    norm_out[...] = norm_ref[...]
+    factor = jnp.minimum(1.0, clip_limit / (norm_ref[:1, :1] + 1e-06))
     one, two = correct_ref[0], correct_ref[1]
 
     def update(which, where, gradient):
@@ -963,11 +1125,30 @@
         lax.fori_loop(0, share // sub, lambda r, c: (body(pl.ds(pl.multiple_of(r * sub, sub), sub)), c)[1], 0)
         save(which)
 
+    for copy in grads:
+        copy.wait()
+    by_rows(1, lambda where: update(1, (where, slice(None)), head_ref[where, :q_width]))
+    load(3)
+
+    def out_tile(t, carry):
+        at = pl.ds(pl.multiple_of(t * 128, 128), 128)
+        source = pl.ds(pl.multiple_of(q_width + 2 * kv_width + t * 128, 128), 128)
+        update(3, (at, slice(None)), head_ref[:, source].T)
+        return carry
+
+    lax.fori_loop(0, outs[9].shape[0] // 128, out_tile, 0)
+    save(3)
+
+    load(2)
+    both = head_ref[:, q_width:q_width + 2 * kv_width].T
+    for t in (0, 1):
+        update(2, (t, slice(None), slice(None)), both[t * kv_width:(t + 1) * kv_width])
+    save(2)
+
     def gateup_rows(where):
         for t in (0, 1):
             update(4, (t, where, slice(None)), ff_grad[where, t * ff:(t + 1) * ff].astype(jnp.float32))
 
-    by_rows(4, gateup_rows)
     load(5)
 
     def down_tile(t, carry):
@@ -978,59 +1159,49 @@
 
     lax.fori_loop(0, ff // 128, down_tile, 0)
     save(5)
-    by_rows(1, lambda where: update(1, (where, slice(None)), head_ref[where, :q_width]))
-    load(3)
-
-    def out_tile(t, carry):
-        at = pl.ds(pl.multiple_of(t * 128, 128), 128)
-        source = pl.ds(pl.multiple_of(q_width + 2 * kv_width + t * 128, 128), 128)
-        update(3, (at, slice(None)), head_ref[:, source].T)
-        return carry
-
-    lax.fori_loop(0, outs[9].shape[0] // 128, out_tile, 0)
-    save(3)
-
-    def keyval_rows(where):
-        both = head_ref[where, q_width:q_width + 2 * kv_width]
-        for t in (0, 1):
-            update(2, (t, where, slice(None)), both[:, t * kv_width:(t + 1) * kv_width])
-
-    by_rows(2, keyval_rows)
+    by_rows(4, gateup_rows)
     load(0)
-    update(0, (slice(None), slice(None)), gains)
+    update(0, (slice(None), slice(None)), gain_ref[...])
     save(0)
-    for copy in saves:
+    for copy in saves + moves:
         copy.wait()
 
 
-def finish_step(gains, correct, ff_grad, head_grad, params, rates, kv_width, n, m, cid):
+def finish_step(gains, correct, ff_grad, head_grad, layer, grad_in, params, rates, kv_width, n, m, cid):
     share = gains.shape[1] // m
     parts = gains.reshape(2, m, share).transpose(1, 0, 2)
     vmem = pl.BlockSpec(memory_space=pltpu.VMEM)
     hbm = pl.BlockSpec(memory_space=pl.ANY)
     dma = pltpu.SemaphoreType.DMA
-    shapes = [jax.ShapeDtypeStruct(p.shape, jnp.float32) for p in params]
-    size = sum(p.size for p in params)
-    norm, *outs = pl.pallas_call(
-        functools.partial(tail_kernel, n, m, rates, kv_width),
-        out_shape=(jax.ShapeDtypeStruct((8, 128), jnp.float32), *shapes),
-        in_specs=[vmem, pl.BlockSpec(memory_space=pltpu.SMEM), hbm, vmem] + [hbm] * len(params),
-        out_specs=(vmem,) + (hbm,) * len(params),
+    shape = jax.ShapeDtypeStruct
+    norm, gain = pl.pallas_call(
+        functools.partial(norm_kernel, n, m),
+        out_shape=(shape((8, 128), jnp.float32), shape((2, share), jnp.float32)),
+        in_specs=[vmem, vmem, vmem],
+        out_specs=(vmem, vmem),
         scratch_shapes=[
             pltpu.VMEM((2, 8, 128), jnp.float32),
             pltpu.VMEM((m, 2, share), jnp.float32),
             pltpu.VMEM((n, 8, 128), jnp.float32),
             pltpu.VMEM((m, 8, 128), jnp.float32),
-            pltpu.VMEM(ff_grad.shape, ff_grad.dtype),
-            pltpu.VMEM((8, 128), jnp.float32),
-        ] + [pltpu.VMEM(p.shape, jnp.float32) for p in params] + [
-            dma((m,)), dma((m,)), dma((n,)), dma((n,)), dma((m,)), dma((m,)), dma,
-            dma((len(params),)), dma((len(params),)),
+            dma((m,)), dma((m,)), dma((n,)), dma((n,)), dma((m,)), dma((m,)),
         ],
-        compiler_params=pltpu.CompilerParams(collective_id=cid, has_side_effects=True, vmem_limit_bytes=60 << 20),
-        cost_estimate=pl.CostEstimate(flops=20 * size, bytes_accessed=8 * size, transcendentals=size),
-    )(parts, correct, ff_grad, head_grad, *params)
-    return norm, outs
+        compiler_params=pltpu.CompilerParams(collective_id=cid, has_side_effects=True),
+    )(parts, ff_grad, head_grad)
+    size = sum(p.size for p in params)
+    norm, layer, grad_in, *outs = pl.pallas_call(
+        functools.partial(adam_kernel, rates, kv_width),
+        out_shape=(shape((8, 128), jnp.float32), shape(layer.shape, layer.dtype), shape(grad_in.shape, grad_in.dtype))
+        + tuple(shape(p.shape, jnp.float32) for p in params),
+        in_specs=[pl.BlockSpec(memory_space=pltpu.SMEM), vmem, vmem] + [hbm] * (4 + len(params)),
+        out_specs=(vmem,) + (hbm,) * (2 + len(params)),
+        scratch_shapes=[pltpu.VMEM(ff_grad.shape, ff_grad.dtype), pltpu.VMEM(head_grad.shape, jnp.float32)]
+        + [pltpu.VMEM(p.shape, jnp.float32) for p in params]
+        + [dma((2,)), dma((len(params),)), dma((len(params),)), dma((2, 4))],
+        compiler_params=pltpu.CompilerParams(vmem_limit_bytes=40 << 20),
+        cost_estimate=pl.CostEstimate(flops=20 * size, bytes_accessed=24 * size, transcendentals=size),
+    )(correct, norm, gain, ff_grad, head_grad, layer, grad_in, *params)
+    return norm, layer, grad_in, outs
 
 
 norm_eps = 1e-05
@@ -1091,29 +1262,24 @@
     low = jnp.bfloat16
     width = w_query.shape[1]
     kv_width = w_keyval.shape[2]
-    gain_rows = lax.all_gather(norm_gains.astype(low), "dp", axis=1, tiled=True)
-    qkv_shard = jnp.concatenate([w_query, w_keyval[0], w_keyval[1]], axis=1).astype(low)
-    qkv_weight = lax.all_gather(qkv_shard, "dp", axis=0, tiled=True)
-    out_weight = lax.all_gather(w_out.astype(low), "dp", axis=1, tiled=True)
     gateup_weight = lax.all_gather(w_gateup.astype(low), "dp", axis=1, tiled=True)
     down_weight = lax.all_gather(w_down.astype(low), "dp", axis=1, tiled=True)
-    gain_values = gain_rows.astype(jnp.float32)
+    qkv_shard = jnp.concatenate([w_query, w_keyval[0], w_keyval[1]], axis=1).astype(low)
+    out_shard = w_out.T.astype(low)
+    share = norm_gains.shape[1]
+    gain_part = lax.dynamic_update_slice(
+        jnp.zeros((2, tokens.shape[1]), jnp.float32), norm_gains, (0, lax.axis_index("dp") * share)
+    )
     length = tokens.shape[0]
     size = min(256, length)
     segment = segment_ids[0]
     places = positions(segment)
     cosines, sines = paired_tables(places)
-    first = (jnp.arange(length, dtype=jnp.int32) - places)[::size] // size
     seg_col, seg_row = segment[:, None], segment[None, :]
 
-    values_in = tokens.astype(jnp.float32)
-    inverse_one = lax.rsqrt(jnp.mean(values_in * values_in, axis=-1, keepdims=True) + norm_eps)
-    unit_one = values_in * inverse_one
-    normed_one = (unit_one * gain_values[0]).astype(low)
-    raw = jnp.dot(normed_one, qkv_weight, preferred_element_type=jnp.float32)
-    mixture, q, k, v, lse = attention_forward(raw, cosines, sines, seg_col, seg_row, first, size)
-    branch_part = jnp.dot(mixture, out_weight, preferred_element_type=jnp.float32).astype(low)
-    (branch,) = line_reduce((branch_part,), n, 16, 1)
+    branch, mixture, q, k, v, lse, qkv_weight, out_weight, gain_values = attention_head(
+        tokens, gain_part, qkv_shard, out_shard, cosines, sines, seg_col, seg_row, n, m, 1, size
+    )
     feed_part, grad_middle, grad_branch, gain_grad_two, grad_ff_weight = feed_forward(
         branch, gain_values[1:], tokens, cotangent, gateup_weight, down_weight, n, 2
     )
@@ -1128,7 +1294,7 @@
     params = (
         (norm_gains, gains_first, gains_second),
         (w_query, query_first, query_second),
-        (w_keyval, keyval_first, keyval_second),
+        tuple(a.swapaxes(1, 2) for a in (w_keyval, keyval_first, keyval_second)),
         (w_out, out_first, out_second),
         (w_gateup, gateup_first, gateup_second),
         (w_down, down_first, down_second),
@@ -1141,13 +1307,15 @@
         (weight_rate, weight_decay),
         (weight_rate, weight_decay),
     )
-    norm, updated = finish_step(
-        gain_grads, correct, ff_reduced, head_reduced, [a for group in params for a in group], rates, kv_width, n, m, 4
+    norm, layer_out, input_grad, updated = finish_step(
+        gain_grads, correct, ff_reduced, head_reduced, layer_out, input_grad,
+        [a for group in params for a in group], rates, kv_width, n, m, 4
     )
     results = []
     for k in range(len(params)):
         weight, first_state, second_state = updated[3 * k : 3 * k + 3]
-        results += [first_state, second_state, weight]
+        group = [first_state, second_state, weight]
+        results += [a.swapaxes(1, 2) for a in group] if k == 2 else group
     return (layer_out, input_grad, norm[0, :1], *results)
 
 

time: 638 us -> 988 us (1.55)
  Pallas kernels: 532 us -> 942 us
  local copies, waits for them, and re-layouts: 42.8 us -> 20 us
  waiting for transfers between devices: 11.1 us -> 0.05 us
  matrix products: 10.7 us -> 0 us
  blocking collectives: 10.6 us -> 0 us
    pallas_call x3, Pallas kernels: 163 us -> 573 us  [the longest x1 385 us: finish_step(): pl.pallas_call(functools.partial(adam_kernel, rates, kv_width), out_shape...]
    unnamed x91 -> x50, local copies, waits for them, and re-layouts: 40 us -> 16.3 us
    dot_general x2 -> x0, matrix products: 10.7 us -> none  [the longest x1 6.28 us: on_device(): raw = jnp.dot(normed_one, qkv_weight, preferred_element_type=jnp.float32)]
    all_gather x1 -> x0, blocking collectives: 10.6 us -> none  [on_device(): gain_rows = lax.all_gather(norm_gains.astype(low), 'dp', axis=1, tiled=True)]
    all_gather x2 -> x0, waiting for transfers between devices: 10.2 us -> none  [the longest x1 10.2 us: on_device(): qkv_weight = lax.all_gather(qkv_shard, 'dp', axis=0, tiled=True)]
  transfers between devices with their start and end apart: 5 -> 3, of which waited for: 2 -> 0; matrix products, arithmetic and copies ran while one was open for 4% -> 1% of each run, Pallas kernels for 56% -> 40%
where the time goes in v7:
time: 988 us; the launch traced here: 987 us
  Pallas kernels  942 us (95%)
  local copies, waits for them, and re-layouts  20 us (2%)
  between operations  15.4 us (2%)
  other arithmetic  10.3 us (1%)
    pallas_call x1, Pallas kernels, finish_step(): pl.pallas_call(functools.partial(adam_kernel, rates, kv_width), out_shape...  385 us
    pallas_call x1, Pallas kernels, attention_back(): pl.pallas_call(functools.partial(back_kernel, n, m, chunks, lag, norm_eps...  227 us
    pallas_call x1, Pallas kernels, attention_head(): pl.pallas_call(functools.partial(head_kernel, n, m, chunks, lag, norm_eps...  169 us
    pallas_call x1, Pallas kernels, feed_forward(): pl.pallas_call(functools.partial(ff_kernel, n, chunks, lag, norm_eps), ou...  142 us
  transfers between devices with their start and end apart: 3, of which 0 were waited for; matrix products, arithmetic and copies ran while one was open for 1% of the time, Pallas kernels for 40%

profile of v7, /device:TPU:0, one launch (start us, length us, event | category | flops | bytes accessed | tf_op | source)
XLA Modules:
  0.0 987.5 jit_solution(17548994952301726483)
XLA Ops:
  7.2 0.0 copy-start
  7.2 0.0 all-gather.5.cloned.1.call-start
  7.2 2.4 convert_element_type.28
  9.7 0.0 all-gather.5.cloned.1.call-update
  9.7 0.0 copy-start.22
  9.7 0.0 copy-start.10
  9.7 0.0 copy-start.5
  9.8 0.0 all-gather.3.cloned.1.call-start
  9.8 0.0 copy-done
  9.8 1.2 convert_element_type.27
  11.1 0.0 copy-start.6
  11.1 0.0 copy-start.17
  11.1 0.0 all-gather.3.cloned.1.call-update
  11.1 0.0 reduce-scatter.2.cloned.1.call-start
  11.1 0.0 copy-done.22
  11.2 0.5 slice.36
  12.3 0.1 add_select_fusion
  12.4 0.3 reduce-window.9
  12.7 0.1 slice.39
  12.8 0.0 copy-done.10
  12.8 0.1 copy.49
  12.9 0.0 copy-done.5
  13.0 1.0 copy.52.seg_col_ref
  14.0 0.0 copy-done.6
  14.0 0.8 copy.50
  14.9 0.0 copy-done.17
  14.9 0.0 copy-start.23
  14.9 0.1 slice_reduce_fusion
  15.0 0.8 pad_maximum_fusion.2.qkv_shard
  15.8 0.1 fusion.2
  15.9 1.9 fusion
  17.8 1.8 pad_maximum_fusion
  19.7 0.0 copy-done.23
  19.7 168.7 %shard_map.373 = (bf16[1024,2048]{1,0:T(8,128)(2,1)}, bf16[1024,512]{1,0:T(8,128)(2,1)}, bf16[1024,512]{1,0:T(8,128)(2,1)}, bf16[1024,128]{1,0:T(8,128)(2,1)}, b...) custom-call(bf16[1024,2048]{1,0:T(8,128)(2,1)} %x_hbm.1, ...), custom_call_target="tpu_custom_call" | custom-call | flops 21474836480 | bytes 356515840 | tf_op jit(solution)/shard_map/pallas_call | solution.py:638
  188.3 1.4 fusion.3
  189.7 141.6 %shard_map.374 = (bf16[1024,2048]{1,0:T(8,128)(2,1)}, f32[1024,2048]{1,0:T(8,128)}, bf16[1024,2048]{1,0:T(8,128)(2,1)}, f32[1,2048]{1,0:T(1,128)}, bf16[2048,4224]{1,0:T(8,128)(2,1)}) custom-call(bf16[1024,2048]{1,0:T(8,128)(2,1)} %get-tuple-element.62.branch.branch_hbm, f32[1,2048]{1,0:T(1,128)} %get-tuple-element.106.gain, bf16[1024,2048]{1,0:T(8,128)(2,1)} %x_hbm.1, ...), custom_call_target="tpu_custom_call" | custom-call | flops 53150220288 | bytes 314572800 | tf_op jit(solution)/shard_map/pallas_call | solution.py:398
  331.3 0.0 reduce-scatter.2.cloned.1.call-update
  332.1 0.1 pad_maximum_fusion.4.correct_ref
  332.1 226.7 %shard_map.375 = (bf16[1024,2048]{1,0:T(8,128)(2,1)}, f32[1024,2048]{1,0:T(8,128)}, f32[1,2048]{1,0:T(1,128)}, f32[256,1152]{1,0:T(8,128)}) custom-call(bf16[1024,2048]{1,0:T(8,128)(2,1)} %get-tuple-element.64.feed_part, bf16[1024,2048]{1,0:T(8,128)(2,1)} %get-tuple-element.65.grad_low, f32[1,2048]{1,0:T(1,128)} %get-tuple-element.105.gain, ...), custom_call_target="tpu_custom_call" | custom-call | flops 42949672960 | bytes 545259520 | tf_op jit(solution)/shard_map/pallas_call | solution.py:955
  558.9 0.0 copy-start.1
  558.9 0.0 copy-start.19
  558.9 0.0 copy-start.20
  558.9 1.5 pad_maximum_fusion.3
  560.4 19.2 %shard_map.376 = (f32[8,128]{1,0:T(8,128)}, f32[2,256]{1,0:T(2,128)}) custom-call(f32[8,2,256]{2,1,0:T(2,128)} %bitcast.36, bf16[256,4224]{1,0:T(8,128)(2,1)} %reduce-scatter.2.cloned.1.call-done.ff_ref.ff_hbm, f32[256,1152]{1,0:T(8,128)} %get-tuple-element.77.head_ref.head_hbm), custom_call_target="tpu_custom_call" | custom-call | tf_op jit(solution)/shard_map/pallas_call | solution.py:1177
  579.6 0.0 copy-done.1
  579.7 0.0 copy-done.19
  579.7 0.0 copy-done.20
  579.7 0.0 copy-start.2
  579.7 1.6 copy-done.2
  581.3 1.4 copy-done.3
  582.7 1.3 copy-done.4
  583.9 1.0 copy-done.7
  585.0 1.4 copy-done.8
  586.3 1.4 copy-done.9
  587.7 1.0 copy-done.11
  588.7 1.0 copy-done.12
  589.8 1.0 copy-done.13
  590.8 1.0 copy-done.14
  591.9 0.9 copy-done.15
  592.8 0.9 copy-done.16
  593.7 0.7 copy-done.18
  594.3 0.7 copy-done.21
  595.0 385.4 %shard_map.377 = (f32[8,128]{1,0:T(8,128)S(1)}, bf16[1024,2048]{1,0:T(8,128)(2,1)}, f32[1024,2048]{1,0:T(8,128)}, f32[2,256]{1,0:T(2,128)}, f32[2,256]{1,0:T(2,1...) custom-call(f32[2]{0:T(128)S(1)} %pad_maximum_fusion.4.correct_ref, ...), custom_call_target="tpu_custom_call" | custom-call | flops 82606080 | bytes 99127296 | tf_op jit(solution)/shard_map/pallas_call | solution.py:1192
  980.4 0.5 slice.43
  (22 shorter events, 0.1 us)
Async XLA Ops:
  7.2 2.6 copy-start
  7.2 182.5 %all-gather.5.cloned.1.call-start = ((), (), s32[]{:S(2)}) async-start(), calls=%async_computation.2 | async-start | bytes 6488064 | tf_op jit(solution)/shard_map/all_gather | solution.py:1266
  9.7 1.4 copy-start.22
  9.7 3.1 copy-start.10
  9.7 3.2 copy-start.5
  9.8 180.0 %all-gather.3.cloned.1.call-start = ((), (), s32[]{:S(2)}) async-start(), calls=%async_computation.1 | async-start | bytes 12976128 | tf_op jit(solution)/shard_map/all_gather | solution.py:1265
  11.1 2.9 copy-start.6
  11.1 3.8 copy-start.17
  11.1 549.3 %reduce-scatter.2.cloned.1.call-start = ((), (), s32[]{:S(2)}) async-start(), calls=%async_computation.3 | async-start | bytes 19464192 | tf_op jit(solution)/shard_map/reduce_scatter | solution.py:1286
  14.9 4.8 copy-start.23
  558.9 20.8 %copy-start.1 = (f32[2,256,1408]{2,1,0:T(8,128)S(1)}, f32[2,256,1408]{2,1,0:T(8,128)}, u32[]{:S(2)}) copy-start(f32[2,256,1408]{2,1,0:T(8,128)} %refs_12_.1) | copy-start | bytes 8650756
  558.9 20.8 %copy-start.19 = (f32[2,256]{1,0:T(2,128)S(1)}, f32[2,256]{1,0:T(2,128)}, u32[]{:S(2)}) copy-start(f32[2,256]{1,0:T(2,128)} %refs_1_.1) | copy-start | bytes 6148
  558.9 20.8 %copy-start.20 = (f32[2,256]{1,0:T(2,128)S(1)}, f32[2,256]{1,0:T(2,128)}, u32[]{:S(2)}) copy-start(f32[2,256]{1,0:T(2,128)} %refs_2_.1) | copy-start | bytes 6148
  579.7 1.6 copy-start.2
  581.3 1.4 copy-start.3
  582.7 1.3 copy-start.4
  583.9 1.0 copy-start.7
  585.0 1.4 copy-start.8
  586.3 1.4 copy-start.9
  587.7 1.0 copy-start.11
  588.7 1.0 copy-start.12
  589.8 1.0 copy-start.13
  590.8 1.0 copy-start.14
  591.9 0.9 copy-start.15
  592.8 0.9 copy-start.16
  593.7 0.7 copy-start.18
  594.3 0.7 copy-start.21
Sparse Core Ops, SparseCore 0:
  10.5 66.1 all-gather.4
  79.2 67.6 all-gather.2
  331.5 149.8 reduce-scatter.1

commit v8 on v7

--- a/solution.py
+++ b/solution.py
@@ -208,13 +208,14 @@
     rows, width = branch.shape
     ff = down_w.shape[0]
     rc = rows // (2 * chunks)
-    per = 4
+    per = 8
+    offset = per - 1
     half = rows // 2
     hb = per * rc
     block = 2 * hb
     blocks = chunks // per
     line = Line(n, chunks, rc, lag, two_part, got, two_sum, (sa, ra, sg, rg))
-    landed = 2 * lag * (n - 1) + per
+    landed = 2 * lag * (n - 1) + offset
     tile = 256
     full, rest = ff // tile, ff % tile
     wide = width // tile
@@ -280,7 +281,7 @@
         lax.fori_loop(0, per, some, 0)
 
     def step(s, carry):
-        line.step(s - per)
+        line.step(s - offset)
         b = s // per
         phase = s - b * per
         live = s < chunks
@@ -310,11 +311,11 @@
                 wait(weights)
             wait(load_cot(b))
 
-        @pl.when(live & (phase < 2))
-        def _():
-            lax.fori_loop(phase * 2, jnp.where(phase == 0, 2, full), unit_tile, 0)
-
-        @pl.when(live & (phase == 2))
+        @pl.when(live & (phase < 3))
+        def _():
+            lax.fori_loop(jnp.maximum(2 * phase - 1, 0), jnp.minimum(2 * phase + 1, full), unit_tile, 0)
+
+        @pl.when(live & (phase == 3))
         def _():
             if rest:
                 units(full * tile, rest)
@@ -323,24 +324,29 @@
             def _():
                 wait(save_feed(b - 1))
 
+        @pl.when(live & ((phase == 3) | (phase == 4)))
+        def _():
             def feed_tile(t, c):
-                columns = pl.ds(pl.multiple_of(t * tile, tile), tile)
+                columns = pl.ds(pl.multiple_of(t * 2 * tile, 2 * tile), 2 * tile)
                 feed[:, columns] = dot_n(hidden[mine, :], down_w[:, columns]).astype(jnp.bfloat16)
                 return c
 
-            lax.fori_loop(0, wide, feed_tile, 0)
-            start(save_feed(b))
-
-        @pl.when(live & (phase == 3))
+            lax.fori_loop((phase - 3) * (wide // 4), (phase - 2) * (wide // 4), feed_tile, 0)
+
+            @pl.when(phase == 4)
+            def _():
+                start(save_feed(b))
+
+        @pl.when(live & ((phase == 5) | (phase == 6)))
         def _():
             def two_tile(t, c):
-                at = pl.ds(pl.multiple_of(t * tile, tile), tile)
+                at = pl.ds(pl.multiple_of(t * 2 * tile, 2 * tile), 2 * tile)
                 value = (dot_t(gg[0, mine, :], gu_w[0, at, :]) + dot_t(gg[1, mine, :], gu_w[1, at, :])).astype(jnp.bfloat16)
                 for k in (0, 1):
                     two_part[natural(k, b), at] = value[k * hb:(k + 1) * hb]
                 return c
 
-            lax.fori_loop(0, wide, two_tile, 0)
+            lax.fori_loop((phase - 5) * (wide // 4), (phase - 4) * (wide // 4), two_tile, 0)
 
         d = s - landed
 
@@ -352,19 +358,36 @@
             for k in (0, 1):
                 where = line.rows(k, d)
                 at = pl.ds(pl.multiple_of((d // per) * block + k * hb + (d - (d // per) * per) * rc, rc), rc)
-                unit, inverse = unit_rows(where)
-                grad = two_sum[where, :].astype(jnp.float32)
-                scaled = grad * gain[...]
-                inner = jnp.mean(scaled * unit, axis=-1, keepdims=True)
-                value = cot[at, :].astype(jnp.float32) + inverse * (scaled - unit * inner)
-                middle_stage[k] = value
-                low_stage[k] = value.astype(jnp.bfloat16)
-                gain_out[...] += jnp.sum(grad * unit, axis=0, keepdims=True)
+                pieces = [pl.ds(c * tile, tile) for c in range(wide)]
+
+                def middle_at(c):
+                    return x[where, c].astype(jnp.float32) + branch[where, c].astype(jnp.float32)
+
+                def folded(value):
+                    return value[:, :128] + value[:, 128:]
+
+                total = jnp.zeros((rc, 128), jnp.float32)
+                for c in pieces:
+                    middle = middle_at(c)
+                    total = total + folded(middle * middle)
+                inverse = lax.rsqrt(jnp.sum(total, axis=-1, keepdims=True) * (1.0 / width) + eps)
+                total = jnp.zeros((rc, 128), jnp.float32)
+                for c in pieces:
+                    product = two_sum[where, c].astype(jnp.float32) * (middle_at(c) * inverse)
+                    gain_out[:, c] += jnp.sum(product, axis=0, keepdims=True)
+                    total = total + folded(product * gain[:, c])
+                inner = jnp.sum(total, axis=-1, keepdims=True) * (1.0 / width)
+                for c in pieces:
+                    scaled = two_sum[where, c].astype(jnp.float32) * gain[:, c]
+                    value = cot[at, c].astype(jnp.float32) + inverse * (scaled - middle_at(c) * inverse * inner)
+                    middle_stage[k, :, c] = value
+                    low_stage[k, :, c] = value.astype(jnp.bfloat16)
             start(save_rows(d))
 
-        w = s - chunks
-
-        @pl.when((w >= 0) & (w < wide))
+        late = s - chunks
+        w = late // 2
+
+        @pl.when((late >= 0) & (late == 2 * w) & (w < wide))
         def _():
             @pl.when(w > 0)
             def _():
@@ -377,19 +400,19 @@
             start(save_units(w))
         return carry
 
-    lax.fori_loop(0, per + line.steps, step, 0)
+    lax.fori_loop(0, offset + line.steps, step, 0)
     line.drain()
     wait(save_feed(blocks - 1))
     wait(save_rows(chunks - 1))
     wait(save_units(wide - 1))
 
 
-def feed_forward(branch, gain, x, cot, gateup_w, down_w, n, cid, chunks=16, lag=2):
+def feed_forward(branch, gain, x, cot, gateup_w, down_w, n, cid, chunks=32, lag=2):
     rows, width = branch.shape
     ff = down_w.shape[0]
     rc = rows // (2 * chunks)
-    block = 8 * rc
-    blocks = chunks // 4
+    block = 16 * rc
+    blocks = chunks // 8
     low = jnp.bfloat16
     vmem = pl.BlockSpec(memory_space=pltpu.VMEM)
     hbm = pl.BlockSpec(memory_space=pl.ANY)
@@ -624,7 +647,7 @@
 
 
 def attention_head(x, gain_part, qkv_shard, out_shard, cosines, sines, seg_col, seg_row, n, m, cid, size,
-                   chunks=16, lag=2):
+                   chunks=32, lag=2):
     rows, width = x.shape
     q_width = out_shard.shape[1]
     pairs = q_width // 128
@@ -988,8 +1011,8 @@
       x, qkv_w, branch, grad_middle)
 
 
-def norm_kernel(n, m, gains_ref, ff_ref, head_ref, norm_ref, gain_ref, line, got_gains, got_line, got_plane,
-                send_gains, recv_gains, send_line, recv_line, send_plane, recv_plane):
+def norm_kernel(n, m, gains_ref, ff_ref, head_ref, norm_ref, gain_ref, line, got_gains, got_line, got_plane, got_squares,
+                send_squares, recv_squares, send_gains, recv_gains, send_line, recv_line, send_plane, recv_plane):
     z = lax.axis_index("tensor")
     d = lax.axis_index("dp")
     share = head_ref.shape[0]
@@ -1007,6 +1030,11 @@
             src_ref=gains_ref.at[peer], dst_ref=got_gains.at[sender], send_sem=send_gains.at[k],
             recv_sem=recv_gains.at[sender], device_id={"dp": peer}, device_id_type=MESH)
 
+    def squares_to(k, sender):
+        return pltpu.make_async_remote_copy(
+            src_ref=line.at[2], dst_ref=got_squares.at[sender], send_sem=send_squares.at[k],
+            recv_sem=recv_squares.at[sender], device_id={"dp": lax.rem(d + k, m)}, device_id_type=MESH)
+
     def along_line(k, sender):
         return pltpu.make_async_remote_copy(
             src_ref=line.at[0], dst_ref=got_line.at[sender], send_sem=send_line.at[k], recv_sem=recv_line.at[sender],
@@ -1042,36 +1070,41 @@
         return acc + squares(value)
 
     local = lax.fori_loop(0, share // sub, ff_rows, local)
+    line[2] = jnp.broadcast_to(local, (8, 128))
+    for k in range(1, m):
+        squares_to(k, d).start()
+    got_squares[d] = line[2]
     for k in range(1, m):
         gains_to(k, d).wait_send()
         gains_to(k, lax.rem(d + m - k, m)).wait_recv()
+    for k in range(1, m):
+        squares_to(k, d).wait_send()
+        squares_to(k, lax.rem(d + m - k, m)).wait_recv()
+    line[0] = summed(got_squares, m)
     gains = summed(got_gains, m)
     gain_ref[...] = gains
-    own = squares(gains)
-    local = local + jnp.where(z == 0, own, jnp.zeros_like(own))
-    line[0] = jnp.broadcast_to(local, (8, 128))
+    line[1] = jnp.broadcast_to(squares(gains), (8, 128))
+    for k in range(1, m):
+        over_plane(k, d).start()
+    got_plane[d] = line[1]
     for k in range(1, n):
         along_line(k, z).start()
     got_line[z] = line[0]
     for k in range(1, n):
         along_line(k, z).wait_send()
         along_line(k, lax.rem(z + n - k, n)).wait_recv()
-    line[1] = summed(got_line, n)
-    for k in range(1, m):
-        over_plane(k, d).start()
-    got_plane[d] = line[1]
     for k in range(1, m):
         over_plane(k, d).wait_send()
         over_plane(k, lax.rem(d + m - k, m)).wait_recv()
-    norm = jnp.sqrt(summed(got_plane, m))
-    norm_ref[...] = norm
+    norm_ref[...] = jnp.sqrt(summed(got_line, n) + summed(got_plane, m))
 
 
 def adam_kernel(rates, kv_width, correct_ref, norm_ref, gain_ref, ff_hbm, head_hbm, layer_hbm, input_hbm, *refs):
     count = len(rates)
     params, refs = refs[:3 * count], refs[3 * count:]
     norm_out, layer_out, input_out, outs, refs = refs[0], refs[1], refs[2], refs[3:3 * count + 3], refs[3 * count + 3:]
-    (ff_grad, head_ref), held, (grad_sem, load_sem, save_sem, whole_sem) = refs[:2], refs[2:3 * count + 2], refs[3 * count + 2:]
+    (ff_grad, head_ref, layer_held, input_held), held = refs[:4], refs[4:3 * count + 4]
+    grad_sem, load_sem, save_sem, in_sem, back_sem = refs[3 * count + 4:]
     share = gain_ref.shape[1]
     q_width = outs[3].shape[1]
     ff = outs[12].shape[2]
@@ -1084,17 +1117,19 @@
     loads = [pltpu.make_async_copy(params[k], held[k], load_sem.at[k]) for k in range(3 * count)]
     saves = [pltpu.make_async_copy(held[k], outs[k], save_sem.at[k]) for k in range(3 * count)]
     quarter = layer_hbm.shape[0] // 4
-    moves = []
+    arrive, depart = [], []
     for k in range(4):
         at = pl.ds(k * quarter, quarter)
-        moves.append(pltpu.make_async_copy(layer_hbm.at[at], layer_out.at[at], whole_sem.at[0, k]))
-        moves.append(pltpu.make_async_copy(input_hbm.at[at], input_out.at[at], whole_sem.at[1, k]))
+        for t, (source, kept, target) in enumerate(
+                ((layer_hbm, layer_held, layer_out), (input_hbm, input_held, input_out))):
+            arrive.append(pltpu.make_async_copy(source.at[at], kept.at[at], in_sem.at[t, k]))
+            depart.append(pltpu.make_async_copy(kept.at[at], target.at[at], back_sem.at[t, k]))
     for copy in grads:
         copy.start()
-    for which in (1, 2, 3, 5, 4, 0):
+    for which in (1, 3, 2, 5, 4, 0):
         for k in range(3):
             loads[3 * which + k].start()
-    for copy in moves:
+    for copy in arrive:
         copy.start()
     norm_out[...] = norm_ref[...]
     factor = jnp.minimum(1.0, clip_limit / (norm_ref[:1, :1] + 1e-06))
@@ -1160,10 +1195,13 @@
     lax.fori_loop(0, ff // 128, down_tile, 0)
     save(5)
     by_rows(4, gateup_rows)
+    for came, left in zip(arrive, depart):
+        came.wait()
+        left.start()
     load(0)
     update(0, (slice(None), slice(None)), gain_ref[...])
     save(0)
-    for copy in saves + moves:
+    for copy in saves + depart:
         copy.wait()
 
 
@@ -1180,11 +1218,12 @@
         in_specs=[vmem, vmem, vmem],
         out_specs=(vmem, vmem),
         scratch_shapes=[
-            pltpu.VMEM((2, 8, 128), jnp.float32),
+            pltpu.VMEM((3, 8, 128), jnp.float32),
             pltpu.VMEM((m, 2, share), jnp.float32),
             pltpu.VMEM((n, 8, 128), jnp.float32),
             pltpu.VMEM((m, 8, 128), jnp.float32),
-            dma((m,)), dma((m,)), dma((n,)), dma((n,)), dma((m,)), dma((m,)),
+            pltpu.VMEM((m, 8, 128), jnp.float32),
+            dma((m,)), dma((m,)), dma((m,)), dma((m,)), dma((n,)), dma((n,)), dma((m,)), dma((m,)),
         ],
         compiler_params=pltpu.CompilerParams(collective_id=cid, has_side_effects=True),
     )(parts, ff_grad, head_grad)
@@ -1195,10 +1234,10 @@
         + tuple(shape(p.shape, jnp.float32) for p in params),
         in_specs=[pl.BlockSpec(memory_space=pltpu.SMEM), vmem, vmem] + [hbm] * (4 + len(params)),
         out_specs=(vmem,) + (hbm,) * (2 + len(params)),
-        scratch_shapes=[pltpu.VMEM(ff_grad.shape, ff_grad.dtype), pltpu.VMEM(head_grad.shape, jnp.float32)]
+        scratch_shapes=[pltpu.VMEM(a.shape, a.dtype) for a in (ff_grad, head_grad, layer, grad_in)]
         + [pltpu.VMEM(p.shape, jnp.float32) for p in params]
-        + [dma((2,)), dma((len(params),)), dma((len(params),)), dma((2, 4))],
-        compiler_params=pltpu.CompilerParams(vmem_limit_bytes=40 << 20),
+        + [dma((2,)), dma((len(params),)), dma((len(params),)), dma((2, 4)), dma((2, 4))],
+        compiler_params=pltpu.CompilerParams(vmem_limit_bytes=63 << 20),
         cost_estimate=pl.CostEstimate(flops=20 * size, bytes_accessed=24 * size, transcendentals=size),
     )(correct, norm, gain, ff_grad, head_grad, layer, grad_in, *params)
     return norm, layer, grad_in, outs
@@ -1224,13 +1263,11 @@
 
 
 def paired_tables(places):
-    frequency = jnp.power(10000.0, -jnp.arange(HD // 2, dtype=jnp.float32) * (2.0 / HD))
+    lane = jnp.arange(128, dtype=jnp.int32) % HD
+    frequency = jnp.power(10000.0, -(lane % (HD // 2)).astype(jnp.float32) * (2.0 / HD))
     angles = places.astype(jnp.float32)[:, None] * frequency[None, :]
-    cosines, sines = jnp.cos(angles), jnp.sin(angles)
-    return (
-        jnp.concatenate([cosines] * 4, axis=-1),
-        jnp.concatenate([-sines, sines, -sines, sines], axis=-1),
-    )
+    sines = jnp.sin(angles)
+    return jnp.cos(angles), jnp.where(lane < HD // 2, -sines, sines)
 
 
 def on_device(
@@ -1262,8 +1299,6 @@
     low = jnp.bfloat16
     width = w_query.shape[1]
     kv_width = w_keyval.shape[2]
-    gateup_weight = lax.all_gather(w_gateup.astype(low), "dp", axis=1, tiled=True)
-    down_weight = lax.all_gather(w_down.astype(low), "dp", axis=1, tiled=True)
     qkv_shard = jnp.concatenate([w_query, w_keyval[0], w_keyval[1]], axis=1).astype(low)
     out_shard = w_out.T.astype(low)
     share = norm_gains.shape[1]
@@ -1276,6 +1311,11 @@
     places = positions(segment)
     cosines, sines = paired_tables(places)
     seg_col, seg_row = segment[:, None], segment[None, :]
+    qkv_shard, out_shard, gain_part, cosines, sines, seg_col, late_gateup, late_down = lax.optimization_barrier(
+        (qkv_shard, out_shard, gain_part, cosines, sines, seg_col, w_gateup, w_down)
+    )
+    gateup_weight = lax.all_gather(late_gateup.astype(low), "dp", axis=1, tiled=True)
+    down_weight = lax.all_gather(late_down.astype(low), "dp", axis=1, tiled=True)
 
     branch, mixture, q, k, v, lse, qkv_weight, out_weight, gain_values = attention_head(
         tokens, gain_part, qkv_shard, out_shard, cosines, sines, seg_col, seg_row, n, m, 1, size

time: 988 us -> 607 us (0.61)
  Pallas kernels: 942 us -> 571 us
  local copies, waits for them, and re-layouts: 20 us -> 8.77 us
    pallas_call x1, Pallas kernels: 385 us -> 25.1 us  [finish_step(): pl.pallas_call(functools.partial(adam_kernel, rates, kv_width), out_shape...]
    unnamed x50 -> x10, local copies, waits for them, and re-layouts: 16.3 us -> 3.08 us
  transfers between devices with their start and end apart: 3 -> 3, of which waited for: 0 -> 0; matrix products, arithmetic and copies ran while one was open for 1% -> 1% of each run, Pallas kernels for 40% -> 65%
where the time goes in v8:
time: 607 us
  Pallas kernels  571 us (94%)
  between operations  15.3 us (3%)
  other arithmetic  11.6 us (2%)
  local copies, waits for them, and re-layouts  8.77 us (1%)
    pallas_call x1, Pallas kernels, attention_back(): pl.pallas_call(functools.partial(back_kernel, n, m, chunks, lag, norm_eps...  227 us
    pallas_call x1, Pallas kernels, attention_head(): pl.pallas_call(functools.partial(head_kernel, n, m, chunks, lag, norm_eps...  166 us
    pallas_call x1, Pallas kernels, feed_forward(): pl.pallas_call(functools.partial(ff_kernel, n, chunks, lag, norm_eps), ou...  135 us
    pallas_call x1, Pallas kernels, finish_step(): pl.pallas_call(functools.partial(adam_kernel, rates, kv_width), out_shape...  25.1 us
    pallas_call x1, Pallas kernels, finish_step(): pl.pallas_call(functools.partial(norm_kernel, n, m), out_shape=(shape((8,...  18 us
  transfers between devices with their start and end apart: 3, of which 0 were waited for; matrix products, arithmetic and copies ran while one was open for 1% of the time, Pallas kernels for 65%

profile of v8, /device:TPU:0, one launch (start us, length us, event | category | flops | bytes accessed | tf_op | source)
XLA Modules:
  0.0 606.6 jit_solution(6212772626465629271)
XLA Ops:
  7.2 0.0 all-gather.5.cloned.1.call-start
  7.3 1.2 slice.36
  9.1 0.8 add_select_fusion
  9.9 0.3 reduce-window.9
  10.2 0.1 slice.39
  10.3 0.1 slice_reduce_fusion
  10.4 0.1 fusion.1
  10.5 1.0 copy.45
  11.6 1.1 convert.11
  12.6 0.0 copy-start
  12.7 2.0 copy.46
  14.7 0.7 constant_dynamic-update-slice_fusion.gain_part
  15.4 0.0 copy-start.2
  15.4 3.1 negate_select_fusion
  18.4 0.8 pad_maximum_fusion.qkv_shard
  19.3 2.3 convert_element_type.37
  21.5 0.0 all-gather.5.cloned.1.call-update
  21.6 0.0 copy-start.1
  21.6 0.0 all-gather.3.cloned.1.call-start
  21.6 0.0 copy-done
  21.6 1.2 convert_element_type.36
  22.9 0.0 copy-done.2
  22.9 0.0 all-gather.3.cloned.1.call-update
  22.9 0.0 reduce-scatter.2.cloned.1.call-start
  23.0 0.0 copy-done.1
  23.0 1.0 copy.47.seg_col_ref
  24.0 165.5 %shard_map.373 = (bf16[1024,2048]{1,0:T(8,128)(2,1)}, bf16[1024,512]{1,0:T(8,128)(2,1)}, bf16[1024,512]{1,0:T(8,128)(2,1)}, bf16[1024,128]{1,0:T(8,128)(2,1)}, b...) custom-call(bf16[1024,2048]{1,0:T(8,128)(2,1)} %x_hbm.1, ...), custom_call_target="tpu_custom_call" | custom-call | flops 21474836480 | bytes 356515840 | tf_op jit(solution)/shard_map/pallas_call | solution.py:661
  189.6 1.4 fusion.7
  191.0 0.0 all-gather.5.cloned.1.call-done.down_hbm
  191.0 0.0 all-gather.3.cloned.1.call-done.gu_hbm
  191.0 135.5 %shard_map.374 = (bf16[1024,2048]{1,0:T(8,128)(2,1)}, f32[1024,2048]{1,0:T(8,128)}, bf16[1024,2048]{1,0:T(8,128)(2,1)}, f32[1,2048]{1,0:T(1,128)}, bf16[2048,4224]{1,0:T(8,128)(2,1)}) custom-call(bf16[1024,2048]{1,0:T(8,128)(2,1)} %get-tuple-element.76.branch.branch_hbm, f32[1,2048]{1,0:T(1,128)} %get-tuple-element.122.gain, bf16[1024,2048]{1,0:T(8,128)(2,1)} %x_hbm.1, ...), custom_call_target="tpu_custom_call" | custom-call | flops 53150220288 | bytes 314572800 | tf_op jit(solution)/shard_map/pallas_call | solution.py:421
  326.5 0.0 reduce-scatter.2.cloned.1.call-update
  327.2 0.6 pad_maximum_fusion.2.correct_ref
  327.8 0.0 copy-start.3
  327.8 226.6 %shard_map.375 = (bf16[1024,2048]{1,0:T(8,128)(2,1)}, f32[1024,2048]{1,0:T(8,128)}, f32[1,2048]{1,0:T(1,128)}, f32[256,1152]{1,0:T(8,128)}) custom-call(bf16[1024,2048]{1,0:T(8,128)(2,1)} %get-tuple-element.80.feed_part, bf16[1024,2048]{1,0:T(8,128)(2,1)} %get-tuple-element.81.grad_low, f32[1,2048]{1,0:T(1,128)} %get-tuple-element.121.gain, ...), custom_call_target="tpu_custom_call" | custom-call | flops 42949672960 | bytes 545259520 | tf_op jit(solution)/shard_map/pallas_call | solution.py:978
  554.4 0.0 copy-done.3
  554.4 1.3 pad_maximum_fusion.1
  555.7 0.0 reduce-scatter.2.cloned.1.call-done.ff_ref.ff_hbm
  555.7 18.0 %shard_map.376 = (f32[8,128]{1,0:T(8,128)}, f32[2,256]{1,0:T(2,128)}) custom-call(f32[8,2,256]{2,1,0:T(2,128)} %bitcast.36, bf16[256,4224]{1,0:T(8,128)(2,1)} %reduce-scatter.2.cloned.1.call-done.ff_ref.ff_hbm, f32[256,1152]{1,0:T(8,128)} %get-tuple-element.93.head_ref.head_hbm), custom_call_target="tpu_custom_call" | custom-call | tf_op jit(solution)/shard_map/pallas_call | solution.py:1215
  573.7 25.1 %shard_map.377 = (f32[8,128]{1,0:T(8,128)}, bf16[1024,2048]{1,0:T(8,128)(2,1)}, f32[1024,2048]{1,0:T(8,128)}, f32[2,256]{1,0:T(2,128)}, f32[2,256]{1,0:T(2,128)}...) custom-call(f32[2]{0:T(128)} %pad_maximum_fusion.2.correct_ref, ...), custom_call_target="tpu_custom_call" | custom-call | flops 82606080 | bytes 99127296 | tf_op jit(solution)/shard_map/pallas_call | solution.py:1231
  598.9 1.2 slice.43
  (5 shorter events, 0.1 us)
Async XLA Ops:
  7.2 183.8 %all-gather.5.cloned.1.call-start = ((), (), s32[]{:S(2)}) async-start(), calls=%async_computation.2 | async-start | bytes 6488064 | tf_op jit(solution)/shard_map/all_gather | solution.py:1318
  12.6 9.0 %copy-start = (f32[2,256,1408]{2,1,0:T(8,128)S(1)}, f32[2,256,1408]{2,1,0:T(8,128)}, u32[]{:S(2)}) copy-start(f32[2,256,1408]{2,1,0:T(8,128)} %refs_12_.1) | copy-start | bytes 8650756
  15.4 7.5 %copy-start.2 = (f32[2,2048]{1,0:T(2,128)}, f32[2,2048]{1,0:T(2,128)S(1)}, u32[]{:S(2)}) copy-start(f32[2,2048]{1,0:T(2,128)S(1)} %constant_dynamic-update-slice_fusion.gain_part) | copy-start | bytes 49156
  21.6 1.4 copy-start.1
  21.6 169.4 %all-gather.3.cloned.1.call-start = ((), (), s32[]{:S(2)}) async-start(), calls=%async_computation.1 | async-start | bytes 12976128 | tf_op jit(solution)/shard_map/all_gather | solution.py:1317
  22.9 532.8 %reduce-scatter.2.cloned.1.call-start = ((), (), s32[]{:S(2)}) async-start(), calls=%async_computation.3 | async-start | bytes 19464192 | tf_op jit(solution)/shard_map/reduce_scatter | solution.py:1326
  327.8 226.6 %copy-start.3 = (f32[1,2048]{1,0:T(1,128)S(1)}, f32[1,2048]{1,0:T(1,128)}, u32[]{:S(2)}) copy-start(f32[1,2048]{1,0:T(1,128)} %get-tuple-element.91) | copy-start | bytes 24580
Sparse Core Ops, SparseCore 0:
  21.7 66.1 all-gather.4
  90.4 67.6 all-gather.2
  326.6 149.6 reduce-scatter.1

commit v9 on v8

--- a/solution.py
+++ b/solution.py
@@ -201,12 +201,12 @@
     return lax.dot_general(left, right, (((0,), (0,)), ((), ())), preferred_element_type=jnp.float32)
 
 
-def ff_kernel(n, chunks, lag, eps, branch, gain, x, cot_hbm, gu_hbm, down_hbm,
+def ff_kernel(n, chunks, lag, eps, branch, gain, x, cot_hbm, w_hbm,
               feed_hbm, middle_hbm, low_hbm, gain_out, grads_hbm,
-              got, sa, ra, sg, rg, two_sum, two_part, gu_w, down_w, cot, normed, hidden, gg, feed,
+              got, sa, ra, sg, rg, two_sum, two_part, weight, cot, normed, hidden, gg, feed,
               middle_stage, low_stage, unit_stage, w_sem, cot_sem, feed_sem, stage_sem, grad_sem):
     rows, width = branch.shape
-    ff = down_w.shape[0]
+    ff = hidden.shape[1]
     rc = rows // (2 * chunks)
     per = 8
     offset = per - 1
@@ -220,11 +220,14 @@
     full, rest = ff // tile, ff % tile
     wide = width // tile
 
-    weights = (
-        pltpu.make_async_copy(gu_hbm, gu_w, w_sem.at[0]),
-        pltpu.make_async_copy(down_hbm, down_w, w_sem.at[1]),
-    )
-    for copy in weights:
+    groups = []
+    for g, (begin, end) in enumerate(((0, tile), (tile, 2 * tile), (2 * tile, ff))):
+        groups.append([
+            pltpu.make_async_copy(w_hbm.at[:, pl.ds(t * ff + begin, end - begin)],
+                                  weight.at[:, pl.ds(t * ff + begin, end - begin)], w_sem.at[g, t])
+            for t in range(3)
+        ])
+    for copy in sum(groups, []):
         copy.start()
 
     def natural(k, b):
@@ -289,26 +292,28 @@
 
         def units(at, count):
             columns = pl.ds(at, count)
-            gate = dot_n(normed[mine, :], gu_w[0, :, columns])
-            up = dot_n(normed[mine, :], gu_w[1, :, columns])
-            grad_hidden = dot_t(cot[mine, :], down_w[columns, :])
+            second = pl.ds(pl.multiple_of(ff + at, 128), count)
+            third = pl.ds(pl.multiple_of(2 * ff + at, 128), count)
+            gate = dot_n(normed[mine, :], weight[:, columns])
+            up = dot_n(normed[mine, :], weight[:, second])
+            grad_hidden = dot_n(cot[mine, :], weight[:, third])
             sg_gate = 1.0 / (1.0 + jnp.exp(-gate))
             silu = gate * sg_gate
             hidden[mine, columns] = (silu * up).astype(jnp.bfloat16)
-            gg[0, mine, columns] = (grad_hidden * up * sg_gate * (1.0 + gate * (1.0 - sg_gate))).astype(jnp.bfloat16)
-            gg[1, mine, columns] = (grad_hidden * silu).astype(jnp.bfloat16)
+            gg[mine, columns] = (grad_hidden * up * sg_gate * (1.0 + gate * (1.0 - sg_gate))).astype(jnp.bfloat16)
+            gg[mine, second] = (grad_hidden * silu).astype(jnp.bfloat16)
 
         def unit_tile(t, c):
+            for g in range(3):
+                @pl.when((b == 0) & (t == g))
+                def _():
+                    wait(groups[g])
             units(pl.multiple_of(t * tile, tile), tile)
             return c
 
         @pl.when(live & (phase == 0))
         def _():
             normalize(b)
-
-            @pl.when(b == 0)
-            def _():
-                wait(weights)
             wait(load_cot(b))
 
         @pl.when(live & (phase < 3))
@@ -328,7 +333,7 @@
         def _():
             def feed_tile(t, c):
                 columns = pl.ds(pl.multiple_of(t * 2 * tile, 2 * tile), 2 * tile)
-                feed[:, columns] = dot_n(hidden[mine, :], down_w[:, columns]).astype(jnp.bfloat16)
+                feed[:, columns] = dot_t(hidden[mine, :], weight[columns, 2 * ff:]).astype(jnp.bfloat16)
                 return c
 
             lax.fori_loop((phase - 3) * (wide // 4), (phase - 2) * (wide // 4), feed_tile, 0)
@@ -341,7 +346,7 @@
         def _():
             def two_tile(t, c):
                 at = pl.ds(pl.multiple_of(t * 2 * tile, 2 * tile), 2 * tile)
-                value = (dot_t(gg[0, mine, :], gu_w[0, at, :]) + dot_t(gg[1, mine, :], gu_w[1, at, :])).astype(jnp.bfloat16)
+                value = dot_t(gg[mine, :], weight[at, :2 * ff]).astype(jnp.bfloat16)
                 for k in (0, 1):
                     two_part[natural(k, b), at] = value[k * hb:(k + 1) * hb]
                 return c
@@ -395,7 +400,7 @@
             columns = pl.ds(pl.multiple_of(w * tile, tile), tile)
             left = normed[:, columns]
             for t in (0, 1):
-                unit_stage[:, t * ff:(t + 1) * ff] = dot_rows(left, gg[t]).astype(jnp.bfloat16)
+                unit_stage[:, t * ff:(t + 1) * ff] = dot_rows(left, gg[:, t * ff:(t + 1) * ff]).astype(jnp.bfloat16)
             unit_stage[:, 2 * ff:] = dot_rows(cot[:, columns], hidden[...]).astype(jnp.bfloat16)
             start(save_units(w))
         return carry
@@ -407,9 +412,9 @@
     wait(save_units(wide - 1))
 
 
-def feed_forward(branch, gain, x, cot, gateup_w, down_w, n, cid, chunks=32, lag=2):
+def feed_forward(branch, gain, x, cot, weight, n, cid, chunks=32, lag=2):
     rows, width = branch.shape
-    ff = down_w.shape[0]
+    ff = weight.shape[1] // 3
     rc = rows // (2 * chunks)
     block = 16 * rc
     blocks = chunks // 8
@@ -424,34 +429,36 @@
             shape((rows, width), low), shape((rows, width), jnp.float32), shape((rows, width), low),
             shape((1, width), jnp.float32), shape((width, 3 * ff), low),
         ),
-        in_specs=[vmem, vmem, vmem, hbm, hbm, hbm],
+        in_specs=[vmem, vmem, vmem, hbm, hbm],
         out_specs=(hbm, hbm, hbm, vmem, hbm),
         scratch_shapes=line_scratch(chunks, rc, width) + [
             pltpu.VMEM((rows, width), low),
             pltpu.VMEM((rows, width), low),
-            pltpu.VMEM((2, width, ff), low),
-            pltpu.VMEM((ff, width), low),
+            pltpu.VMEM((width, 3 * ff), low),
             pltpu.VMEM((rows, width), low),
             pltpu.VMEM((rows, width), low),
             pltpu.VMEM((rows, ff), low),
-            pltpu.VMEM((2, rows, ff), low),
+            pltpu.VMEM((rows, 2 * ff), low),
             pltpu.VMEM((block, width), low),
             pltpu.VMEM((2, rc, width), jnp.float32),
             pltpu.VMEM((2, rc, width), low),
             pltpu.VMEM((256, 3 * ff), low),
-            dma((2,)), dma((blocks, 2)), dma((2,)), dma((2, 2)), dma((1,)),
+            dma((3, 3)), dma((blocks, 2)), dma((2,)), dma((2, 2)), dma((1,)),
         ],
         compiler_params=pltpu.CompilerParams(collective_id=cid, has_side_effects=True, vmem_limit_bytes=63 << 20),
         cost_estimate=pl.CostEstimate(flops=18 * rows * width * ff, bytes_accessed=rows * width * 150,
                                       transcendentals=rows * ff),
-    )(branch, gain, x, cot, gateup_w, down_w)
+    )(branch, gain, x, cot, weight)
 
 
 def head_kernel(n, m, chunks, lag, eps, size, pairs,
-                x, gain_part, qkv_shard, out_shard, cos_ref, sin_ref, seg_col_ref, seg_row_ref,
-                branch, mix_ref, q_ref, k_ref, v_ref, lse_ref, qkv_w, out_w, gain,
+                x, gain_part, query_own, keyval_own, out_own, cos_ref, sin_ref, seg_col_ref, seg_row_ref,
+                gateup_hbm, down_hbm,
+                branch, mix_ref, q_ref, k_ref, v_ref, lse_ref, qkv_w, out_w, gain, ff_hbm,
                 got, sa, ra, sg, rg, part, normed, raw, bias, scores, v_turned, got_gain,
-                send_gain, recv_gain, send_direct, send_forward, recv_w):
+                gateup_own, down_own, ff_own,
+                send_gain, recv_gain, send_direct, send_forward, recv_w, own_sem, save_sem,
+                send_ff, pass_ff, recv_ff):
     rows, width = x.shape
     q_width = pairs * 128
     z = lax.axis_index("tensor")
@@ -467,7 +474,17 @@
     wide = width // tile
     low_lanes, first_half = lane_tests(size)
     low_rows = lax.broadcasted_iota(jnp.int32, (128, size), 0) < 64
-    shards, wholes = (qkv_shard, out_shard), (qkv_w, out_w)
+    wholes = (qkv_w, out_w)
+    ff = down_own.shape[0]
+    piece = 32
+    pieces = share // piece
+    spacing = 40 // pieces
+    owned = (
+        pltpu.make_async_copy(gateup_hbm, gateup_own, own_sem.at[0]),
+        pltpu.make_async_copy(down_hbm, down_own, own_sem.at[1]),
+    )
+    for copy in owned:
+        copy.start()
 
     def ascending(stream, c):
         b = c // per
@@ -481,7 +498,7 @@
     def direct(kind, k):
         peer = 2 * lax.rem(chip + k, chips) + core
         return pltpu.make_async_remote_copy(
-            src_ref=shards[kind], dst_ref=wholes[kind].at[shard_rows(dp)], send_sem=send_direct.at[kind, k],
+            src_ref=wholes[kind].at[shard_rows(dp)], dst_ref=wholes[kind].at[shard_rows(dp)], send_sem=send_direct.at[kind, k],
             recv_sem=recv_w.at[kind, dp], device_id={"dp": peer}, device_id_type=MESH)
 
     def forward(kind, c, side):
@@ -491,6 +508,28 @@
             src_ref=wholes[kind].at[where], dst_ref=wholes[kind].at[where], send_sem=send_forward.at[kind, c],
             recv_sem=recv_w.at[kind, shard], device_id={"dp": 2 * chip + 1 - core}, device_id_type=MESH)
 
+    def piece_rows(shard, p):
+        return pl.ds(pl.multiple_of(shard * share + p * piece, piece), piece)
+
+    def own_piece(p):
+        return ff_own.at[pl.ds(pl.multiple_of(p * piece, piece), piece)]
+
+    def send_piece(k, p):
+        peer = 2 * lax.rem(chip + k, chips) + core
+        return pltpu.make_async_remote_copy(
+            src_ref=own_piece(p), dst_ref=ff_hbm.at[piece_rows(dp, p)], send_sem=send_ff.at[k, p],
+            recv_sem=recv_ff.at[dp, p], device_id={"dp": peer}, device_id_type=MESH)
+
+    def pass_piece(c, side, p, src=None):
+        shard = 2 * c + side
+        where = ff_hbm.at[piece_rows(shard, p)]
+        return pltpu.make_async_remote_copy(
+            src_ref=where if src is None else src, dst_ref=where, send_sem=pass_ff.at[c, p],
+            recv_sem=recv_ff.at[shard, p], device_id={"dp": 2 * chip + 1 - core}, device_id_type=MESH)
+
+    def save_own():
+        return pltpu.make_async_copy(ff_own, ff_hbm.at[shard_rows(dp)], save_sem)
+
     def send_gains(k, sender):
         return pltpu.make_async_remote_copy(
             src_ref=gain_part, dst_ref=got_gain.at[sender], send_sem=send_gain.at[k], recv_sem=recv_gain.at[sender],
@@ -509,8 +548,11 @@
     for k in range(1, m):
         pl.semaphore_signal(barrier, inc=1, device_id={"dp": lax.rem(dp + k, m)}, device_id_type=MESH)
 
-    for kind in (0, 1):
-        wholes[kind][shard_rows(dp), :] = shards[kind][...]
+    qkv_w[shard_rows(dp), :q_width] = query_own[...].astype(jnp.bfloat16)
+    both_own = jnp.concatenate([keyval_own[0], keyval_own[1]], axis=0)
+    qkv_w[shard_rows(dp), q_width:] = both_own.T.astype(jnp.bfloat16)
+    for t in range(q_width // 128):
+        out_w[shard_rows(dp), t * 128:(t + 1) * 128] = out_own[t * 128:(t + 1) * 128, :].T.astype(jnp.bfloat16)
     got_gain[dp] = gain_part[...]
 
     @pl.when((z > 0) & (z < n - 1))
@@ -542,6 +584,24 @@
         return carry
 
     lax.fori_loop(0, rows // rc, norm_rows, 0)
+    for copy in owned:
+        copy.wait()
+
+    def own_rows(r, carry):
+        where = pl.ds(pl.multiple_of(r * piece, piece), piece)
+        for t in (0, 1):
+            ff_own[where, t * ff:(t + 1) * ff] = gateup_own[t, where, :].astype(jnp.bfloat16)
+        return carry
+
+    lax.fori_loop(0, pieces, own_rows, 0)
+
+    def own_columns(t, carry):
+        at = pl.ds(pl.multiple_of(2 * ff + t * 128, 128), 128)
+        ff_own[:, at] = down_own[pl.ds(pl.multiple_of(t * 128, 128), 128), :].T.astype(jnp.bfloat16)
+        return carry
+
+    lax.fori_loop(0, ff // 128, own_columns, 0)
+    save_own().start()
 
     def gather(kind):
         for k in range(1, chips):
@@ -552,6 +612,9 @@
             forward(kind, c, 1 - core).wait_recv()
 
     gather(0)
+    for p in range(min(2, pieces)):
+        for k in range(1, chips):
+            send_piece(k, p).start()
 
     def prepare(i, carry):
         where = pl.ds(pl.multiple_of(i * size, size), size)
@@ -603,6 +666,22 @@
 
     def step(s, carry):
         line.step(s - per)
+        p_send = (s - 1) // spacing + 2
+        p_pass = (s - 4) // spacing
+
+        @pl.when((s >= 1) & ((p_send - 2) * spacing == s - 1) & (p_send < pieces))
+        def _():
+            for k in range(1, chips):
+                send_piece(k, p_send).start()
+
+        @pl.when((s >= 4) & (p_pass * spacing == s - 4) & (p_pass < pieces))
+        def _():
+            pass_piece(chip, core, p_pass, own_piece(p_pass)).start()
+            for k in range(1, chips):
+                c = lax.rem(chip + chips - k, chips)
+                pass_piece(c, core, p_pass).wait_recv()
+                pass_piece(c, core, p_pass).start()
+
         i = s // per
         hp = s - i * per
         live = s < blocks * per
@@ -637,6 +716,17 @@
 
     lax.fori_loop(0, per + line.steps, step, 0)
     line.drain()
+    save_own().wait()
+
+    def settle(p, carry):
+        for k in range(1, chips):
+            send_piece(k, p).wait_send()
+        for c in range(chips):
+            pass_piece(c, core, p).wait_send()
+            pass_piece(c, 1 - core, p).wait_recv()
+        return carry
+
+    lax.fori_loop(0, pieces, settle, 0)
     for k in range(1, m):
         send_gains(k, dp).wait_send()
     for kind in (0, 1):
@@ -646,16 +736,18 @@
             forward(kind, c, core).wait_send()
 
 
-def attention_head(x, gain_part, qkv_shard, out_shard, cosines, sines, seg_col, seg_row, n, m, cid, size,
+def attention_head(x, gain_part, query, keyval, out, cosines, sines, seg_col, seg_row, gateup, down, n, m, cid, size,
                    chunks=32, lag=2):
     rows, width = x.shape
-    q_width = out_shard.shape[1]
+    q_width = query.shape[1]
+    share, ff = width // m, down.shape[0]
     pairs = q_width // 128
     rc = rows // (2 * chunks)
     blocks = rows // size
     chips = m // 2
     low = jnp.bfloat16
     vmem = pl.BlockSpec(memory_space=pltpu.VMEM)
+    hbm = pl.BlockSpec(memory_space=pl.ANY)
     dma = pltpu.SemaphoreType.DMA
     shape = jax.ShapeDtypeStruct
     return pl.pallas_call(
@@ -664,9 +756,10 @@
             shape((rows, width), low), shape((rows, q_width), low), shape((rows, q_width), low),
             shape((rows, 128), low), shape((rows, 128), low), shape((blocks, pairs, 1, 2 * size), jnp.float32),
             shape((width, q_width + 128), low), shape((width, q_width), low), shape((2, width), jnp.float32),
+            shape((width, 3 * ff), low),
         ),
-        in_specs=[vmem] * 8,
-        out_specs=(vmem,) * 9,
+        in_specs=[vmem] * 9 + [hbm] * 2,
+        out_specs=(vmem,) * 9 + (hbm,),
         scratch_shapes=line_scratch(chunks, rc, width) + [
             pltpu.VMEM((rows, width), low),
             pltpu.VMEM((rows, width), low),
@@ -675,12 +768,16 @@
             pltpu.VMEM((blocks, size, 2 * size), jnp.float32),
             pltpu.VMEM((blocks, 128, size), low),
             pltpu.VMEM((m, 2, width), jnp.float32),
-            dma((m,)), dma((m,)), dma((2, chips)), dma((2, chips)), dma((2, m)),
+            pltpu.VMEM(gateup.shape, jnp.float32),
+            pltpu.VMEM(down.shape, jnp.float32),
+            pltpu.VMEM((share, 3 * ff), low),
+            dma((m,)), dma((m,)), dma((2, chips)), dma((2, chips)), dma((2, m)), dma((2,)), dma,
+            dma((chips, share // 32)), dma((chips, share // 32)), dma((m, share // 32)),
         ],
         compiler_params=pltpu.CompilerParams(collective_id=cid, has_side_effects=True, vmem_limit_bytes=56 << 20),
         cost_estimate=pl.CostEstimate(flops=20 * rows * width * q_width, bytes_accessed=rows * width * 170,
                                       transcendentals=rows * rows * pairs),
-    )(x, gain_part, qkv_shard, out_shard, cosines, sines, seg_col, seg_row)
+    )(x, gain_part, query, keyval, out, cosines, sines, seg_col, seg_row, gateup, down)
 
 
 def back_kernel(n, m, chunks, lag, eps, size, pairs,
@@ -1299,8 +1396,6 @@
     low = jnp.bfloat16
     width = w_query.shape[1]
     kv_width = w_keyval.shape[2]
-    qkv_shard = jnp.concatenate([w_query, w_keyval[0], w_keyval[1]], axis=1).astype(low)
-    out_shard = w_out.T.astype(low)
     share = norm_gains.shape[1]
     gain_part = lax.dynamic_update_slice(
         jnp.zeros((2, tokens.shape[1]), jnp.float32), norm_gains, (0, lax.axis_index("dp") * share)
@@ -1311,17 +1406,12 @@
     places = positions(segment)
     cosines, sines = paired_tables(places)
     seg_col, seg_row = segment[:, None], segment[None, :]
-    qkv_shard, out_shard, gain_part, cosines, sines, seg_col, late_gateup, late_down = lax.optimization_barrier(
-        (qkv_shard, out_shard, gain_part, cosines, sines, seg_col, w_gateup, w_down)
-    )
-    gateup_weight = lax.all_gather(late_gateup.astype(low), "dp", axis=1, tiled=True)
-    down_weight = lax.all_gather(late_down.astype(low), "dp", axis=1, tiled=True)
-
-    branch, mixture, q, k, v, lse, qkv_weight, out_weight, gain_values = attention_head(
-        tokens, gain_part, qkv_shard, out_shard, cosines, sines, seg_col, seg_row, n, m, 1, size
+    branch, mixture, q, k, v, lse, qkv_weight, out_weight, gain_values, ff_weight = attention_head(
+        tokens, gain_part, w_query, w_keyval.swapaxes(1, 2), w_out, cosines, sines, seg_col, seg_row,
+        w_gateup, w_down, n, m, 1, size
     )
     feed_part, grad_middle, grad_branch, gain_grad_two, grad_ff_weight = feed_forward(
-        branch, gain_values[1:], tokens, cotangent, gateup_weight, down_weight, n, 2
+        branch, gain_values[1:], tokens, cotangent, ff_weight, n, 2
     )
     ff_reduced = lax.psum_scatter(grad_ff_weight, "dp", scatter_dimension=0, tiled=True)
     layer_out, input_grad, gain_grad_one, head_reduced = attention_back(

time: 607 us -> 607 us (level)
  Pallas kernels: 571 us -> 578 us
    pallas_call x1, Pallas kernels: 166 us -> 175 us  [attention_head(): pl.pallas_call(functools.partial(head_kernel, n, m, chunks, lag, norm_eps...]
  transfers between devices with their start and end apart: 3 -> 1, of which waited for: 0 -> 0; matrix products, arithmetic and copies ran while one was open for 1% -> 0% of each run, Pallas kernels for 65% -> 37%
where the time goes in v9:
time: 607 us; the launch traced here: 606 us
  Pallas kernels  578 us (95%)
  between operations  15.5 us (3%)
  local copies, waits for them, and re-layouts  6.36 us (1%)
  other arithmetic  6.21 us (1%)
    pallas_call x1, Pallas kernels, attention_back(): pl.pallas_call(functools.partial(back_kernel, n, m, chunks, lag, norm_eps...  227 us
    pallas_call x1, Pallas kernels, attention_head(): pl.pallas_call(functools.partial(head_kernel, n, m, chunks, lag, norm_eps...  175 us
    pallas_call x1, Pallas kernels, feed_forward(): pl.pallas_call(functools.partial(ff_kernel, n, chunks, lag, norm_eps), ou...  134 us
    pallas_call x1, Pallas kernels, finish_step(): pl.pallas_call(functools.partial(adam_kernel, rates, kv_width), out_shape...  25.1 us
    pallas_call x1, Pallas kernels, finish_step(): pl.pallas_call(functools.partial(norm_kernel, n, m), out_shape=(shape((8,...  17 us
  transfers between devices with their start and end apart: 1, of which 0 were waited for; matrix products, arithmetic and copies ran while one was open for 0% of the time, Pallas kernels for 37%

profile of v9, /device:TPU:0, one launch (start us, length us, event | category | flops | bytes accessed | tf_op | source)
XLA Modules:
  0.0 605.9 jit_solution(1396844798852626023)
XLA Ops:
  7.2 0.0 reduce-scatter.2.cloned.1.call-start
  7.3 1.2 slice.26
  9.1 0.8 add_select_fusion
  9.9 0.3 reduce-window.9
  10.2 0.1 slice.29
  10.3 0.1 slice_reduce_fusion
  10.4 0.1 fusion.1
  10.5 1.7 copy.43.seg_col_ref
  12.2 0.7 constant_dynamic-update-slice_fusion.gain_part
  12.9 0.0 copy-start
  12.9 3.1 negate_select_fusion
  16.0 0.0 copy-done
  16.0 175.3 %shard_map.373 = (bf16[1024,2048]{1,0:T(8,128)(2,1)}, bf16[1024,512]{1,0:T(8,128)(2,1)}, bf16[1024,512]{1,0:T(8,128)(2,1)}, bf16[1024,128]{1,0:T(8,128)(2,1)}, b...) custom-call(bf16[1024,2048]{1,0:T(8,128)(2,1)} %x_hbm.1, ...), custom_call_target="tpu_custom_call" | custom-call | flops 21474836480 | bytes 356515840 | tf_op jit(solution)/shard_map/pallas_call | solution.py:753
  191.3 1.4 fusion.7
  192.7 133.6 %shard_map.374 = (bf16[1024,2048]{1,0:T(8,128)(2,1)}, f32[1024,2048]{1,0:T(8,128)}, bf16[1024,2048]{1,0:T(8,128)(2,1)}, f32[1,2048]{1,0:T(1,128)}, bf16[2048,4224]{1,0:T(8,128)(2,1)}) custom-call(bf16[1024,2048]{1,0:T(8,128)(2,1)} %get-tuple-element.63.branch.branch_hbm, f32[1,2048]{1,0:T(1,128)} %get-tuple-element.106.gain, bf16[1024,2048]{1,0:T(8,128)(2,1)} %x_hbm.1, ...), custom_call_target="tpu_custom_call" | custom-call | flops 53150220288 | bytes 314572800 | tf_op jit(solution)/shard_map/pallas_call | solution.py:426
  326.3 0.0 reduce-scatter.2.cloned.1.call-update
  327.0 0.6 pad_maximum_fusion.1.correct_ref
  327.6 0.0 copy-start.1
  327.6 226.8 %shard_map.375 = (bf16[1024,2048]{1,0:T(8,128)(2,1)}, f32[1024,2048]{1,0:T(8,128)}, f32[1,2048]{1,0:T(1,128)}, f32[256,1152]{1,0:T(8,128)}) custom-call(bf16[1024,2048]{1,0:T(8,128)(2,1)} %get-tuple-element.66.feed_part, bf16[1024,2048]{1,0:T(8,128)(2,1)} %get-tuple-element.67.grad_low, f32[1,2048]{1,0:T(1,128)} %get-tuple-element.105.gain, ...), custom_call_target="tpu_custom_call" | custom-call | flops 42949672960 | bytes 545259520 | tf_op jit(solution)/shard_map/pallas_call | solution.py:1075
  554.4 0.0 copy-done.1
  554.4 1.3 pad_maximum_fusion
  555.7 0.0 reduce-scatter.2.cloned.1.call-done.ff_ref.ff_hbm
  555.7 17.0 %shard_map.376 = (f32[8,128]{1,0:T(8,128)}, f32[2,256]{1,0:T(2,128)}) custom-call(f32[8,2,256]{2,1,0:T(2,128)} %bitcast.29, bf16[256,4224]{1,0:T(8,128)(2,1)} %reduce-scatter.2.cloned.1.call-done.ff_ref.ff_hbm, f32[256,1152]{1,0:T(8,128)} %get-tuple-element.79.head_ref.head_hbm), custom_call_target="tpu_custom_call" | custom-call | tf_op jit(solution)/shard_map/pallas_call | solution.py:1312
  572.7 25.1 %shard_map.377 = (f32[8,128]{1,0:T(8,128)}, bf16[1024,2048]{1,0:T(8,128)(2,1)}, f32[1024,2048]{1,0:T(8,128)}, f32[2,256]{1,0:T(2,128)}, f32[2,256]{1,0:T(2,128)}...) custom-call(f32[2]{0:T(128)} %pad_maximum_fusion.1.correct_ref, ...), custom_call_target="tpu_custom_call" | custom-call | flops 82606080 | bytes 99127296 | tf_op jit(solution)/shard_map/pallas_call | solution.py:1328
  597.8 1.2 slice.33
  (4 shorter events, 0.0 us)
Async XLA Ops:
  7.2 548.5 %reduce-scatter.2.cloned.1.call-start = ((), (), s32[]{:S(2)}) async-start(), calls=%async_computation.1 | async-start | bytes 19464192 | tf_op jit(solution)/shard_map/reduce_scatter | solution.py:1416
  12.9 3.1 copy-start
  327.6 226.8 %copy-start.1 = (f32[1,2048]{1,0:T(1,128)S(1)}, f32[1,2048]{1,0:T(1,128)}, u32[]{:S(2)}) copy-start(f32[1,2048]{1,0:T(1,128)} %get-tuple-element.77) | copy-start | bytes 24580
Sparse Core Ops, SparseCore 0:
  326.4 148.8 reduce-scatter.1

commit v10 on v9

--- a/solution.py
+++ b/solution.py
@@ -603,15 +603,18 @@
     lax.fori_loop(0, ff // 128, own_columns, 0)
     save_own().start()
 
-    def gather(kind):
+    def pass_on(kind):
         for k in range(1, chips):
             c = lax.rem(chip + chips - k, chips)
             forward(kind, c, core).wait_recv()
             forward(kind, c, core).start()
+
+    def receive(kind):
         for c in range(chips):
             forward(kind, c, 1 - core).wait_recv()
 
-    gather(0)
+    pass_on(0)
+    receive(0)
     for p in range(min(2, pieces)):
         for k in range(1, chips):
             send_piece(k, p).start()
@@ -635,7 +638,7 @@
         return carry
 
     lax.fori_loop(0, blocks, prepare, 0)
-    gather(1)
+    pass_on(1)
 
     def attend(i, hp):
         where = pl.ds(pl.multiple_of(i * size, size), size)
@@ -667,14 +670,14 @@
     def step(s, carry):
         line.step(s - per)
         p_send = (s - 1) // spacing + 2
-        p_pass = (s - 4) // spacing
+        p_pass = (s - 12) // spacing
 
         @pl.when((s >= 1) & ((p_send - 2) * spacing == s - 1) & (p_send < pieces))
         def _():
             for k in range(1, chips):
                 send_piece(k, p_send).start()
 
-        @pl.when((s >= 4) & (p_pass * spacing == s - 4) & (p_pass < pieces))
+        @pl.when((s >= 12) & (p_pass * spacing == s - 12) & (p_pass < pieces))
         def _():
             pass_piece(chip, core, p_pass, own_piece(p_pass)).start()
             for k in range(1, chips):
@@ -701,6 +704,10 @@
                 return c
 
             lax.fori_loop(hp * pairs // per, (hp + 1) * pairs // per, each, 0)
+
+        @pl.when(s == per - 1)
+        def _():
+            receive(1)
 
         @pl.when(live & (hp == per - 1))
         def _():
@@ -801,6 +808,7 @@
     share = width // m
     owners = tile // share
     lead = 2 * lag * (n - 1)
+    shift = chunks + per
     low_lanes, first_half = lane_tests(size)
     low_rows = lax.broadcasted_iota(jnp.int32, (128, size), 0) < 64
 
@@ -911,7 +919,7 @@
 
     def step(s, carry):
         two.step(s)
-        four.step(s - per)
+        four.step(s - shift)
         b = s // per
         hp = s - b * per
         i = blocks - 1 - b
@@ -1003,13 +1011,13 @@
                 ).astype(jnp.bfloat16)
             start(save_layer(d))
 
-        e4 = s - lead - per + 1
+        e4 = s - lead - shift + 1
 
         @pl.when((e4 >= 0) & (e4 < chunks))
         def _():
             start(load_middle(e4, e4 % 2))
 
-        d4 = s - lead - per
+        d4 = s - lead - shift
 
         @pl.when(d4 >= 0)
         def _():
@@ -1029,7 +1037,7 @@
             start(save_input(d4))
         return carry
 
-    lax.fori_loop(0, per + four.steps, step, 0)
+    lax.fori_loop(0, shift + four.steps, step, 0)
     two.drain()
     four.drain()
     wait(save_layer(chunks - 1))
@@ -1223,11 +1231,14 @@
             depart.append(pltpu.make_async_copy(kept.at[at], target.at[at], back_sem.at[t, k]))
     for copy in grads:
         copy.start()
-    for which in (1, 3, 2, 5, 4, 0):
+    for which in (1, 3, 2):
         for k in range(3):
             loads[3 * which + k].start()
     for copy in arrive:
         copy.start()
+    for which in (5, 4, 0):
+        for k in range(3):
+            loads[3 * which + k].start()
     norm_out[...] = norm_ref[...]
     factor = jnp.minimum(1.0, clip_limit / (norm_ref[:1, :1] + 1e-06))
     one, two = correct_ref[0], correct_ref[1]
@@ -1281,6 +1292,9 @@
         for t in (0, 1):
             update(4, (t, where, slice(None)), ff_grad[where, t * ff:(t + 1) * ff].astype(jnp.float32))
 
+    for came, left in zip(arrive, depart):
+        came.wait()
+        left.start()
     load(5)
 
     def down_tile(t, carry):
@@ -1292,9 +1306,6 @@
     lax.fori_loop(0, ff // 128, down_tile, 0)
     save(5)
     by_rows(4, gateup_rows)
-    for came, left in zip(arrive, depart):
-        came.wait()
-        left.start()
     load(0)
     update(0, (slice(None), slice(None)), gain_ref[...])
     save(0)

time: 607 us -> 580 us (0.956)
  Pallas kernels: 578 us -> 551 us
    pallas_call x1, Pallas kernels: 175 us -> 164 us  [attention_head(): pl.pallas_call(functools.partial(head_kernel, n, m, chunks, lag, norm_eps...]
    pallas_call x1, Pallas kernels: 227 us -> 219 us  [attention_back(): pl.pallas_call(functools.partial(back_kernel, n, m, chunks, lag, norm_eps...]
  transfers between devices with their start and end apart: 1 -> 1, of which waited for: 0 -> 0; matrix products, arithmetic and copies ran while one was open for 0% -> 0% of each run, Pallas kernels for 37% -> 38%
where the time goes in v10:
time: 580 us; the launch traced here: 579 us
  Pallas kernels  551 us (95%)
  between operations  15.5 us (3%)
  local copies, waits for them, and re-layouts  6.36 us (1%)
  other arithmetic  6.21 us (1%)
    pallas_call x1, Pallas kernels, attention_back(): pl.pallas_call(functools.partial(back_kernel, n, m, chunks, lag, norm_eps...  219 us
    pallas_call x1, Pallas kernels, attention_head(): pl.pallas_call(functools.partial(head_kernel, n, m, chunks, lag, norm_eps...  164 us
    pallas_call x1, Pallas kernels, feed_forward(): pl.pallas_call(functools.partial(ff_kernel, n, chunks, lag, norm_eps), ou...  133 us
    pallas_call x1, Pallas kernels, finish_step(): pl.pallas_call(functools.partial(adam_kernel, rates, kv_width), out_shape...  22.1 us
    pallas_call x1, Pallas kernels, finish_step(): pl.pallas_call(functools.partial(norm_kernel, n, m), out_shape=(shape((8,...  13.4 us
  transfers between devices with their start and end apart: 1, of which 0 were waited for; matrix products, arithmetic and copies ran while one was open for 0% of the time, Pallas kernels for 38%

profile of v10, /device:TPU:0, one launch (start us, length us, event | category | flops | bytes accessed | tf_op | source)
XLA Modules:
  0.0 579.4 jit_solution(9548846718552062637)
XLA Ops:
  7.2 0.0 reduce-scatter.2.cloned.1.call-start
  7.3 1.2 slice.26
  9.1 0.8 add_select_fusion
  9.9 0.3 reduce-window.9
  10.2 0.1 slice.29
  10.3 0.1 slice_reduce_fusion
  10.4 0.1 fusion.1
  10.5 1.7 copy.43.seg_col_ref
  12.2 0.7 constant_dynamic-update-slice_fusion.gain_part
  12.9 0.0 copy-start
  12.9 3.1 negate_select_fusion
  16.0 0.0 copy-done
  16.0 163.5 %shard_map.373 = (bf16[1024,2048]{1,0:T(8,128)(2,1)}, bf16[1024,512]{1,0:T(8,128)(2,1)}, bf16[1024,512]{1,0:T(8,128)(2,1)}, bf16[1024,128]{1,0:T(8,128)(2,1)}, b...) custom-call(bf16[1024,2048]{1,0:T(8,128)(2,1)} %x_hbm.1, ...), custom_call_target="tpu_custom_call" | custom-call | flops 21474836480 | bytes 356515840 | tf_op jit(solution)/shard_map/pallas_call | solution.py:760
  179.5 1.4 fusion.7
  180.9 133.3 %shard_map.374 = (bf16[1024,2048]{1,0:T(8,128)(2,1)}, f32[1024,2048]{1,0:T(8,128)}, bf16[1024,2048]{1,0:T(8,128)(2,1)}, f32[1,2048]{1,0:T(1,128)}, bf16[2048,4224]{1,0:T(8,128)(2,1)}) custom-call(bf16[1024,2048]{1,0:T(8,128)(2,1)} %get-tuple-element.63.branch.branch_hbm, f32[1,2048]{1,0:T(1,128)} %get-tuple-element.106.gain, bf16[1024,2048]{1,0:T(8,128)(2,1)} %x_hbm.1, ...), custom_call_target="tpu_custom_call" | custom-call | flops 53150220288 | bytes 314572800 | tf_op jit(solution)/shard_map/pallas_call | solution.py:426
  314.2 0.0 reduce-scatter.2.cloned.1.call-update
  315.0 0.6 pad_maximum_fusion.1.correct_ref
  315.6 0.0 copy-start.1
  315.6 219.0 %shard_map.375 = (bf16[1024,2048]{1,0:T(8,128)(2,1)}, f32[1024,2048]{1,0:T(8,128)}, f32[1,2048]{1,0:T(1,128)}, f32[256,1152]{1,0:T(8,128)}) custom-call(bf16[1024,2048]{1,0:T(8,128)(2,1)} %get-tuple-element.66.feed_part, bf16[1024,2048]{1,0:T(8,128)(2,1)} %get-tuple-element.67.grad_low, f32[1,2048]{1,0:T(1,128)} %get-tuple-element.105.gain, ...), custom_call_target="tpu_custom_call" | custom-call | flops 42949672960 | bytes 545259520 | tf_op jit(solution)/shard_map/pallas_call | solution.py:1083
  534.5 0.0 copy-done.1
  534.6 1.3 pad_maximum_fusion
  535.9 0.0 reduce-scatter.2.cloned.1.call-done.ff_ref.ff_hbm
  535.9 13.4 %shard_map.376 = (f32[8,128]{1,0:T(8,128)}, f32[2,256]{1,0:T(2,128)}) custom-call(f32[8,2,256]{2,1,0:T(2,128)} %bitcast.29, bf16[256,4224]{1,0:T(8,128)(2,1)} %reduce-scatter.2.cloned.1.call-done.ff_ref.ff_hbm, f32[256,1152]{1,0:T(8,128)} %get-tuple-element.79.head_ref.head_hbm), custom_call_target="tpu_custom_call" | custom-call | tf_op jit(solution)/shard_map/pallas_call | solution.py:1323
  549.3 22.1 %shard_map.377 = (f32[8,128]{1,0:T(8,128)}, bf16[1024,2048]{1,0:T(8,128)(2,1)}, f32[1024,2048]{1,0:T(8,128)}, f32[2,256]{1,0:T(2,128)}, f32[2,256]{1,0:T(2,128)}...) custom-call(f32[2]{0:T(128)} %pad_maximum_fusion.1.correct_ref, ...), custom_call_target="tpu_custom_call" | custom-call | flops 82606080 | bytes 99127296 | tf_op jit(solution)/shard_map/pallas_call | solution.py:1339
  571.4 1.2 slice.33
  (4 shorter events, 0.0 us)
Async XLA Ops:
  7.2 528.7 %reduce-scatter.2.cloned.1.call-start = ((), (), s32[]{:S(2)}) async-start(), calls=%async_computation.1 | async-start | bytes 19464192 | tf_op jit(solution)/shard_map/reduce_scatter | solution.py:1427
  12.9 3.1 copy-start
  315.6 219.0 %copy-start.1 = (f32[1,2048]{1,0:T(1,128)S(1)}, f32[1,2048]{1,0:T(1,128)}, u32[]{:S(2)}) copy-start(f32[1,2048]{1,0:T(1,128)} %get-tuple-element.77) | copy-start | bytes 24580
Sparse Core Ops, SparseCore 0:
  314.4 173.6 reduce-scatter.1

commit v11 on v10

--- a/solution.py
+++ b/solution.py
@@ -278,7 +278,7 @@
             for k in (0, 1):
                 where = pl.ds(pl.multiple_of(k * half + b * hb + r * rc, rc), rc)
                 at = pl.ds(pl.multiple_of(b * block + k * hb + r * rc, rc), rc)
-                normed[at, :] = (unit_rows(where)[0] * gain[...]).astype(jnp.bfloat16)
+                normed[at, :] = (unit_rows(where)[0] * gain[1:2, :]).astype(jnp.bfloat16)
             return carry
 
         lax.fori_loop(0, per, some, 0)
@@ -380,10 +380,10 @@
                 for c in pieces:
                     product = two_sum[where, c].astype(jnp.float32) * (middle_at(c) * inverse)
                     gain_out[:, c] += jnp.sum(product, axis=0, keepdims=True)
-                    total = total + folded(product * gain[:, c])
+                    total = total + folded(product * gain[1:2, c])
                 inner = jnp.sum(total, axis=-1, keepdims=True) * (1.0 / width)
                 for c in pieces:
-                    scaled = two_sum[where, c].astype(jnp.float32) * gain[:, c]
+                    scaled = two_sum[where, c].astype(jnp.float32) * gain[1:2, c]
                     value = cot[at, c].astype(jnp.float32) + inverse * (scaled - middle_at(c) * inverse * inner)
                     middle_stage[k, :, c] = value
                     low_stage[k, :, c] = value.astype(jnp.bfloat16)
@@ -452,15 +452,23 @@
 
 
 def head_kernel(n, m, chunks, lag, eps, size, pairs,
-                x, gain_part, query_own, keyval_own, out_own, cos_ref, sin_ref, seg_col_ref, seg_row_ref,
-                gateup_hbm, down_hbm,
-                branch, mix_ref, q_ref, k_ref, v_ref, lse_ref, qkv_w, out_w, gain, ff_hbm,
+                gain_part, query_own, keyval_own, out_own, frequency, seg_row_ref,
+                x_hbm, gateup_hbm, down_hbm,
+                branch, gain, lse_ref, seg_col_ref, cos_hbm, sin_hbm, mix_hbm, q_hbm, k_hbm, v_hbm, qkv_hbm, out_hbm, ff_hbm,
                 got, sa, ra, sg, rg, part, normed, raw, bias, scores, v_turned, got_gain,
-                gateup_own, down_own, ff_own,
-                send_gain, recv_gain, send_direct, send_forward, recv_w, own_sem, save_sem,
+                x, cos_ref, sin_ref, mix_ref, q_ref, k_ref, v_ref, qkv_w, out_w, gateup_own, down_own, ff_own,
+                send_gain, recv_gain, send_direct, send_forward, recv_w, own_sem, save_sem, result_sem, x_sem,
                 send_ff, pass_ff, recv_ff):
-    rows, width = x.shape
+    rows, width = branch.shape
     q_width = pairs * 128
+    x_load = pltpu.make_async_copy(x_hbm, x, x_sem)
+    x_load.start()
+    results = [
+        pltpu.make_async_copy(source, target, result_sem.at[k])
+        for k, (source, target) in enumerate((
+            (q_ref, q_hbm), (k_ref, k_hbm), (v_ref, v_hbm), (cos_ref, cos_hbm), (sin_ref, sin_hbm),
+            (qkv_w, qkv_hbm), (out_w, out_hbm), (mix_ref, mix_hbm)))
+    ]
     z = lax.axis_index("tensor")
     dp = lax.axis_index("dp")
     share = width // m
@@ -576,6 +584,8 @@
         whole = whole + got_gain[k]
     gain[...] = whole.astype(jnp.bfloat16).astype(jnp.float32)
 
+    x_load.wait()
+
     def norm_rows(r, carry):
         where = pl.ds(pl.multiple_of(r * rc, rc), rc)
         values = x[where, :].astype(jnp.float32)
@@ -584,6 +594,20 @@
         return carry
 
     lax.fori_loop(0, rows // rc, norm_rows, 0)
+    def tables(i, carry):
+        where = pl.ds(pl.multiple_of(i * size, size), size)
+        ids = jnp.broadcast_to(seg_row_ref[:, where].astype(jnp.float32), (128, size)).T[:, :1]
+        seg_col_ref[where, :] = ids.astype(jnp.int32)
+        earlier = jnp.where(seg_row_ref[...].astype(jnp.float32) < ids, 1.0, 0.0)
+        place = (i * size + lax.broadcasted_iota(jnp.int32, (size, 1), 0)).astype(jnp.float32) - jnp.sum(
+            earlier, axis=1, keepdims=True)
+        angles = place * frequency[...]
+        sines = jnp.sin(angles)
+        cos_ref[where, :] = jnp.cos(angles)
+        sin_ref[where, :] = jnp.where(first_half, -sines, sines)
+        return carry
+
+    lax.fori_loop(0, blocks, tables, 0)
     for copy in owned:
         copy.wait()
 
@@ -638,6 +662,8 @@
         return carry
 
     lax.fori_loop(0, blocks, prepare, 0)
+    for copy in results[:5]:
+        copy.start()
     pass_on(1)
 
     def attend(i, hp):
@@ -708,6 +734,12 @@
         @pl.when(s == per - 1)
         def _():
             receive(1)
+            for copy in results[5:7]:
+                copy.start()
+
+        @pl.when(s == blocks * per)
+        def _():
+            results[7].start()
 
         @pl.when(live & (hp == per - 1))
         def _():
@@ -724,6 +756,8 @@
     lax.fori_loop(0, per + line.steps, step, 0)
     line.drain()
     save_own().wait()
+    for copy in results:
+        copy.wait()
 
     def settle(p, carry):
         for k in range(1, chips):
@@ -743,7 +777,7 @@
             forward(kind, c, core).wait_send()
 
 
-def attention_head(x, gain_part, query, keyval, out, cosines, sines, seg_col, seg_row, gateup, down, n, m, cid, size,
+def attention_head(x, gain_part, query, keyval, out, frequency, seg_row, gateup, down, n, m, cid, size,
                    chunks=32, lag=2):
     rows, width = x.shape
     q_width = query.shape[1]
@@ -760,13 +794,14 @@
     return pl.pallas_call(
         functools.partial(head_kernel, n, m, chunks, lag, norm_eps, size, pairs),
         out_shape=(
-            shape((rows, width), low), shape((rows, q_width), low), shape((rows, q_width), low),
-            shape((rows, 128), low), shape((rows, 128), low), shape((blocks, pairs, 1, 2 * size), jnp.float32),
-            shape((width, q_width + 128), low), shape((width, q_width), low), shape((2, width), jnp.float32),
-            shape((width, 3 * ff), low),
+            shape((rows, width), low), shape((2, width), jnp.float32),
+            shape((blocks, pairs, 1, 2 * size), jnp.float32), shape((rows, 1), jnp.int32),
+            shape((rows, 128), jnp.float32), shape((rows, 128), jnp.float32), shape((rows, q_width), low),
+            shape((rows, q_width), low), shape((rows, 128), low), shape((rows, 128), low),
+            shape((width, q_width + 128), low), shape((width, q_width), low), shape((width, 3 * ff), low),
         ),
-        in_specs=[vmem] * 9 + [hbm] * 2,
-        out_specs=(vmem,) * 9 + (hbm,),
+        in_specs=[vmem] * 6 + [hbm] * 3,
+        out_specs=(vmem,) * 4 + (hbm,) * 9,
         scratch_shapes=line_scratch(chunks, rc, width) + [
             pltpu.VMEM((rows, width), low),
             pltpu.VMEM((rows, width), low),
@@ -775,24 +810,35 @@
             pltpu.VMEM((blocks, size, 2 * size), jnp.float32),
             pltpu.VMEM((blocks, 128, size), low),
             pltpu.VMEM((m, 2, width), jnp.float32),
+            pltpu.VMEM((rows, width), low),
+            pltpu.VMEM((rows, 128), jnp.float32),
+            pltpu.VMEM((rows, 128), jnp.float32),
+            pltpu.VMEM((rows, q_width), low),
+            pltpu.VMEM((rows, q_width), low),
+            pltpu.VMEM((rows, 128), low),
+            pltpu.VMEM((rows, 128), low),
+            pltpu.VMEM((width, q_width + 128), low),
+            pltpu.VMEM((width, q_width), low),
             pltpu.VMEM(gateup.shape, jnp.float32),
             pltpu.VMEM(down.shape, jnp.float32),
             pltpu.VMEM((share, 3 * ff), low),
-            dma((m,)), dma((m,)), dma((2, chips)), dma((2, chips)), dma((2, m)), dma((2,)), dma,
+            dma((m,)), dma((m,)), dma((2, chips)), dma((2, chips)), dma((2, m)), dma((2,)), dma, dma((8,)), dma,
             dma((chips, share // 32)), dma((chips, share // 32)), dma((m, share // 32)),
         ],
         compiler_params=pltpu.CompilerParams(collective_id=cid, has_side_effects=True, vmem_limit_bytes=56 << 20),
         cost_estimate=pl.CostEstimate(flops=20 * rows * width * q_width, bytes_accessed=rows * width * 170,
                                       transcendentals=rows * rows * pairs),
-    )(x, gain_part, query, keyval, out, cosines, sines, seg_col, seg_row, gateup, down)
+    )(gain_part, query, keyval, out, frequency, seg_row, x, gateup, down)
 
 
 def back_kernel(n, m, chunks, lag, eps, size, pairs,
-                feed_part, grad_low, gain, q_ref, k_ref, v_ref, mix_ref, lse_ref, cos_ref, sin_ref,
-                seg_col_ref, seg_row_ref, out_w, x_hbm, qkv_hbm, branch_hbm, middle_hbm,
+                feed_part, gain, lse_ref, seg_row_ref,
+                low_hbm, q_hbm, k_hbm, v_hbm, mix_hbm, cos_hbm, sin_hbm, seg_hbm, out_hbm, x_hbm, qkv_hbm,
+                branch_hbm, middle_hbm,
                 layer_hbm, input_hbm, gain_out, reduced,
                 got2, sa2, ra2, sg2, rg2, got4, sa4, ra4, sg4, rg4, feed_sum, part, grad_sum,
-                x, qkv_w, normed, grad_mix, bias, k_turned, grad_k, grad_v, grad_qkv, send, recv,
+                grad_low, q_ref, k_ref, v_ref, mix_ref, cos_ref, sin_ref, seg_col_ref, out_w, x, qkv_w,
+                normed, grad_mix, bias, k_turned, grad_k, grad_v, grad_qkv, send, recv,
                 branch_stage, layer_stage, middle_stage, input_stage,
                 w_sem, branch_sem, middle_sem, layer_sem, input_sem, send_sem, recv_sem):
     rows, width = feed_part.shape
@@ -818,10 +864,12 @@
 
     two = Line(n, chunks, rc, lag, feed_part, got2, feed_sum, (sa2, ra2, sg2, rg2))
     four = Line(n, chunks, rc, lag, part, got4, grad_sum, (sa4, ra4, sg4, rg4), descending)
-    loads = (
-        pltpu.make_async_copy(x_hbm, x, w_sem.at[0]),
-        pltpu.make_async_copy(qkv_hbm, qkv_w, w_sem.at[1]),
-    )
+    loads = [
+        pltpu.make_async_copy(source, target, w_sem.at[k])
+        for k, (source, target) in enumerate((
+            (k_hbm, k_ref), (q_hbm, q_ref), (low_hbm, grad_low), (out_hbm, out_w), (v_hbm, v_ref), (mix_hbm, mix_ref),
+            (cos_hbm, cos_ref), (sin_hbm, sin_ref), (seg_hbm, seg_col_ref), (x_hbm, x), (qkv_hbm, qkv_w)))
+    ]
     for copy in loads:
         copy.start()
 
@@ -861,8 +909,6 @@
         grad_k[i] = jnp.zeros((size, 128), jnp.float32)
         grad_v[i] = jnp.zeros((size, 128), jnp.float32)
         return carry
-
-    lax.fori_loop(0, blocks, prepare, 0)
 
     barrier = pltpu.get_barrier_semaphore()
 
@@ -929,6 +975,7 @@
         @pl.when(s == 0)
         def _():
             wait(loads)
+            lax.fori_loop(0, blocks, prepare, 0)
 
         @pl.when(live & (hp == 0))
         def _():
@@ -950,7 +997,7 @@
 
             def some(r, c):
                 at = pl.ds(pl.multiple_of(s * 2 * rc + r * rc, rc), rc)
-                normed[at, :] = (unit_rows(at)[0] * gain[...]).astype(jnp.bfloat16)
+                normed[at, :] = (unit_rows(at)[0] * gain[0:1, :]).astype(jnp.bfloat16)
                 return c
 
             lax.fori_loop(0, 2, some, 0)
@@ -1030,7 +1077,7 @@
                 where = four.rows(k, d4)
                 unit, inverse = unit_rows(where)
                 grad = grad_sum[where, :].astype(jnp.float32)
-                scaled = grad * gain[...]
+                scaled = grad * gain[0:1, :]
                 inner = jnp.mean(scaled * unit, axis=-1, keepdims=True)
                 input_stage[k] = middle_stage[d4 % 2, k] + inverse * (scaled - unit * inner)
                 gain_out[...] += jnp.sum(grad * unit, axis=0, keepdims=True)
@@ -1086,12 +1133,21 @@
             shape((rows, width), low), shape((rows, width), jnp.float32), shape((1, width), jnp.float32),
             shape((share, cat), jnp.float32),
         ),
-        in_specs=[vmem] * 13 + [hbm] * 4,
+        in_specs=[vmem] * 4 + [hbm] * 13,
         out_specs=(hbm, hbm, vmem, vmem),
         scratch_shapes=line_scratch(chunks, rc, width) + line_scratch(chunks, rc, width) + [
             pltpu.VMEM((rows, width), low),
             pltpu.VMEM((rows, width), low),
             pltpu.VMEM((rows, width), low),
+            pltpu.VMEM((rows, width), low),
+            pltpu.VMEM((rows, q_width), low),
+            pltpu.VMEM((rows, 128), low),
+            pltpu.VMEM((rows, 128), low),
+            pltpu.VMEM((rows, q_width), low),
+            pltpu.VMEM((rows, 128), jnp.float32),
+            pltpu.VMEM((rows, 128), jnp.float32),
+            pltpu.VMEM((rows, 1), jnp.int32),
+            pltpu.VMEM((width, q_width), low),
             pltpu.VMEM((rows, width), low),
             pltpu.VMEM((width, q_width + 128), low),
             pltpu.VMEM((rows, width), low),
@@ -1107,12 +1163,12 @@
             pltpu.VMEM((2, rc, width), low),
             pltpu.VMEM((2, 2, rc, width), jnp.float32),
             pltpu.VMEM((2, rc, width), jnp.float32),
-            dma((2,)), dma((2, 2)), dma((2, 2)), dma((2,)), dma((2,)), dma((m,)), dma((m,)),
+            dma((11,)), dma((2, 2)), dma((2, 2)), dma((2,)), dma((2,)), dma((m,)), dma((m,)),
         ],
         compiler_params=pltpu.CompilerParams(collective_id=cid, has_side_effects=True, vmem_limit_bytes=63 << 20),
         cost_estimate=pl.CostEstimate(flops=40 * rows * width * q_width, bytes_accessed=rows * width * 260,
                                       transcendentals=rows * rows * pairs),
-    )(feed_part, grad_low, gain, q, k, v, mix, lse, cosines, sines, seg_col, seg_row, out_w,
+    )(feed_part, gain, lse, seg_row, grad_low, q, k, v, mix, cosines, sines, seg_col, out_w,
       x, qkv_w, branch, grad_middle)
 
 
@@ -1239,7 +1295,7 @@
     for which in (5, 4, 0):
         for k in range(3):
             loads[3 * which + k].start()
-    norm_out[...] = norm_ref[...]
+    norm_out[0] = norm_ref[0, 0]
     factor = jnp.minimum(1.0, clip_limit / (norm_ref[:1, :1] + 1e-06))
     one, two = correct_ref[0], correct_ref[1]
 
@@ -1338,10 +1394,10 @@
     size = sum(p.size for p in params)
     norm, layer, grad_in, *outs = pl.pallas_call(
         functools.partial(adam_kernel, rates, kv_width),
-        out_shape=(shape((8, 128), jnp.float32), shape(layer.shape, layer.dtype), shape(grad_in.shape, grad_in.dtype))
+        out_shape=(shape((1,), jnp.float32), shape(layer.shape, layer.dtype), shape(grad_in.shape, grad_in.dtype))
         + tuple(shape(p.shape, jnp.float32) for p in params),
         in_specs=[pl.BlockSpec(memory_space=pltpu.SMEM), vmem, vmem] + [hbm] * (4 + len(params)),
-        out_specs=(vmem,) + (hbm,) * (2 + len(params)),
+        out_specs=(pl.BlockSpec(memory_space=pltpu.SMEM),) + (hbm,) * (2 + len(params)),
         scratch_shapes=[pltpu.VMEM(a.shape, a.dtype) for a in (ff_grad, head_grad, layer, grad_in)]
         + [pltpu.VMEM(p.shape, jnp.float32) for p in params]
         + [dma((2,)), dma((len(params),)), dma((len(params),)), dma((2, 4)), dma((2, 4))],
@@ -1360,22 +1416,6 @@
 out_rate = 0.1
 gain_rate = 0.2
 clip_limit = 1.0
-
-
-def positions(segment):
-    length = segment.shape[0]
-    indices = jnp.arange(length, dtype=jnp.int32)
-    earlier = jnp.concatenate([segment[:1] - 1, segment[:-1]])
-    begins = jnp.where(segment != earlier, indices, jnp.zeros_like(indices))
-    return indices - lax.cummax(begins, axis=0)
-
-
-def paired_tables(places):
-    lane = jnp.arange(128, dtype=jnp.int32) % HD
-    frequency = jnp.power(10000.0, -(lane % (HD // 2)).astype(jnp.float32) * (2.0 / HD))
-    angles = places.astype(jnp.float32)[:, None] * frequency[None, :]
-    sines = jnp.sin(angles)
-    return jnp.cos(angles), jnp.where(lane < HD // 2, -sines, sines)
 
 
 def on_device(
@@ -1414,19 +1454,18 @@
     length = tokens.shape[0]
     size = min(256, length)
     segment = segment_ids[0]
-    places = positions(segment)
-    cosines, sines = paired_tables(places)
-    seg_col, seg_row = segment[:, None], segment[None, :]
-    branch, mixture, q, k, v, lse, qkv_weight, out_weight, gain_values, ff_weight = attention_head(
-        tokens, gain_part, w_query, w_keyval.swapaxes(1, 2), w_out, cosines, sines, seg_col, seg_row,
-        w_gateup, w_down, n, m, 1, size
+    seg_row = segment[None, :]
+    lane = jnp.arange(128, dtype=jnp.int32) % (HD // 2)
+    frequency = jnp.power(10000.0, -lane.astype(jnp.float32) * (2.0 / HD))[None, :]
+    (branch, gain_values, lse, seg_col, cosines, sines, mixture, q, k, v, qkv_weight, out_weight, ff_weight) = attention_head(
+        tokens, gain_part, w_query, w_keyval.swapaxes(1, 2), w_out, frequency, seg_row, w_gateup, w_down, n, m, 1, size
     )
     feed_part, grad_middle, grad_branch, gain_grad_two, grad_ff_weight = feed_forward(
-        branch, gain_values[1:], tokens, cotangent, ff_weight, n, 2
+        branch, gain_values, tokens, cotangent, ff_weight, n, 2
     )
     ff_reduced = lax.psum_scatter(grad_ff_weight, "dp", scatter_dimension=0, tiled=True)
     layer_out, input_grad, gain_grad_one, head_reduced = attention_back(
-        feed_part, grad_branch, gain_values[:1], q, k, v, mixture, lse, cosines, sines, seg_col, seg_row,
+        feed_part, grad_branch, gain_values, q, k, v, mixture, lse, cosines, sines, seg_col, seg_row,
         out_weight, tokens, qkv_weight, branch, grad_middle, n, m, 3, size
     )
     gain_grads = jnp.concatenate([gain_grad_one, gain_grad_two])
@@ -1457,7 +1496,7 @@
         weight, first_state, second_state = updated[3 * k : 3 * k + 3]
         group = [first_state, second_state, weight]
         results += [a.swapaxes(1, 2) for a in group] if k == 2 else group
-    return (layer_out, input_grad, norm[0, :1], *results)
+    return (layer_out, input_grad, norm, *results)
 
 
 def solution(mesh):

time: 580 us -> 565 us (0.974)
  no operation moved by 1% of the time
where the time goes in v11:
time: 565 us
  Pallas kernels  546 us (97%)
  between operations  14.8 us (3%)
    pallas_call x1, Pallas kernels, attention_back(): pl.pallas_call(functools.partial(back_kernel, n, m, chunks, lag, norm_eps...  216 us
    pallas_call x1, Pallas kernels, attention_head(): pl.pallas_call(functools.partial(head_kernel, n, m, chunks, lag, norm_eps...  160 us
    pallas_call x1, Pallas kernels, feed_forward(): pl.pallas_call(functools.partial(ff_kernel, n, chunks, lag, norm_eps), ou...  133 us
    pallas_call x1, Pallas kernels, finish_step(): pl.pallas_call(functools.partial(adam_kernel, rates, kv_width), out_shape...  22 us
    pallas_call x1, Pallas kernels, finish_step(): pl.pallas_call(functools.partial(norm_kernel, n, m), out_shape=(shape((8,...  15.3 us
  transfers between devices with their start and end apart: 1, of which 0 were waited for; matrix products, arithmetic and copies ran while one was open for 0% of the time, Pallas kernels for 38%

profile of v11, /device:TPU:0, one launch (start us, length us, event | category | flops | bytes accessed | tf_op | source)
XLA Modules:
  0.0 564.9 jit_solution(15339209672097713830)
XLA Ops:
  7.2 0.0 reduce-scatter.2.cloned.1.call-start
  7.2 0.5 fusion.3.frequency
  7.8 0.7 constant_dynamic-update-slice_fusion.gain_part
  8.5 0.0 copy-start
  8.5 0.6 copy-done
  9.1 159.8 %shard_map.373 = (bf16[1024,2048]{1,0:T(8,128)(2,1)}, f32[2,2048]{1,0:T(2,128)}, f32[4,4,1,512]{3,2,1,0:T(1,128)}, s32[1024,1]{1,0:T(8,128)}, f32[1024,128]{1,0:...) custom-call(f32[2,2048]{1,0:T(2,128)} %copy-done, ...), custom_call_target="tpu_custom_call" | custom-call | flops 21474836480 | bytes 356515840 | tf_op jit(solution)/shard_map/pallas_call | solution.py:794
  168.9 133.2 %shard_map.374 = (bf16[1024,2048]{1,0:T(8,128)(2,1)}, f32[1024,2048]{1,0:T(8,128)}, bf16[1024,2048]{1,0:T(8,128)(2,1)}, f32[1,2048]{1,0:T(1,128)}, bf16[2048,4224]{1,0:T(8,128)(2,1)}) custom-call(bf16[1024,2048]{1,0:T(8,128)(2,1)} %get-tuple-element.66.branch.branch_hbm, f32[2,2048]{1,0:T(2,128)} %get-tuple-element.67.gain, bf16[1024,2048]{1,0:T(8,128)(2,1)} %x_hbm.3, ...), custom_call_target="tpu_custom_call" | custom-call | flops 53150220288 | bytes 314572800 | tf_op jit(solution)/shard_map/pallas_call | solution.py:426
  302.1 0.0 reduce-scatter.2.cloned.1.call-update
  302.9 0.7 pad_maximum_fusion.1.correct_ref
  303.5 0.0 copy-start.1
  303.5 215.9 %shard_map.375 = (bf16[1024,2048]{1,0:T(8,128)(2,1)}, f32[1024,2048]{1,0:T(8,128)}, f32[1,2048]{1,0:T(1,128)}, f32[256,1152]{1,0:T(8,128)}) custom-call(bf16[1024,2048]{1,0:T(8,128)(2,1)} %get-tuple-element.69.feed_part, f32[2,2048]{1,0:T(2,128)} %get-tuple-element.67.gain, f32[4,4,1,512]{3,2,1,0:T(1,128)} %get-tuple-element.70.lse_ref, ...), custom_call_target="tpu_custom_call" | custom-call | flops 42949672960 | bytes 545259520 | tf_op jit(solution)/shard_map/pallas_call | solution.py:1130
  519.4 0.0 copy-done.1
  519.5 1.3 pad_maximum_fusion
  520.8 0.0 reduce-scatter.2.cloned.1.call-done.ff_ref.ff_hbm
  520.8 15.3 %shard_map.376 = (f32[8,128]{1,0:T(8,128)}, f32[2,256]{1,0:T(2,128)}) custom-call(f32[8,2,256]{2,1,0:T(2,128)} %bitcast.13, bf16[256,4224]{1,0:T(8,128)(2,1)} %reduce-scatter.2.cloned.1.call-done.ff_ref.ff_hbm, f32[256,1152]{1,0:T(8,128)} %get-tuple-element.85.head_ref.head_hbm), custom_call_target="tpu_custom_call" | custom-call | tf_op jit(solution)/shard_map/pallas_call | solution.py:1379
  536.1 22.0 %shard_map.377 = (f32[1]{0:T(128)}, bf16[1024,2048]{1,0:T(8,128)(2,1)}, f32[1024,2048]{1,0:T(8,128)}, f32[2,256]{1,0:T(2,128)}, f32[2,256]{1,0:T(2,128)}, /*inde...) custom-call(f32[2]{0:T(128)} %pad_maximum_fusion.1.correct_ref, ...), custom_call_target="tpu_custom_call" | custom-call | flops 82606080 | bytes 99127296 | tf_op jit(solution)/shard_map/pallas_call | solution.py:1395
  (1 shorter events, 0.0 us)
Async XLA Ops:
  7.2 513.6 %reduce-scatter.2.cloned.1.call-start = ((), (), s32[]{:S(2)}) async-start(), calls=%async_computation.1 | async-start | bytes 19464192 | tf_op jit(solution)/shard_map/reduce_scatter | solution.py:1466
  8.5 0.6 copy-start
  303.5 215.9 %copy-start.1 = (f32[1,2048]{1,0:T(1,128)S(1)}, f32[1,2048]{1,0:T(1,128)}, u32[]{:S(2)}) copy-start(f32[1,2048]{1,0:T(1,128)} %get-tuple-element.83) | copy-start | bytes 24580
Sparse Core Ops, SparseCore 0:
  302.3 167.5 reduce-scatter.1

commit v12 on v11

--- a/solution.py
+++ b/solution.py
@@ -963,6 +963,19 @@
         turned = acc * cos_ref[at_rows, :] - swap_halves(acc, first_half) * sin_ref[at_rows, :]
         grad_qkv[at_rows, columns] = turned.astype(jnp.bfloat16)
 
+    def finish(k, carry):
+        owner = lax.rem(dp + k, m)
+        w = owner // owners
+
+        def copy(peer):
+            return pltpu.make_async_remote_copy(
+                src_ref=send.at[0, pl.ds(0, share)], dst_ref=recv.at[peer], send_sem=send_sem.at[peer],
+                recv_sem=recv_sem.at[peer], device_id={"dp": peer}, device_id_type=MESH)
+
+        copy(owner).wait_send()
+        copy(owner).wait_recv()
+        return carry
+
     def step(s, carry):
         two.step(s)
         four.step(s - shift)
@@ -1034,6 +1047,17 @@
                 @pl.when(owner == dp)
                 def _():
                     recv[dp] = send[w, o * share:(o + 1) * share, :]
+
+        @pl.when(s == shift + lead + per)
+        def _():
+            lax.fori_loop(1, m, finish, 0)
+            reduced[...] = recv[0].astype(jnp.float32)
+
+            def add(k, c):
+                reduced[...] += recv[k].astype(jnp.float32)
+                return c
+
+            lax.fori_loop(1, m, add, 0)
 
         e = s - lead + 1
 
@@ -1089,28 +1113,6 @@
     four.drain()
     wait(save_layer(chunks - 1))
     wait(save_input(chunks - 1))
-
-    def finish(k, carry):
-        owner = lax.rem(dp + k, m)
-        w = owner // owners
-
-        def copy(peer):
-            return pltpu.make_async_remote_copy(
-                src_ref=send.at[0, pl.ds(0, share)], dst_ref=recv.at[peer], send_sem=send_sem.at[peer],
-                recv_sem=recv_sem.at[peer], device_id={"dp": peer}, device_id_type=MESH)
-
-        copy(owner).wait_send()
-        copy(owner).wait_recv()
-        return carry
-
-    lax.fori_loop(1, m, finish, 0)
-    reduced[...] = recv[0].astype(jnp.float32)
-
-    def add(k, carry):
-        reduced[...] += recv[k].astype(jnp.float32)
-        return carry
-
-    lax.fori_loop(1, m, add, 0)
 
 
 def attention_back(feed_part, grad_low, gain, q, k, v, mix, lse, cosines, sines, seg_col, seg_row, out_w,
@@ -1172,8 +1174,16 @@
       x, qkv_w, branch, grad_middle)
 
 
-def norm_kernel(n, m, gains_ref, ff_ref, head_ref, norm_ref, gain_ref, line, got_gains, got_line, got_plane, got_squares,
-                send_squares, recv_squares, send_gains, recv_gains, send_line, recv_line, send_plane, recv_plane):
+def norm_kernel(n, m, count, gains_ref, ff_ref, head_ref, *refs):
+    sources, (norm_ref, gain_ref), kept = refs[:count], refs[count:count + 2], refs[count + 2:2 * count + 2]
+    norm_body(n, m, gains_ref, ff_ref, head_ref, sources, kept, norm_ref, gain_ref, *refs[2 * count + 2:])
+
+
+def norm_body(n, m, gains_ref, ff_ref, head_ref, sources, kept, norm_ref, gain_ref, line, got_gains, got_line, got_plane, got_squares,
+                send_squares, recv_squares, send_gains, recv_gains, send_line, recv_line, send_plane, recv_plane, fetch_sem):
+    fetches = [pltpu.make_async_copy(a, b, fetch_sem.at[k]) for k, (a, b) in enumerate(zip(sources, kept))]
+    for copy in fetches:
+        copy.start()
     z = lax.axis_index("tensor")
     d = lax.axis_index("dp")
     share = head_ref.shape[0]
@@ -1258,6 +1268,8 @@
         over_plane(k, d).wait_send()
         over_plane(k, lax.rem(d + m - k, m)).wait_recv()
     norm_ref[...] = jnp.sqrt(summed(got_line, n) + summed(got_plane, m))
+    for copy in fetches:
+        copy.wait()
 
 
 def adam_kernel(rates, kv_width, correct_ref, norm_ref, gain_ref, ff_hbm, head_hbm, layer_hbm, input_hbm, *refs):
@@ -1271,12 +1283,11 @@
     ff = outs[12].shape[2]
     sub = 32
 
+    saves = [pltpu.make_async_copy(held[k], outs[k], save_sem.at[k]) for k in range(3 * count)]
     grads = (
+        pltpu.make_async_copy(head_hbm, head_ref, grad_sem.at[1]),
         pltpu.make_async_copy(ff_hbm, ff_grad, grad_sem.at[0]),
-        pltpu.make_async_copy(head_hbm, head_ref, grad_sem.at[1]),
     )
-    loads = [pltpu.make_async_copy(params[k], held[k], load_sem.at[k]) for k in range(3 * count)]
-    saves = [pltpu.make_async_copy(held[k], outs[k], save_sem.at[k]) for k in range(3 * count)]
     quarter = layer_hbm.shape[0] // 4
     arrive, depart = [], []
     for k in range(4):
@@ -1285,49 +1296,43 @@
                 ((layer_hbm, layer_held, layer_out), (input_hbm, input_held, input_out))):
             arrive.append(pltpu.make_async_copy(source.at[at], kept.at[at], in_sem.at[t, k]))
             depart.append(pltpu.make_async_copy(kept.at[at], target.at[at], back_sem.at[t, k]))
+    loads = [pltpu.make_async_copy(params[k], held[k], load_sem.at[k]) for k in range(12)]
     for copy in grads:
         copy.start()
-    for which in (1, 3, 2):
-        for k in range(3):
-            loads[3 * which + k].start()
+    for copy in loads:
+        copy.start()
     for copy in arrive:
         copy.start()
-    for which in (5, 4, 0):
-        for k in range(3):
-            loads[3 * which + k].start()
     norm_out[0] = norm_ref[0, 0]
     factor = jnp.minimum(1.0, clip_limit / (norm_ref[:1, :1] + 1e-06))
     one, two = correct_ref[0], correct_ref[1]
 
     def update(which, where, gradient):
         rate, decay = rates[which]
-        p, a, b = (held[3 * which + k] for k in range(3))
+        p, a, b = ((params if which > 3 else held)[3 * which + k] for k in range(3))
+        p_new, a_new, b_new = (held[3 * which + k] for k in range(3))
         gradient = gradient * factor
         first = beta_first * a[where] + (1.0 - beta_first) * gradient
         second = beta_second * b[where] + (1.0 - beta_second) * gradient * gradient
-        a[where] = first
-        b[where] = second
+        a_new[where] = first
+        b_new[where] = second
         change = first / one / (jnp.sqrt(second / two) + adam_eps)
         old = p[where]
-        p[where] = old - rate * (change + decay * old)
-
-    def load(which):
-        for k in range(3):
-            loads[3 * which + k].wait()
+        p_new[where] = old - rate * (change + decay * old)
 
     def save(which):
         for k in range(3):
             saves[3 * which + k].start()
 
     def by_rows(which, body):
-        load(which)
         lax.fori_loop(0, share // sub, lambda r, c: (body(pl.ds(pl.multiple_of(r * sub, sub), sub)), c)[1], 0)
         save(which)
 
     for copy in grads:
         copy.wait()
+    for copy in loads:
+        copy.wait()
     by_rows(1, lambda where: update(1, (where, slice(None)), head_ref[where, :q_width]))
-    load(3)
 
     def out_tile(t, carry):
         at = pl.ds(pl.multiple_of(t * 128, 128), 128)
@@ -1338,7 +1343,6 @@
     lax.fori_loop(0, outs[9].shape[0] // 128, out_tile, 0)
     save(3)
 
-    load(2)
     both = head_ref[:, q_width:q_width + 2 * kv_width].T
     for t in (0, 1):
         update(2, (t, slice(None), slice(None)), both[t * kv_width:(t + 1) * kv_width])
@@ -1348,10 +1352,10 @@
         for t in (0, 1):
             update(4, (t, where, slice(None)), ff_grad[where, t * ff:(t + 1) * ff].astype(jnp.float32))
 
+
     for came, left in zip(arrive, depart):
         came.wait()
         left.start()
-    load(5)
 
     def down_tile(t, carry):
         at = pl.ds(pl.multiple_of(t * 128, 128), 128)
@@ -1362,7 +1366,6 @@
     lax.fori_loop(0, ff // 128, down_tile, 0)
     save(5)
     by_rows(4, gateup_rows)
-    load(0)
     update(0, (slice(None), slice(None)), gain_ref[...])
     save(0)
     for copy in saves + depart:
@@ -1376,11 +1379,13 @@
     hbm = pl.BlockSpec(memory_space=pl.ANY)
     dma = pltpu.SemaphoreType.DMA
     shape = jax.ShapeDtypeStruct
-    norm, gain = pl.pallas_call(
-        functools.partial(norm_kernel, n, m),
-        out_shape=(shape((8, 128), jnp.float32), shape((2, share), jnp.float32)),
-        in_specs=[vmem, vmem, vmem],
-        out_specs=(vmem, vmem),
+    fetched = list(params[12:])
+    norm, gain, *kept = pl.pallas_call(
+        functools.partial(norm_kernel, n, m, len(fetched)),
+        out_shape=(shape((8, 128), jnp.float32), shape((2, share), jnp.float32))
+        + tuple(pltpu.VMEM(a.shape, a.dtype) for a in fetched),
+        in_specs=[vmem, vmem, vmem] + [pl.BlockSpec(memory_space=pltpu.HBM)] * len(fetched),
+        out_specs=(vmem,) * (2 + len(fetched)),
         scratch_shapes=[
             pltpu.VMEM((3, 8, 128), jnp.float32),
             pltpu.VMEM((m, 2, share), jnp.float32),
@@ -1388,22 +1393,23 @@
             pltpu.VMEM((m, 8, 128), jnp.float32),
             pltpu.VMEM((m, 8, 128), jnp.float32),
             dma((m,)), dma((m,)), dma((m,)), dma((m,)), dma((n,)), dma((n,)), dma((m,)), dma((m,)),
+            dma((len(fetched),)),
         ],
-        compiler_params=pltpu.CompilerParams(collective_id=cid, has_side_effects=True),
-    )(parts, ff_grad, head_grad)
+        compiler_params=pltpu.CompilerParams(collective_id=cid, has_side_effects=True, vmem_limit_bytes=40 << 20),
+    )(parts, ff_grad, head_grad, *fetched)
     size = sum(p.size for p in params)
     norm, layer, grad_in, *outs = pl.pallas_call(
         functools.partial(adam_kernel, rates, kv_width),
         out_shape=(shape((1,), jnp.float32), shape(layer.shape, layer.dtype), shape(grad_in.shape, grad_in.dtype))
         + tuple(shape(p.shape, jnp.float32) for p in params),
-        in_specs=[pl.BlockSpec(memory_space=pltpu.SMEM), vmem, vmem] + [hbm] * (4 + len(params)),
+        in_specs=[pl.BlockSpec(memory_space=pltpu.SMEM), vmem, vmem] + [hbm] * 16 + [vmem] * len(fetched),
         out_specs=(pl.BlockSpec(memory_space=pltpu.SMEM),) + (hbm,) * (2 + len(params)),
         scratch_shapes=[pltpu.VMEM(a.shape, a.dtype) for a in (ff_grad, head_grad, layer, grad_in)]
         + [pltpu.VMEM(p.shape, jnp.float32) for p in params]
-        + [dma((2,)), dma((len(params),)), dma((len(params),)), dma((2, 4)), dma((2, 4))],
-        compiler_params=pltpu.CompilerParams(vmem_limit_bytes=63 << 20),
+        + [dma((2,)), dma((12,)), dma((len(params),)), dma((2, 4)), dma((2, 4))],
+        compiler_params=pltpu.CompilerParams(vmem_limit_bytes=34 << 20),
         cost_estimate=pl.CostEstimate(flops=20 * size, bytes_accessed=24 * size, transcendentals=size),
-    )(correct, norm, gain, ff_grad, head_grad, layer, grad_in, *params)
+    )(correct, norm, gain, ff_grad, head_grad, layer, grad_in, *params[:12], *kept)
     return norm, layer, grad_in, outs
 
 

time: 565 us -> 562 us (level)
  no operation moved by 1% of the time
where the time goes in v12:
time: 562 us
  Pallas kernels  543 us (97%)
  between operations  15.1 us (3%)
    pallas_call x1, Pallas kernels, attention_back(): pl.pallas_call(functools.partial(back_kernel, n, m, chunks, lag, norm_eps...  215 us
    pallas_call x1, Pallas kernels, attention_head(): pl.pallas_call(functools.partial(head_kernel, n, m, chunks, lag, norm_eps...  160 us
    pallas_call x1, Pallas kernels, feed_forward(): pl.pallas_call(functools.partial(ff_kernel, n, chunks, lag, norm_eps), ou...  133 us
    pallas_call x1, Pallas kernels, finish_step(): pl.pallas_call(functools.partial(adam_kernel, rates, kv_width), out_shape...  20.3 us
    pallas_call x1, Pallas kernels, finish_step(): pl.pallas_call(functools.partial(norm_kernel, n, m, len(fetched)), out_sh...  14.6 us
  transfers between devices with their start and end apart: 1, of which 0 were waited for; matrix products, arithmetic and copies ran while one was open for 0% of the time, Pallas kernels for 38%

profile of v12, /device:TPU:0, one launch (start us, length us, event | category | flops | bytes accessed | tf_op | source)
XLA Modules:
  0.0 562.2 jit_solution(9400527278415348546)
XLA Ops:
  7.2 0.0 reduce-scatter.2.cloned.1.call-start
  7.2 0.5 fusion.3.frequency
  7.8 0.7 constant_dynamic-update-slice_fusion.gain_part
  8.5 0.0 copy-start.15
  8.5 0.6 copy-done.15
  9.1 159.8 %shard_map.373 = (bf16[1024,2048]{1,0:T(8,128)(2,1)}, f32[2,2048]{1,0:T(2,128)}, f32[4,4,1,512]{3,2,1,0:T(1,128)}, s32[1024,1]{1,0:T(8,128)}, f32[1024,128]{1,0:...) custom-call(f32[2,2048]{1,0:T(2,128)} %copy-done.15, ...), custom_call_target="tpu_custom_call" | custom-call | flops 21474836480 | bytes 356515840 | tf_op jit(solution)/shard_map/pallas_call | solution.py:794
  168.9 133.4 %shard_map.374 = (bf16[1024,2048]{1,0:T(8,128)(2,1)}, f32[1024,2048]{1,0:T(8,128)}, bf16[1024,2048]{1,0:T(8,128)(2,1)}, f32[1,2048]{1,0:T(1,128)}, bf16[2048,4224]{1,0:T(8,128)(2,1)}) custom-call(bf16[1024,2048]{1,0:T(8,128)(2,1)} %get-tuple-element.72.branch.branch_hbm, f32[2,2048]{1,0:T(2,128)} %get-tuple-element.73.gain, bf16[1024,2048]{1,0:T(8,128)(2,1)} %x_hbm.3, ...), custom_call_target="tpu_custom_call" | custom-call | flops 53150220288 | bytes 314572800 | tf_op jit(solution)/shard_map/pallas_call | solution.py:426
  302.3 0.0 reduce-scatter.2.cloned.1.call-update
  303.1 0.1 pad_maximum_fusion.1.correct_ref
  303.1 0.0 copy-start.16
  303.1 214.9 %shard_map.375 = (bf16[1024,2048]{1,0:T(8,128)(2,1)}, f32[1024,2048]{1,0:T(8,128)}, f32[1,2048]{1,0:T(1,128)}, f32[256,1152]{1,0:T(8,128)}) custom-call(bf16[1024,2048]{1,0:T(8,128)(2,1)} %get-tuple-element.75.feed_part, f32[2,2048]{1,0:T(2,128)} %get-tuple-element.73.gain, f32[4,4,1,512]{3,2,1,0:T(1,128)} %get-tuple-element.76.lse_ref, ...), custom_call_target="tpu_custom_call" | custom-call | flops 42949672960 | bytes 545259520 | tf_op jit(solution)/shard_map/pallas_call | solution.py:1132
  518.1 0.0 copy-done.16
  518.1 0.7 pad_maximum_fusion
  518.8 0.0 reduce-scatter.2.cloned.1.call-done.ff_ref.ff_hbm
  518.8 0.0 copy-start.1
  518.8 1.3 copy-done.1
  520.1 0.0 copy-start
  520.1 0.0 copy-start.2
  520.1 0.0 copy-start.3
  520.1 0.0 copy-start.4
  520.1 0.0 copy-start.5
  520.1 0.0 copy-start.6
  520.1 0.0 copy-start.7
  520.1 0.0 copy-start.8
  520.2 0.0 copy-start.9
  520.2 0.0 copy-start.10
  520.2 0.0 copy-start.11
  520.2 0.0 copy-start.12
  520.2 0.0 copy-start.13
  520.2 0.0 copy-start.14
  520.2 14.6 %shard_map.376 = (f32[8,128]{1,0:T(8,128)S(1)}, f32[2,256]{1,0:T(2,128)S(1)}, f32[2,256,1408]{2,1,0:T(8,128)S(1)}, f32[2,256,1408]{2,1,0:T(8,128)S(1)}, f32[2,25...) custom-call(f32[8,2,256]{2,1,0:T(2,128)S(1)} %bitcast.13, ...), custom_call_target="tpu_custom_call" | custom-call | tf_op jit(solution)/shard_map/pallas_call | solution.py:1383
  534.9 0.0 copy-done
  534.9 0.0 copy-done.2
  534.9 0.0 copy-done.3
  534.9 0.0 copy-done.4
  534.9 0.0 copy-done.5
  534.9 0.0 copy-done.6
  534.9 0.0 copy-done.7
  534.9 0.0 copy-done.8
  534.9 0.0 copy-done.9
  534.9 0.0 copy-done.10
  535.0 0.0 copy-done.11
  535.0 0.0 copy-done.12
  535.0 0.0 copy-done.13
  535.0 0.0 copy-done.14
  535.0 20.3 %shard_map.377 = (f32[1]{0:T(128)}, bf16[1024,2048]{1,0:T(8,128)(2,1)}, f32[1024,2048]{1,0:T(8,128)}, f32[2,256]{1,0:T(2,128)}, f32[2,256]{1,0:T(2,128)}, /*inde...) custom-call(f32[2]{0:T(128)S(1)} %pad_maximum_fusion.1.correct_ref, ...), custom_call_target="tpu_custom_call" | custom-call | flops 82606080 | bytes 99127296 | tf_op jit(solution)/shard_map/pallas_call | solution.py:1401
  (1 shorter events, 0.0 us)
Async XLA Ops:
  7.2 511.6 %reduce-scatter.2.cloned.1.call-start = ((), (), s32[]{:S(2)}) async-start(), calls=%async_computation.1 | async-start | bytes 19464192 | tf_op jit(solution)/shard_map/reduce_scatter | solution.py:1472
  8.5 0.6 copy-start.15
  303.1 214.9 %copy-start.16 = (f32[1,2048]{1,0:T(1,128)S(1)}, f32[1,2048]{1,0:T(1,128)}, u32[]{:S(2)}) copy-start(f32[1,2048]{1,0:T(1,128)} %get-tuple-element.89) | copy-start | bytes 24580
  518.8 1.3 copy-start.1
  520.1 14.8 %copy-start = (bf16[256,4224]{1,0:T(8,128)(2,1)S(1)}, bf16[256,4224]{1,0:T(8,128)(2,1)}, u32[]{:S(2)}) copy-start(bf16[256,4224]{1,0:T(8,128)(2,1)} %reduce-scatter.2.cloned.1.call-done.ff_ref.ff_hbm) | copy-start | bytes 6488068
  520.1 14.8 %copy-start.2 = (f32[256,1152]{1,0:T(8,128)S(1)}, f32[256,1152]{1,0:T(8,128)}, u32[]{:S(2)}) copy-start(f32[256,1152]{1,0:T(8,128)} %get-tuple-element.91.head_ref.head_hbm) | copy-start | bytes 3538948
  520.1 14.8 %copy-start.3 = (f32[256,512]{1,0:T(8,128)S(1)}, f32[256,512]{1,0:T(8,128)}, u32[]{:S(2)}) copy-start(f32[256,512]{1,0:T(8,128)} %refs_3_.3) | copy-start | bytes 1572868
  520.1 14.8 %copy-start.4 = (f32[512,256]{1,0:T(8,128)S(1)}, f32[512,256]{1,0:T(8,128)}, u32[]{:S(2)}) copy-start(f32[512,256]{1,0:T(8,128)} %refs_9_.1) | copy-start | bytes 1572868
  520.1 14.8 %copy-start.5 = (f32[256,512]{1,0:T(8,128)S(1)}, f32[256,512]{1,0:T(8,128)}, u32[]{:S(2)}) copy-start(f32[256,512]{1,0:T(8,128)} %refs_4_.3) | copy-start | bytes 1572868
  520.1 14.8 %copy-start.6 = (f32[256,512]{1,0:T(8,128)S(1)}, f32[256,512]{1,0:T(8,128)}, u32[]{:S(2)}) copy-start(f32[256,512]{1,0:T(8,128)} %refs_5_.3) | copy-start | bytes 1572868
  520.1 14.8 %copy-start.7 = (f32[512,256]{1,0:T(8,128)S(1)}, f32[512,256]{1,0:T(8,128)}, u32[]{:S(2)}) copy-start(f32[512,256]{1,0:T(8,128)} %refs_10_.1) | copy-start | bytes 1572868
  520.1 14.8 %copy-start.8 = (f32[512,256]{1,0:T(8,128)S(1)}, f32[512,256]{1,0:T(8,128)}, u32[]{:S(2)}) copy-start(f32[512,256]{1,0:T(8,128)} %refs_11_.1) | copy-start | bytes 1572868
  520.2 14.8 %copy-start.9 = (f32[2,256,64]{1,2,0:T(8,128)S(1)}, f32[2,256,64]{1,2,0:T(8,128)}, u32[]{:S(2)}) copy-start(f32[2,256,64]{1,2,0:T(8,128)} %param.32) | copy-start | bytes 393220
  520.2 14.8 %copy-start.10 = (f32[2,256,64]{1,2,0:T(8,128)S(1)}, f32[2,256,64]{1,2,0:T(8,128)}, u32[]{:S(2)}) copy-start(f32[2,256,64]{1,2,0:T(8,128)} %param.33) | copy-start | bytes 393220
  520.2 14.8 %copy-start.11 = (f32[2,256,64]{1,2,0:T(8,128)S(1)}, f32[2,256,64]{1,2,0:T(8,128)}, u32[]{:S(2)}) copy-start(f32[2,256,64]{1,2,0:T(8,128)} %param.34) | copy-start | bytes 393220
  520.2 14.8 %copy-start.12 = (f32[2,256]{1,0:T(2,128)S(1)}, f32[2,256]{1,0:T(2,128)}, u32[]{:S(2)}) copy-start(f32[2,256]{1,0:T(2,128)} %refs_0_.3) | copy-start | bytes 6148
  520.2 14.8 %copy-start.13 = (f32[2,256]{1,0:T(2,128)S(1)}, f32[2,256]{1,0:T(2,128)}, u32[]{:S(2)}) copy-start(f32[2,256]{1,0:T(2,128)} %refs_1_.3) | copy-start | bytes 6148
  520.2 14.8 %copy-start.14 = (f32[2,256]{1,0:T(2,128)S(1)}, f32[2,256]{1,0:T(2,128)}, u32[]{:S(2)}) copy-start(f32[2,256]{1,0:T(2,128)} %refs_2_.3) | copy-start | bytes 6148
Sparse Core Ops, SparseCore 0:
  302.5 166.6 reduce-scatter.1

commit v13 on v12

--- a/solution.py
+++ b/solution.py
@@ -1316,7 +1316,7 @@
         second = beta_second * b[where] + (1.0 - beta_second) * gradient * gradient
         a_new[where] = first
         b_new[where] = second
-        change = first / one / (jnp.sqrt(second / two) + adam_eps)
+        change = first * one / (jnp.sqrt(second * two) + adam_eps)
         old = p[where]
         p_new[where] = old - rate * (change + decay * old)
 
@@ -1330,6 +1330,29 @@
 
     for copy in grads:
         copy.wait()
+
+    def gateup_rows(where):
+        for t in (0, 1):
+            update(4, (t, where, slice(None)), ff_grad[where, t * ff:(t + 1) * ff].astype(jnp.float32))
+
+    by_rows(4, gateup_rows)
+
+    def pass_on(begin, end):
+        for came, left in zip(arrive[begin:end], depart[begin:end]):
+            came.wait()
+            left.start()
+
+    pass_on(0, 4)
+
+    def down_tile(t, carry):
+        at = pl.ds(pl.multiple_of(t * 128, 128), 128)
+        source = pl.ds(pl.multiple_of(2 * ff + t * 128, 128), 128)
+        update(5, (at, slice(None)), ff_grad[:, source].astype(jnp.float32).T)
+        return carry
+
+    lax.fori_loop(0, ff // 128, down_tile, 0)
+    save(5)
+    pass_on(4, 8)
     for copy in loads:
         copy.wait()
     by_rows(1, lambda where: update(1, (where, slice(None)), head_ref[where, :q_width]))
@@ -1347,25 +1370,6 @@
     for t in (0, 1):
         update(2, (t, slice(None), slice(None)), both[t * kv_width:(t + 1) * kv_width])
     save(2)
-
-    def gateup_rows(where):
-        for t in (0, 1):
-            update(4, (t, where, slice(None)), ff_grad[where, t * ff:(t + 1) * ff].astype(jnp.float32))
-
-
-    for came, left in zip(arrive, depart):
-        came.wait()
-        left.start()
-
-    def down_tile(t, carry):
-        at = pl.ds(pl.multiple_of(t * 128, 128), 128)
-        source = pl.ds(pl.multiple_of(2 * ff + t * 128, 128), 128)
-        update(5, (at, slice(None)), ff_grad[:, source].astype(jnp.float32).T)
-        return carry
-
-    lax.fori_loop(0, ff // 128, down_tile, 0)
-    save(5)
-    by_rows(4, gateup_rows)
     update(0, (slice(None), slice(None)), gain_ref[...])
     save(0)
     for copy in saves + depart:
@@ -1476,7 +1480,7 @@
     )
     gain_grads = jnp.concatenate([gain_grad_one, gain_grad_two])
     step_float = step_count[0].astype(jnp.float32)
-    correct = jnp.stack([1.0 - jnp.power(beta_first, step_float), 1.0 - jnp.power(beta_second, step_float)])
+    correct = 1.0 / jnp.stack([1.0 - jnp.power(beta_first, step_float), 1.0 - jnp.power(beta_second, step_float)])
     params = (
         (norm_gains, gains_first, gains_second),
         (w_query, query_first, query_second),

time: 562 us -> 558 us (level)
  transfers between devices with their start and end apart: 1 -> 1, of which waited for: 0 -> 0; matrix products, arithmetic and copies ran while one was open for 0% -> 0% of each run, Pallas kernels for 38% -> 39%
where the time goes in v13:
time: 558 us
  Pallas kernels  539 us (97%)
  between operations  15.1 us (3%)
    pallas_call x1, Pallas kernels, attention_back(): pl.pallas_call(functools.partial(back_kernel, n, m, chunks, lag, norm_eps...  215 us
    pallas_call x1, Pallas kernels, attention_head(): pl.pallas_call(functools.partial(head_kernel, n, m, chunks, lag, norm_eps...  160 us
    pallas_call x1, Pallas kernels, feed_forward(): pl.pallas_call(functools.partial(ff_kernel, n, chunks, lag, norm_eps), ou...  133 us
    pallas_call x1, Pallas kernels, finish_step(): pl.pallas_call(functools.partial(adam_kernel, rates, kv_width), out_shape...  15.8 us
    pallas_call x1, Pallas kernels, finish_step(): pl.pallas_call(functools.partial(norm_kernel, n, m, len(fetched)), out_sh...  14.6 us
  transfers between devices with their start and end apart: 1, of which 0 were waited for; matrix products, arithmetic and copies ran while one was open for 0% of the time, Pallas kernels for 39%

profile of v13, /device:TPU:0, one launch (start us, length us, event | category | flops | bytes accessed | tf_op | source)
XLA Modules:
  0.0 557.6 jit_solution(10994822934123412938)
XLA Ops:
  7.2 0.0 reduce-scatter.2.cloned.1.call-start
  7.2 0.5 fusion.3.frequency
  7.8 0.7 constant_dynamic-update-slice_fusion.gain_part
  8.5 0.0 copy-start.15
  8.5 0.6 copy-done.15
  9.1 159.8 %shard_map.373 = (bf16[1024,2048]{1,0:T(8,128)(2,1)}, f32[2,2048]{1,0:T(2,128)}, f32[4,4,1,512]{3,2,1,0:T(1,128)}, s32[1024,1]{1,0:T(8,128)}, f32[1024,128]{1,0:...) custom-call(f32[2,2048]{1,0:T(2,128)} %copy-done.15, ...), custom_call_target="tpu_custom_call" | custom-call | flops 21474836480 | bytes 356515840 | tf_op jit(solution)/shard_map/pallas_call | solution.py:794
  168.9 133.4 %shard_map.374 = (bf16[1024,2048]{1,0:T(8,128)(2,1)}, f32[1024,2048]{1,0:T(8,128)}, bf16[1024,2048]{1,0:T(8,128)(2,1)}, f32[1,2048]{1,0:T(1,128)}, bf16[2048,4224]{1,0:T(8,128)(2,1)}) custom-call(bf16[1024,2048]{1,0:T(8,128)(2,1)} %get-tuple-element.72.branch.branch_hbm, f32[2,2048]{1,0:T(2,128)} %get-tuple-element.73.gain, bf16[1024,2048]{1,0:T(8,128)(2,1)} %x_hbm.3, ...), custom_call_target="tpu_custom_call" | custom-call | flops 53150220288 | bytes 314572800 | tf_op jit(solution)/shard_map/pallas_call | solution.py:426
  302.3 0.0 reduce-scatter.2.cloned.1.call-update
  303.1 0.1 maximum_divide_fusion.correct_ref
  303.1 0.0 copy-start.16
  303.2 214.9 %shard_map.375 = (bf16[1024,2048]{1,0:T(8,128)(2,1)}, f32[1024,2048]{1,0:T(8,128)}, f32[1,2048]{1,0:T(1,128)}, f32[256,1152]{1,0:T(8,128)}) custom-call(bf16[1024,2048]{1,0:T(8,128)(2,1)} %get-tuple-element.75.feed_part, f32[2,2048]{1,0:T(2,128)} %get-tuple-element.73.gain, f32[4,4,1,512]{3,2,1,0:T(1,128)} %get-tuple-element.76.lse_ref, ...), custom_call_target="tpu_custom_call" | custom-call | flops 42949672960 | bytes 545259520 | tf_op jit(solution)/shard_map/pallas_call | solution.py:1132
  518.0 0.0 copy-done.16
  518.1 0.7 pad_maximum_fusion
  518.8 0.0 reduce-scatter.2.cloned.1.call-done.ff_ref.ff_hbm
  518.8 0.0 copy-start.1
  518.8 1.3 copy-done.1
  520.1 0.0 copy-start
  520.1 0.0 copy-start.2
  520.1 0.0 copy-start.3
  520.1 0.0 copy-start.4
  520.1 0.0 copy-start.5
  520.1 0.0 copy-start.6
  520.1 0.0 copy-start.7
  520.1 0.0 copy-start.8
  520.1 0.0 copy-start.9
  520.2 0.0 copy-start.10
  520.2 0.0 copy-start.11
  520.2 0.0 copy-start.12
  520.2 0.0 copy-start.13
  520.2 0.0 copy-start.14
  520.2 14.6 %shard_map.376 = (f32[8,128]{1,0:T(8,128)S(1)}, f32[2,256]{1,0:T(2,128)S(1)}, f32[2,256,1408]{2,1,0:T(8,128)S(1)}, f32[2,256,1408]{2,1,0:T(8,128)S(1)}, f32[2,25...) custom-call(f32[8,2,256]{2,1,0:T(2,128)S(1)} %bitcast.13, ...), custom_call_target="tpu_custom_call" | custom-call | tf_op jit(solution)/shard_map/pallas_call | solution.py:1387
  534.8 0.0 copy-done
  534.8 0.0 copy-done.2
  534.9 0.0 copy-done.3
  534.9 0.0 copy-done.4
  534.9 0.0 copy-done.5
  534.9 0.0 copy-done.6
  534.9 0.0 copy-done.7
  534.9 0.0 copy-done.8
  534.9 0.0 copy-done.9
  534.9 0.0 copy-done.10
  534.9 0.0 copy-done.11
  534.9 0.0 copy-done.12
  535.0 0.0 copy-done.13
  535.0 0.0 copy-done.14
  535.0 15.8 %shard_map.377 = (f32[1]{0:T(128)}, bf16[1024,2048]{1,0:T(8,128)(2,1)}, f32[1024,2048]{1,0:T(8,128)}, f32[2,256]{1,0:T(2,128)}, f32[2,256]{1,0:T(2,128)}, /*inde...) custom-call(f32[2]{0:T(128)S(1)} %maximum_divide_fusion.correct_ref,, ...), custom_call_target="tpu_custom_call" | custom-call | flops 82606080 | bytes 99127296 | tf_op jit(solution)/shard_map/pallas_call | solution.py:1405
  (1 shorter events, 0.0 us)
Async XLA Ops:
  7.2 511.6 %reduce-scatter.2.cloned.1.call-start = ((), (), s32[]{:S(2)}) async-start(), calls=%async_computation.1 | async-start | bytes 19464192 | tf_op jit(solution)/shard_map/reduce_scatter | solution.py:1476
  8.5 0.6 copy-start.15
  303.1 214.9 %copy-start.16 = (f32[1,2048]{1,0:T(1,128)S(1)}, f32[1,2048]{1,0:T(1,128)}, u32[]{:S(2)}) copy-start(f32[1,2048]{1,0:T(1,128)} %get-tuple-element.89) | copy-start | bytes 24580
  518.8 1.3 copy-start.1
  520.1 14.8 %copy-start = (bf16[256,4224]{1,0:T(8,128)(2,1)S(1)}, bf16[256,4224]{1,0:T(8,128)(2,1)}, u32[]{:S(2)}) copy-start(bf16[256,4224]{1,0:T(8,128)(2,1)} %reduce-scatter.2.cloned.1.call-done.ff_ref.ff_hbm) | copy-start | bytes 6488068
  520.1 14.8 %copy-start.2 = (f32[256,1152]{1,0:T(8,128)S(1)}, f32[256,1152]{1,0:T(8,128)}, u32[]{:S(2)}) copy-start(f32[256,1152]{1,0:T(8,128)} %get-tuple-element.91.head_ref.head_hbm) | copy-start | bytes 3538948
  520.1 14.8 %copy-start.3 = (f32[256,512]{1,0:T(8,128)S(1)}, f32[256,512]{1,0:T(8,128)}, u32[]{:S(2)}) copy-start(f32[256,512]{1,0:T(8,128)} %refs_3_.3) | copy-start | bytes 1572868
  520.1 14.8 %copy-start.4 = (f32[512,256]{1,0:T(8,128)S(1)}, f32[512,256]{1,0:T(8,128)}, u32[]{:S(2)}) copy-start(f32[512,256]{1,0:T(8,128)} %refs_9_.1) | copy-start | bytes 1572868
  520.1 14.8 %copy-start.5 = (f32[256,512]{1,0:T(8,128)S(1)}, f32[256,512]{1,0:T(8,128)}, u32[]{:S(2)}) copy-start(f32[256,512]{1,0:T(8,128)} %refs_4_.3) | copy-start | bytes 1572868
  520.1 14.8 %copy-start.6 = (f32[256,512]{1,0:T(8,128)S(1)}, f32[256,512]{1,0:T(8,128)}, u32[]{:S(2)}) copy-start(f32[256,512]{1,0:T(8,128)} %refs_5_.3) | copy-start | bytes 1572868
  520.1 14.8 %copy-start.7 = (f32[512,256]{1,0:T(8,128)S(1)}, f32[512,256]{1,0:T(8,128)}, u32[]{:S(2)}) copy-start(f32[512,256]{1,0:T(8,128)} %refs_10_.1) | copy-start | bytes 1572868
  520.1 14.8 %copy-start.8 = (f32[512,256]{1,0:T(8,128)S(1)}, f32[512,256]{1,0:T(8,128)}, u32[]{:S(2)}) copy-start(f32[512,256]{1,0:T(8,128)} %refs_11_.1) | copy-start | bytes 1572868
  520.1 14.8 %copy-start.9 = (f32[2,256,64]{1,2,0:T(8,128)S(1)}, f32[2,256,64]{1,2,0:T(8,128)}, u32[]{:S(2)}) copy-start(f32[2,256,64]{1,2,0:T(8,128)} %param.32) | copy-start | bytes 393220
  520.2 14.8 %copy-start.10 = (f32[2,256,64]{1,2,0:T(8,128)S(1)}, f32[2,256,64]{1,2,0:T(8,128)}, u32[]{:S(2)}) copy-start(f32[2,256,64]{1,2,0:T(8,128)} %param.33) | copy-start | bytes 393220
  520.2 14.8 %copy-start.11 = (f32[2,256,64]{1,2,0:T(8,128)S(1)}, f32[2,256,64]{1,2,0:T(8,128)}, u32[]{:S(2)}) copy-start(f32[2,256,64]{1,2,0:T(8,128)} %param.34) | copy-start | bytes 393220
  520.2 14.8 %copy-start.12 = (f32[2,256]{1,0:T(2,128)S(1)}, f32[2,256]{1,0:T(2,128)}, u32[]{:S(2)}) copy-start(f32[2,256]{1,0:T(2,128)} %refs_0_.3) | copy-start | bytes 6148
  520.2 14.8 %copy-start.13 = (f32[2,256]{1,0:T(2,128)S(1)}, f32[2,256]{1,0:T(2,128)}, u32[]{:S(2)}) copy-start(f32[2,256]{1,0:T(2,128)} %refs_1_.3) | copy-start | bytes 6148
  520.2 14.8 %copy-start.14 = (f32[2,256]{1,0:T(2,128)S(1)}, f32[2,256]{1,0:T(2,128)}, u32[]{:S(2)}) copy-start(f32[2,256]{1,0:T(2,128)} %refs_2_.3) | copy-start | bytes 6148
Sparse Core Ops, SparseCore 0:
  302.5 166.6 reduce-scatter.1

commit v14 on v13

--- a/solution.py
+++ b/solution.py
@@ -201,10 +201,10 @@
     return lax.dot_general(left, right, (((0,), (0,)), ((), ())), preferred_element_type=jnp.float32)
 
 
-def ff_kernel(n, chunks, lag, eps, branch, gain, x, cot_hbm, w_hbm,
+def ff_kernel(n, chunks, lag, eps, gain, branch_hbm, x_hbm, cot_hbm, w_hbm,
               feed_hbm, middle_hbm, low_hbm, gain_out, grads_hbm,
-              got, sa, ra, sg, rg, two_sum, two_part, weight, cot, normed, hidden, gg, feed,
-              middle_stage, low_stage, unit_stage, w_sem, cot_sem, feed_sem, stage_sem, grad_sem):
+              got, sa, ra, sg, rg, two_sum, two_part, branch, x, weight, cot, normed, hidden, gg, feed,
+              middle_stage, low_stage, unit_stage, w_sem, rows_sem, cot_sem, feed_sem, stage_sem, grad_sem):
     rows, width = branch.shape
     ff = hidden.shape[1]
     rc = rows // (2 * chunks)
@@ -220,6 +220,12 @@
     full, rest = ff // tile, ff % tile
     wide = width // tile
 
+    whole_rows = (
+        pltpu.make_async_copy(branch_hbm, branch, rows_sem.at[0]),
+        pltpu.make_async_copy(x_hbm, x, rows_sem.at[1]),
+    )
+    for copy in whole_rows:
+        copy.start()
     groups = []
     for g, (begin, end) in enumerate(((0, tile), (tile, 2 * tile), (2 * tile, ff))):
         groups.append([
@@ -313,6 +319,9 @@
 
         @pl.when(live & (phase == 0))
         def _():
+            @pl.when(b == 0)
+            def _():
+                wait(whole_rows)
             normalize(b)
             wait(load_cot(b))
 
@@ -429,9 +438,11 @@
             shape((rows, width), low), shape((rows, width), jnp.float32), shape((rows, width), low),
             shape((1, width), jnp.float32), shape((width, 3 * ff), low),
         ),
-        in_specs=[vmem, vmem, vmem, hbm, hbm],
+        in_specs=[vmem] + [hbm] * 4,
         out_specs=(hbm, hbm, hbm, vmem, hbm),
         scratch_shapes=line_scratch(chunks, rc, width) + [
+            pltpu.VMEM((rows, width), low),
+            pltpu.VMEM((rows, width), low),
             pltpu.VMEM((rows, width), low),
             pltpu.VMEM((rows, width), low),
             pltpu.VMEM((width, 3 * ff), low),
@@ -443,12 +454,12 @@
             pltpu.VMEM((2, rc, width), jnp.float32),
             pltpu.VMEM((2, rc, width), low),
             pltpu.VMEM((256, 3 * ff), low),
-            dma((3, 3)), dma((blocks, 2)), dma((2,)), dma((2, 2)), dma((1,)),
+            dma((3, 3)), dma((2,)), dma((blocks, 2)), dma((2,)), dma((2, 2)), dma((1,)),
         ],
         compiler_params=pltpu.CompilerParams(collective_id=cid, has_side_effects=True, vmem_limit_bytes=63 << 20),
         cost_estimate=pl.CostEstimate(flops=18 * rows * width * ff, bytes_accessed=rows * width * 150,
                                       transcendentals=rows * ff),
-    )(branch, gain, x, cot, weight)
+    )(gain, branch, x, cot, weight)
 
 
 def head_kernel(n, m, chunks, lag, eps, size, pairs,

time: 558 us -> 560 us (level)
  transfers between devices with their start and end apart: 1 -> 1, of which waited for: 0 -> 0; matrix products, arithmetic and copies ran while one was open for 0% -> 0% of each run, Pallas kernels for 39% -> 38%
where the time goes in v14:
time: 560 us; the launch traced here: 559 us
  Pallas kernels  540 us (96%)
  between operations  15.1 us (3%)
    pallas_call x1, Pallas kernels, attention_back(): pl.pallas_call(functools.partial(back_kernel, n, m, chunks, lag, norm_eps...  215 us
    pallas_call x1, Pallas kernels, attention_head(): pl.pallas_call(functools.partial(head_kernel, n, m, chunks, lag, norm_eps...  160 us
    pallas_call x1, Pallas kernels, feed_forward(): pl.pallas_call(functools.partial(ff_kernel, n, chunks, lag, norm_eps), ou...  135 us
    pallas_call x1, Pallas kernels, finish_step(): pl.pallas_call(functools.partial(adam_kernel, rates, kv_width), out_shape...  15.8 us
    pallas_call x1, Pallas kernels, finish_step(): pl.pallas_call(functools.partial(norm_kernel, n, m, len(fetched)), out_sh...  14.6 us
  transfers between devices with their start and end apart: 1, of which 0 were waited for; matrix products, arithmetic and copies ran while one was open for 0% of the time, Pallas kernels for 38%

profile of v14, /device:TPU:0, one launch (start us, length us, event | category | flops | bytes accessed | tf_op | source)
XLA Modules:
  0.0 559.4 jit_solution(6738098564066558397)
XLA Ops:
  7.2 0.0 reduce-scatter.2.cloned.1.call-start
  7.2 0.5 fusion.3.frequency
  7.8 0.7 constant_dynamic-update-slice_fusion.gain_part
  8.5 0.0 copy-start.15
  8.5 0.6 copy-done.15
  9.1 159.8 %shard_map.373 = (bf16[1024,2048]{1,0:T(8,128)(2,1)}, f32[2,2048]{1,0:T(2,128)}, f32[4,4,1,512]{3,2,1,0:T(1,128)}, s32[1024,1]{1,0:T(8,128)}, f32[1024,128]{1,0:...) custom-call(f32[2,2048]{1,0:T(2,128)} %copy-done.15, ...), custom_call_target="tpu_custom_call" | custom-call | flops 21474836480 | bytes 356515840 | tf_op jit(solution)/shard_map/pallas_call | solution.py:805
  168.9 135.3 %shard_map.374 = (bf16[1024,2048]{1,0:T(8,128)(2,1)}, f32[1024,2048]{1,0:T(8,128)}, bf16[1024,2048]{1,0:T(8,128)(2,1)}, f32[1,2048]{1,0:T(1,128)}, bf16[2048,4224]{1,0:T(8,128)(2,1)}) custom-call(f32[2,2048]{1,0:T(2,128)} %get-tuple-element.72.gain, bf16[1024,2048]{1,0:T(8,128)(2,1)} %get-tuple-element.73.branch_hbm, bf16[1024,2048]{1,0:T(8,128)(2,1)} %x_hbm.5, ...), custom_call_target="tpu_custom_call" | custom-call | flops 53150220288 | bytes 314572800 | tf_op jit(solution)/shard_map/pallas_call | solution.py:435
  304.2 0.0 reduce-scatter.2.cloned.1.call-update
  305.0 0.1 maximum_divide_fusion.correct_ref
  305.1 0.0 copy-start.16
  305.1 214.8 %shard_map.375 = (bf16[1024,2048]{1,0:T(8,128)(2,1)}, f32[1024,2048]{1,0:T(8,128)}, f32[1,2048]{1,0:T(1,128)}, f32[256,1152]{1,0:T(8,128)}) custom-call(bf16[1024,2048]{1,0:T(8,128)(2,1)} %get-tuple-element.75.feed_part, f32[2,2048]{1,0:T(2,128)} %get-tuple-element.72.gain, f32[4,4,1,512]{3,2,1,0:T(1,128)} %get-tuple-element.76.lse_ref, ...), custom_call_target="tpu_custom_call" | custom-call | flops 42949672960 | bytes 545259520 | tf_op jit(solution)/shard_map/pallas_call | solution.py:1143
  519.8 0.0 copy-done.16
  519.8 0.7 pad_maximum_fusion
  520.5 0.0 reduce-scatter.2.cloned.1.call-done.ff_ref.ff_hbm
  520.6 0.0 copy-start.1
  520.6 1.3 copy-done.1
  521.8 0.0 copy-start
  521.9 0.0 copy-start.2
  521.9 0.0 copy-start.3
  521.9 0.0 copy-start.4
  521.9 0.0 copy-start.5
  521.9 0.0 copy-start.6
  521.9 0.0 copy-start.7
  521.9 0.0 copy-start.8
  521.9 0.0 copy-start.9
  521.9 0.0 copy-start.10
  521.9 0.0 copy-start.11
  521.9 0.0 copy-start.12
  522.0 0.0 copy-start.13
  522.0 0.0 copy-start.14
  522.0 14.6 %shard_map.376 = (f32[8,128]{1,0:T(8,128)S(1)}, f32[2,256]{1,0:T(2,128)S(1)}, f32[2,256,1408]{2,1,0:T(8,128)S(1)}, f32[2,256,1408]{2,1,0:T(8,128)S(1)}, f32[2,25...) custom-call(f32[8,2,256]{2,1,0:T(2,128)S(1)} %bitcast.13, ...), custom_call_target="tpu_custom_call" | custom-call | tf_op jit(solution)/shard_map/pallas_call | solution.py:1398
  536.6 0.0 copy-done
  536.6 0.0 copy-done.2
  536.6 0.0 copy-done.3
  536.6 0.0 copy-done.4
  536.6 0.0 copy-done.5
  536.6 0.0 copy-done.6
  536.6 0.0 copy-done.7
  536.6 0.0 copy-done.8
  536.7 0.0 copy-done.9
  536.7 0.0 copy-done.10
  536.7 0.0 copy-done.11
  536.7 0.0 copy-done.12
  536.7 0.0 copy-done.13
  536.7 0.0 copy-done.14
  536.7 15.8 %shard_map.377 = (f32[1]{0:T(128)}, bf16[1024,2048]{1,0:T(8,128)(2,1)}, f32[1024,2048]{1,0:T(8,128)}, f32[2,256]{1,0:T(2,128)}, f32[2,256]{1,0:T(2,128)}, /*inde...) custom-call(f32[2]{0:T(128)S(1)} %maximum_divide_fusion.correct_ref,, ...), custom_call_target="tpu_custom_call" | custom-call | flops 82606080 | bytes 99127296 | tf_op jit(solution)/shard_map/pallas_call | solution.py:1416
  (1 shorter events, 0.0 us)
Async XLA Ops:
  7.2 513.4 %reduce-scatter.2.cloned.1.call-start = ((), (), s32[]{:S(2)}) async-start(), calls=%async_computation.1 | async-start | bytes 19464192 | tf_op jit(solution)/shard_map/reduce_scatter | solution.py:1487
  8.5 0.6 copy-start.15
  305.1 214.8 %copy-start.16 = (f32[1,2048]{1,0:T(1,128)S(1)}, f32[1,2048]{1,0:T(1,128)}, u32[]{:S(2)}) copy-start(f32[1,2048]{1,0:T(1,128)} %get-tuple-element.89) | copy-start | bytes 24580
  520.6 1.3 copy-start.1
  521.8 14.7 %copy-start = (bf16[256,4224]{1,0:T(8,128)(2,1)S(1)}, bf16[256,4224]{1,0:T(8,128)(2,1)}, u32[]{:S(2)}) copy-start(bf16[256,4224]{1,0:T(8,128)(2,1)} %reduce-scatter.2.cloned.1.call-done.ff_ref.ff_hbm) | copy-start | bytes 6488068
  521.9 14.7 %copy-start.2 = (f32[256,1152]{1,0:T(8,128)S(1)}, f32[256,1152]{1,0:T(8,128)}, u32[]{:S(2)}) copy-start(f32[256,1152]{1,0:T(8,128)} %get-tuple-element.91.head_ref.head_hbm) | copy-start | bytes 3538948
  521.9 14.7 %copy-start.3 = (f32[256,512]{1,0:T(8,128)S(1)}, f32[256,512]{1,0:T(8,128)}, u32[]{:S(2)}) copy-start(f32[256,512]{1,0:T(8,128)} %refs_3_.3) | copy-start | bytes 1572868
  521.9 14.7 %copy-start.4 = (f32[512,256]{1,0:T(8,128)S(1)}, f32[512,256]{1,0:T(8,128)}, u32[]{:S(2)}) copy-start(f32[512,256]{1,0:T(8,128)} %refs_9_.1) | copy-start | bytes 1572868
  521.9 14.8 %copy-start.5 = (f32[256,512]{1,0:T(8,128)S(1)}, f32[256,512]{1,0:T(8,128)}, u32[]{:S(2)}) copy-start(f32[256,512]{1,0:T(8,128)} %refs_4_.3) | copy-start | bytes 1572868
  521.9 14.8 %copy-start.6 = (f32[256,512]{1,0:T(8,128)S(1)}, f32[256,512]{1,0:T(8,128)}, u32[]{:S(2)}) copy-start(f32[256,512]{1,0:T(8,128)} %refs_5_.3) | copy-start | bytes 1572868
  521.9 14.8 %copy-start.7 = (f32[512,256]{1,0:T(8,128)S(1)}, f32[512,256]{1,0:T(8,128)}, u32[]{:S(2)}) copy-start(f32[512,256]{1,0:T(8,128)} %refs_10_.1) | copy-start | bytes 1572868
  521.9 14.7 %copy-start.8 = (f32[512,256]{1,0:T(8,128)S(1)}, f32[512,256]{1,0:T(8,128)}, u32[]{:S(2)}) copy-start(f32[512,256]{1,0:T(8,128)} %refs_11_.1) | copy-start | bytes 1572868
  521.9 14.7 %copy-start.9 = (f32[2,256,64]{1,2,0:T(8,128)S(1)}, f32[2,256,64]{1,2,0:T(8,128)}, u32[]{:S(2)}) copy-start(f32[2,256,64]{1,2,0:T(8,128)} %param.32) | copy-start | bytes 393220
  521.9 14.7 %copy-start.10 = (f32[2,256,64]{1,2,0:T(8,128)S(1)}, f32[2,256,64]{1,2,0:T(8,128)}, u32[]{:S(2)}) copy-start(f32[2,256,64]{1,2,0:T(8,128)} %param.33) | copy-start | bytes 393220
  521.9 14.7 %copy-start.11 = (f32[2,256,64]{1,2,0:T(8,128)S(1)}, f32[2,256,64]{1,2,0:T(8,128)}, u32[]{:S(2)}) copy-start(f32[2,256,64]{1,2,0:T(8,128)} %param.34) | copy-start | bytes 393220
  521.9 14.7 %copy-start.12 = (f32[2,256]{1,0:T(2,128)S(1)}, f32[2,256]{1,0:T(2,128)}, u32[]{:S(2)}) copy-start(f32[2,256]{1,0:T(2,128)} %refs_0_.3) | copy-start | bytes 6148
  522.0 14.7 %copy-start.13 = (f32[2,256]{1,0:T(2,128)S(1)}, f32[2,256]{1,0:T(2,128)}, u32[]{:S(2)}) copy-start(f32[2,256]{1,0:T(2,128)} %refs_1_.3) | copy-start | bytes 6148
  522.0 14.7 %copy-start.14 = (f32[2,256]{1,0:T(2,128)S(1)}, f32[2,256]{1,0:T(2,128)}, u32[]{:S(2)}) copy-start(f32[2,256]{1,0:T(2,128)} %refs_2_.3) | copy-start | bytes 6148
Sparse Core Ops, SparseCore 0:
  304.4 166.6 reduce-scatter.1
